TPU v7x, 32 devices: a whole 2x2x4 slice. The times are simulated.
32 devices in a mesh: ctx: 4 (over y, x), fsdp: 8 (over z, core).
Axes of the slice: x: 2, y: 2, z: 4, core: 2. Of those that a mesh axis runs over, the one named last changes fastest.
Arguments:
- block_in: bfloat16 [8, 2048, 1024], P('fsdp', 'ctx'), may hold values from -6 to 6
- cotangent: bfloat16 [8, 2048, 1024], P('fsdp', 'ctx'), may hold values from -6 to 6
- doc_ids: int32 [8, 2048], P('fsdp', 'ctx'), may hold values from 0 to 1, never falling along the last dimension, each value on 1 to 1536 neighbouring positions
- block_ids: int32 [8, 2048], P('fsdp', 'ctx'), may hold values from 0 to 7, never falling along the last dimension, each value on 1 to 512 neighbouring positions
- gain_attn: bfloat16 [1024], P('fsdp'), may hold values from 0.099609375 to 1.8984375
- w_query: bfloat16 [1024, 1024], P('fsdp'), may hold values from -0.1875 to 0.1875
- w_key: bfloat16 [1024, 1024], P('fsdp'), may hold values from -0.1875 to 0.1875
- w_value: bfloat16 [1024, 1024], P('fsdp'), may hold values from -0.1875 to 0.1875
- w_out: bfloat16 [1024, 1024], P('fsdp'), may hold values from -2 to 2
- gain_ffn: bfloat16 [1024], P('fsdp'), may hold values from 0.099609375 to 1.8984375
- w_gate: bfloat16 [1024, 4096], P('fsdp'), may hold values from -0.1875 to 0.1875
- w_up: bfloat16 [1024, 4096], P('fsdp'), may hold values from -0.1875 to 0.1875
- w_down: bfloat16 [4096, 1024], P('fsdp'), may hold values from -0.09375 to 0.09375
Outputs:
- block_out: bfloat16 [8, 2048, 1024], P('fsdp', 'ctx')
- input_grad: float32 [8, 2048, 1024], P('fsdp', 'ctx')
- grad_gain_attn: float32 [1024], P('fsdp')
- grad_query: float32 [1024, 1024], P('fsdp')
- grad_key: float32 [1024, 1024], P('fsdp')
- grad_value: float32 [1024, 1024], P('fsdp')
- grad_out: float32 [1024, 1024], P('fsdp')
- grad_gain_ffn: float32 [1024], P('fsdp')
- grad_gate: float32 [1024, 4096], P('fsdp')
- grad_up: float32 [1024, 4096], P('fsdp')
- grad_down: float32 [4096, 1024], P('fsdp')
Inputs may be any that keep to these rules, and one draw needn't show every extreme that they name: doc_ids never fall along a sequence; each sequence holds two documents, each of 512 to 1536 tokens. block_ids never fall along a sequence; every block has 1 to 512 tokens, and in every sequence one block has exactly 512 tokens.
All inputs are finite; a program needn't handle non-finite values.
Results may differ from a plain program's by a relative error of at most 0.022.
Values may be sent and summed in bfloat16 or wider, within the bound.
No kernel may reach another device: no remote copies, remote signals or barrier semaphores. Data moves between devices by JAX's collectives and lax.ppermute only.
A program may use at most 192 MiB of HBM per device.

v0:
```python
import jax
import jax.numpy as jnp
from jax import lax
from jax.sharding import PartitionSpec as P

D = 1024
HEADS = 16
HEAD_DIM = 64


NORM_EPS = 1e-05
MASKED = -1e30


def shifted(value, axis, steps):
    count = lax.axis_size(axis)
    pairs = [(source, (source + steps) % count) for source in range(count)]
    return lax.ppermute(value, axis, pairs)


def shortened(shard):
    return jax.tree.map(lambda a: a.astype(jnp.bfloat16) if a.dtype == jnp.float32 else a, shard)


def grouped(values, groups):
    rows = values.shape[0]
    return values.reshape(rows, groups, values.shape[1] // groups).transpose(1, 0, 2)


def ungrouped(values):
    groups, rows, width = values.shape
    return values.transpose(1, 0, 2).reshape(rows, groups * width)


def split_heads(values):
    rows = values.shape[0]
    return values.reshape(rows, values.shape[1] // HEAD_DIM, HEAD_DIM)


def head_scores(q_group, k_group):
    return jnp.einsum(
        "qhd,khd->hqk",
        split_heads(q_group),
        split_heads(k_group),
        preferred_element_type=jnp.float32,
    ) * HEAD_DIM ** (-0.5)


def head_mix(weights, v_group):
    mixed = jnp.einsum(
        "hqk,khd->qhd", weights, split_heads(v_group), preferred_element_type=jnp.float32
    )
    return mixed.reshape(mixed.shape[0], -1)


def key_sum(weights, q_group):
    mixed = jnp.einsum(
        "hqk,qhd->khd", weights, split_heads(q_group), preferred_element_type=jnp.float32
    )
    return mixed.reshape(mixed.shape[0], -1)


def head_cols(per_head):
    return jnp.repeat(per_head.T, HEAD_DIM, axis=1)


def rotate_keys(pair):
    return shifted(pair, "ctx", 1)


def pass_grads(pair):
    return shifted(pair.astype(jnp.bfloat16), "ctx", 1).astype(pair.dtype)


def fetch_attn(gain_attn, w_query, w_key, w_value, w_out):
    return (
        lax.all_gather(gain_attn, "fsdp", axis=0, tiled=True),
        lax.all_gather(w_query, "fsdp", axis=0, tiled=True),
        lax.all_gather(w_key, "fsdp", axis=0, tiled=True),
        lax.all_gather(w_value, "fsdp", axis=0, tiled=True),
        lax.all_gather(w_out, "fsdp", axis=0, tiled=True),
    )


def fetch_ffn(gain_ffn, w_gate, w_up, w_down):
    return (
        lax.all_gather(gain_ffn, "fsdp", axis=0, tiled=True),
        lax.all_gather(w_gate, "fsdp", axis=0, tiled=True),
        lax.all_gather(w_up, "fsdp", axis=0, tiled=True),
        lax.all_gather(w_down, "fsdp", axis=0, tiled=True),
    )


def forward_step(q_groups, pair, allowed, state):

    def forward_one_group(items):
        q_group, k_group, v_group, run_max, run_sum, run_acc = items
        scores = jnp.where(allowed[None], head_scores(q_group, k_group), MASKED)
        new_max = jnp.maximum(run_max, jnp.max(scores, axis=-1))
        weights = jnp.where(allowed[None], jnp.exp(scores - new_max[..., None]), 0.0)
        factor = jnp.exp(run_max - new_max)
        new_sum = run_sum * factor + jnp.sum(weights, axis=-1)
        new_acc = run_acc * head_cols(factor) + head_mix(weights.astype(jnp.bfloat16), v_group)
        return (new_max, new_sum, new_acc)

    return lax.map(forward_one_group, (q_groups, pair[0], pair[1]) + state)


def backward_step(q_groups, do_groups, lse, delta, pair, allowed, dq_acc, dkv_acc):

    def backward_one_group(items):
        (
            q_group,
            do_group,
            k_group,
            v_group,
            lse_group,
            delta_group,
            dq_group,
            dk_group,
            dv_group,
        ) = items
        scores = head_scores(q_group, k_group)
        probs = jnp.where(allowed[None], jnp.exp(scores - lse_group[..., None]), 0.0)
        dv_group = dv_group + key_sum(probs.astype(jnp.bfloat16), do_group)
        dprobs = jnp.einsum(
            "qhd,khd->hqk",
            split_heads(do_group),
            split_heads(v_group),
            preferred_element_type=jnp.float32,
        )
        dscores = (probs * (dprobs - delta_group[..., None])).astype(jnp.bfloat16)
        dq_group = dq_group + head_mix(dscores, k_group) * HEAD_DIM ** (-0.5)
        dk_group = dk_group + key_sum(dscores, q_group) * HEAD_DIM ** (-0.5)
        return (dq_group, dk_group, dv_group)

    dq_new, dk_new, dv_new = lax.map(
        backward_one_group,
        (q_groups, do_groups, pair[0], pair[1], lse, delta, dq_acc, dkv_acc[0], dkv_acc[1]),
    )
    return (dq_new, jnp.stack([dk_new, dv_new]))


def rows_grad(left, right):
    return jnp.einsum("td,te->de", left, right, preferred_element_type=jnp.float32)


def body(
    block_in,
    cotangent,
    doc_ids,
    block_ids,
    gain_attn,
    w_query,
    w_key,
    w_value,
    w_out,
    gain_ffn,
    w_gate,
    w_up,
    w_down,
):
    n_ctx = lax.axis_size("ctx")
    place = lax.axis_index("ctx")
    tok_rows = block_in.shape[1]
    per_group = min(4, HEADS)
    groups = HEADS // per_group
    attn_full = fetch_attn(gain_attn, w_query, w_key, w_value, w_out)
    ffn_full = fetch_ffn(gain_ffn, w_gate, w_up, w_down)
    all_docs, all_blocks = (
        lax.all_gather(doc_ids, "ctx", axis=1, tiled=True),
        lax.all_gather(block_ids, "ctx", axis=1, tiled=True),
    )
    my_docs = doc_ids[0]
    my_blocks = block_ids[0]

    def allowed_for(owner):
        key_docs = lax.dynamic_slice_in_dim(all_docs[0], owner * tok_rows, tok_rows)
        key_blocks = lax.dynamic_slice_in_dim(all_blocks[0], owner * tok_rows, tok_rows)
        return (my_docs[:, None] == key_docs[None, :]) & (key_blocks[None, :] <= my_blocks[:, None])

    g_attn, wq_full, wk_full, wv_full, wo_full = attn_full
    x_rows = block_in[0].astype(jnp.float32)
    inv1 = lax.rsqrt(jnp.mean(x_rows * x_rows, axis=-1, keepdims=True) + NORM_EPS)
    norm_one = x_rows * inv1
    a_one = (norm_one * g_attn.astype(jnp.float32)).astype(jnp.bfloat16)
    query = jnp.dot(a_one, wq_full, preferred_element_type=jnp.float32).astype(jnp.bfloat16)
    keys = jnp.dot(a_one, wk_full, preferred_element_type=jnp.float32).astype(jnp.bfloat16)
    values = jnp.dot(a_one, wv_full, preferred_element_type=jnp.float32).astype(jnp.bfloat16)
    q_groups = grouped(query, groups)
    own_pair = jnp.stack([grouped(keys, groups), grouped(values, groups)])
    start_state = (
        jnp.full((groups, per_group, tok_rows), MASKED, jnp.float32),
        jnp.zeros((groups, per_group, tok_rows), jnp.float32),
        jnp.zeros((groups, tok_rows, D // groups), jnp.float32),
    )
    state = forward_step(q_groups, own_pair, allowed_for(place), start_state)

    def cycle_forward(turn, carry):
        pair, state_now = carry
        pair = rotate_keys(pair)
        state_now = forward_step(q_groups, pair, allowed_for((place - turn) % n_ctx), state_now)
        return (pair, state_now)

    moved_pair, state = lax.fori_loop(1, n_ctx, cycle_forward, (own_pair, state))
    run_max, run_sum, run_acc = state
    lse = run_max + jnp.log(run_sum)
    attended = ungrouped(run_acc / jnp.swapaxes(jnp.repeat(run_sum, HEAD_DIM, axis=1), 1, 2))
    attended_low = attended.astype(jnp.bfloat16)
    hidden = x_rows + jnp.dot(attended_low, wo_full, preferred_element_type=jnp.float32)
    g_ffn, wg_full, wu_full, wd_full = ffn_full
    inv2 = lax.rsqrt(jnp.mean(hidden * hidden, axis=-1, keepdims=True) + NORM_EPS)
    norm_two = hidden * inv2
    a_two = (norm_two * g_ffn.astype(jnp.float32)).astype(jnp.bfloat16)
    gate = jnp.dot(a_two, wg_full, preferred_element_type=jnp.float32)
    upper = jnp.dot(a_two, wu_full, preferred_element_type=jnp.float32)
    sigma = jax.nn.sigmoid(gate)
    silu_gate = gate * sigma
    inner = (silu_gate * upper).astype(jnp.bfloat16)
    block_out = (hidden + jnp.dot(inner, wd_full, preferred_element_type=jnp.float32)).astype(
        jnp.bfloat16
    )
    attn_back = (
        lax.all_gather(gain_attn, "fsdp", axis=0, tiled=True),
        lax.all_gather(w_query, "fsdp", axis=0, tiled=True),
        lax.all_gather(w_key, "fsdp", axis=0, tiled=True),
        lax.all_gather(w_value, "fsdp", axis=0, tiled=True),
        lax.all_gather(w_out, "fsdp", axis=0, tiled=True),
    )
    ffn_back = (
        lax.all_gather(gain_ffn, "fsdp", axis=0, tiled=True),
        lax.all_gather(w_gate, "fsdp", axis=0, tiled=True),
        lax.all_gather(w_up, "fsdp", axis=0, tiled=True),
        lax.all_gather(w_down, "fsdp", axis=0, tiled=True),
    )
    g_attn, wq_full, wk_full, wv_full, wo_full = attn_back
    g_ffn, wg_full, wu_full, wd_full = ffn_back
    cot_rows = cotangent[0]
    grad_wd = rows_grad(inner, cot_rows)
    d_inner = lax.dot_general(
        cot_rows, wd_full, (((1,), (1,)), ((), ())), preferred_element_type=jnp.float32
    )
    d_gate = (d_inner * upper * sigma * (1.0 + gate * (1.0 - sigma))).astype(jnp.bfloat16)
    d_upper = (d_inner * silu_gate).astype(jnp.bfloat16)
    grad_wg = rows_grad(a_two, d_gate)
    grad_wu = rows_grad(a_two, d_upper)
    d_two = lax.dot_general(
        d_gate, wg_full, (((1,), (1,)), ((), ())), preferred_element_type=jnp.float32
    )
    d_two = d_two + lax.dot_general(
        d_upper, wu_full, (((1,), (1,)), ((), ())), preferred_element_type=jnp.float32
    )
    grad_g2 = jnp.sum(d_two * norm_two, axis=0)
    d_norm2 = d_two * g_ffn.astype(jnp.float32)
    d_hidden = cot_rows.astype(jnp.float32) + inv2 * (
        d_norm2 - norm_two * jnp.mean(d_norm2 * norm_two, axis=-1, keepdims=True)
    )
    ffn_shards = (
        lax.psum_scatter(
            grad_g2.astype(jnp.bfloat16), "fsdp", scatter_dimension=0, tiled=True
        ).astype(jnp.float32),
        lax.psum_scatter(
            grad_wg.astype(jnp.bfloat16), "fsdp", scatter_dimension=0, tiled=True
        ).astype(jnp.float32),
        lax.psum_scatter(
            grad_wu.astype(jnp.bfloat16), "fsdp", scatter_dimension=0, tiled=True
        ).astype(jnp.float32),
        lax.psum_scatter(
            grad_wd.astype(jnp.bfloat16), "fsdp", scatter_dimension=0, tiled=True
        ).astype(jnp.float32),
    )
    e_rows = d_hidden.astype(jnp.bfloat16)
    grad_wo = rows_grad(attended_low, e_rows)
    d_att = lax.dot_general(
        e_rows, wo_full, (((1,), (1,)), ((), ())), preferred_element_type=jnp.float32
    ).astype(jnp.bfloat16)
    do_groups = grouped(d_att, groups)
    delta = jnp.sum(
        split_heads(d_att.astype(jnp.float32) * attended).reshape(
            tok_rows, groups, per_group, HEAD_DIM
        ),
        axis=-1,
    ).transpose(1, 2, 0)
    dq_acc = jnp.zeros((groups, tok_rows, D // groups), jnp.float32)
    dkv_acc = jnp.zeros((2, groups, tok_rows, D // groups), jnp.float32)
    dq_acc, dkv_acc = backward_step(
        q_groups, do_groups, lse, delta, own_pair, allowed_for(place), dq_acc, dkv_acc
    )

    def cycle_backward(turn, carry):
        pair, dq_now, dkv_now = carry
        pair = shifted(pair, "ctx", 1)
        dkv_now = pass_grads(dkv_now)
        dq_now, dkv_now = backward_step(
            q_groups,
            do_groups,
            lse,
            delta,
            pair,
            allowed_for((place - turn) % n_ctx),
            dq_now,
            dkv_now,
        )
        return (pair, dq_now, dkv_now)

    last_pair, dq_acc, dkv_acc = lax.fori_loop(
        1, n_ctx, cycle_backward, (own_pair, dq_acc, dkv_acc)
    )
    dkv_acc = pass_grads(dkv_acc)
    d_query = ungrouped(dq_acc).astype(jnp.bfloat16)
    d_keys = ungrouped(dkv_acc[0]).astype(jnp.bfloat16)
    d_values = ungrouped(dkv_acc[1]).astype(jnp.bfloat16)
    grad_wq = rows_grad(a_one, d_query)
    grad_wk = rows_grad(a_one, d_keys)
    grad_wv = rows_grad(a_one, d_values)
    d_one = lax.dot_general(
        d_query, wq_full, (((1,), (1,)), ((), ())), preferred_element_type=jnp.float32
    )
    d_one = d_one + lax.dot_general(
        d_keys, wk_full, (((1,), (1,)), ((), ())), preferred_element_type=jnp.float32
    )
    d_one = d_one + lax.dot_general(
        d_values, wv_full, (((1,), (1,)), ((), ())), preferred_element_type=jnp.float32
    )
    grad_g1 = jnp.sum(d_one * norm_one, axis=0)
    d_norm1 = d_one * g_attn.astype(jnp.float32)
    input_grad = d_hidden + inv1 * (
        d_norm1 - norm_one * jnp.mean(d_norm1 * norm_one, axis=-1, keepdims=True)
    )
    attn_shards = (
        lax.psum_scatter(
            grad_g1.astype(jnp.bfloat16), "fsdp", scatter_dimension=0, tiled=True
        ).astype(jnp.float32),
        lax.psum_scatter(
            grad_wq.astype(jnp.bfloat16), "fsdp", scatter_dimension=0, tiled=True
        ).astype(jnp.float32),
        lax.psum_scatter(
            grad_wk.astype(jnp.bfloat16), "fsdp", scatter_dimension=0, tiled=True
        ).astype(jnp.float32),
        lax.psum_scatter(
            grad_wv.astype(jnp.bfloat16), "fsdp", scatter_dimension=0, tiled=True
        ).astype(jnp.float32),
        lax.psum_scatter(
            grad_wo.astype(jnp.bfloat16), "fsdp", scatter_dimension=0, tiled=True
        ).astype(jnp.float32),
    )
    totals = jax.tree.map(
        lambda part: part.astype(jnp.float32), lax.psum(shortened(attn_shards + ffn_shards), "ctx")
    )
    return (
        block_out.reshape(1, tok_rows, D),
        input_grad.reshape(1, tok_rows, D),
        totals[0],
        totals[1],
        totals[2],
        totals[3],
        totals[4],
        totals[5],
        totals[6],
        totals[7],
        totals[8],
    )


def solution(mesh):
    return jax.shard_map(
        body,
        mesh=mesh,
        in_specs=(
            P("fsdp", "ctx", None),
            P("fsdp", "ctx", None),
            P("fsdp", "ctx"),
            P("fsdp", "ctx"),
            P("fsdp"),
            P("fsdp", None),
            P("fsdp", None),
            P("fsdp", None),
            P("fsdp", None),
            P("fsdp"),
            P("fsdp", None),
            P("fsdp", None),
            P("fsdp", None),
        ),
        out_specs=(
            P("fsdp", "ctx", None),
            P("fsdp", "ctx", None),
            P("fsdp"),
            P("fsdp", None),
            P("fsdp", None),
            P("fsdp", None),
            P("fsdp", None),
            P("fsdp"),
            P("fsdp", None),
            P("fsdp", None),
            P("fsdp", None),
        ),
        check_vma=False,
    )
```

profile of v0, /device:TPU:0, one launch (start us, length us, event | category | flops | bytes accessed | tf_op | source)
XLA Modules:
  0.0 1464.8 jit_solution(15637142796177125039)
XLA Ops:
  13.1 13.4 all-gather
  26.9 8.1 all_gather.45
  34.9 8.0 all_gather.46
  43.0 8.4 all-gather.1
  57.9 13.8 all-gather.10.cloned.1.call-done
  71.7 3.9 convolution_convert_fusion.10
  77.0 24.9 %all-gather.12.cloned.1.call-done = bf16[1024,1024]{1,0:T(8,128)(2,1)} async-done(((bf16[128,1024]{1,0:T(8,128)(2,1)}), bf16[1024,1024]{1,0:T(8,128)(2,1)}) %all-gather.12.cloned.1.call-update) | async-done | bytes 2097168 | tf_op jit(solution)/shard_map/all_gather | solution.py:80
  101.9 3.9 convolution_convert_fusion.9
  108.9 18.1 %while.156 = (s32[]{:T(128)}, f32[4,4,512]{2,1,0:T(4,128)S(1)}, f32[4,4,512]{2,1,0:T(4,128)S(1)}, f32[4,512,256]{1,2,0:T(8,128)}, bf16[4,512,256]{1,2,0:T(8,128)...) while((s32[]{:T(128)}, f32[4,4,512]{2,1,0:T(4,128)S(1)}, ...), condition=%wide.region_4.5_spmd.clone, body=%wide.region_1.4_spmd.clone.sunk | while | flops 282994688 | bytes 17670784 | solution.py:106
  130.3 232.4 %while.153 = (s32[]{:T(128)}, bf16[2,4,512,256]{2,3,1,0:T(8,128)(2,1)}, f32[4,4,512]{2,1,0:T(4,128)S(1)}, f32[4,4,512]{2,1,0:T(4,128)S(1)}, f32[4,512,256]{1,2,0...) while((s32[]{:T(128)}, ...), condition=%wide.region_10.11_spmd, body=%wide.region_5.10_spmd.sunk | while | flops 283123744 | bytes 35005532 | solution.py:205
  131.8 47.4 %collective-permute-done.2 = bf16[2,4,512,256]{2,3,1,0:T(8,128)(2,1)S(1)} collective-permute-done((bf16[2,4,512,256]{2,3,1,0:T(8,128)(2,1)}, bf16[2,4,512,256]{2,3,1,0:T(8,128)(2,1)S(1)}, u32[]{:S(2)}, u32[]{:S(2)}) %collective-permute-start.2) | collective-permute-done | bytes 2097184 | tf_op jit(solution)/shard_map/while/body/eval_jaxpr/ppermute | solution.py:18
  180.7 26.4 %while.158 = (s32[]{:T(128)}, f32[4,4,512]{2,1,0:T(4,128)S(1)}, f32[4,4,512]{2,1,0:T(4,128)S(1)}, f32[4,512,256]{1,2,0:T(8,128)}, bf16[4,512,256]{1,2,0:T(8,128)...) while((s32[]{:T(128)}, f32[4,4,512]{2,1,0:T(4,128)S(1)}, ...), condition=%wide.region_9.9_spmd.clone.clone, body=%wide.region_6.8_spmd.clone.clone.sunk | while | flops 283123712 | bytes 18219652 | solution.py:106
  209.1 47.6 %collective-permute-done.2 = bf16[2,4,512,256]{2,3,1,0:T(8,128)(2,1)S(1)} collective-permute-done((bf16[2,4,512,256]{2,3,1,0:T(8,128)(2,1)}, bf16[2,4,512,256]{2,3,1,0:T(8,128)(2,1)S(1)}, u32[]{:S(2)}, u32[]{:S(2)}) %collective-permute-start.2) | collective-permute-done | bytes 2097184 | tf_op jit(solution)/shard_map/while/body/eval_jaxpr/ppermute | solution.py:18
  258.2 26.4 %while.158 = (s32[]{:T(128)}, f32[4,4,512]{2,1,0:T(4,128)S(1)}, f32[4,4,512]{2,1,0:T(4,128)S(1)}, f32[4,512,256]{1,2,0:T(8,128)}, bf16[4,512,256]{1,2,0:T(8,128)...) while((s32[]{:T(128)}, f32[4,4,512]{2,1,0:T(4,128)S(1)}, ...), condition=%wide.region_9.9_spmd.clone.clone, body=%wide.region_6.8_spmd.clone.clone.sunk | while | flops 283123712 | bytes 18219652 | solution.py:106
  286.0 47.4 %collective-permute-done.2 = bf16[2,4,512,256]{2,3,1,0:T(8,128)(2,1)S(1)} collective-permute-done((bf16[2,4,512,256]{2,3,1,0:T(8,128)(2,1)}, bf16[2,4,512,256]{2,3,1,0:T(8,128)(2,1)S(1)}, u32[]{:S(2)}, u32[]{:S(2)}) %collective-permute-start.2) | collective-permute-done | bytes 2097184 | tf_op jit(solution)/shard_map/while/body/eval_jaxpr/ppermute | solution.py:18
  334.9 26.4 %while.158 = (s32[]{:T(128)}, f32[4,4,512]{2,1,0:T(4,128)S(1)}, f32[4,4,512]{2,1,0:T(4,128)S(1)}, f32[4,512,256]{1,2,0:T(8,128)}, bf16[4,512,256]{1,2,0:T(8,128)...) while((s32[]{:T(128)}, f32[4,4,512]{2,1,0:T(4,128)S(1)}, ...), condition=%wide.region_9.9_spmd.clone.clone, body=%wide.region_6.8_spmd.clone.clone.sunk | while | flops 283123712 | bytes 18219652 | solution.py:106
  362.7 3.3 bitcast_divide_fusion
  368.2 3.9 multiply_reduce_fusion.2
  374.7 11.5 fusion.88
  386.1 11.5 fusion.89
  397.6 16.4 %multiply_convert_fusion.2 = (bf16[512,4096]{1,0:T(8,128)(2,1)}, bf16[512,4096]{1,0:T(8,128)(2,1)}, bf16[512,4096]{1,0:T(8,128)(2,1)}) fusion(f32[512,4096]{1,0:T(8,128)} %fusion.88, f32[512,4096]{1,0:T(8,128)} %fusion.89, bf16[4096,1024]{1,0:T(8,128)(2,1)} %all-gather.22.cloned.1.call-done, bf16[1,512,1024]{2,1,0:T(8,128)(2,1)} %param.26), kind=kOutput, calls=%fused_computation.106 | convolution fusion | flops 4326424576 | bytes 38797312 | tf_op jit(solution)/shard_map/dot_general | solution.py:240
  414.0 8.8 fusion.90
  422.9 7.6 multiply_reduce_fusion
  432.0 3.0 convert_multiply_fusion.1
  439.8 34.9 %while.157 = (s32[]{:T(128)}, f32[4,512,256]{1,2,0:T(8,128)S(1)}, bf16[4,512,256]{1,2,0:T(8,128)(2,1)}, bf16[4,512,256]{1,2,0:T(8,128)(2,1)}, bf16[4,512,256]{1,...) while((s32[]{:T(128)}, f32[4,512,256]{1,2,0:T(8,128)S(1)}, ...), condition=%wide.region_15.16_spmd.clone, body=%wide.region_14.15_spmd.clone.sunk | while | flops 682754048 | bytes 26805404 | solution.py:137
  474.7 3.1 pad_maximum_fusion.1
  477.8 441.2 %while.155 = (s32[]{:T(128)}, bf16[2,4,512,256]{2,3,1,0:T(8,128)(2,1)}, f32[4,512,256]{1,2,0:T(8,128)S(1)}, bf16[2,4,512,256]{2,3,1,0:T(8,128)(2,1)}, s32[1,512]...) while((s32[]{:T(128)}, ...), condition=%wide.region_19.20_spmd, body=%wide.region_16.19_spmd.sunk | while | flops 685375488 | bytes 90253584 | solution.py:306
  480.9 46.8 %collective-permute-done.1 = bf16[2,4,512,256]{2,3,1,0:T(8,128)(2,1)} collective-permute-done((bf16[2,4,512,256]{2,3,1,0:T(8,128)(2,1)}, bf16[2,4,512,256]{2,3,1,0:T(8,128)(2,1)}, u32[]{:S(2)}, u32[]{:S(2)}) %collective-permute-start.1) | collective-permute-done | bytes 2097184 | tf_op jit(solution)/shard_map/while/body/eval_jaxpr/ppermute | solution.py:18
  531.9 37.8 %collective-permute-done = bf16[2,4,512,256]{2,3,1,0:T(8,128)(2,1)} collective-permute-done((bf16[2,4,512,256]{2,3,1,0:T(8,128)(2,1)}, bf16[2,4,512,256]{2,3,1,0:T(8,128)(2,1)}, u32[]{:S(2)}, u32[]{:S(2)}) %collective-permute-start) | collective-permute-done | bytes 2097184 | tf_op jit(solution)/shard_map/while/body/eval_jaxpr/ppermute | solution.py:18
  569.7 3.0 slice_bitcast_fusion.10
  572.7 46.9 %while.159 = (s32[]{:T(128)}, f32[4,512,256]{1,2,0:T(8,128)}, bf16[4,512,256]{1,2,0:T(8,128)(2,1)}, bf16[4,512,256]{1,2,0:T(8,128)(2,1)}, bf16[4,512,256]{1,2,0:...) while((s32[]{:T(128)}, f32[4,512,256]{1,2,0:T(8,128)}, ...), condition=%wide.region_18.18_spmd.clone.clone, body=%wide.region_17.17_spmd.clone.clone.sunk | while | flops 683278336 | bytes 29427368 | solution.py:137
  619.7 3.1 pad_maximum_fusion.4
  622.7 3.2 copy.138
  625.9 2.9 collective-permute-start
  628.9 46.8 %collective-permute-done.1 = bf16[2,4,512,256]{2,3,1,0:T(8,128)(2,1)} collective-permute-done((bf16[2,4,512,256]{2,3,1,0:T(8,128)(2,1)}, bf16[2,4,512,256]{2,3,1,0:T(8,128)(2,1)}, u32[]{:S(2)}, u32[]{:S(2)}) %collective-permute-start.1) | collective-permute-done | bytes 2097184 | tf_op jit(solution)/shard_map/while/body/eval_jaxpr/ppermute | solution.py:18
  679.8 36.9 %collective-permute-done = bf16[2,4,512,256]{2,3,1,0:T(8,128)(2,1)} collective-permute-done((bf16[2,4,512,256]{2,3,1,0:T(8,128)(2,1)}, bf16[2,4,512,256]{2,3,1,0:T(8,128)(2,1)}, u32[]{:S(2)}, u32[]{:S(2)}) %collective-permute-start) | collective-permute-done | bytes 2097184 | tf_op jit(solution)/shard_map/while/body/eval_jaxpr/ppermute | solution.py:18
  716.7 3.0 slice_bitcast_fusion.10
  719.7 46.9 %while.159 = (s32[]{:T(128)}, f32[4,512,256]{1,2,0:T(8,128)}, bf16[4,512,256]{1,2,0:T(8,128)(2,1)}, bf16[4,512,256]{1,2,0:T(8,128)(2,1)}, bf16[4,512,256]{1,2,0:...) while((s32[]{:T(128)}, f32[4,512,256]{1,2,0:T(8,128)}, ...), condition=%wide.region_18.18_spmd.clone.clone, body=%wide.region_17.17_spmd.clone.clone.sunk | while | flops 683278336 | bytes 29427368 | solution.py:137
  766.7 3.1 pad_maximum_fusion.4
  769.7 3.2 copy.138
  775.9 46.8 %collective-permute-done.1 = bf16[2,4,512,256]{2,3,1,0:T(8,128)(2,1)} collective-permute-done((bf16[2,4,512,256]{2,3,1,0:T(8,128)(2,1)}, bf16[2,4,512,256]{2,3,1,0:T(8,128)(2,1)}, u32[]{:S(2)}, u32[]{:S(2)}) %collective-permute-start.1) | collective-permute-done | bytes 2097184 | tf_op jit(solution)/shard_map/while/body/eval_jaxpr/ppermute | solution.py:18
  826.8 36.0 %collective-permute-done = bf16[2,4,512,256]{2,3,1,0:T(8,128)(2,1)} collective-permute-done((bf16[2,4,512,256]{2,3,1,0:T(8,128)(2,1)}, bf16[2,4,512,256]{2,3,1,0:T(8,128)(2,1)}, u32[]{:S(2)}, u32[]{:S(2)}) %collective-permute-start) | collective-permute-done | bytes 2097184 | tf_op jit(solution)/shard_map/while/body/eval_jaxpr/ppermute | solution.py:18
  862.8 3.0 slice_bitcast_fusion.10
  865.8 46.9 %while.159 = (s32[]{:T(128)}, f32[4,512,256]{1,2,0:T(8,128)}, bf16[4,512,256]{1,2,0:T(8,128)(2,1)}, bf16[4,512,256]{1,2,0:T(8,128)(2,1)}, bf16[4,512,256]{1,2,0:...) while((s32[]{:T(128)}, f32[4,512,256]{1,2,0:T(8,128)}, ...), condition=%wide.region_18.18_spmd.clone.clone, body=%wide.region_17.17_spmd.clone.clone.sunk | while | flops 683278336 | bytes 29427368 | solution.py:137
  912.7 3.1 pad_maximum_fusion.4
  915.8 3.2 copy.138
  925.0 4.2 convolution_convert_fusion.3
  929.3 43.9 %collective-permute-done.3 = bf16[2,4,512,256]{2,3,1,0:T(8,128)(2,1)S(1)} collective-permute-done((bf16[2,4,512,256]{2,3,1,0:T(8,128)(2,1)}, bf16[2,4,512,256]{2,3,1,0:T(8,128)(2,1)S(1)}, u32[]{:S(2)}, u32[]{:S(2)}) %collective-permute-start.3) | collective-permute-done | bytes 2097184 | tf_op jit(solution)/shard_map/ppermute | solution.py:18
  978.3 4.0 convolution_convert_fusion.4
  982.6 10.4 convolution_convert_fusion.2
  993.0 10.4 convolution_convert_fusion.1
  1003.8 10.3 convolution_convert_fusion
  1014.2 17.3 %reduce-scatter.10.cloned.1.call-done = bf16[128,1024]{1,0:T(8,128)(2,1)} async-done(((bf16[1024,1024]{1,0:T(8,128)(2,1)}), bf16[128,1024]{1,0:T(8,128)(2,1)}) %reduce-scatter.10.cloned.1.call-update) | async-done | bytes 262160 | tf_op jit(solution)/shard_map/reduce_scatter | solution.py:337
  1031.6 37.4 %reduce-scatter.12.cloned.1.call-done = bf16[128,1024]{1,0:T(8,128)(2,1)} async-done(((bf16[1024,1024]{1,0:T(8,128)(2,1)}), bf16[128,1024]{1,0:T(8,128)(2,1)}) %reduce-scatter.12.cloned.1.call-update) | async-done | bytes 262160 | tf_op jit(solution)/shard_map/reduce_scatter | solution.py:340
  1068.9 90.4 %reduce-scatter.16.cloned.1.call-done = bf16[128,4096]{1,0:T(8,128)(2,1)} async-done(((bf16[1024,4096]{1,0:T(8,128)(2,1)}), bf16[128,4096]{1,0:T(8,128)(2,1)}) %reduce-scatter.16.cloned.1.call-update) | async-done | bytes 1048592 | tf_op jit(solution)/shard_map/reduce_scatter | solution.py:262
  1159.3 90.3 %reduce-scatter.18.cloned.1.call-done = bf16[128,4096]{1,0:T(8,128)(2,1)} async-done(((bf16[1024,4096]{1,0:T(8,128)(2,1)}), bf16[128,4096]{1,0:T(8,128)(2,1)}) %reduce-scatter.18.cloned.1.call-update) | async-done | bytes 1048592 | tf_op jit(solution)/shard_map/reduce_scatter | solution.py:265
  1249.6 90.1 %reduce-scatter.20.cloned.1.call-done = bf16[512,1024]{1,0:T(8,128)(2,1)} async-done(((bf16[4096,1024]{1,0:T(8,128)(2,1)}), bf16[512,1024]{1,0:T(8,128)(2,1)}) %reduce-scatter.20.cloned.1.call-update) | async-done | bytes 1048592 | tf_op jit(solution)/shard_map/reduce_scatter | solution.py:268
  1341.7 3.4 fusion.91
  1345.4 8.4 fusion.69
  1355.9 3.2 fusion.65
  1359.1 13.6 all-reduce.2
  1372.8 9.9 all-reduce.3
  1383.7 3.4 fusion.64
  1387.2 61.5 %all-reduce.7.cloned.1.call-done = (bf16[128,1024]{1,0:T(8,128)(2,1)}, bf16[128,1024]{1,0:T(8,128)(2,1)}, bf16[128,1024]{1,0:T(8,128)(2,1)}, bf16[128,1024]{1,0:...) async-done(((bf16[128,1024]{1,0:T(8,128)(2,1)}, bf16[128,1024]{1,0:T(8,128)(2,1)}, bf16[128,1024]{1,0:T(8,128)(2,1)}, ...) | async-done | bytes 4194320 | tf_op jit(solution)/shard_map/psum | solution.py:348
  (553 shorter events, 358.0 us)
Async XLA Ops:
  7.2 47.1 %all-gather.14.cloned.1.call-start = ((), (), s32[]{:S(2)}) async-start(), calls=%async_computation.9 | async-start | bytes 2359296 | tf_op jit(solution)/shard_map/all_gather | solution.py:78
  7.9 63.8 %all-gather.10.cloned.1.call-start = ((), (), s32[]{:S(2)}) async-start(), calls=%async_computation.7 | async-start | bytes 2359296 | tf_op jit(solution)/shard_map/all_gather | solution.py:79
  8.7 93.3 %all-gather.12.cloned.1.call-start = ((), (), s32[]{:S(2)}) async-start(), calls=%async_computation.8 | async-start | bytes 2359296 | tf_op jit(solution)/shard_map/all_gather | solution.py:80
  9.4 358.8 %all-gather.16.cloned.1.call-start = ((), (), s32[]{:S(2)}) async-start(), calls=%async_computation.10 | async-start | bytes 2359296 | tf_op jit(solution)/shard_map/all_gather | solution.py:81
  10.0 3.1 copy-start.41
  10.0 16.6 %copy-start.7 = (bf16[1,512,1024]{2,1,0:T(8,128)(2,1)S(1)}, bf16[1,512,1024]{2,1,0:T(8,128)(2,1)}, u32[]{:S(2)}) copy-start(bf16[1,512,1024]{2,1,0:T(8,128)(2,1)} %param.25) | copy-start | bytes 3145732
  10.0 364.7 %all-gather.18.cloned.1.call-start = ((), (), s32[]{:S(2)}) async-start(), calls=%async_computation.11 | async-start | bytes 9437184 | tf_op jit(solution)/shard_map/all_gather | solution.py:88
  10.6 16.3 %copy-start.14 = (s32[1,512]{1,0:T(1,128)S(1)}, s32[1,512]{1,0:T(1,128)}, u32[]{:S(2)}) copy-start(s32[1,512]{1,0:T(1,128)} %param.27) | copy-start | bytes 6148
  10.6 24.3 %copy-start.15 = (s32[1,512]{1,0:T(1,128)S(1)}, s32[1,512]{1,0:T(1,128)}, u32[]{:S(2)}) copy-start(s32[1,512]{1,0:T(1,128)} %param.28) | copy-start | bytes 6148
  10.6 32.4 %copy-start.42 = (bf16[128]{0:T(256)(128)(2,1)S(1)}, bf16[128]{0:T(256)(128)(2,1)}, u32[]{:S(2)}) copy-start(bf16[128]{0:T(256)(128)(2,1)} %param.34) | copy-start | bytes 772
  10.6 375.5 %all-gather.20.cloned.1.call-start = ((), (), s32[]{:S(2)}) async-start(), calls=%async_computation.12 | async-start | bytes 9437184 | tf_op jit(solution)/shard_map/all_gather | solution.py:89
  11.2 386.4 %all-gather.22.cloned.1.call-start = ((), (), s32[]{:S(2)}) async-start(), calls=%async_computation.13 | async-start | bytes 9437184 | tf_op jit(solution)/shard_map/all_gather | solution.py:90
  11.9 1002.3 %reduce-scatter.8.cloned.1.call-start = ((), (), s32[]{:S(2)}) async-start(), calls=%async_computation.14 | async-start | bytes 2359296 | tf_op jit(solution)/shard_map/reduce_scatter | solution.py:334
  26.5 75.4 %copy-start.35 = (f32[8,1,128]{2,1,0:T(1,128)}, f32[8,1,128]{2,1,0:T(1,128)S(1)}, u32[]{:S(2)}) copy-start(f32[8,1,128]{2,1,0:T(1,128)S(1)} %convert_element_type.278) | copy-start | bytes 12292
  26.8 75.1 %copy-start.38 = (f32[512]{0:T(512)}, f32[512]{0:T(512)S(1)}, u32[]{:S(2)}) copy-start(f32[512]{0:T(512)S(1)} %add_rsqrt_fusion.1) | copy-start | bytes 6148
  128.3 2.0 copy-start.10
  130.3 48.9 %collective-permute-start.2 = (bf16[2,4,512,256]{2,3,1,0:T(8,128)(2,1)}, bf16[2,4,512,256]{2,3,1,0:T(8,128)(2,1)S(1)}, u32[]{:S(2)}, u32[]{:S(2)}) collective-permute-start(bf16[2,4,512,256]{2,3,1,0:T(8,128)(2,1)} %get-tuple-element.2017), channel_id=1, source_target_pairs={{0,8},{8,16},{16,24},{24,0},{1,9},{9,17},{17,25},{25,1},{2,10},{10... | collective-permute-start | bytes 6291464 | tf_op jit(solution)/shard_map/while/body/eval_jaxpr/ppermute | solution.py:18
  208.5 48.2 %collective-permute-start.2 = (bf16[2,4,512,256]{2,3,1,0:T(8,128)(2,1)}, bf16[2,4,512,256]{2,3,1,0:T(8,128)(2,1)S(1)}, u32[]{:S(2)}, u32[]{:S(2)}) collective-permute-start(bf16[2,4,512,256]{2,3,1,0:T(8,128)(2,1)} %get-tuple-element.2017), channel_id=1, source_target_pairs={{0,8},{8,16},{16,24},{24,0},{1,9},{9,17},{17,25},{25,1},{2,10},{10... | collective-permute-start | bytes 6291464 | tf_op jit(solution)/shard_map/while/body/eval_jaxpr/ppermute | solution.py:18
  286.0 47.4 %collective-permute-start.2 = (bf16[2,4,512,256]{2,3,1,0:T(8,128)(2,1)}, bf16[2,4,512,256]{2,3,1,0:T(8,128)(2,1)S(1)}, u32[]{:S(2)}, u32[]{:S(2)}) collective-permute-start(bf16[2,4,512,256]{2,3,1,0:T(8,128)(2,1)} %get-tuple-element.2017), channel_id=1, source_target_pairs={{0,8},{8,16},{16,24},{24,0},{1,9},{9,17},{17,25},{25,1},{2,10},{10... | collective-permute-start | bytes 6291464 | tf_op jit(solution)/shard_map/while/body/eval_jaxpr/ppermute | solution.py:18
  362.7 3.3 copy-start.17
  368.1 62.9 %copy-start.6 = (f32[512,1024]{1,0:T(8,128)}, f32[512,1024]{1,0:T(8,128)S(1)}, u32[]{:S(2)}) copy-start(f32[512,1024]{1,0:T(8,128)S(1)} %copy.52) | copy-start | bytes 6291460
  368.1 4.0 copy-start.18
  368.1 5.3 copy-start.37
  414.0 8.8 copy-start.12
  414.0 8.9 copy-start.43
  422.9 7.6 copy-start.24
  430.4 1.6 copy-start.20
  432.0 3.0 copy-start.2
  437.3 2.6 copy-start.32
  437.3 2.6 copy-start.34
  477.9 49.8 %copy-start = (f32[4,512,256]{1,2,0:T(8,128)}, f32[4,512,256]{1,2,0:T(8,128)S(1)}, u32[]{:S(2)}) copy-start(f32[4,512,256]{1,2,0:T(8,128)S(1)} %get-tuple-element.2119) | copy-start | bytes 6291460 | tf_op jit(solution)/shard_map/while
  478.0 49.8 %collective-permute-start.1 = (bf16[2,4,512,256]{2,3,1,0:T(8,128)(2,1)}, bf16[2,4,512,256]{2,3,1,0:T(8,128)(2,1)}, u32[]{:S(2)}, u32[]{:S(2)}) collective-permute-start(bf16[2,4,512,256]{2,3,1,0:T(8,128)(2,1)} %get-tuple-element.2120), channel_id=1, source_target_pairs={{0,8},{8,16},{16,24},{24,0},{1,9},{9,17},{17,25},{25,1},{2,10},{10... | collective-permute-start | bytes 6291464 | tf_op jit(solution)/shard_map/while/body/eval_jaxpr/ppermute | solution.py:18
  478.0 91.7 %collective-permute-start = (bf16[2,4,512,256]{2,3,1,0:T(8,128)(2,1)}, bf16[2,4,512,256]{2,3,1,0:T(8,128)(2,1)}, u32[]{:S(2)}, u32[]{:S(2)}) collective-permute-start(bf16[2,4,512,256]{2,3,1,0:T(8,128)(2,1)} %get-tuple-element.2118), channel_id=1, source_target_pairs={{0,8},{8,16},{16,24},{24,0},{1,9},{9,17},{17,25},{25,1},{2,10},{10... | collective-permute-start | bytes 6291464 | tf_op jit(solution)/shard_map/while/body/eval_jaxpr/ppermute | solution.py:18
  622.7 3.2 copy-start.1
  625.9 49.8 %copy-start = (f32[4,512,256]{1,2,0:T(8,128)}, f32[4,512,256]{1,2,0:T(8,128)S(1)}, u32[]{:S(2)}) copy-start(f32[4,512,256]{1,2,0:T(8,128)S(1)} %get-tuple-element.2119) | copy-start | bytes 6291460 | tf_op jit(solution)/shard_map/while
  625.9 49.8 %collective-permute-start.1 = (bf16[2,4,512,256]{2,3,1,0:T(8,128)(2,1)}, bf16[2,4,512,256]{2,3,1,0:T(8,128)(2,1)}, u32[]{:S(2)}, u32[]{:S(2)}) collective-permute-start(bf16[2,4,512,256]{2,3,1,0:T(8,128)(2,1)} %get-tuple-element.2120), channel_id=1, source_target_pairs={{0,8},{8,16},{16,24},{24,0},{1,9},{9,17},{17,25},{25,1},{2,10},{10... | collective-permute-start | bytes 6291464 | tf_op jit(solution)/shard_map/while/body/eval_jaxpr/ppermute | solution.py:18
  625.9 90.8 %collective-permute-start = (bf16[2,4,512,256]{2,3,1,0:T(8,128)(2,1)}, bf16[2,4,512,256]{2,3,1,0:T(8,128)(2,1)}, u32[]{:S(2)}, u32[]{:S(2)}) collective-permute-start(bf16[2,4,512,256]{2,3,1,0:T(8,128)(2,1)} %get-tuple-element.2118), channel_id=1, source_target_pairs={{0,8},{8,16},{16,24},{24,0},{1,9},{9,17},{17,25},{25,1},{2,10},{10... | collective-permute-start | bytes 6291464 | tf_op jit(solution)/shard_map/while/body/eval_jaxpr/ppermute | solution.py:18
  769.7 3.2 copy-start.1
  772.9 49.8 %copy-start = (f32[4,512,256]{1,2,0:T(8,128)}, f32[4,512,256]{1,2,0:T(8,128)S(1)}, u32[]{:S(2)}) copy-start(f32[4,512,256]{1,2,0:T(8,128)S(1)} %get-tuple-element.2119) | copy-start | bytes 6291460 | tf_op jit(solution)/shard_map/while
  772.9 49.8 %collective-permute-start.1 = (bf16[2,4,512,256]{2,3,1,0:T(8,128)(2,1)}, bf16[2,4,512,256]{2,3,1,0:T(8,128)(2,1)}, u32[]{:S(2)}, u32[]{:S(2)}) collective-permute-start(bf16[2,4,512,256]{2,3,1,0:T(8,128)(2,1)} %get-tuple-element.2120), channel_id=1, source_target_pairs={{0,8},{8,16},{16,24},{24,0},{1,9},{9,17},{17,25},{25,1},{2,10},{10... | collective-permute-start | bytes 6291464 | tf_op jit(solution)/shard_map/while/body/eval_jaxpr/ppermute | solution.py:18
  772.9 89.9 %collective-permute-start = (bf16[2,4,512,256]{2,3,1,0:T(8,128)(2,1)}, bf16[2,4,512,256]{2,3,1,0:T(8,128)(2,1)}, u32[]{:S(2)}, u32[]{:S(2)}) collective-permute-start(bf16[2,4,512,256]{2,3,1,0:T(8,128)(2,1)} %get-tuple-element.2118), channel_id=1, source_target_pairs={{0,8},{8,16},{16,24},{24,0},{1,9},{9,17},{17,25},{25,1},{2,10},{10... | collective-permute-start | bytes 6291464 | tf_op jit(solution)/shard_map/while/body/eval_jaxpr/ppermute | solution.py:18
  915.8 3.2 copy-start.1
  919.0 1.6 copy-start.39
  923.4 1.6 copy-start.3
  923.4 90.8 %reduce-scatter.14.cloned.1.call-start = ((), (), s32[]{:S(2)}) async-start(), calls=%async_computation.17 | async-start | bytes 2359296 | tf_op jit(solution)/shard_map/reduce_scatter | solution.py:343
  929.2 102.4 %reduce-scatter.10.cloned.1.call-start = ((), (), s32[]{:S(2)}) async-start(), calls=%async_computation.15 | async-start | bytes 2359296 | tf_op jit(solution)/shard_map/reduce_scatter | solution.py:337
  929.2 46.2 %copy-start.9 = (bf16[1,512,1024]{2,1,0:T(8,128)(2,1)S(1)}, bf16[1,512,1024]{2,1,0:T(8,128)(2,1)}, u32[]{:S(2)}) copy-start(bf16[1,512,1024]{2,1,0:T(8,128)(2,1)} %param.25) | copy-start | bytes 3145732
  929.2 44.0 %collective-permute-start.3 = (bf16[2,4,512,256]{2,3,1,0:T(8,128)(2,1)}, bf16[2,4,512,256]{2,3,1,0:T(8,128)(2,1)S(1)}, u32[]{:S(2)}, u32[]{:S(2)}) collective-permute-start(bf16[2,4,512,256]{2,3,1,0:T(8,128)(2,1)} %get-tuple-element.854), channel_id=1, source_target_pairs={{0,8},{8,16},{16,24},{24,0},{1,9},{9,17},{17,25},{25,1},{2,10},{10... | collective-permute-start | bytes 6291464 | tf_op jit(solution)/shard_map/ppermute | solution.py:18
  978.2 90.7 %reduce-scatter.12.cloned.1.call-start = ((), (), s32[]{:S(2)}) async-start(), calls=%async_computation.16 | async-start | bytes 2359296 | tf_op jit(solution)/shard_map/reduce_scatter | solution.py:340
  982.3 177.0 %reduce-scatter.16.cloned.1.call-start = ((), (), s32[]{:S(2)}) async-start(), calls=%async_computation.18 | async-start | bytes 9437184 | tf_op jit(solution)/shard_map/reduce_scatter | solution.py:262
  993.0 256.6 %reduce-scatter.18.cloned.1.call-start = ((), (), s32[]{:S(2)}) async-start(), calls=%async_computation.19 | async-start | bytes 9437184 | tf_op jit(solution)/shard_map/reduce_scatter | solution.py:265
  1003.5 336.3 %reduce-scatter.20.cloned.1.call-start = ((), (), s32[]{:S(2)}) async-start(), calls=%async_computation.20 | async-start | bytes 9437184 | tf_op jit(solution)/shard_map/reduce_scatter | solution.py:268
  1014.1 434.5 %all-reduce.7.cloned.1.call-start = ((), (), s32[]{:S(2)}) async-start(), calls=%async_computation.21 | async-start | bytes 8388608 | tf_op jit(solution)/shard_map/psum | solution.py:348
  1341.6 3.4 copy-start.13
  1341.6 3.8 copy-start.46
  1345.4 8.4 copy-start.26
  1345.4 8.4 copy-start.44
  1353.8 2.1 copy-start.19
  1355.9 3.2 copy-start.40
  1448.7 2.9 copy-start.23
  1453.0 1.6 copy-start.30
  1453.0 2.4 copy-start.29
  1453.0 3.3 copy-start.28
  1453.0 4.1 copy-start.27
  (12 other events, 14.9 us)
Sparse Core Ops, SparseCore 0:
  9.6 31.8 all-gather.13
  43.1 28.5 all-gather.9
  73.3 28.5 all-gather.11
  103.4 28.5 all-gather.15
  133.4 81.5 all-gather.17
  216.5 80.5 all-gather.19
  298.7 80.5 all-gather.21
  923.5 34.0 reduce-scatter.7
  959.9 34.2 reduce-scatter.13
  996.9 34.6 reduce-scatter.9
  1034.4 34.4 reduce-scatter.11
  1071.1 88.1 reduce-scatter.15
  1161.6 87.9 reduce-scatter.17
  1251.8 87.9 reduce-scatter.19
  1344.1 104.5 all-reduce.6
where the time goes:
time: 1470 us; the launch traced here: 1460 us
  waiting for transfers between devices  868 us (59%)
  matrix products  246 us (17%)
  other arithmetic  144 us (10%)
  local copies, waits for them, and re-layouts  116 us (8%)
  blocking collectives  61.3 us (4%)
  between operations  15.4 us (1%)
    ppermute x10, waiting for transfers between devices, shifted(): return lax.ppermute(value, axis, pairs)  438 us
    reduce_scatter x1, waiting for transfers between devices, body(): lax.psum_scatter(grad_wg.astype(jnp.bfloat16), 'fsdp', scatter_dimension=...  90.4 us
    reduce_scatter x1, waiting for transfers between devices, body(): lax.psum_scatter(grad_wu.astype(jnp.bfloat16), 'fsdp', scatter_dimension=...  90.3 us
    reduce_scatter x1, waiting for transfers between devices, body(): lax.psum_scatter(grad_wd.astype(jnp.bfloat16), 'fsdp', scatter_dimension=...  90.1 us
    dynamic_update_slice x64, other arithmetic, forward_step(): return lax.map(forward_one_group, (q_groups, pair[0], pair[1]) + state)  77.9 us
    psum x1, waiting for transfers between devices, body(): lax.psum(shortened(attn_shards + ffn_shards), 'ctx')  61.5 us
    dynamic_slice x64, local copies, waits for them, and re-layouts, forward_step(): return lax.map(forward_one_group, (q_groups, pair[0], pair[1]) + state)  46.3 us
    dot_general x7, matrix products, rows_grad(): jnp.einsum('td,te->de', left, right, preferred_element_type=jnp.float32)  44.9 us
  transfers between devices with their start and end apart: 25, of which 18 were waited for; matrix products, arithmetic and copies ran while one was open for 16% of the time, Pallas kernels for 0%

commit v1 on v0

v1 whole, which is shorter than its diff:
```python
import functools

import jax
import jax.numpy as jnp
from jax import lax
from jax.experimental import pallas as pl
from jax.experimental.pallas import tpu as pltpu
from jax.sharding import Mesh
from jax.sharding import PartitionSpec as P

HEAD_DIM = 64
NORM_EPS = 1e-05
MASKED = -1e30
START_MAX = -1e29
SCALE = HEAD_DIM ** (-0.5)
BQ = 256
BK = 256
F32 = jnp.float32
BF16 = jnp.bfloat16
NT = (((1,), (1,)), ((), ()))
TN = (((0,), (0,)), ((), ()))


def mm(a, b):
    return jnp.dot(a, b, preferred_element_type=F32)


def mm_nt(a, b):
    return lax.dot_general(a, b, NT, preferred_element_type=F32)


def mm_tn(a, b):
    return lax.dot_general(a, b, TN, preferred_element_type=F32)


def head_stack(rows, heads):
    lane = lax.broadcasted_iota(jnp.int32, rows.shape, 1) // HEAD_DIM
    return jnp.concatenate(
        [jnp.where(lane == h, rows, jnp.zeros_like(rows)) for h in range(heads)], axis=0
    )


def tile_place(tile, per_piece, chip):
    return ((tile // per_piece) ^ chip) * per_piece + tile % per_piece


def allowed_tile(doc_col, blk_col, doc_row, blk_row, k_at, q_at, heads):
    kd, kb = doc_col[pl.ds(k_at, BK), :], blk_col[pl.ds(k_at, BK), :]
    qd, qb = doc_row[:, pl.ds(q_at, BQ)], blk_row[:, pl.ds(q_at, BQ)]
    ok = (kd == qd) & (kb <= qb)
    return jnp.concatenate([ok] * heads, axis=1)


def attend_kernel(heads, piece, info, qkv, doc_col, blk_col, doc_row, blk_row, out, lse, v_t):
    width = heads * HEAD_DIM
    step = pl.program_id(0)
    chip = info[0]
    tiles = qkv.shape[0] // BQ

    @pl.when(step == 0)
    def _():
        v_t[...] = qkv[:, 2 * width : 3 * width].T

    at = tile_place(step, piece // BQ, chip)
    q_at = pl.multiple_of(at * BQ, BQ)
    q_rows = qkv[pl.ds(pl.multiple_of(step * BQ, BQ), BQ), 0:width] * jnp.asarray(SCALE, BF16)
    q_heads = head_stack(q_rows, heads)

    def one(j, carry):
        run_max, run_sum, accs = carry
        k_at = pl.multiple_of(j * BK, BK)
        pos = pl.multiple_of(tile_place(j, piece // BK, chip) * BK, BK)
        keys = qkv[pl.ds(pos, BK), width : 2 * width]
        scores = mm_nt(keys, q_heads)
        ok = allowed_tile(doc_col, blk_col, doc_row, blk_row, k_at, q_at, heads)
        scores = jnp.where(ok, scores, MASKED)
        new_max = jnp.maximum(run_max, jnp.max(scores, axis=0, keepdims=True))
        weights = jnp.exp(scores - new_max)
        factor = jnp.exp(run_max - new_max)
        new_sum = run_sum * factor + jnp.sum(weights, axis=0, keepdims=True)
        weights = weights.astype(BF16)
        new_accs = []
        for h in range(heads):
            v_head = v_t[h * HEAD_DIM : (h + 1) * HEAD_DIM, pl.ds(pos, BK)]
            part = slice(h * BQ, (h + 1) * BQ)
            new_accs.append(accs[h] * factor[:, part] + mm(v_head, weights[:, part]))
        return new_max, new_sum, tuple(new_accs)

    start = (
        jnp.full((1, heads * BQ), START_MAX, F32),
        jnp.zeros((1, heads * BQ), F32),
        tuple(jnp.zeros((HEAD_DIM, BQ), F32) for _ in range(heads)),
    )
    run_max, run_sum, accs = lax.fori_loop(info[1 + at], info[1 + tiles + at], one, start)
    outs = [accs[h] / run_sum[:, h * BQ : (h + 1) * BQ] for h in range(heads)]
    out[...] = jnp.concatenate(outs, axis=0).T.astype(BF16)
    logs = run_max + jnp.log(run_sum)
    for h in range(heads):
        lse[h : h + 1, :] = logs[:, h * BQ : (h + 1) * BQ]


def attend_back_kernel(
    heads, piece, info, qkv, mixed, d_mixed, lse, doc_col, blk_col, doc_row, blk_row, out, k_t, dk, dv
):
    width = heads * HEAD_DIM
    step = pl.program_id(0)
    chip = info[0]
    tiles = qkv.shape[0] // BQ

    @pl.when(step == 0)
    def _():
        k_t[...] = qkv[:, width : 2 * width].T
        dk[...] = jnp.zeros_like(dk)
        dv[...] = jnp.zeros_like(dv)

    at = tile_place(step, piece // BQ, chip)
    q_at = pl.multiple_of(at * BQ, BQ)
    rows = pl.ds(pl.multiple_of(step * BQ, BQ), BQ)
    q_heads = head_stack(qkv[rows, 0:width] * jnp.asarray(SCALE, BF16), heads)
    do_rows = d_mixed[...]
    do_heads = head_stack(do_rows, heads)
    prod = (do_rows.astype(F32) * mixed[...].astype(F32)).T
    delta = jnp.concatenate(
        [
            jnp.sum(prod[h * HEAD_DIM : (h + 1) * HEAD_DIM], axis=0, keepdims=True)
            for h in range(heads)
        ],
        axis=1,
    )
    logs = jnp.concatenate([lse[h : h + 1, :] for h in range(heads)], axis=1)

    def one(j, dqs):
        k_at = pl.multiple_of(j * BK, BK)
        pos = pl.multiple_of(tile_place(j, piece // BK, chip) * BK, BK)
        keys = qkv[pl.ds(pos, BK), width : 2 * width]
        values = qkv[pl.ds(pos, BK), 2 * width : 3 * width]
        scores = mm_nt(keys, q_heads)
        ok = allowed_tile(doc_col, blk_col, doc_row, blk_row, k_at, q_at, heads)
        probs = jnp.where(ok, jnp.exp(scores - logs), 0.0)
        d_probs = mm_nt(values, do_heads)
        d_scores = (probs * (d_probs - delta)).astype(BF16)
        dv[pl.ds(pos, BK), :] += mm(probs.astype(BF16), do_heads)
        dk[pl.ds(pos, BK), :] += mm(d_scores, q_heads)
        new = []
        for h in range(heads):
            k_head = k_t[h * HEAD_DIM : (h + 1) * HEAD_DIM, pl.ds(pos, BK)]
            new.append(dqs[h] + mm(k_head, d_scores[:, h * BQ : (h + 1) * BQ]))
        return tuple(new)

    dqs = lax.fori_loop(
        info[1 + at],
        info[1 + tiles + at],
        one,
        tuple(jnp.zeros((HEAD_DIM, BQ), F32) for _ in range(heads)),
    )
    out[rows, 0:width] = (jnp.concatenate(dqs, axis=0) * SCALE).T.astype(BF16)

    @pl.when(step == tiles - 1)
    def _():
        out[:, width : 2 * width] = dk[...].astype(BF16)
        out[:, 2 * width : 3 * width] = dv[...].astype(BF16)


def whole_spec(shape):
    return pl.BlockSpec(shape, lambda *_: (0,) * len(shape))


def attend(qkv, ids, piece):
    info, doc_col, blk_col, doc_row, blk_row = ids
    rows, width3 = qkv.shape
    width = width3 // 3
    heads = width // HEAD_DIM
    grid_spec = pltpu.PrefetchScalarGridSpec(
        num_scalar_prefetch=1,
        grid=(rows // BQ,),
        in_specs=[
            whole_spec((rows, width3)),
            whole_spec((rows, 1)),
            whole_spec((rows, 1)),
            whole_spec((1, rows)),
            whole_spec((1, rows)),
        ],
        out_specs=[
            pl.BlockSpec((BQ, width), lambda i, *_: (i, 0)),
            pl.BlockSpec((heads, BQ), lambda i, *_: (0, i)),
        ],
        scratch_shapes=[pltpu.VMEM((width, rows), BF16)],
    )
    return pl.pallas_call(
        functools.partial(attend_kernel, heads, piece),
        out_shape=[
            jax.ShapeDtypeStruct((rows, width), BF16),
            jax.ShapeDtypeStruct((heads, rows), F32),
        ],
        grid_spec=grid_spec,
        cost_estimate=pl.CostEstimate(
            flops=8 * rows * rows * width, bytes_accessed=16 * rows * width, transcendentals=rows * rows
        ),
        name="attend",
    )(info, qkv, doc_col, blk_col, doc_row, blk_row)


def attend_back(qkv, mixed, d_mixed, lse, ids, piece):
    info, doc_col, blk_col, doc_row, blk_row = ids
    rows, width3 = qkv.shape
    width = width3 // 3
    heads = width // HEAD_DIM
    grid_spec = pltpu.PrefetchScalarGridSpec(
        num_scalar_prefetch=1,
        grid=(rows // BQ,),
        in_specs=[
            whole_spec((rows, width3)),
            pl.BlockSpec((BQ, width), lambda i, *_: (i, 0)),
            pl.BlockSpec((BQ, width), lambda i, *_: (i, 0)),
            pl.BlockSpec((heads, BQ), lambda i, *_: (0, i)),
            whole_spec((rows, 1)),
            whole_spec((rows, 1)),
            whole_spec((1, rows)),
            whole_spec((1, rows)),
        ],
        out_specs=whole_spec((rows, width3)),
        scratch_shapes=[
            pltpu.VMEM((width, rows), BF16),
            pltpu.VMEM((rows, width), F32),
            pltpu.VMEM((rows, width), F32),
        ],
    )
    return pl.pallas_call(
        functools.partial(attend_back_kernel, heads, piece),
        out_shape=jax.ShapeDtypeStruct((rows, width3), BF16),
        grid_spec=grid_spec,
        cost_estimate=pl.CostEstimate(
            flops=20 * rows * rows * width, bytes_accessed=16 * rows * width, transcendentals=rows * rows
        ),
        name="attend_back",
    )(info, qkv, mixed, d_mixed, lse, doc_col, blk_col, doc_row, blk_row)


def send(value, step):
    count = lax.axis_size("ctx")
    return lax.ppermute(value, "ctx", [(i, i ^ step) for i in range(count)])


def swap(value):
    return lax.ppermute(value, "core", [(0, 1), (1, 0)])


def plane_gather(own):
    count = lax.axis_size("ctx")
    mine = [own] + [send(own, r) for r in range(1, count)]
    return mine, [swap(block) for block in mine]


def plane_sum(mine, other):
    count = lax.axis_size("ctx")
    total = None
    for r in list(range(1, count)) + [0]:
        part = mine[r].astype(F32) + swap(other[r]).astype(F32)
        if r:
            part = send(part.astype(BF16), r).astype(F32)
        total = part if total is None else total + part
    return total


def ordered(first, second, core):
    return jnp.where(core == 0, jnp.stack([first, second]), jnp.stack([second, first]))


def mask_ids(docs, blocks, chip):
    rows = docs.shape[0]
    first_doc = docs[0::BQ][:, None]
    last_doc, last_block = docs[BQ - 1 :: BQ][:, None], blocks[BQ - 1 :: BQ][:, None]
    low = jnp.sum((docs[None] < first_doc).astype(jnp.int32), axis=1) // BK
    ends = jnp.minimum(
        jnp.sum((docs[None] <= last_doc).astype(jnp.int32), axis=1),
        jnp.sum((blocks[None] <= last_block).astype(jnp.int32), axis=1),
    )
    high = (ends + BK - 1) // BK
    info = jnp.concatenate([chip[None].astype(jnp.int32), low, high])
    return (info, docs.reshape(rows, 1), blocks.reshape(rows, 1), docs.reshape(1, rows), blocks.reshape(1, rows))


def body(
    block_in, cotangent, doc_ids, block_ids, gain_attn, w_query, w_key, w_value, w_out, gain_ffn, w_gate, w_up, w_down
):
    n_ctx, n_z = lax.axis_size("ctx"), lax.axis_size("z")
    chip, core = lax.axis_index("ctx"), lax.axis_index("core")
    piece, dim = block_in.shape[1], block_in.shape[2]
    shard = w_query.shape[0]
    width = dim // (2 * n_ctx)
    down_rows = w_down.shape[0]
    cut = down_rows // n_ctx
    hidden_cols = n_z * cut

    all_ids = lax.all_gather(jnp.stack([doc_ids[0], block_ids[0]]), ("ctx", "core"))
    all_ids = all_ids.reshape(n_ctx, 2, 2, piece)

    def ids_of(which):
        seq = lax.dynamic_index_in_dim(all_ids, which, axis=1, keepdims=False)
        return mask_ids(seq[:, 0].reshape(-1), seq[:, 1].reshape(-1), chip)

    def head_cols(which):
        at = (chip * 2 + which) * width
        return jnp.concatenate(
            [lax.dynamic_slice_in_dim(w, at, width, axis=1) for w in (w_query, w_key, w_value)], axis=1
        )

    def hidden_slices(which):
        return jnp.concatenate(
            [
                lax.dynamic_slice_in_dim(w, (2 * z + which) * down_rows + chip * cut, cut, axis=1)
                for w in (w_gate, w_up)
                for z in range(n_z)
            ],
            axis=1,
        )

    def scaled(w, gain):
        return (w.astype(F32) * gain.astype(F32)[:, None]).astype(BF16)

    def over_z(mine, theirs):
        both = ordered(mine, swap(theirs), core).reshape(2 * shard, -1)
        return lax.all_gather(both, "z", axis=0, tiled=True)

    w_qkv = over_z(scaled(head_cols(core), gain_attn), scaled(head_cols(1 - core), gain_attn))
    w_out_full = lax.all_gather(w_out, ("z", "core"), axis=0, tiled=True)
    w_gu = over_z(scaled(hidden_slices(core), gain_ffn), scaled(hidden_slices(1 - core), gain_ffn))
    w_dn = lax.all_gather(
        lax.dynamic_slice_in_dim(w_down, chip * cut, cut, axis=0), "z", axis=0, tiled=True
    )

    x_rows = block_in[0].astype(F32)
    inv1 = lax.rsqrt(jnp.mean(x_rows * x_rows, axis=-1, keepdims=True) + NORM_EPS)
    n_one = x_rows * inv1
    one_mine, one_other = plane_gather(n_one.astype(BF16))
    ids_mine, ids_other = ids_of(core), ids_of(1 - core)

    def project(blocks):
        return jnp.concatenate([mm(b, w_qkv).astype(BF16) for b in blocks], axis=0)

    qkv_mine, qkv_other = project(one_mine), project(one_other)
    mix_mine, lse_mine = attend(qkv_mine, ids_mine, piece)
    mix_other, lse_other = attend(qkv_other, ids_other, piece)
    mixes = jnp.stack([mix_mine, swap(mix_other)]).reshape(2, n_ctx, piece, width)
    parts = [mixes[:, 0]] + [send(mixes[:, r], r) for r in range(1, n_ctx)]
    attended = jnp.concatenate([p[q] for p in parts for q in range(2)], axis=1)

    def relative(rows):
        me = chip * 2 + core
        return jnp.concatenate(
            [lax.dynamic_slice_in_dim(rows, (j ^ me) * width, width, axis=0) for j in range(2 * n_ctx)],
            axis=0,
        )

    w_out_rel = relative(w_out_full)
    hidden = x_rows + mm(attended, w_out_rel)
    inv2 = lax.rsqrt(jnp.mean(hidden * hidden, axis=-1, keepdims=True) + NORM_EPS)
    n_two = hidden * inv2

    cot_mine, cot_other = plane_gather(cotangent[0])
    two_mine, two_other = plane_gather(n_two.astype(BF16))

    def feed(rows, cots):
        gu = mm(rows, w_gu)
        gate, upper = gu[:, :hidden_cols], gu[:, hidden_cols:]
        sigma = jax.nn.sigmoid(gate)
        silu_gate = gate * sigma
        inner = (silu_gate * upper).astype(BF16)
        d_inner = mm_nt(cots, w_dn)
        d_gate = d_inner * upper * sigma * (1.0 + gate * (1.0 - sigma))
        d_gu = jnp.concatenate([d_gate, d_inner * silu_gate], axis=1).astype(BF16)
        return inner, d_gu, mm_nt(d_gu, w_gu).astype(BF16)

    fed_mine = [feed(a, c) for a, c in zip(two_mine, cot_mine)]
    fed_other = [feed(a, c) for a, c in zip(two_other, cot_other)]
    d_norm2 = plane_sum([f[2] for f in fed_mine], [f[2] for f in fed_other])
    out_rows = plane_sum(
        [mm(f[0], w_dn).astype(BF16) for f in fed_mine], [mm(f[0], w_dn).astype(BF16) for f in fed_other]
    )
    block_out = (hidden + out_rows).astype(BF16)
    two_all = jnp.concatenate(two_mine + two_other, axis=0)
    cot_all = jnp.concatenate(cot_mine + cot_other, axis=0)
    inner_all = jnp.concatenate([f[0] for f in fed_mine + fed_other], axis=0)
    d_gu_all = jnp.concatenate([f[1] for f in fed_mine + fed_other], axis=0)
    grad_dn = mm_tn(inner_all, cot_all).astype(BF16)
    grad_gu = mm_tn(two_all, d_gu_all).astype(BF16)
    grad_dn = lax.psum_scatter(grad_dn, "z", scatter_dimension=0, tiled=True)
    grad_gu = lax.psum_scatter(grad_gu, "z", scatter_dimension=0, tiled=True)

    d_hidden = cotangent[0].astype(F32) + inv2 * (
        d_norm2 - n_two * jnp.mean(d_norm2 * n_two, axis=-1, keepdims=True)
    )
    e_rows = d_hidden.astype(BF16)
    d_att = mm_nt(e_rows, w_out_rel).astype(BF16)
    grad_wo = lax.psum_scatter(
        relative(mm_tn(attended, e_rows).astype(BF16)), ("z", "core"), scatter_dimension=0, tiled=True
    )
    grad_wo = lax.psum(grad_wo, "ctx").astype(F32)

    d_parts = [d_att[:, : 2 * width]] + [
        send(d_att[:, 2 * width * r : 2 * width * (r + 1)], r) for r in range(1, n_ctx)
    ]
    d_mix_mine = jnp.concatenate([p[:, :width] for p in d_parts], axis=0)
    d_mix_other = swap(jnp.concatenate([p[:, width:] for p in d_parts], axis=0))
    d_qkv_mine = attend_back(qkv_mine, mix_mine, d_mix_mine, lse_mine, ids_mine, piece)
    d_qkv_other = attend_back(qkv_other, mix_other, d_mix_other, lse_other, ids_other, piece)

    def by_piece(rows):
        return [rows[r * piece : (r + 1) * piece] for r in range(n_ctx)]

    d_norm1 = plane_sum(
        [mm_nt(b, w_qkv).astype(BF16) for b in by_piece(d_qkv_mine)],
        [mm_nt(b, w_qkv).astype(BF16) for b in by_piece(d_qkv_other)],
    )
    input_grad = d_hidden + inv1 * (d_norm1 - n_one * jnp.mean(d_norm1 * n_one, axis=-1, keepdims=True))
    one_all = jnp.concatenate(one_mine + one_other, axis=0)
    grad_qkv = mm_tn(one_all, jnp.concatenate([d_qkv_mine, d_qkv_other], axis=0)).astype(BF16)
    grad_qkv = lax.psum_scatter(grad_qkv, "z", scatter_dimension=0, tiled=True)

    def to_owner(part):
        mine = lax.dynamic_slice_in_dim(part, core * shard, shard, axis=0)
        theirs = lax.dynamic_slice_in_dim(part, (1 - core) * shard, shard, axis=0)
        both = ordered(mine, swap(theirs), core)
        return lax.all_gather(both, "ctx", axis=0).transpose(2, 0, 1, 3)

    qkv_shard = to_owner(grad_qkv).reshape(shard, 2 * n_ctx, 3, width).astype(F32)
    raw_q, raw_k, raw_v = (qkv_shard[:, :, i].reshape(shard, dim) for i in range(3))
    gu_shard = to_owner(grad_gu).reshape(shard, n_ctx, 2, 2, n_z, cut).astype(F32)
    raw_g, raw_u = (
        gu_shard[:, :, :, i].transpose(0, 3, 2, 1, 4).reshape(shard, -1) for i in range(2)
    )
    grad_down = lax.all_gather(grad_dn, "ctx", axis=0, tiled=True).astype(F32)

    def row_sum(pairs):
        return sum(jnp.sum(w.astype(F32) * g, axis=1) for w, g in pairs)

    g1, g2 = gain_attn.astype(F32)[:, None], gain_ffn.astype(F32)[:, None]
    return (
        block_out[None],
        input_grad[None],
        row_sum([(w_query, raw_q), (w_key, raw_k), (w_value, raw_v)]),
        raw_q * g1,
        raw_k * g1,
        raw_v * g1,
        grad_wo,
        row_sum([(w_gate, raw_g), (w_up, raw_u)]),
        raw_g * g2,
        raw_u * g2,
        grad_down,
    )


def solution(mesh):
    n_ctx, n_fsdp = mesh.devices.shape
    inner = Mesh(mesh.devices.reshape(n_ctx, n_fsdp // 2, 2), ("ctx", "z", "core"))
    fsdp = ("z", "core")
    act, ids, vec, mat = P(fsdp, "ctx", None), P(fsdp, "ctx"), P(fsdp), P(fsdp, None)
    return jax.shard_map(
        body,
        mesh=inner,
        in_specs=(act, act, ids, ids, vec, mat, mat, mat, mat, vec, mat, mat, mat),
        out_specs=(act, act, vec, mat, mat, mat, mat, vec, mat, mat, mat),
        check_vma=False,
    )
```

time: 1470 us -> 769 us (0.52)
  waiting for transfers between devices: 868 us -> 148 us
  matrix products: 246 us -> 139 us
  Pallas kernels: 0 us -> 87.6 us
  other arithmetic: 144 us -> 66.3 us
  blocking collectives: 61.3 us -> 139 us
  starting transfers between devices: 12 us -> 41.1 us
    reduce_scatter x7 -> x4, waiting for transfers between devices: 326 us -> 0.02 us  [the longest x1 0.01 us: body(): lax.psum_scatter(relative(mm_tn(attended, e_rows).astype(BF16)), ('z', 'c...]
    ppermute x10 -> x54, waiting for transfers between devices: 438 us -> 137 us  [the longest x24 137 us: send(): return lax.ppermute(value, 'ctx', [(i, i ^ step) for i in range(count)])]
    dot_general x133 -> x54, matrix products: 246 us -> 139 us  [the longest x25 56.9 us: mm_nt(): return lax.dot_general(a, b, NT, preferred_element_type=F32)]
    all_gather x4 -> x3, blocking collectives: 37.9 us -> 139 us  [the longest x1 64.7 us: body(): lax.all_gather(jnp.stack([doc_ids[0], block_ids[0]]), ('ctx', 'core'))]
    pallas_call x0 -> x4, Pallas kernels: none -> 87.6 us  [the longest x2 45.1 us: attend_back(): pl.pallas_call(functools.partial(attend_back_kernel, heads, piece), out_s...]
    dynamic_update_slice x64 -> x0, other arithmetic: 77.9 us -> none  [forward_step(): return lax.map(forward_one_group, (q_groups, pair[0], pair[1]) + state)]
    unnamed x95 -> x228, local copies, waits for them, and re-layouts: 14.3 us -> 77.3 us
    psum x1, waiting for transfers between devices: 61.5 us -> 0.01 us  [body(): grad_wo = lax.psum(grad_wo, 'ctx').astype(F32)]
  transfers between devices with their start and end apart: 25 -> 64, of which waited for: 18 -> 13; matrix products, arithmetic and copies ran while one was open for 16% -> 38% of each run, Pallas kernels for 0% -> 12%
where the time goes in v1:
time: 769 us; the launch traced here: 758 us
  waiting for transfers between devices  148 us (19%)
  blocking collectives  139 us (18%)
  matrix products  139 us (18%)
  local copies, waits for them, and re-layouts  121 us (16%)
  Pallas kernels  87.6 us (11%)
  other arithmetic  66.3 us (9%)
  starting transfers between devices  41.1 us (5%)
  between operations  16.1 us (2%)
    ppermute x24, waiting for transfers between devices, send(): return lax.ppermute(value, 'ctx', [(i, i ^ step) for i in range(count)])  137 us
    unnamed x228, local copies, waits for them, and re-layouts  77.3 us
    all_gather x1, blocking collectives, body(): lax.all_gather(jnp.stack([doc_ids[0], block_ids[0]]), ('ctx', 'core'))  64.7 us
    dot_general x25, matrix products, mm_nt(): return lax.dot_general(a, b, NT, preferred_element_type=F32)  56.9 us
    all_gather x1, blocking collectives, to_owner(): return lax.all_gather(both, 'ctx', axis=0).transpose(2, 0, 1, 3)  53.3 us
    dot_general x25, matrix products, mm(): return jnp.dot(a, b, preferred_element_type=F32)  46.7 us
    pallas_call x2, Pallas kernels, attend_back(): pl.pallas_call(functools.partial(attend_back_kernel, heads, piece), out_s...  45.1 us
    pallas_call x2, Pallas kernels, attend(): pl.pallas_call(functools.partial(attend_kernel, heads, piece), out_shape=...  42.5 us
  transfers between devices with their start and end apart: 64, of which 13 were waited for; matrix products, arithmetic and copies ran while one was open for 38% of the time, Pallas kernels for 12%

profile of v1, /device:TPU:0, one launch (start us, length us, event | category | flops | bytes accessed | tf_op | source)
XLA Modules:
  0.0 758.1 jit_solution(9165452700624525001)
XLA Ops:
  24.4 2.6 collective-permute-start.31
  35.6 64.7 %all-gather.1 = s32[8,2,512]{2,1,0:T(2,128)S(1)} all-gather(s32[1,2,512]{2,1,0:T(2,128)S(1)} %add_bitcast_fusion), channel_id=2, replica_groups=mesh['ctx'=4,'z'=4,'core'=2] {'ctx','core'}, dimensions={0}, use_global_device_ids=true | all-gather | bytes 36864 | tf_op jit(solution)/shard_map/all_gather | solution.py:295
  110.1 21.2 %all_gather.31 = bf16[1024,384]{1,0:T(8,128)(2,1)S(1)} all-gather(bf16[256,384]{1,0:T(8,128)(2,1)S(1)} %bitcast.298), channel_id=1, replica_groups=mesh['ctx'=4,'z'=4,'core'=2] {'z'}, dimensions={0}, use_global_device_ids=true | all-gather | bytes 983040 | tf_op jit(solution)/shard_map/all_gather | solution.py:323
  133.5 2.4 collective-permute-start.35
  136.0 2.3 constant_dynamic-update-slice_fusion.54
  138.2 2.3 constant_dynamic-update-slice_fusion.53
  147.5 11.3 %collective-permute-done.35 = bf16[512,1024]{1,0:T(8,128)(2,1)} collective-permute-done((bf16[512,1024]{1,0:T(8,128)(2,1)S(1)}, bf16[512,1024]{1,0:T(8,128)(2,1)}, u32[]{:S(2)}, u32[]{:S(2)}) %collective-permute-start.35) | collective-permute-done | bytes 1048608 | tf_op jit(solution)/shard_map/ppermute | solution.py:241
  164.2 20.2 %attend.2 = (bf16[2048,128]{1,0:T(8,128)(2,1)}, f32[2,2048]{1,0:T(2,128)}) custom-call(s32[17]{0:T(128)} %pad_add_fusion.info, bf16[2048,384]{1,0:T(8,128)(2,1)} %pad_maximum_fusion.qkv, s32[2048,1]{1,0:T(8,128)} %bitcast.290, s32[2048,1]{1,0:T(8,128)} %bitcast.292, s32[1,2048]{1,0:T(1,128)} %bitcast.314, s32[1,2048]{1,0:T(1,128)} %bitcast.311), custom_call_target="tpu_custom_call" | custom-call | flops 4294967296 | bytes 4194304 | tf_op jit(solution)/shard_map/attend/pallas_call | solution.py:189
  184.3 2.5 collective-permute-start.32
  194.0 22.3 %attend.3 = (bf16[2048,128]{1,0:T(8,128)(2,1)}, f32[2,2048]{1,0:T(2,128)}) custom-call(s32[17]{0:T(128)} %pad_add_fusion.1.info, bf16[2048,384]{1,0:T(8,128)(2,1)} %pad_maximum_fusion.1.qkv, s32[2048,1]{1,0:T(8,128)} %bitcast.286, s32[2048,1]{1,0:T(8,128)} %bitcast.288, s32[1,2048]{1,0:T(1,128)} %bitcast.308, s32[1,2048]{1,0:T(1,128)} %bitcast.305), custom_call_target="tpu_custom_call" | custom-call | flops 4294967296 | bytes 4194304 | tf_op jit(solution)/shard_map/attend/pallas_call | solution.py:189
  216.5 2.3 constant_dynamic-update-slice_fusion.51
  219.5 2.3 constant_dynamic-update-slice_fusion.50
  221.8 2.3 constant_dynamic-update-slice_fusion.49
  230.6 2.7 collective-permute-done.9
  234.7 8.4 %collective-permute-done.10 = bf16[2,512,128]{2,1,0:T(8,128)(2,1)S(1)} collective-permute-done((bf16[2,512,128]{2,1,0:T(8,128)(2,1)S(1)}, bf16[2,512,128]{2,1,0:T(8,128)(2,1)S(1)}, u32[]{:S(2)}, u32[]{:S(2)}) %collective-permute-start.10) | collective-permute-done | bytes 262176 | tf_op jit(solution)/shard_map/ppermute | solution.py:241
  250.1 3.3 multiply_reduce_fusion.3
  258.9 4.5 fusion.67
  263.4 2.9 multiply_convert_fusion.4
  275.9 27.9 %collective-permute-done.12 = bf16[512,1024]{1,0:T(8,128)(2,1)S(1)} collective-permute-done((bf16[512,1024]{1,0:T(8,128)(2,1)}, bf16[512,1024]{1,0:T(8,128)(2,1)S(1)}, u32[]{:S(2)}, u32[]{:S(2)}) %collective-permute-start.12) | collective-permute-done | bytes 1048608 | tf_op jit(solution)/shard_map/ppermute | solution.py:241
  308.3 2.5 fusion.63
  315.7 2.5 fusion.65
  321.4 3.3 copy-done.59
  326.3 2.4 constant_dynamic-update-slice_fusion.37
  348.7 2.7 multiply_convert_fusion.14
  357.4 8.1 %convolution_convert_fusion.2 = bf16[512,1024]{1,0:T(8,128)(2,1)} fusion(bf16[4096,512]{1,0:T(8,128)(2,1)S(1)} %get-tuple-element.23, bf16[4096,1024]{1,0:T(8,128)(2,1)} %constant_dynamic-update-slice_fusion.48), kind=kOutput, calls=%fused_computation.41 | convolution fusion | flops 4295491584 | bytes 13631488 | tf_op jit(solution)/shard_map/dot_general | solution.py:33
  365.6 3.2 convolution_convert_fusion.26
  368.8 2.5 fusion.31
  376.9 14.8 %convolution_convert_fusion = bf16[1024,1024]{1,0:T(8,128)(2,1)} fusion(bf16[4096,1024]{1,0:T(8,128)(2,1)} %constant_dynamic-update-slice_fusion.32, bf16[4096,1024]{1,0:T(8,128)(2,1)} %fusion.27), kind=kOutput, calls=%fused_computation.36 | convolution fusion | flops 8590983168 | bytes 18874368 | tf_op jit(solution)/shard_map/dot_general | solution.py:33
  397.4 2.6 add_convert_fusion.3
  400.2 2.7 add_convert_fusion.4
  405.8 2.5 add_convert_fusion.5
  414.6 15.3 %collective-permute-done.38 = bf16[512,1024]{1,0:T(8,128)(2,1)S(1)} collective-permute-done((bf16[512,1024]{1,0:T(8,128)(2,1)S(1)}, bf16[512,1024]{1,0:T(8,128)(2,1)S(1)}, u32[]{:S(2)}, u32[]{:S(2)}) %collective-permute-start.38) | collective-permute-done | bytes 1048608 | tf_op jit(solution)/shard_map/ppermute | solution.py:241
  431.2 20.6 %collective-permute-done.34 = bf16[512,1024]{1,0:T(8,128)(2,1)S(1)} collective-permute-done((bf16[512,1024]{1,0:T(8,128)(2,1)S(1)}, bf16[512,1024]{1,0:T(8,128)(2,1)S(1)}, u32[]{:S(2)}, u32[]{:S(2)}) %collective-permute-start.34) | collective-permute-done | bytes 1048608 | tf_op jit(solution)/shard_map/ppermute | solution.py:241
  456.6 18.1 %collective-permute-done.16 = bf16[512,1024]{1,0:T(8,128)(2,1)S(1)} collective-permute-done((bf16[512,1024]{1,0:T(8,128)(2,1)S(1)}, bf16[512,1024]{1,0:T(8,128)(2,1)S(1)}, u32[]{:S(2)}, u32[]{:S(2)}) %collective-permute-start.16) | collective-permute-done | bytes 1048608 | tf_op jit(solution)/shard_map/ppermute | solution.py:241
  474.8 21.9 %collective-permute-done.24 = bf16[512,1024]{1,0:T(8,128)(2,1)S(1)} collective-permute-done((bf16[512,1024]{1,0:T(8,128)(2,1)S(1)}, bf16[512,1024]{1,0:T(8,128)(2,1)S(1)}, u32[]{:S(2)}, u32[]{:S(2)}) %collective-permute-start.24) | collective-permute-done | bytes 1048608 | tf_op jit(solution)/shard_map/ppermute | solution.py:241
  496.7 5.0 multiply_add_fusion
  501.7 2.5 convolution_convert_fusion.1
  512.5 2.4 constant_dynamic-update-slice_fusion.29
  518.2 2.5 constant_dynamic-update-slice_fusion.26
  520.7 2.4 constant_dynamic-update-slice_fusion.25
  526.6 2.3 constant_dynamic-update-slice_fusion.24
  531.3 3.4 collective-permute-done.41
  535.7 4.1 collective-permute-done.43
  540.8 2.7 collective-permute-done.42
  544.5 21.6 %attend_back.2 = bf16[2048,384]{1,0:T(8,128)(2,1)} custom-call(s32[17]{0:T(128)} %pad_add_fusion.info, bf16[2048,384]{1,0:T(8,128)(2,1)} %pad_maximum_fusion.qkv, bf16[2048,128]{1,0:T(8,128)(2,1)} %get-tuple-element.15.mixed, bf16[2048,128]{1,0:T(8,128)(2,1)} %pad_maximum_fusion.18.d_mixed, f32[2,2048]{1,0:T(2,128)} %get-tuple-element.17.lse, ...), custom_call_target="tpu_custom_call" | custom-call | flops 10737418240 | bytes 4194304 | tf_op jit(solution)/shard_map/attend_back/pallas_call | solution.py:228
  566.0 23.5 %attend_back.3 = bf16[2048,384]{1,0:T(8,128)(2,1)} custom-call(s32[17]{0:T(128)} %pad_add_fusion.1.info, bf16[2048,384]{1,0:T(8,128)(2,1)} %pad_maximum_fusion.1.qkv, bf16[2048,128]{1,0:T(8,128)(2,1)} %get-tuple-element.16.mixed, bf16[2048,128]{1,0:T(8,128)(2,1)} %collective-permute-done.44.d_mixed, f32[2,2048]{1,0:T(2,128)} %get-tuple-element.18.lse, ...), custom_call_target="tpu_custom_call" | custom-call | flops 10737418240 | bytes 4194304 | tf_op jit(solution)/shard_map/attend_back/pallas_call | solution.py:228
  589.6 9.7 %fusion.13 = bf16[1024,384]{1,0:T(8,128)(2,1)} fusion(bf16[4096,1024]{1,0:T(8,128)(2,1)} %constant_dynamic-update-slice_fusion.24, bf16[2048,384]{1,0:T(8,128)(2,1)} %attend_back.3, bf16[2048,384]{1,0:T(8,128)(2,1)} %attend_back.2), kind=kOutput, calls=%fused_computation.67 | convolution fusion | flops 3227910144 | bytes 12320768 | tf_op jit(solution)/shard_map/dot_general | solution.py:33
  599.4 2.9 convolution_convert_fusion.6
  613.4 2.7 convolution_convert_fusion.3
  616.6 2.8 convert_element_type.531
  621.4 3.0 add_convert_fusion.2
  625.9 2.7 add_convert_fusion.1
  630.1 2.9 add_convert_fusion
  634.5 53.3 %all_gather.35 = bf16[4,2,128,384]{3,2,1,0:T(8,128)(2,1)} all-gather(bf16[1,2,128,384]{3,2,1,0:T(8,128)(2,1)S(1)} %maximum_select_fusion.3), channel_id=1, replica_groups=mesh['ctx'=4,'z'=4,'core'=2] {'ctx'}, dimensions={0}, use_global_device_ids=true | all-gather | bytes 983040 | tf_op jit(solution)/shard_map/all_gather | solution.py:424
  687.8 2.3 copy.119
  698.7 2.9 broadcast_multiply_fusion.2
  702.2 3.5 fusion.7
  705.7 4.5 fusion.11
  712.1 10.7 %all-gather.14.cloned.1.call-done = bf16[4,2,128,1024]{3,2,1,0:T(8,128)(2,1)} async-done(((bf16[1,2,128,1024]{3,2,1,0:T(8,128)(2,1)}), bf16[4,2,128,1024]{3,2,1,0:T(8,128)(2,1)}) %all-gather.14.cloned.1.call-update) | async-done | bytes 2097168 | tf_op jit(solution)/shard_map/all_gather | solution.py:424
  722.7 4.1 convert_bitcast_fusion
  726.8 5.6 reshape.412
  732.5 3.9 slice_bitcast_fusion
  739.6 2.9 copy.126
  744.4 5.9 broadcast_multiply_fusion
  (461 shorter events, 209.2 us)
Async XLA Ops:
  7.2 238.6 %all-gather.8.cloned.1.call-start = ((), (), s32[]{:S(2)}) async-start(), calls=%async_computation.4 | async-start | bytes 2359296 | tf_op jit(solution)/shard_map/all_gather | solution.py:326
  8.0 251.0 %all-gather.10.cloned.1.call-start = ((), (), s32[]{:S(2)}) async-start(), calls=%async_computation.5 | async-start | bytes 2621440 | tf_op jit(solution)/shard_map/all_gather | solution.py:323
  15.7 6.8 collective-permute-start.13
  24.4 239.1 %all-gather.12.cloned.1.call-start = ((), (), s32[]{:S(2)}) async-start(), calls=%async_computation.6 | async-start | bytes 1310720 | tf_op jit(solution)/shard_map/all_gather | solution.py:328
  24.4 109.1 %collective-permute-start.31 = (bf16[512,1024]{1,0:T(8,128)(2,1)S(1)}, bf16[512,1024]{1,0:T(8,128)(2,1)}, u32[]{:S(2)}, u32[]{:S(2)}) collective-permute-start(bf16[512,1024]{1,0:T(8,128)(2,1)S(1)} %bitcast.278), channel_id=1, source_target_pairs={{0,16},{8,24},{16,0},{24,8},{1,17},{9,25},{17,1},{25,9},{2,18},{10... | collective-permute-start | bytes 3145736 | tf_op jit(solution)/shard_map/ppermute | solution.py:241
  27.0 108.9 %collective-permute-start.27 = (bf16[512,1024]{1,0:T(8,128)(2,1)S(1)}, bf16[512,1024]{1,0:T(8,128)(2,1)}, u32[]{:S(2)}, u32[]{:S(2)}) collective-permute-start(bf16[512,1024]{1,0:T(8,128)(2,1)S(1)} %bitcast.279), channel_id=1, source_target_pairs={{0,8},{8,0},{16,24},{24,16},{1,9},{9,1},{17,25},{25,17},{2,10},{10... | collective-permute-start | bytes 3145736 | tf_op jit(solution)/shard_map/ppermute | solution.py:241
  31.0 109.6 %collective-permute-start.3 = (bf16[512,1024]{1,0:T(8,128)(2,1)}, bf16[512,1024]{1,0:T(8,128)(2,1)}, u32[]{:S(2)}, u32[]{:S(2)}) collective-permute-start(bf16[512,1024]{1,0:T(8,128)(2,1)} %get-tuple-element.42), channel_id=1, source_target_pairs={{0,24},{8,16},{16,8},{24,0},{1,25},{9,17},{17,9},{25,1},{2,26},{10... | collective-permute-start | bytes 3145736 | tf_op jit(solution)/shard_map/ppermute | solution.py:241
  31.0 112.0 %collective-permute-start.2 = (bf16[512,1024]{1,0:T(8,128)(2,1)}, bf16[512,1024]{1,0:T(8,128)(2,1)}, u32[]{:S(2)}, u32[]{:S(2)}) collective-permute-start(bf16[512,1024]{1,0:T(8,128)(2,1)} %get-tuple-element.42), channel_id=1, source_target_pairs={{0,16},{8,24},{16,0},{24,8},{1,17},{9,25},{17,1},{25,9},{2,18},{10... | collective-permute-start | bytes 3145736 | tf_op jit(solution)/shard_map/ppermute | solution.py:241
  34.7 75.1 %collective-permute-start = (bf16[128,384]{1,0:T(8,128)(2,1)S(1)}, bf16[128,384]{1,0:T(8,128)(2,1)S(1)}, u32[]{:S(2)}, u32[]{:S(2)}) collective-permute-start(bf16[128,384]{1,0:T(8,128)(2,1)S(1)} %multiply_convert_fusion.27), channel_id=1, source_target_pairs={{0,1},{1,0},{2,3},{3,2},{4,5},{5,4},{6,7},{7,6},{8,9},{9,8},{10,11... | collective-permute-start | bytes 294920 | tf_op jit(solution)/shard_map/ppermute | solution.py:245
  35.5 495.7 %reduce-scatter.11.cloned.1.call-start = ((), (), s32[]{:S(2)}) async-start(), calls=%async_computation.12 | async-start | bytes 1310720 | tf_op jit(solution)/shard_map/reduce_scatter | solution.py:387
  109.7 35.3 %collective-permute-start.1 = (bf16[512,1024]{1,0:T(8,128)(2,1)}, bf16[512,1024]{1,0:T(8,128)(2,1)}, u32[]{:S(2)}, u32[]{:S(2)}) collective-permute-start(bf16[512,1024]{1,0:T(8,128)(2,1)} %get-tuple-element.42), channel_id=1, source_target_pairs={{0,8},{8,0},{16,24},{24,16},{1,9},{9,1},{17,25},{25,17},{2,10},{10... | collective-permute-start | bytes 3145736 | tf_op jit(solution)/shard_map/ppermute | solution.py:241
  133.5 25.4 %collective-permute-start.35 = (bf16[512,1024]{1,0:T(8,128)(2,1)S(1)}, bf16[512,1024]{1,0:T(8,128)(2,1)}, u32[]{:S(2)}, u32[]{:S(2)}) collective-permute-start(bf16[512,1024]{1,0:T(8,128)(2,1)S(1)} %bitcast.280), channel_id=1, source_target_pairs={{0,24},{8,16},{16,8},{24,0},{1,25},{9,17},{17,9},{25,1},{2,26},{10... | collective-permute-start | bytes 3145736 | tf_op jit(solution)/shard_map/ppermute | solution.py:241
  135.9 22.9 %collective-permute-start.4 = (bf16[512,1024]{1,0:T(8,128)(2,1)}, bf16[512,1024]{1,0:T(8,128)(2,1)S(1)}, u32[]{:S(2)}, u32[]{:S(2)}) collective-permute-start(bf16[512,1024]{1,0:T(8,128)(2,1)} %get-tuple-element.42), channel_id=1, source_target_pairs={{0,1},{1,0},{2,3},{3,2},{4,5},{5,4},{6,7},{7,6},{8,9},{9,8},{10,11... | collective-permute-start | bytes 3145736 | tf_op jit(solution)/shard_map/ppermute | solution.py:245
  140.6 75.9 %collective-permute-start.39 = (bf16[512,1024]{1,0:T(8,128)(2,1)S(1)}, bf16[512,1024]{1,0:T(8,128)(2,1)}, u32[]{:S(2)}, u32[]{:S(2)}) collective-permute-start(bf16[512,1024]{1,0:T(8,128)(2,1)S(1)} %bitcast.281), channel_id=1, source_target_pairs={{0,1},{1,0},{2,3},{3,2},{4,5},{5,4},{6,7},{7,6},{8,9},{9,8},{10,11... | collective-permute-start | bytes 3145736 | tf_op jit(solution)/shard_map/ppermute | solution.py:245
  143.0 41.3 %collective-permute-start.7 = (bf16[512,1024]{1,0:T(8,128)(2,1)}, bf16[512,1024]{1,0:T(8,128)(2,1)}, u32[]{:S(2)}, u32[]{:S(2)}) collective-permute-start(bf16[512,1024]{1,0:T(8,128)(2,1)} %collective-permute-done.3), channel_id=1, source_target_pairs={{0,1},{1,0},{2,3},{3,2},{4,5},{5,4},{6,7},{7,6},{8,9},{9,8},{10,11... | collective-permute-start | bytes 3145736 | tf_op jit(solution)/shard_map/ppermute | solution.py:245
  145.0 43.7 %collective-permute-start.6 = (bf16[512,1024]{1,0:T(8,128)(2,1)}, bf16[512,1024]{1,0:T(8,128)(2,1)}, u32[]{:S(2)}, u32[]{:S(2)}) collective-permute-start(bf16[512,1024]{1,0:T(8,128)(2,1)} %collective-permute-done.2), channel_id=1, source_target_pairs={{0,1},{1,0},{2,3},{3,2},{4,5},{5,4},{6,7},{7,6},{8,9},{9,8},{10,11... | collective-permute-start | bytes 3145736 | tf_op jit(solution)/shard_map/ppermute | solution.py:245
  158.9 31.9 %collective-permute-start.5 = (bf16[512,1024]{1,0:T(8,128)(2,1)}, bf16[512,1024]{1,0:T(8,128)(2,1)}, u32[]{:S(2)}, u32[]{:S(2)}) collective-permute-start(bf16[512,1024]{1,0:T(8,128)(2,1)} %collective-permute-done.1), channel_id=1, source_target_pairs={{0,1},{1,0},{2,3},{3,2},{4,5},{5,4},{6,7},{7,6},{8,9},{9,8},{10,11... | collective-permute-start | bytes 3145736 | tf_op jit(solution)/shard_map/ppermute | solution.py:245
  158.9 66.8 %collective-permute-start.36 = (bf16[512,1024]{1,0:T(8,128)(2,1)}, bf16[512,1024]{1,0:T(8,128)(2,1)}, u32[]{:S(2)}, u32[]{:S(2)}) collective-permute-start(bf16[512,1024]{1,0:T(8,128)(2,1)} %collective-permute-done.35), channel_id=1, source_target_pairs={{0,1},{1,0},{2,3},{3,2},{4,5},{5,4},{6,7},{7,6},{8,9},{9,8},{10,11... | collective-permute-start | bytes 3145736 | tf_op jit(solution)/shard_map/ppermute | solution.py:245
  184.3 37.4 %collective-permute-start.32 = (bf16[512,1024]{1,0:T(8,128)(2,1)}, bf16[512,1024]{1,0:T(8,128)(2,1)}, u32[]{:S(2)}, u32[]{:S(2)}) collective-permute-start(bf16[512,1024]{1,0:T(8,128)(2,1)} %collective-permute-done.31), channel_id=1, source_target_pairs={{0,1},{1,0},{2,3},{3,2},{4,5},{5,4},{6,7},{7,6},{8,9},{9,8},{10,11... | collective-permute-start | bytes 3145736 | tf_op jit(solution)/shard_map/ppermute | solution.py:245
  188.8 30.7 %collective-permute-start.28 = (bf16[512,1024]{1,0:T(8,128)(2,1)}, bf16[512,1024]{1,0:T(8,128)(2,1)}, u32[]{:S(2)}, u32[]{:S(2)}) collective-permute-start(bf16[512,1024]{1,0:T(8,128)(2,1)} %collective-permute-done.27), channel_id=1, source_target_pairs={{0,1},{1,0},{2,3},{3,2},{4,5},{5,4},{6,7},{7,6},{8,9},{9,8},{10,11... | collective-permute-start | bytes 3145736 | tf_op jit(solution)/shard_map/ppermute | solution.py:245
  216.4 7.7 %collective-permute-start.8 = (bf16[2048,128]{1,0:T(8,128)(2,1)}, bf16[2048,128]{1,0:T(8,128)(2,1)S(1)}, u32[]{:S(2)}, u32[]{:S(2)}) collective-permute-start(bf16[2048,128]{1,0:T(8,128)(2,1)} %get-tuple-element.16.mixed), channel_id=1, source_target_pairs={{0,1},{1,0},{2,3},{3,2},{4,5},{5,4},{6,7},{7,6},{8,9},{9,8},{10,11... | collective-permute-start | bytes 1572872 | tf_op jit(solution)/shard_map/ppermute | solution.py:245
  224.1 9.2 %collective-permute-start.9 = (bf16[2,512,128]{2,1,0:T(8,128)(2,1)S(1)}, bf16[2,512,128]{2,1,0:T(8,128)(2,1)S(1)}, u32[]{:S(2)}, u32[]{:S(2)}) collective-permute-start(bf16[2,512,128]{2,1,0:T(8,128)(2,1)S(1)} %get-tuple-element.77), channel_id=1, source_target_pairs={{0,8},{8,0},{16,24},{24,16},{1,9},{9,1},{17,25},{25,17},{2,10},{10... | collective-permute-start | bytes 786440 | tf_op jit(solution)/shard_map/ppermute | solution.py:241
  227.9 16.5 %collective-permute-start.11 = (bf16[2,512,128]{2,1,0:T(8,128)(2,1)S(1)}, bf16[2,512,128]{2,1,0:T(8,128)(2,1)S(1)}, u32[]{:S(2)}, u32[]{:S(2)}) collective-permute-start(bf16[2,512,128]{2,1,0:T(8,128)(2,1)S(1)} %get-tuple-element.75), channel_id=1, source_target_pairs={{0,24},{8,16},{16,8},{24,0},{1,25},{9,17},{17,9},{25,1},{2,26},{10... | collective-permute-start | bytes 786440 | tf_op jit(solution)/shard_map/ppermute | solution.py:241
  229.4 13.7 %collective-permute-start.10 = (bf16[2,512,128]{2,1,0:T(8,128)(2,1)S(1)}, bf16[2,512,128]{2,1,0:T(8,128)(2,1)S(1)}, u32[]{:S(2)}, u32[]{:S(2)}) collective-permute-start(bf16[2,512,128]{2,1,0:T(8,128)(2,1)S(1)} %get-tuple-element.76), channel_id=1, source_target_pairs={{0,16},{8,24},{16,0},{24,8},{1,17},{9,25},{17,1},{25,9},{2,18},{10... | collective-permute-start | bytes 786440 | tf_op jit(solution)/shard_map/ppermute | solution.py:241
  255.4 14.0 %collective-permute-start.25 = (bf16[512,1024]{1,0:T(8,128)(2,1)}, bf16[512,1024]{1,0:T(8,128)(2,1)S(1)}, u32[]{:S(2)}, u32[]{:S(2)}) collective-permute-start(bf16[512,1024]{1,0:T(8,128)(2,1)} %get-tuple-element.40), channel_id=1, source_target_pairs={{0,1},{1,0},{2,3},{3,2},{4,5},{5,4},{6,7},{7,6},{8,9},{9,8},{10,11... | collective-permute-start | bytes 3145736 | tf_op jit(solution)/shard_map/ppermute | solution.py:245
  255.4 60.3 %collective-permute-start.21 = (bf16[512,1024]{1,0:T(8,128)(2,1)}, bf16[512,1024]{1,0:T(8,128)(2,1)}, u32[]{:S(2)}, u32[]{:S(2)}) collective-permute-start(bf16[512,1024]{1,0:T(8,128)(2,1)} %get-tuple-element.40), channel_id=1, source_target_pairs={{0,24},{8,16},{16,8},{24,0},{1,25},{9,17},{17,9},{25,1},{2,26},{10... | collective-permute-start | bytes 3145736 | tf_op jit(solution)/shard_map/ppermute | solution.py:241
  256.9 51.4 %collective-permute-start.17 = (bf16[512,1024]{1,0:T(8,128)(2,1)}, bf16[512,1024]{1,0:T(8,128)(2,1)}, u32[]{:S(2)}, u32[]{:S(2)}) collective-permute-start(bf16[512,1024]{1,0:T(8,128)(2,1)} %get-tuple-element.40), channel_id=1, source_target_pairs={{0,16},{8,24},{16,0},{24,8},{1,17},{9,25},{17,1},{25,9},{2,18},{10... | collective-permute-start | bytes 3145736 | tf_op jit(solution)/shard_map/ppermute | solution.py:241
  258.4 45.4 %collective-permute-start.12 = (bf16[512,1024]{1,0:T(8,128)(2,1)}, bf16[512,1024]{1,0:T(8,128)(2,1)S(1)}, u32[]{:S(2)}, u32[]{:S(2)}) collective-permute-start(bf16[512,1024]{1,0:T(8,128)(2,1)} %get-tuple-element.40), channel_id=1, source_target_pairs={{0,8},{8,0},{16,24},{24,16},{1,9},{9,1},{17,25},{25,17},{2,10},{10... | collective-permute-start | bytes 3145736 | tf_op jit(solution)/shard_map/ppermute | solution.py:241
  275.9 137.3 %collective-permute-start.40 = (bf16[512,1024]{1,0:T(8,128)(2,1)}, bf16[512,1024]{1,0:T(8,128)(2,1)S(1)}, u32[]{:S(2)}, u32[]{:S(2)}) collective-permute-start(bf16[512,1024]{1,0:T(8,128)(2,1)} %convolution_convert_fusion.12), channel_id=1, source_target_pairs={{0,1},{1,0},{2,3},{3,2},{4,5},{5,4},{6,7},{7,6},{8,9},{9,8},{10,11... | collective-permute-start | bytes 3145736 | tf_op jit(solution)/shard_map/ppermute | solution.py:245
  324.8 10.4 %collective-permute-start.22 = (bf16[512,1024]{1,0:T(8,128)(2,1)}, bf16[512,1024]{1,0:T(8,128)(2,1)S(1)}, u32[]{:S(2)}, u32[]{:S(2)}) collective-permute-start(bf16[512,1024]{1,0:T(8,128)(2,1)} %collective-permute-done.21), channel_id=1, source_target_pairs={{0,1},{1,0},{2,3},{3,2},{4,5},{5,4},{6,7},{7,6},{8,9},{9,8},{10,11... | collective-permute-start | bytes 3145736 | tf_op jit(solution)/shard_map/ppermute | solution.py:245
  324.8 16.7 %collective-permute-start.18 = (bf16[512,1024]{1,0:T(8,128)(2,1)}, bf16[512,1024]{1,0:T(8,128)(2,1)S(1)}, u32[]{:S(2)}, u32[]{:S(2)}) collective-permute-start(bf16[512,1024]{1,0:T(8,128)(2,1)} %collective-permute-done.17), channel_id=1, source_target_pairs={{0,1},{1,0},{2,3},{3,2},{4,5},{5,4},{6,7},{7,6},{8,9},{9,8},{10,11... | collective-permute-start | bytes 3145736 | tf_op jit(solution)/shard_map/ppermute | solution.py:245
  325.3 22.1 %collective-permute-start.14 = (bf16[512,1024]{1,0:T(8,128)(2,1)S(1)}, bf16[512,1024]{1,0:T(8,128)(2,1)S(1)}, u32[]{:S(2)}, u32[]{:S(2)}) collective-permute-start(bf16[512,1024]{1,0:T(8,128)(2,1)S(1)} %collective-permute-done.12), channel_id=1, source_target_pairs={{0,1},{1,0},{2,3},{3,2},{4,5},{5,4},{6,7},{7,6},{8,9},{9,8},{10,11... | collective-permute-start | bytes 3145736 | tf_op jit(solution)/shard_map/ppermute | solution.py:245
  341.0 55.9 %collective-permute-start.37 = (bf16[512,1024]{1,0:T(8,128)(2,1)}, bf16[512,1024]{1,0:T(8,128)(2,1)}, u32[]{:S(2)}, u32[]{:S(2)}) collective-permute-start(bf16[512,1024]{1,0:T(8,128)(2,1)} %convolution_convert_fusion.14), channel_id=1, source_target_pairs={{0,1},{1,0},{2,3},{3,2},{4,5},{5,4},{6,7},{7,6},{8,9},{9,8},{10,11... | collective-permute-start | bytes 3145736 | tf_op jit(solution)/shard_map/ppermute | solution.py:245
  347.4 52.7 %collective-permute-start.33 = (bf16[512,1024]{1,0:T(8,128)(2,1)}, bf16[512,1024]{1,0:T(8,128)(2,1)}, u32[]{:S(2)}, u32[]{:S(2)}) collective-permute-start(bf16[512,1024]{1,0:T(8,128)(2,1)} %convolution_convert_fusion.16), channel_id=1, source_target_pairs={{0,1},{1,0},{2,3},{3,2},{4,5},{5,4},{6,7},{7,6},{8,9},{9,8},{10,11... | collective-permute-start | bytes 3145736 | tf_op jit(solution)/shard_map/ppermute | solution.py:245
  353.6 49.3 %collective-permute-start.29 = (bf16[512,1024]{1,0:T(8,128)(2,1)}, bf16[512,1024]{1,0:T(8,128)(2,1)}, u32[]{:S(2)}, u32[]{:S(2)}) collective-permute-start(bf16[512,1024]{1,0:T(8,128)(2,1)} %convolution_convert_fusion.18), channel_id=1, source_target_pairs={{0,1},{1,0},{2,3},{3,2},{4,5},{5,4},{6,7},{7,6},{8,9},{9,8},{10,11... | collective-permute-start | bytes 3145736 | tf_op jit(solution)/shard_map/ppermute | solution.py:245
  365.6 246.4 %reduce-scatter.9.cloned.1.call-start = ((), (), s32[]{:S(2)}) async-start(), calls=%async_computation.10 | async-start | bytes 2621440 | tf_op jit(solution)/shard_map/reduce_scatter | solution.py:388
  368.8 36.4 %collective-permute-start.15 = (bf16[512,1024]{1,0:T(8,128)(2,1)}, bf16[512,1024]{1,0:T(8,128)(2,1)}, u32[]{:S(2)}, u32[]{:S(2)}) collective-permute-start(bf16[512,1024]{1,0:T(8,128)(2,1)} %convolution_convert_fusion.26), channel_id=1, source_target_pairs={{0,1},{1,0},{2,3},{3,2},{4,5},{5,4},{6,7},{7,6},{8,9},{9,8},{10,11... | collective-permute-start | bytes 3145736 | tf_op jit(solution)/shard_map/ppermute | solution.py:245
  391.7 221.4 %reduce-scatter.7.cloned.1.call-start = ((), (), s32[]{:S(2)}) async-start(), calls=%async_computation.8 | async-start | bytes 2359296 | tf_op jit(solution)/shard_map/reduce_scatter | solution.py:395
  396.9 11.4 %collective-permute-start.19 = (bf16[512,1024]{1,0:T(8,128)(2,1)S(1)}, bf16[512,1024]{1,0:T(8,128)(2,1)S(1)}, u32[]{:S(2)}, u32[]{:S(2)}) collective-permute-start(bf16[512,1024]{1,0:T(8,128)(2,1)S(1)} %convolution_convert_fusion.24), channel_id=1, source_target_pairs={{0,1},{1,0},{2,3},{3,2},{4,5},{5,4},{6,7},{7,6},{8,9},{9,8},{10,11... | collective-permute-start | bytes 3145736 | tf_op jit(solution)/shard_map/ppermute | solution.py:245
  400.1 11.8 %collective-permute-start.23 = (bf16[512,1024]{1,0:T(8,128)(2,1)S(1)}, bf16[512,1024]{1,0:T(8,128)(2,1)S(1)}, u32[]{:S(2)}, u32[]{:S(2)}) collective-permute-start(bf16[512,1024]{1,0:T(8,128)(2,1)S(1)} %convolution_convert_fusion.22), channel_id=1, source_target_pairs={{0,1},{1,0},{2,3},{3,2},{4,5},{5,4},{6,7},{7,6},{8,9},{9,8},{10,11... | collective-permute-start | bytes 3145736 | tf_op jit(solution)/shard_map/ppermute | solution.py:245
  402.9 27.0 %collective-permute-start.38 = (bf16[512,1024]{1,0:T(8,128)(2,1)S(1)}, bf16[512,1024]{1,0:T(8,128)(2,1)S(1)}, u32[]{:S(2)}, u32[]{:S(2)}) collective-permute-start(bf16[512,1024]{1,0:T(8,128)(2,1)S(1)} %add_convert_fusion.3), channel_id=1, source_target_pairs={{0,24},{8,16},{16,8},{24,0},{1,25},{9,17},{17,9},{25,1},{2,26},{10... | collective-permute-start | bytes 3145736 | tf_op jit(solution)/shard_map/ppermute | solution.py:241
  405.2 46.6 %collective-permute-start.34 = (bf16[512,1024]{1,0:T(8,128)(2,1)S(1)}, bf16[512,1024]{1,0:T(8,128)(2,1)S(1)}, u32[]{:S(2)}, u32[]{:S(2)}) collective-permute-start(bf16[512,1024]{1,0:T(8,128)(2,1)S(1)} %add_convert_fusion.4), channel_id=1, source_target_pairs={{0,16},{8,24},{16,0},{24,8},{1,17},{9,25},{17,1},{25,9},{2,18},{10... | collective-permute-start | bytes 3145736 | tf_op jit(solution)/shard_map/ppermute | solution.py:241
  408.3 46.5 %collective-permute-start.30 = (bf16[512,1024]{1,0:T(8,128)(2,1)S(1)}, bf16[512,1024]{1,0:T(8,128)(2,1)S(1)}, u32[]{:S(2)}, u32[]{:S(2)}) collective-permute-start(bf16[512,1024]{1,0:T(8,128)(2,1)S(1)} %add_convert_fusion.5), channel_id=1, source_target_pairs={{0,8},{8,0},{16,24},{24,16},{1,9},{9,1},{17,25},{25,17},{2,10},{10... | collective-permute-start | bytes 3145736 | tf_op jit(solution)/shard_map/ppermute | solution.py:241
  412.3 44.3 %collective-permute-start.26 = (bf16[512,1024]{1,0:T(8,128)(2,1)S(1)}, bf16[512,1024]{1,0:T(8,128)(2,1)S(1)}, u32[]{:S(2)}, u32[]{:S(2)}) collective-permute-start(bf16[512,1024]{1,0:T(8,128)(2,1)S(1)} %copy-done.78), channel_id=1, source_target_pairs={{0,1},{1,0},{2,3},{3,2},{4,5},{5,4},{6,7},{7,6},{8,9},{9,8},{10,11... | collective-permute-start | bytes 3145736 | tf_op jit(solution)/shard_map/ppermute | solution.py:245
  413.2 61.5 %collective-permute-start.16 = (bf16[512,1024]{1,0:T(8,128)(2,1)S(1)}, bf16[512,1024]{1,0:T(8,128)(2,1)S(1)}, u32[]{:S(2)}, u32[]{:S(2)}) collective-permute-start(bf16[512,1024]{1,0:T(8,128)(2,1)S(1)} %add_convert_fusion.9), channel_id=1, source_target_pairs={{0,8},{8,0},{16,24},{24,16},{1,9},{9,1},{17,25},{25,17},{2,10},{10... | collective-permute-start | bytes 3145736 | tf_op jit(solution)/shard_map/ppermute | solution.py:241
  429.9 44.9 %collective-permute-start.20 = (bf16[512,1024]{1,0:T(8,128)(2,1)S(1)}, bf16[512,1024]{1,0:T(8,128)(2,1)S(1)}, u32[]{:S(2)}, u32[]{:S(2)}) collective-permute-start(bf16[512,1024]{1,0:T(8,128)(2,1)S(1)} %add_convert_fusion.8), channel_id=1, source_target_pairs={{0,16},{8,24},{16,0},{24,8},{1,17},{9,25},{17,1},{25,9},{2,18},{10... | collective-permute-start | bytes 3145736 | tf_op jit(solution)/shard_map/ppermute | solution.py:241
  451.8 44.9 %collective-permute-start.24 = (bf16[512,1024]{1,0:T(8,128)(2,1)S(1)}, bf16[512,1024]{1,0:T(8,128)(2,1)S(1)}, u32[]{:S(2)}, u32[]{:S(2)}) collective-permute-start(bf16[512,1024]{1,0:T(8,128)(2,1)S(1)} %add_convert_fusion.7), channel_id=1, source_target_pairs={{0,24},{8,16},{16,8},{24,0},{1,25},{9,17},{17,9},{25,1},{2,26},{10... | collective-permute-start | bytes 3145736 | tf_op jit(solution)/shard_map/ppermute | solution.py:241
  510.0 106.6 %all-gather.16.cloned.1.call-start = ((), (), s32[]{:S(2)}) async-start(), calls=%async_computation.13 | async-start | bytes 1310720 | tf_op jit(solution)/shard_map/all_gather | solution.py:432
  525.3 9.4 %collective-permute-start.41 = (bf16[512,256]{1,0:T(8,128)(2,1)}, bf16[512,256]{1,0:T(8,128)(2,1)}, u32[]{:S(2)}, u32[]{:S(2)}) collective-permute-start(bf16[512,256]{1,0:T(8,128)(2,1)} %get-tuple-element.72), channel_id=1, source_target_pairs={{0,8},{8,0},{16,24},{24,16},{1,9},{9,1},{17,25},{25,17},{2,10},{10... | collective-permute-start | bytes 786440 | tf_op jit(solution)/shard_map/ppermute | solution.py:241
  528.9 10.9 %collective-permute-start.43 = (bf16[512,256]{1,0:T(8,128)(2,1)}, bf16[512,256]{1,0:T(8,128)(2,1)}, u32[]{:S(2)}, u32[]{:S(2)}) collective-permute-start(bf16[512,256]{1,0:T(8,128)(2,1)} %get-tuple-element.73), channel_id=1, source_target_pairs={{0,24},{8,16},{16,8},{24,0},{1,25},{9,17},{17,9},{25,1},{2,26},{10... | collective-permute-start | bytes 786440 | tf_op jit(solution)/shard_map/ppermute | solution.py:241
  530.4 13.1 %collective-permute-start.42 = (bf16[512,256]{1,0:T(8,128)(2,1)}, bf16[512,256]{1,0:T(8,128)(2,1)S(1)}, u32[]{:S(2)}, u32[]{:S(2)}) collective-permute-start(bf16[512,256]{1,0:T(8,128)(2,1)} %get-tuple-element.74), channel_id=1, source_target_pairs={{0,16},{8,24},{16,0},{24,8},{1,17},{9,25},{17,1},{25,9},{2,18},{10... | collective-permute-start | bytes 786440 | tf_op jit(solution)/shard_map/ppermute | solution.py:241
  531.2 97.8 %reduce-scatter.5.cloned.1.call-start = ((), (), s32[]{:S(2)}) async-start(), calls=%async_computation.7 | async-start | bytes 983040 | tf_op jit(solution)/shard_map/reduce_scatter | solution.py:418
  543.6 22.5 %collective-permute-start.44 = (bf16[2048,128]{1,0:T(8,128)(2,1)S(1)}, bf16[2048,128]{1,0:T(8,128)(2,1)}, u32[]{:S(2)}, u32[]{:S(2)}) collective-permute-start(bf16[2048,128]{1,0:T(8,128)(2,1)S(1)} %pad_maximum_fusion.19), channel_id=1, source_target_pairs={{0,1},{1,0},{2,3},{3,2},{4,5},{5,4},{6,7},{7,6},{8,9},{9,8},{10,11... | collective-permute-start | bytes 1572872 | tf_op jit(solution)/shard_map/ppermute | solution.py:245
  599.3 110.9 %all-reduce.2.cloned.1.call-start = ((), (), s32[]{:S(2)}) async-start(), calls=%async_computation.9 | async-start | bytes 524288 | tf_op jit(solution)/shard_map/psum | solution.py:398
  607.5 13.8 %collective-permute-start.45 = (bf16[512,1024]{1,0:T(8,128)(2,1)}, bf16[512,1024]{1,0:T(8,128)(2,1)}, u32[]{:S(2)}, u32[]{:S(2)}) collective-permute-start(bf16[512,1024]{1,0:T(8,128)(2,1)} %convolution_convert_fusion.9), channel_id=1, source_target_pairs={{0,1},{1,0},{2,3},{3,2},{4,5},{5,4},{6,7},{7,6},{8,9},{9,8},{10,11... | collective-permute-start | bytes 3145736 | tf_op jit(solution)/shard_map/ppermute | solution.py:245
  609.7 16.1 %collective-permute-start.47 = (bf16[512,1024]{1,0:T(8,128)(2,1)}, bf16[512,1024]{1,0:T(8,128)(2,1)}, u32[]{:S(2)}, u32[]{:S(2)}) collective-permute-start(bf16[512,1024]{1,0:T(8,128)(2,1)} %convolution_convert_fusion.7), channel_id=1, source_target_pairs={{0,1},{1,0},{2,3},{3,2},{4,5},{5,4},{6,7},{7,6},{8,9},{9,8},{10,11... | collective-permute-start | bytes 3145736 | tf_op jit(solution)/shard_map/ppermute | solution.py:245
  611.4 18.7 %collective-permute-start.49 = (bf16[512,1024]{1,0:T(8,128)(2,1)}, bf16[512,1024]{1,0:T(8,128)(2,1)}, u32[]{:S(2)}, u32[]{:S(2)}) collective-permute-start(bf16[512,1024]{1,0:T(8,128)(2,1)} %convolution_convert_fusion.5), channel_id=1, source_target_pairs={{0,1},{1,0},{2,3},{3,2},{4,5},{5,4},{6,7},{7,6},{8,9},{9,8},{10,11... | collective-permute-start | bytes 3145736 | tf_op jit(solution)/shard_map/ppermute | solution.py:245
  613.0 6.4 collective-permute-start.53
  613.1 109.6 %all-gather.14.cloned.1.call-start = ((), (), s32[]{:S(2)}) async-start(), calls=%async_computation.11 | async-start | bytes 2621440 | tf_op jit(solution)/shard_map/all_gather | solution.py:424
  616.1 86.0 %collective-permute-start.51 = (bf16[512,1024]{1,0:T(8,128)(2,1)}, bf16[512,1024]{1,0:T(8,128)(2,1)}, u32[]{:S(2)}, u32[]{:S(2)}) collective-permute-start(bf16[512,1024]{1,0:T(8,128)(2,1)} %convolution_convert_fusion.3), channel_id=1, source_target_pairs={{0,1},{1,0},{2,3},{3,2},{4,5},{5,4},{6,7},{7,6},{8,9},{9,8},{10,11... | collective-permute-start | bytes 3145736 | tf_op jit(solution)/shard_map/ppermute | solution.py:245
  624.4 77.8 %collective-permute-start.46 = (bf16[512,1024]{1,0:T(8,128)(2,1)}, bf16[512,1024]{1,0:T(8,128)(2,1)}, u32[]{:S(2)}, u32[]{:S(2)}) collective-permute-start(bf16[512,1024]{1,0:T(8,128)(2,1)} %add_convert_fusion.2), channel_id=1, source_target_pairs={{0,8},{8,0},{16,24},{24,16},{1,9},{9,1},{17,25},{25,17},{2,10},{10... | collective-permute-start | bytes 3145736 | tf_op jit(solution)/shard_map/ppermute | solution.py:241
  628.5 73.6 %collective-permute-start.48 = (bf16[512,1024]{1,0:T(8,128)(2,1)}, bf16[512,1024]{1,0:T(8,128)(2,1)}, u32[]{:S(2)}, u32[]{:S(2)}) collective-permute-start(bf16[512,1024]{1,0:T(8,128)(2,1)} %add_convert_fusion.1), channel_id=1, source_target_pairs={{0,16},{8,24},{16,0},{24,8},{1,17},{9,25},{17,1},{25,9},{2,18},{10... | collective-permute-start | bytes 3145736 | tf_op jit(solution)/shard_map/ppermute | solution.py:241
  630.0 4.5 collective-permute-start.52
  633.0 69.2 %collective-permute-start.50 = (bf16[512,1024]{1,0:T(8,128)(2,1)}, bf16[512,1024]{1,0:T(8,128)(2,1)}, u32[]{:S(2)}, u32[]{:S(2)}) collective-permute-start(bf16[512,1024]{1,0:T(8,128)(2,1)} %add_convert_fusion), channel_id=1, source_target_pairs={{0,24},{8,16},{16,8},{24,0},{1,25},{9,17},{17,9},{25,1},{2,26},{10... | collective-permute-start | bytes 3145736 | tf_op jit(solution)/shard_map/ppermute | solution.py:241
  (80 other events, 712.6 us)
Sparse Core Ops, SparseCore 0:
  9.7 31.7 all-gather.7
  43.6 45.3 all-gather.9
  91.2 29.4 all-gather.11
  365.7 25.2 reduce-scatter.10
  393.8 42.4 reduce-scatter.8
  510.1 33.7 reduce-scatter.6
  545.7 25.3 all-gather.15
  599.5 20.8 reduce-scatter.4
  623.3 62.4 all-reduce.1
  687.6 35.0 all-gather.13

commit v2 on v1

v2 whole, which is shorter than its diff:
```python
import functools

import jax
import jax.numpy as jnp
from jax import lax
from jax.experimental import pallas as pl
from jax.experimental.pallas import tpu as pltpu
from jax.sharding import Mesh
from jax.sharding import PartitionSpec as P

HEAD_DIM = 64
NORM_EPS = 1e-05
MASKED = -1e30
START_MAX = -1e29
SCALE = HEAD_DIM ** (-0.5)
DOC = 1 << 16
F32 = jnp.float32
BF16 = jnp.bfloat16
NT = (((1,), (1,)), ((), ()))
TN = (((0,), (0,)), ((), ()))


def mm(a, b):
    return jnp.dot(a, b, preferred_element_type=F32)


def mm_nt(a, b):
    return lax.dot_general(a, b, NT, preferred_element_type=F32)


def mm_tn(a, b):
    return lax.dot_general(a, b, TN, preferred_element_type=F32)


def cost(us):
    return pl.CostEstimate(flops=int(us * 1e9), bytes_accessed=1000, transcendentals=0)


def whole_spec(shape, **kw):
    return pl.BlockSpec(shape, lambda *_: (0,) * len(shape), **kw)


def pick_spec(shape, index):
    return pl.BlockSpec((1,) + shape, lambda *_: (index,) + (0,) * len(shape))


def any_spec():
    return pl.BlockSpec(memory_space=pl.ANY)


def call(kernel, name, out_shape, in_specs, out_specs, grid=(1,), scratch=(), estimate=None, prefetch=1):
    return pl.pallas_call(
        kernel,
        out_shape=out_shape,
        grid_spec=pltpu.PrefetchScalarGridSpec(
            num_scalar_prefetch=prefetch,
            grid=grid,
            in_specs=in_specs,
            out_specs=out_specs,
            scratch_shapes=list(scratch),
        ),
        cost_estimate=estimate,
        name=name,
    )


def shape_of(*dims, dtype=BF16):
    return jax.ShapeDtypeStruct(dims, dtype)


def head_stack(rows, heads):
    lane = lax.broadcasted_iota(jnp.int32, rows.shape, 1) // HEAD_DIM
    return jnp.concatenate(
        [jnp.where(lane == h, rows, jnp.zeros_like(rows)) for h in range(heads)], axis=0
    )


def query_tile(step, n, info):
    r, dp = step % n, step // n
    return r, dp, r * 2 + (dp ^ info[1])


def key_tile(a, n, info):
    r = (a // 2) ^ info[0]
    return ((a % 2) ^ info[1]) * n + r, r * 2 + a % 2


def query_bounds(code_row, q_ids, half, heads):
    high = code_row[:, pl.ds(pl.multiple_of(q_ids * half, half), half)]
    low = (high // DOC) * DOC
    return jnp.concatenate([low] * heads, axis=1), jnp.concatenate([high] * heads, axis=1)


def key_pair(first, last, turn, n, info, half, code_col, bounds):
    low, high = bounds
    for i in range(2):
        a = first + 2 * turn + i
        place, k_ids = key_tile(jnp.minimum(a, last - 1), n, info)
        keys = code_col[pl.ds(pl.multiple_of(k_ids * half, half), half), 0:1]
        if i:
            keys = jnp.where(a < last, keys, -1)
        yield pl.multiple_of(place * half, half), (keys >= low) & (keys <= high)


def attend_kernel(n, heads, half, info, *refs):
    blocks, (w, code_row), (qkv, *outs, lse), (v_t, code_col) = (
        refs[: 2 * n],
        refs[2 * n : 2 * n + 2],
        refs[2 * n + 2 : 3 * n + 4],
        refs[3 * n + 4 :],
    )
    width = heads * HEAD_DIM
    step = pl.program_id(0)

    @pl.when(step == 0)
    def _():
        for k in range(2 * n):
            qkv[k * half : (k + 1) * half, :] = mm(blocks[k][0], w[...]).astype(BF16)
        v_t[...] = qkv[:, 2 * width : 3 * width].T
        code_col[...] = jnp.broadcast_to(code_row[...], (8, code_row.shape[1])).T

    r, dp, q_ids = query_tile(step, n, info)
    q_rows = qkv[pl.ds(pl.multiple_of(step * half, half), half), 0:width] * jnp.asarray(SCALE, BF16)
    q_heads = head_stack(q_rows, heads)

    first, last = info[2 + q_ids], info[2 + 2 * n + q_ids]
    bounds = query_bounds(code_row, q_ids, half, heads)

    def one(turn, carry):
        run_max, run_sum, accs = carry
        new_max, tiles = run_max, []
        for pos, keys_ok in key_pair(first, last, turn, n, info, half, code_col, bounds):
            scores = mm_nt(qkv[pl.ds(pos, half), width : 2 * width], q_heads)
            scores = jnp.where(keys_ok, scores, MASKED)
            new_max = jnp.maximum(new_max, jnp.max(scores, axis=0, keepdims=True))
            tiles.append((pos, scores))
        factor = jnp.exp(run_max - new_max)
        new_sum = run_sum * factor
        new_accs = [accs[h] * factor[:, h * half : (h + 1) * half] for h in range(heads)]
        for pos, scores in tiles:
            weights = jnp.exp(scores - new_max)
            new_sum += jnp.sum(weights, axis=0, keepdims=True)
            weights = weights.astype(BF16)
            for h in range(heads):
                v_head = v_t[h * HEAD_DIM : (h + 1) * HEAD_DIM, pl.ds(pos, half)]
                new_accs[h] += mm(v_head, weights[:, h * half : (h + 1) * half])
        return new_max, new_sum, tuple(new_accs)

    start = (
        jnp.full((1, heads * half), START_MAX, F32),
        jnp.zeros((1, heads * half), F32),
        tuple(jnp.zeros((HEAD_DIM, half), F32) for _ in range(heads)),
    )
    run_max, run_sum, accs = lax.fori_loop(0, (last - first + 1) // 2, one, start)
    parts = [accs[h] / run_sum[:, h * half : (h + 1) * half] for h in range(heads)]
    mixed = jnp.concatenate(parts, axis=0).T.astype(BF16)
    for k in range(n):

        @pl.when(r == k)
        def _():
            outs[k][dp] = mixed

    logs = run_max + jnp.log(run_sum)
    at = pl.ds(pl.multiple_of(step * half, half), half)
    for h in range(heads):
        lse[h : h + 1, at] = logs[:, h * half : (h + 1) * half]


def attend(blocks, which, w_qkv, ids, n):
    info, code_row = ids
    half, dim = blocks[0].shape[1:]
    width = dim // (2 * n)
    heads = width // HEAD_DIM
    rows = 2 * n * half
    return call(
        functools.partial(attend_kernel, n, heads, half),
        "attend",
        [shape_of(rows, 3 * width)]
        + [shape_of(2, half, width)] * n
        + [shape_of(heads, rows, dtype=F32)],
        [pick_spec((half, dim), which)] * (2 * n) + [whole_spec((dim, 3 * width)), whole_spec((1, rows))],
        [whole_spec((rows, 3 * width))] + [whole_spec((2, half, width))] * n + [whole_spec((heads, rows))],
        grid=(2 * n,),
        scratch=[pltpu.VMEM((width, rows), BF16), pltpu.VMEM((rows, 8), jnp.int32)],
        estimate=cost(21),
    )(info, *blocks, w_qkv, code_row)


def attend_back_kernel(n, heads, half, info, *refs):
    qkv, w, lse, code_row = refs[:4]
    mixes, d_mixes, (d_other,) = refs[4 : 4 + n], refs[4 + n : 4 + 2 * n], refs[4 + 2 * n : 5 + 2 * n]
    out, part_mine, part_other, k_t, dk, dv, code_col, do_now, mix_now = refs[5 + 2 * n :]
    width = heads * HEAD_DIM
    step = pl.program_id(0)

    @pl.when(step == 0)
    def _():
        k_t[...] = qkv[:, width : 2 * width].T
        code_col[...] = jnp.broadcast_to(code_row[...], (8, code_row.shape[1])).T
        dk[...] = jnp.zeros_like(dk)
        dv[...] = jnp.zeros_like(dv)

    r, dp, q_ids = query_tile(step, n, info)
    rows = pl.ds(pl.multiple_of(step * half, half), half)
    q_heads = head_stack(qkv[rows, 0:width] * jnp.asarray(SCALE, BF16), heads)
    for k in range(n):

        @pl.when(r == k)
        def _():
            mix_now[...] = mixes[k][dp]

        @pl.when((r == k) & (dp == 0))
        def _():
            do_now[...] = d_mixes[k][0]

    @pl.when(dp == 1)
    def _():
        do_now[...] = d_other[r]

    do_rows = do_now[...]
    do_heads = head_stack(do_rows, heads)
    prod = (do_rows.astype(F32) * mix_now[...].astype(F32)).T
    delta = jnp.concatenate(
        [
            jnp.sum(prod[h * HEAD_DIM : (h + 1) * HEAD_DIM], axis=0, keepdims=True)
            for h in range(heads)
        ],
        axis=1,
    )
    logs = jnp.concatenate([lse[h : h + 1, rows] for h in range(heads)], axis=1)

    first, last = info[2 + q_ids], info[2 + 2 * n + q_ids]
    bounds = query_bounds(code_row, q_ids, half, heads)

    def one(turn, dqs):
        new, done = list(dqs), []
        for pos, keys_ok in key_pair(first, last, turn, n, info, half, code_col, bounds):
            keys = qkv[pl.ds(pos, half), width : 2 * width]
            values = qkv[pl.ds(pos, half), 2 * width : 3 * width]
            scores = mm_nt(keys, q_heads)
            probs = jnp.where(keys_ok, jnp.exp(scores - logs), 0.0)
            d_probs = mm_nt(values, do_heads)
            d_scores = (probs * (d_probs - delta)).astype(BF16)
            done.append((pos, mm(probs.astype(BF16), do_heads), mm(d_scores, q_heads)))
            for h in range(heads):
                k_head = k_t[h * HEAD_DIM : (h + 1) * HEAD_DIM, pl.ds(pos, half)]
                new[h] += mm(k_head, d_scores[:, h * half : (h + 1) * half])
        for pos, d_values, d_keys in done:
            dv[pl.ds(pos, half), :] += d_values
            dk[pl.ds(pos, half), :] += d_keys
        return tuple(new)

    dqs = lax.fori_loop(
        0,
        (last - first + 1) // 2,
        one,
        tuple(jnp.zeros((HEAD_DIM, half), F32) for _ in range(heads)),
    )
    out[rows, 0:width] = (jnp.concatenate(dqs, axis=0) * SCALE).T.astype(BF16)

    @pl.when(step == 2 * n - 1)
    def _():
        out[:, width : 2 * width] = dk[...].astype(BF16)
        out[:, 2 * width : 3 * width] = dv[...].astype(BF16)
        for k in range(n):
            part_mine[k] = mm_nt(out[k * half : (k + 1) * half, :], w[...]).astype(BF16)
            part_other[k] = mm_nt(out[(n + k) * half : (n + k + 1) * half, :], w[...]).astype(BF16)


def attend_back(qkv, w_qkv, lse, mixes, d_mixes, d_other, ids, n):
    info, code_row = ids
    rows, width3 = qkv.shape
    width, dim = width3 // 3, w_qkv.shape[0]
    heads = width // HEAD_DIM
    half = rows // (2 * n)
    tile = (2, half, width)
    return call(
        functools.partial(attend_back_kernel, n, heads, half),
        "attend_back",
        [shape_of(rows, width3), shape_of(n, half, dim), shape_of(n, half, dim)],
        [whole_spec((rows, width3)), whole_spec((dim, width3)), whole_spec((heads, rows)), whole_spec((1, rows))]
        + [whole_spec(tile)] * (2 * n)
        + [whole_spec((n, half, width))],
        [whole_spec((rows, width3)), whole_spec((n, half, dim)), whole_spec((n, half, dim))],
        grid=(2 * n,),
        scratch=[
            pltpu.VMEM((width, rows), BF16),
            pltpu.VMEM((rows, width), F32),
            pltpu.VMEM((rows, width), F32),
            pltpu.VMEM((rows, 8), jnp.int32),
            pltpu.VMEM((half, width), BF16),
            pltpu.VMEM((half, width), BF16),
        ],
        estimate=cost(26),
    )(info, qkv, w_qkv, lse, code_row, *mixes, *d_mixes, d_other)


def normed(rows):
    inv = lax.rsqrt(jnp.mean(rows * rows, axis=-1, keepdims=True) + NORM_EPS)
    return rows * inv, inv


def back_normed(rows, d_norm):
    norm, inv = normed(rows)
    return inv * (d_norm - norm * jnp.mean(d_norm * norm, axis=-1, keepdims=True))


def head_rows(info, j, width):
    return pl.ds(pl.multiple_of((j ^ (info[0] * 2 + info[1])) * width, width), width)


def mix_kernel(n, width, info, *refs):
    parts, (others, x, w), (att, hidden, norm) = refs[:n], refs[n : n + 3], refs[n + 3 :]
    total = x[0].astype(F32)
    for r in range(n):
        for q in range(2):
            j = r * 2 + q
            part = others[r] if q else parts[r][0]
            att[:, j * width : (j + 1) * width] = part
            total += mm(part, w[head_rows(info, j, width), :])
    hidden[...] = total
    norm[...] = normed(total)[0].astype(BF16)


def mix(info, parts, others, x, which, w_out, n):
    half, width = parts[0].shape[1:]
    dim = w_out.shape[0]
    return call(
        functools.partial(mix_kernel, n, width),
        "mix",
        [shape_of(half, dim), shape_of(half, dim, dtype=F32), shape_of(half, dim)],
        [whole_spec((2, half, width))] * n
        + [whole_spec((n, half, width)), pick_spec((half, dim), which), whole_spec((dim, dim))],
        [whole_spec((half, dim))] * 3,
        estimate=cost(5),
    )(info, *parts, others, x, w_out)


def feed_kernel(n, half, cols, which, info, *refs):
    two, cots = refs[: 2 * n], refs[2 * n : 4 * n]
    inner_out, d_gu_out, d_mine, d_other, o_mine, o_other, a_buf, c_buf, w_gu, w_dn, sems = refs[-11:]
    w_ffs = refs[4 * n : -11]
    step = pl.program_id(0)
    slot = step % 2

    def copies(r, at):
        got = []
        for dp in range(2):
            rows = pl.ds(dp * half, half)
            got.append(pltpu.make_async_copy(two[dp * n + r], a_buf.at[at, rows], sems.at[at, dp]))
            got.append(pltpu.make_async_copy(cots[dp * n + r].at[which], c_buf.at[at, rows], sems.at[at, 2 + dp]))
        return got

    @pl.when(step == 0)
    def _():
        for c in copies(0, 0):
            c.start()
        if len(w_ffs) == 1:
            n_z = w_ffs[0].shape[0]
            gu_rows, dn_rows = w_gu.shape[0] // n_z, cols // n_z
            for z in range(n_z):
                w_gu[z * gu_rows : (z + 1) * gu_rows, :] = w_ffs[0][z, :gu_rows, :]
                w_dn[z * dn_rows : (z + 1) * dn_rows, :] = w_ffs[0][z, gu_rows:, :]
        else:
            w_gu[...], w_dn[...] = w_ffs[0][...], w_ffs[1][...]

    for r in range(1, n):

        @pl.when(step + 1 == r)
        def _():
            for c in copies(r, r % 2):
                c.start()

    for c in copies(0, slot):
        c.wait()
    rows, cot = a_buf[slot], c_buf[slot]
    gu = mm(rows, w_gu[...])
    d_inner = mm_nt(cot, w_dn[...])
    gate, upper = gu[:, :cols], gu[:, cols:]
    sigma = jax.nn.sigmoid(gate)
    silu_gate = gate * sigma
    inner = (silu_gate * upper).astype(BF16)
    d_gate = (d_inner * upper * sigma * (1.0 + gate * (1.0 - sigma))).astype(BF16)
    d_upper = (d_inner * silu_gate).astype(BF16)
    inner_out[...] = inner
    d_gu_out[:, :cols] = d_gate
    d_gu_out[:, cols:] = d_upper
    d_rows = (mm_nt(d_gate, w_gu[:, :cols]) + mm_nt(d_upper, w_gu[:, cols:])).astype(BF16)
    d_mine[0] = d_rows[:half]
    d_other[0] = d_rows[half:]
    o_rows = mm(inner, w_dn[...]).astype(BF16)
    o_mine[0] = o_rows[:half]
    o_other[0] = o_rows[half:]


def feed(two, cots, which, w_ffs, cols, info, n):
    half, dim = two[0].shape
    rows = 2 * n * half
    block = pl.BlockSpec((1, half, dim), lambda i, *_: (i, 0, 0))
    return call(
        functools.partial(feed_kernel, n, half, cols, which),
        "feed",
        [shape_of(rows, cols), shape_of(rows, 2 * cols)] + [shape_of(n, half, dim)] * 4,
        [any_spec()] * (4 * n) + [whole_spec(w.shape) for w in w_ffs],
        [
            pl.BlockSpec((2 * half, cols), lambda i, *_: (i, 0)),
            pl.BlockSpec((2 * half, 2 * cols), lambda i, *_: (i, 0)),
        ]
        + [block] * 4,
        grid=(n,),
        scratch=[
            pltpu.VMEM((2, 2 * half, dim), BF16),
            pltpu.VMEM((2, 2 * half, dim), BF16),
            pltpu.VMEM((dim, 2 * cols), BF16),
            pltpu.VMEM((cols, dim), BF16),
            pltpu.SemaphoreType.DMA((2, 4)),
        ],
        estimate=cost(20),
    )(info, *two, *cots, *w_ffs)


def feed_grads_kernel(n, n_z, half, info, *refs):
    two, cots = (refs[: 2 * n], refs[2 * n : 4 * n]), refs[4 * n : 6 * n]
    inners, d_gus = refs[6 * n : 6 * n + 2], refs[6 * n + 2 : 6 * n + 4]
    a_buf, c_buf, z_buf, g_buf, acc_gu, acc_dn, sems = refs[-7:]
    outs = refs[6 * n + 4 : -7]
    step = pl.program_id(0)
    slot = step % 2
    gu_rows, dn_rows = acc_gu.shape[0] // n_z, acc_dn.shape[0] // n_z

    def copies(t, at):
        s, r = t // n, t % n
        got = []
        for dp in range(2):
            rows = pl.ds(dp * half, half)
            got.append(pltpu.make_async_copy(two[s][dp * n + r], a_buf.at[at, rows], sems.at[at, dp]))
            got.append(pltpu.make_async_copy(cots[dp * n + r].at[s], c_buf.at[at, rows], sems.at[at, 2 + dp]))
        rows = pl.ds(2 * r * half, 2 * half)
        got.append(pltpu.make_async_copy(inners[s].at[rows], z_buf.at[at], sems.at[at, 4]))
        got.append(pltpu.make_async_copy(d_gus[s].at[rows], g_buf.at[at], sems.at[at, 5]))
        return got

    @pl.when(step == 0)
    def _():
        for c in copies(0, 0):
            c.start()
        acc_gu[...] = jnp.zeros_like(acc_gu)
        acc_dn[...] = jnp.zeros_like(acc_dn)

    for t in range(1, 2 * n):

        @pl.when(step + 1 == t)
        def _():
            for c in copies(t, t % 2):
                c.start()

    for c in copies(0, slot):
        c.wait()
    acc_gu[...] += mm_tn(a_buf[slot], g_buf[slot])
    acc_dn[...] += mm_tn(z_buf[slot], c_buf[slot])

    @pl.when(step == 2 * n - 1)
    def _():
        if len(outs) == 1:
            for z in range(n_z):
                outs[0][z, :gu_rows, :] = acc_gu[z * gu_rows : (z + 1) * gu_rows, :].astype(BF16)
                outs[0][z, gu_rows:, :] = acc_dn[z * dn_rows : (z + 1) * dn_rows, :].astype(BF16)
        else:
            outs[0][...], outs[1][...] = acc_gu[...].astype(BF16), acc_dn[...].astype(BF16)


def feed_grads(two, cots, inners, d_gus, info, n, n_z):
    half, dim = two[0][0].shape
    cols = inners[0].shape[1]
    shapes = [(n_z, (dim + cols) // n_z, dim)] if 2 * cols == dim else [(dim, 2 * cols), (cols, dim)]
    return call(
        functools.partial(feed_grads_kernel, n, n_z, half),
        "feed_grads",
        [shape_of(*shape) for shape in shapes],
        [any_spec()] * (6 * n + 4),
        [whole_spec(shape) for shape in shapes],
        grid=(2 * n,),
        scratch=[
            pltpu.VMEM((2, 2 * half, dim), BF16),
            pltpu.VMEM((2, 2 * half, dim), BF16),
            pltpu.VMEM((2, 2 * half, cols), BF16),
            pltpu.VMEM((2, 2 * half, 2 * cols), BF16),
            pltpu.VMEM((dim, 2 * cols), F32),
            pltpu.VMEM((cols, dim), F32),
            pltpu.SemaphoreType.DMA((2, 6)),
        ],
        estimate=cost(20),
    )(info, *two[0], *two[1], *cots, *inners, *d_gus)


def turn_kernel(n, width, info, *refs):
    parts, (cot, hidden, w), (d_hidden, e_out), outs = (
        refs[:n],
        refs[n : n + 3],
        refs[n + 3 : n + 5],
        refs[n + 5 :],
    )
    d_norm = parts[0][...].astype(F32)
    for r in range(1, n):
        d_norm += parts[r][...].astype(F32)
    total = cot[0].astype(F32) + back_normed(hidden[...], d_norm)
    d_hidden[...] = total
    e_rows = total.astype(BF16)
    e_out[...] = e_rows
    for r in range(n):
        for q in range(2):
            outs[r][q] = mm_nt(e_rows, w[head_rows(info, r * 2 + q, width), :]).astype(BF16)


def turn(info, parts, cot, which, hidden, w_out, width, n):
    half, dim = hidden.shape
    return call(
        functools.partial(turn_kernel, n, width),
        "turn",
        [shape_of(half, dim, dtype=F32), shape_of(half, dim)] + [shape_of(2, half, width)] * n,
        [whole_spec((half, dim))] * n
        + [pick_spec((half, dim), which), whole_spec((half, dim)), whole_spec((dim, dim))],
        [whole_spec((half, dim))] * 2 + [whole_spec((2, half, width))] * n,
        estimate=cost(6),
    )(info, *parts, cot, hidden, w_out)


def out_grads_kernel(n, width, info, att0, att1, e0, e1, out):
    for j in range(2 * n):
        cols = slice(j * width, (j + 1) * width)
        total = mm_tn(att0[:, cols], e0[...]) + mm_tn(att1[:, cols], e1[...])
        out[head_rows(info, j, width), :] = total.astype(BF16)


def out_grads(info, atts, es, width, n):
    half, dim = es[0].shape
    return call(
        functools.partial(out_grads_kernel, n, width),
        "out_grads",
        shape_of(dim, dim),
        [whole_spec((half, dim))] * 4,
        whole_spec((dim, dim)),
        estimate=cost(5),
    )(info, *atts, *es)


def qkv_grads_kernel(n, half, info, *refs):
    blocks, (d0, d1, out) = refs[: 2 * n], refs[2 * n :]
    total = None
    for s, d_qkv in enumerate((d0, d1)):
        for k in range(2 * n):
            part = mm_tn(d_qkv[k * half : (k + 1) * half, :], blocks[k][s])
            total = part if total is None else total + part
    out[...] = total.T.astype(BF16)


def qkv_grads(info, blocks, d_qkvs, n):
    half, dim = blocks[0].shape[1:]
    rows, width3 = d_qkvs[0].shape
    return call(
        functools.partial(qkv_grads_kernel, n, half),
        "qkv_grads",
        shape_of(dim, width3),
        [whole_spec((2, half, dim))] * (2 * n) + [whole_spec((rows, width3))] * 2,
        whole_spec((dim, width3)),
        estimate=cost(9),
    )(info, *blocks, *d_qkvs)


def pack_qkv_kernel(width, info, gain, wq, wk, wv, mine, theirs):
    scale = gain[...]
    mine[...] = jnp.zeros_like(mine)
    theirs[...] = jnp.zeros_like(theirs)
    for out, flip in ((mine, 0), (theirs, 1)):
        at = (info[0] * 2 + (info[1] ^ flip)) * width
        for i, w in enumerate((wq, wk, wv)):
            rows = w[:, pl.ds(pl.multiple_of(at, width), width)].astype(F32)
            out[:, i * width : (i + 1) * width] = (rows * scale).astype(BF16)


def pack_hidden_kernel(n_z, cut, down_rows, info, gain, wg, wu, mine, theirs):
    scale = gain[...]
    for out, flip in ((mine, 0), (theirs, 1)):
        for i, w in enumerate((wg, wu)):
            for z in range(n_z):
                at = (2 * z + (info[1] ^ flip)) * down_rows + info[0] * cut
                rows = w[:, pl.ds(pl.multiple_of(at, cut), cut)].astype(F32)
                to = (i * n_z + z) * cut
                out[:, to : to + cut] = (rows * scale).astype(BF16)


def pack(kernel, name, info, gain, weights, cols):
    shard = gain.shape[0]
    return call(
        kernel,
        name,
        [shape_of(shard, cols)] * 2,
        [whole_spec(a.shape) for a in (gain, *weights)],
        [whole_spec((shard, cols))] * 2,
        estimate=cost(9),
    )(info, gain, *weights)


def finish_kernel(n, shard, cut, down_rows, info, *refs):
    parts, (gain, wg, wu), (gg, gu, gd, gain_out) = refs[:n], refs[n : n + 3], refs[n + 3 :]
    chip, core = info[0], info[1]
    scale = gain[...]
    half = wg.shape[1] // (2 * n)
    total = jnp.zeros((shard, 1), F32)
    for r in range(n):
        gd[pl.ds(pl.multiple_of((chip ^ r) * cut, cut), cut), :] = parts[r][2 * shard : 2 * shard + cut, :].astype(F32)
        for q in range(2):
            rows = slice(q * shard, (q + 1) * shard)
            for z in range(half // cut):
                at = (2 * z + (core ^ q)) * down_rows + (chip ^ r) * cut
                at = pl.ds(pl.multiple_of(at, cut), cut)
                raw = parts[r][rows, z * cut : (z + 1) * cut].astype(F32)
                total += jnp.sum(raw * wg[:, at].astype(F32), axis=1, keepdims=True)
                gg[:, at] = raw * scale
                raw = parts[r][rows, half + z * cut : half + (z + 1) * cut].astype(F32)
                total += jnp.sum(raw * wu[:, at].astype(F32), axis=1, keepdims=True)
                gu[:, at] = raw * scale
    gain_out[...] = jnp.broadcast_to(total, (shard, 128)).T[0:1, :]


def finish_qkv_kernel(n, width, info, *refs):
    parts, (gain, *ws), (*grads, go, gain_out) = refs[:n], refs[n : n + 4], refs[n + 4 :]
    out = parts[0][:, 6 * width :].astype(F32)
    for r in range(1, n):
        out += parts[r][:, 6 * width :].astype(F32)
    go[...] = out
    scale = gain[...]
    total = jnp.zeros(scale.shape, F32)
    for r in range(n):
        for q in range(2):
            at = head_rows(info, r * 2 + q, width)
            for i in range(3):
                raw = parts[r][:, (3 * q + i) * width : (3 * q + i + 1) * width].astype(F32)
                total += jnp.sum(raw * ws[i][:, at].astype(F32), axis=1, keepdims=True)
                grads[i][:, at] = raw * scale
    gain_out[...] = jnp.broadcast_to(total, (scale.shape[0], 128)).T[0:1, :]


def send(value, step):
    count = lax.axis_size("ctx")
    return lax.ppermute(value, "ctx", [(i, i ^ step) for i in range(count)])


def swap(value):
    return lax.ppermute(value, "core", [(0, 1), (1, 0)])


def after(value, *others):
    return lax.optimization_barrier((value,) + others)[0]


def gather_near(own):
    n = lax.axis_size("ctx")
    return [send(own, r) for r in range(1, 3 if n == 4 else n)]


def gather_far(near):
    n = lax.axis_size("ctx")
    if n != 4:
        return near
    onward = jnp.where(lax.axis_index("core") == 0, near[1], near[0])
    pairs = [(c * 2 + p, (c ^ (1 + p)) * 2 + p) for c in range(n) for p in range(2)]
    return near + [lax.ppermute(onward, ("ctx", "core"), pairs)]


def gather_cores(own, others):
    mine = [own] + others
    return mine + [swap(block) for block in mine]


def together(*values):
    return lax.optimization_barrier(values)


def plane_join(mine, other):
    got = swap(other)
    return [(mine[r].astype(F32) + got[r].astype(F32)).astype(BF16) for r in range(mine.shape[0])]


def plane_send(joined):
    return [joined[0]] + [send(joined[r], r) for r in range(1, len(joined))]


def ordered(first, second, core):
    return jnp.where(core == 0, jnp.stack([first, second]), jnp.stack([second, first]))


def send_heads(parts):
    return [parts[0]] + [send(parts[r], r) for r in range(1, len(parts))]


def other_heads(got):
    return swap(jnp.stack([g[1] for g in got]))


def mask_info(codes, half, chip, core):
    tiles = codes.reshape(-1, half)
    first, last = tiles[:, :1], tiles[:, half - 1 :]
    every = codes.reshape(1, -1)

    def count(test):
        return jnp.sum(test.astype(jnp.int32), axis=1)

    low = count(every // DOC < first // DOC) // half
    ends = jnp.minimum(count(every // DOC <= last // DOC), count(every % DOC <= last % DOC))
    high = (ends + half - 1) // half
    info = jnp.concatenate([jnp.stack([chip, core]).astype(jnp.int32), low, high])
    return info, every


def body(
    block_in, cotangent, doc_ids, block_ids, gain_attn, w_query, w_key, w_value, w_out, gain_ffn, w_gate, w_up, w_down
):
    n, n_z = lax.axis_size("ctx"), lax.axis_size("z")
    chip, core = lax.axis_index("ctx"), lax.axis_index("core")
    piece, dim = block_in.shape[1], block_in.shape[2]
    half = piece // 2
    shard = w_query.shape[0]
    width = dim // (2 * n)
    down_rows = w_down.shape[0]
    cut = down_rows // n
    me = jnp.stack([chip, core]).astype(jnp.int32)

    def own_half(rows, which):
        return lax.dynamic_slice_in_dim(rows, which * half, half, axis=0)

    def both_rows(rows):
        return ordered(own_half(rows, core), swap(own_half(rows, 1 - core)), core)

    x_rows = both_rows(block_in[0])
    n_one, inv1 = normed(x_rows.astype(F32))
    one_own = n_one.astype(BF16)
    one_near = gather_near(one_own)

    def head_cols(which):
        at = (chip * 2 + which) * width
        return jnp.concatenate(
            [lax.dynamic_slice_in_dim(w, at, width, axis=1) for w in (w_query, w_key, w_value)], axis=1
        )

    def hidden_slices(which):
        return jnp.concatenate(
            [
                lax.dynamic_slice_in_dim(w, (2 * z + which) * down_rows + chip * cut, cut, axis=1)
                for w in (w_gate, w_up)
                for z in range(n_z)
            ],
            axis=1,
        )

    def scaled(w, gain):
        return (w.astype(F32) * gain.astype(F32)[:, None]).astype(BF16)

    def over_z(mine, theirs):
        both = ordered(mine, swap(theirs), core).reshape(2 * shard, -1)
        return lax.all_gather(both, "z", axis=0, tiled=True)

    g1, g2 = gain_attn.astype(F32)[:, None], gain_ffn.astype(F32)[:, None]
    if cut % 128 == 0:
        packed = after(me, one_own)
        w_qkv = over_z(
            *pack(functools.partial(pack_qkv_kernel, width), "pack_qkv", packed, g1, (w_query, w_key, w_value), 4 * width)
        )
        hidden_pair = pack(
            functools.partial(pack_hidden_kernel, n_z, cut, down_rows),
            "pack_hidden",
            packed,
            g2,
            (w_gate, w_up),
            2 * n_z * cut,
        )
    else:
        w_qkv = over_z(scaled(head_cols(core), gain_attn), scaled(head_cols(1 - core), gain_attn))
        hidden_pair = scaled(hidden_slices(core), gain_ffn), scaled(hidden_slices(1 - core), gain_ffn)
    w_out_full = lax.all_gather(after(w_out, w_qkv), ("z", "core"), axis=0, tiled=True)
    cols = n_z * cut
    down_cut = lax.dynamic_slice_in_dim(w_down, chip * cut, cut, axis=0)
    if 2 * cols == dim:
        gu_cut = ordered(hidden_pair[0], swap(hidden_pair[1]), core).reshape(2 * shard, dim)
        w_ff = jnp.concatenate([gu_cut, down_cut], axis=0)
        w_ffs = [lax.all_gather(after(w_ff, w_out_full), "z", axis=0)]
    else:
        w_ffs = [over_z(*hidden_pair), lax.all_gather(down_cut, "z", axis=0, tiled=True)]

    one_near, w_qkv, code = together(one_near, w_qkv, doc_ids[0] * DOC + block_ids[0])
    one = gather_cores(one_own, gather_far(one_near))
    codes = jnp.stack([code] + [send(code, r) for r in range(1, n)])
    codes = ordered(codes, swap(codes), core)
    ids = [mask_info(codes[s], half, chip, core) for s in range(2)]
    infos, code_rows = [i[0] for i in ids], [i[1] for i in ids]
    cot_rows = both_rows(after(cotangent[0], one_own))
    one, infos, cot_own = together(one, infos, cot_rows)

    cot_near = gather_near(cot_own)
    qkv0, *mixed0, lse0 = attend(one, 0, w_qkv, (infos[0], code_rows[0]), n)
    mixed0, cot_near, info1 = together(mixed0, cot_near, infos[1])
    got0 = send_heads(mixed0)
    cot_all = gather_far(cot_near)
    qkv1, *mixed1, lse1 = attend(one, 1, w_qkv, (info1, code_rows[1]), n)
    other0 = other_heads(got0)
    mixed1, got0, other0, cot_all, go = together(mixed1, got0, other0, cot_all, me)
    got1 = send_heads(mixed1)
    cots = gather_cores(cot_own, cot_all)
    att0, hidden0, norm0 = mix(go, got0, other0, x_rows, 0, w_out_full, n)
    other1 = other_heads(got1)
    norm0, got1, other1, go = together(norm0, got1, other1, me)
    near0 = gather_near(norm0)
    att1, hidden1, norm1 = mix(go, got1, other1, x_rows, 1, w_out_full, n)
    near0, norm1, cots = together(near0, norm1, cots)
    two0 = gather_cores(norm0, gather_far(near0))
    two0, norm1, go = together(two0, norm1, me)

    near1 = gather_near(norm1)
    inner0, d_gu0, d_mine0, d_other0, o_mine0, o_other0 = feed(two0, cots, 0, w_ffs, cols, go, n)
    near1, d_mine0, d_other0 = together(near1, d_mine0, d_other0)
    far1 = gather_far(near1)
    joined0 = plane_join(d_mine0, d_other0)
    two1 = gather_cores(norm1, far1)
    joined0, two1, go = together(joined0, two1, me)
    parts0 = plane_send(joined0)
    inner1, d_gu1, d_mine1, d_other1, o_mine1, o_other1 = feed(two1, cots, 1, w_ffs, cols, go, n)
    parts0, d_mine1, d_other1, go = together(parts0, d_mine1, d_other1, me)
    joined1 = plane_join(d_mine1, d_other1)
    d_hidden0, e0, *d_mix0 = turn(go, parts0, cot_rows, 0, hidden0, w_out_full, width, n)
    joined1, d_mix0, o_other0, o_other1, go = together(joined1, d_mix0, o_other0, o_other1, me)
    parts1 = plane_send(joined1)
    d_got0 = send_heads(d_mix0)
    out_others = [swap(o_other0), swap(o_other1)]
    grads_ff = feed_grads((two0, two1), cots, (inner0, inner1), (d_gu0, d_gu1), go, n, n_z)
    d_other_heads0 = other_heads(d_got0)
    parts1, d_got0, d_other_heads0, out_others, raw_ff, go = together(
        parts1, d_got0, d_other_heads0, out_others, grads_ff, me
    )
    grads_ff = [lax.psum_scatter(g, "z", scatter_dimension=0, tiled=True) for g in raw_ff]
    d_hidden1, e1, *d_mix1 = turn(go, parts1, cot_rows, 1, hidden1, w_out_full, width, n)
    d_mix1, o_mine0, o_mine1, go = together(d_mix1, o_mine0, o_mine1, me)
    d_got1 = send_heads(d_mix1)
    d_other_heads1 = other_heads(d_got1)
    grads_wo = out_grads(go, (att0, att1), (e0, e1), width, n)
    wo_shard = lax.psum_scatter(grads_wo, ("z", "core"), scatter_dimension=0, tiled=True)
    outs = [
        jnp.stack([(m[r].astype(F32) + t[r].astype(F32)).astype(BF16) for m, t in zip((o_mine0, o_mine1), out_others)])
        for r in range(n)
    ]
    outs, grads_wo, info0 = together(outs, grads_wo, infos[0])

    out_near = [send(outs[r], r) for r in range(1, 3)]
    d_qkv0, a_mine0, a_other0 = attend_back(
        qkv0, w_qkv, lse0, mixed0, d_got0, d_other_heads0, (info0, code_rows[0]), n
    )
    out_near, a_mine0, a_other0, d_got1, d_other_heads1 = together(out_near, a_mine0, a_other0, d_got1, d_other_heads1)
    joined0 = plane_join(a_mine0, a_other0)
    joined0, info1 = together(joined0, infos[1])
    parts0 = plane_send(joined0)
    d_qkv1, a_mine1, a_other1 = attend_back(
        qkv1, w_qkv, lse1, mixed1, d_got1, d_other_heads1, (info1, code_rows[1]), n
    )
    parts0, a_mine1, a_other1, grads_ff = together(parts0, a_mine1, a_other1, grads_ff)
    joined1 = plane_join(a_mine1, a_other1)
    joined1, go, outs_far = together(joined1, me, outs[3:])
    parts1 = plane_send(joined1)
    grad_qkv = qkv_grads(go, one, (d_qkv0, d_qkv1), n)
    grad_qkv = lax.psum_scatter(grad_qkv, "z", scatter_dimension=0, tiled=True)
    out_parts = [outs[0]] + out_near + [send(o, r) for r, o in enumerate(outs_far, 3)]
    out_rows = jnp.stack([hidden0, hidden1])
    for part in out_parts:
        out_rows = out_rows + part.astype(F32)
    out_rows = out_rows.astype(BF16)
    in_rows = [
        d_hidden + back_normed(x_rows[s].astype(F32), sum(p.astype(F32) for p in parts))
        for s, (d_hidden, parts) in enumerate(((d_hidden0, parts0), (d_hidden1, parts1)))
    ]

    def own_rows(pair):
        mine = lax.dynamic_index_in_dim(pair, core, 0, keepdims=False)
        theirs = swap(lax.dynamic_index_in_dim(pair, 1 - core, 0, keepdims=False))
        return ordered(mine, theirs, core).reshape(1, piece, dim)

    block_out = own_rows(out_rows)
    input_grad = own_rows(jnp.stack(in_rows))

    def to_owner(part):
        mine = lax.dynamic_slice_in_dim(part, core * shard, shard, axis=0)
        theirs = lax.dynamic_slice_in_dim(part, (1 - core) * shard, shard, axis=0)
        return mine, swap(theirs)

    if len(grads_ff) == 1:
        gu_part, dn_part = grads_ff[0][0, : 2 * shard], grads_ff[0][0, 2 * shard :]
    else:
        gu_part, dn_part = grads_ff
    if cut % 128 == 0:
        sent = jnp.concatenate([*to_owner(gu_part), dn_part], axis=0)
        packs = [sent] + [send(sent, r) for r in range(1, n)]
        ff = w_gate.shape[1]
        raw = call(
            functools.partial(finish_kernel, n, shard, cut, down_rows),
            "finish",
            [shape_of(shard, ff, dtype=F32)] * 2
            + [shape_of(down_rows, dim, dtype=F32), shape_of(1, shard, dtype=F32)],
            [whole_spec(sent.shape)] * n + [whole_spec((shard, 1)), whole_spec((shard, ff)), whole_spec((shard, ff))],
            [whole_spec((shard, ff))] * 2 + [whole_spec((down_rows, dim)), whole_spec((1, shard))],
            estimate=cost(7),
        )(me, *packs, g2, w_gate, w_up)
        grad_gate, grad_up, grad_down, grad_gain_ffn = raw
        both = jnp.concatenate([*to_owner(grad_qkv), wo_shard], axis=1)
        boths = [both] + [send(both, r) for r in range(1, n)]
        raw = call(
            functools.partial(finish_qkv_kernel, n, width),
            "finish_qkv",
            [shape_of(shard, dim, dtype=F32)] * 4 + [shape_of(1, shard, dtype=F32)],
            [whole_spec(both.shape)] * n + [whole_spec((shard, 1))] + [whole_spec((shard, dim))] * 3,
            [whole_spec((shard, dim))] * 4 + [whole_spec((1, shard))],
            estimate=cost(4),
        )(me, *boths, g1, w_query, w_key, w_value)
        grad_q, grad_k, grad_v, grad_wo, grad_gain_attn = raw
        grad_gain_attn, grad_gain_ffn = grad_gain_attn.reshape(shard), grad_gain_ffn.reshape(shard)
    else:

        def over_ctx(part):
            both = ordered(*to_owner(part), core)
            return lax.all_gather(both, "ctx", axis=0).transpose(2, 0, 1, 3)

        qkv_shard = over_ctx(grad_qkv).reshape(shard, 2 * n, 3, width).astype(F32)
        raw_q, raw_k, raw_v = (qkv_shard[:, :, i].reshape(shard, dim) for i in range(3))
        gu_shard = over_ctx(gu_part).reshape(shard, n, 2, 2, n_z, cut).astype(F32)
        raw_g, raw_u = (
            gu_shard[:, :, :, i].transpose(0, 3, 2, 1, 4).reshape(shard, -1) for i in range(2)
        )
        grad_down = lax.all_gather(dn_part, "ctx", axis=0, tiled=True).astype(F32)
        grad_wo = lax.psum(wo_shard, "ctx").astype(F32)

        def row_sum(pairs):
            return sum(jnp.sum(w.astype(F32) * g, axis=1) for w, g in pairs)

        grad_gain_attn = row_sum([(w_query, raw_q), (w_key, raw_k), (w_value, raw_v)])
        grad_gain_ffn = row_sum([(w_gate, raw_g), (w_up, raw_u)])
        grad_q, grad_k, grad_v, grad_gate, grad_up = raw_q * g1, raw_k * g1, raw_v * g1, raw_g * g2, raw_u * g2
    return (
        block_out,
        input_grad,
        grad_gain_attn,
        grad_q,
        grad_k,
        grad_v,
        grad_wo,
        grad_gain_ffn,
        grad_gate,
        grad_up,
        grad_down,
    )


def solution(mesh):
    n_ctx, n_fsdp = mesh.devices.shape
    inner = Mesh(mesh.devices.reshape(n_ctx, n_fsdp // 2, 2), ("ctx", "z", "core"))
    fsdp = ("z", "core")
    act, ids, vec, mat = P(fsdp, "ctx", None), P(fsdp, "ctx"), P(fsdp), P(fsdp, None)
    return jax.shard_map(
        body,
        mesh=inner,
        in_specs=(act, act, ids, ids, vec, mat, mat, mat, mat, vec, mat, mat, mat),
        out_specs=(act, act, vec, mat, mat, mat, mat, vec, mat, mat, mat),
        check_vma=False,
    )
```

time: 769 us -> 530 us (0.69)
  matrix products: 139 us -> 0 us
  blocking collectives: 139 us -> 0 us
  Pallas kernels: 87.6 us -> 212 us
  local copies, waits for them, and re-layouts: 121 us -> 21.9 us
  other arithmetic: 66.3 us -> 43.8 us
  starting transfers between devices: 41.1 us -> 63 us
  waiting for transfers between devices: 148 us -> 166 us
    all_gather x3 -> x0, blocking collectives: 139 us -> none  [the longest x1 64.7 us: body(): lax.all_gather(jnp.stack([doc_ids[0], block_ids[0]]), ('ctx', 'core'))]
    dot_general x54 -> x0, matrix products: 139 us -> none  [the longest x25 56.9 us: mm_nt(): return lax.dot_general(a, b, NT, preferred_element_type=F32)]
    pallas_call x4 -> x17, Pallas kernels: 87.6 us -> 212 us  [the longest x2 54.2 us: attend_back(): call(functools.partial(attend_back_kernel, n, heads, half), 'attend_back'...]
    unnamed x228 -> x151, local copies, waits for them, and re-layouts: 77.3 us -> 10.9 us
    ppermute x0 -> x4, waiting for transfers between devices: none -> 27.2 us  [gather_far(): return near + [lax.ppermute(onward, ('ctx', 'core'), pairs)]]
    ppermute x24 -> x44, starting transfers between devices: 31.4 us -> 51.4 us  [send(): return lax.ppermute(value, 'ctx', [(i, i ^ step) for i in range(count)])]
    unnamed x17 -> x0, other arithmetic: 14.8 us -> none
    ppermute x24 -> x44, waiting for transfers between devices: 137 us -> 124 us  [send(): return lax.ppermute(value, 'ctx', [(i, i ^ step) for i in range(count)])]
  transfers between devices with their start and end apart: 64 -> 89, of which waited for: 13 -> 30; matrix products, arithmetic and copies ran while one was open for 38% -> 9% of each run, Pallas kernels for 12% -> 36%
where the time goes in v2:
time: 530 us; the launch traced here: 522 us
  Pallas kernels  212 us (40%)
  waiting for transfers between devices  166 us (31%)
  starting transfers between devices  63 us (12%)
  other arithmetic  43.8 us (8%)
  local copies, waits for them, and re-layouts  21.9 us (4%)
  between operations  15.4 us (3%)
    ppermute x44, waiting for transfers between devices, send(): return lax.ppermute(value, 'ctx', [(i, i ^ step) for i in range(count)])  124 us
    pallas_call x2, Pallas kernels, attend_back(): call(functools.partial(attend_back_kernel, n, heads, half), 'attend_back'...  54.2 us
    ppermute x44, starting transfers between devices, send(): return lax.ppermute(value, 'ctx', [(i, i ^ step) for i in range(count)])  51.4 us
    pallas_call x2, Pallas kernels, attend(): call(functools.partial(attend_kernel, n, heads, half), 'attend', [shape_o...  42.8 us
    pallas_call x2, Pallas kernels, feed(): call(functools.partial(feed_kernel, n, half, cols, which), 'feed', [shape...  40.7 us
    ppermute x4, waiting for transfers between devices, gather_far(): return near + [lax.ppermute(onward, ('ctx', 'core'), pairs)]  27.2 us
    pallas_call x1, Pallas kernels, feed_grads(): call(functools.partial(feed_grads_kernel, n, n_z, half), 'feed_grads', [s...  20.4 us
    convert_element_type x4, other arithmetic, plane_join(): (mine[r].astype(F32) + got[r].astype(F32)).astype(BF16)  13.7 us
  transfers between devices with their start and end apart: 89, of which 30 were waited for; matrix products, arithmetic and copies ran while one was open for 9% of the time, Pallas kernels for 36%

profile of v2, /device:TPU:0, one launch (start us, length us, event | category | flops | bytes accessed | tf_op | source)
XLA Modules:
  0.0 522.3 jit_solution(16296373071152706948)
XLA Ops:
  11.4 2.7 pack_qkv.1
  15.7 1.7 maximum_select_fusion.5
  18.3 2.8 collective-permute-start.1
  21.1 1.5 collective-permute-start.2
  22.6 2.1 dynamic-slice_bitcast_fusion.1
  24.7 3.4 pack_hidden.1
  32.0 12.7 %collective-permute-done.1.refs_1_ = bf16[2,256,1024]{2,1,0:T(8,128)(2,1)} collective-permute-done((bf16[2,256,1024]{2,1,0:T(8,128)(2,1)S(1)}, bf16[2,256,1024]{2,1,0:T(8,128)(2,1)}, u32[]{:S(2)}, u32[]{:S(2)}) %collective-permute-start.1) | collective-permute-done | bytes 1048608 | tf_op jit(solution)/shard_map/ppermute | solution.py:646
  44.7 1.5 collective-permute-done.2.refs_2_
  46.2 2.0 all-gather.5.cloned.1.call-done.refs_8_.refs_1_
  48.2 2.4 collective-permute-start.11
  58.1 13.4 %collective-permute-done.4.refs_3_ = bf16[2,256,1024]{2,1,0:T(8,128)(2,1)} collective-permute-done((bf16[2,256,1024]{2,1,0:T(8,128)(2,1)S(1)}, bf16[2,256,1024]{2,1,0:T(8,128)(2,1)}, u32[]{:S(2)}, u32[]{:S(2)}) %collective-permute-start.4) | collective-permute-done | bytes 1048608 | tf_op jit(solution)/shard_map/ppermute | solution.py:668
  75.5 1.5 collective-permute-start.15
  77.2 21.1 %attend.2 = (bf16[2048,384]{1,0:T(8,128)(2,1)}, bf16[2,256,128]{2,1,0:T(8,128)(2,1)}, bf16[2,256,128]{2,1,0:T(8,128)(2,1)}, bf16[2,256,128]{2,1,0:T(8,128)(2,1)}...) custom-call(s32[18]{0:T(128)} %pad_add_fusion.2.info, bf16[2,256,1024]{2,1,0:T(8,128)(2,1)} %copy-done.25, ...), custom_call_target="tpu_custom_call" | custom-call | flops 20999999488 | bytes 1000 | tf_op jit(solution)/shard_map/attend/pallas_call | solution.py:175
  98.4 1.8 collective-permute-done.14.refs_9_.refs_17_
  101.9 1.5 collective-permute-start.17
  106.8 3.6 collective-permute-done.18.refs_3_
  112.7 21.7 %attend.3 = (bf16[2048,384]{1,0:T(8,128)(2,1)}, bf16[2,256,128]{2,1,0:T(8,128)(2,1)}, bf16[2,256,128]{2,1,0:T(8,128)(2,1)}, bf16[2,256,128]{2,1,0:T(8,128)(2,1)}...) custom-call(s32[18]{0:T(128)} %pad_add_fusion.4.info, bf16[2,256,1024]{2,1,0:T(8,128)(2,1)} %copy-done.25, ...), custom_call_target="tpu_custom_call" | custom-call | flops 20999999488 | bytes 1000 | tf_op jit(solution)/shard_map/attend/pallas_call | solution.py:175
  134.4 2.0 collective-permute-start.23
  138.8 3.1 collective-permute-done.23.refs_3_
  141.9 2.4 collective-permute-done.22.refs_2_
  145.8 5.2 mix.2
  151.8 1.4 collective-permute-start.26
  153.3 5.1 mix.3
  158.4 7.2 %collective-permute-done.25.refs_1_ = bf16[256,1024]{1,0:T(8,128)(2,1)} collective-permute-done((bf16[256,1024]{1,0:T(8,128)(2,1)}, bf16[256,1024]{1,0:T(8,128)(2,1)}, u32[]{:S(2)}, u32[]{:S(2)}) %collective-permute-start.25) | collective-permute-done | bytes 524320 | tf_op jit(solution)/shard_map/ppermute | solution.py:646
  168.6 6.7 %collective-permute-done.31.refs_3_ = bf16[256,1024]{1,0:T(8,128)(2,1)S(1)} collective-permute-done((bf16[256,1024]{1,0:T(8,128)(2,1)S(1)}, bf16[256,1024]{1,0:T(8,128)(2,1)S(1)}, u32[]{:S(2)}, u32[]{:S(2)}) %collective-permute-start.31) | collective-permute-done | bytes 524320 | tf_op jit(solution)/shard_map/ppermute | solution.py:668
  175.4 1.9 collective-permute-done.35.refs_7_
  179.3 20.2 %feed.2 = (bf16[2048,512]{1,0:T(8,128)(2,1)}, bf16[2048,1024]{1,0:T(8,128)(2,1)}, bf16[4,256,1024]{2,1,0:T(8,128)(2,1)}, bf16[4,256,1024]{2,1,0:T(8,128)(2,1)}, ...) custom-call(s32[2]{0:T(128)} %pad_add_fusion.1.info, bf16[256,1024]{1,0:T(8,128)(2,1)} %get-tuple-element.290.refs_0_, ...), custom_call_target="tpu_custom_call" | custom-call | flops 20000000000 | bytes 1000 | tf_op jit(solution)/shard_map/feed/pallas_call | solution.py:400
  199.6 1.7 collective-permute-start.40
  201.8 7.1 %collective-permute-done.40.refs_3_.refs_11_ = bf16[256,1024]{1,0:T(8,128)(2,1)S(1)} collective-permute-done((bf16[256,1024]{1,0:T(8,128)(2,1)S(1)}, bf16[256,1024]{1,0:T(8,128)(2,1)S(1)}, u32[]{:S(2)}, u32[]{:S(2)}) %collective-permute-start.40) | collective-permute-done | bytes 524320 | tf_op jit(solution)/shard_map/ppermute | solution.py:668
  208.9 3.5 fusion.28
  212.5 1.7 collective-permute-start.45
  214.6 1.5 collective-permute-start.47
  216.1 20.5 %feed.3 = (bf16[2048,512]{1,0:T(8,128)(2,1)}, bf16[2048,1024]{1,0:T(8,128)(2,1)}, bf16[4,256,1024]{2,1,0:T(8,128)(2,1)}, bf16[4,256,1024]{2,1,0:T(8,128)(2,1)}, ...) custom-call(s32[2]{0:T(128)} %pad_add_fusion.1.info, bf16[256,1024]{1,0:T(8,128)(2,1)} %get-tuple-element.320.refs_0_.refs_8_, ...), custom_call_target="tpu_custom_call" | custom-call | flops 20000000000 | bytes 1000 | tf_op jit(solution)/shard_map/feed/pallas_call | solution.py:400
  236.6 2.6 collective-permute-done.46.refs_2_
  240.3 6.0 %turn.2 = (f32[256,1024]{1,0:T(8,128)}, bf16[256,1024]{1,0:T(8,128)(2,1)}, bf16[2,256,128]{2,1,0:T(8,128)(2,1)}, bf16[2,256,128]{2,1,0:T(8,128)(2,1)}, bf16[2,25...) custom-call(s32[2]{0:T(128)} %pad_add_fusion.1.info, bf16[256,1024]{1,0:T(8,128)(2,1)} %get-tuple-element.333.refs_0_, ...), custom_call_target="tpu_custom_call" | custom-call | flops 6000000000 | bytes 1000 | tf_op jit(solution)/shard_map/turn/pallas_call | solution.py:517
  246.3 3.5 fusion.32
  251.7 1.6 collective-permute-start.52
  253.3 3.8 collective-permute-done.54.refs_11_
  261.5 1.7 collective-permute-start.51
  263.3 20.4 %feed_grads.1 = bf16[4,384,1024]{2,1,0:T(8,128)(2,1)} custom-call(s32[2]{0:T(128)} %pad_add_fusion.1.info, bf16[256,1024]{1,0:T(8,128)(2,1)} %get-tuple-element.290.refs_0_, bf16[256,1024]{1,0:T(8,128)(2,1)} %collective-permute-done.25.refs_1_, bf16[256,1024]{1,0:T(8,128)(2,1)} %copy-done.32, bf16[256,1024]{1,0:T(8,128)(2,1)} %copy-done.52, ...), custom_call_target="tpu_custom_call" | custom-call | flops 20000000000 | bytes 1000 | tf_op jit(solution)/shard_map/feed_grads/pallas_call | solution.py:476
  283.7 1.9 collective-permute-done.51.refs_3_
  286.9 6.0 %turn.3 = (f32[256,1024]{1,0:T(8,128)}, bf16[256,1024]{1,0:T(8,128)(2,1)}, bf16[2,256,128]{2,1,0:T(8,128)(2,1)}, bf16[2,256,128]{2,1,0:T(8,128)(2,1)}, bf16[2,25...) custom-call(s32[2]{0:T(128)} %pad_add_fusion.1.info, bf16[256,1024]{1,0:T(8,128)(2,1)} %get-tuple-element.359.refs_0_, ...), custom_call_target="tpu_custom_call" | custom-call | flops 6000000000 | bytes 1000 | tf_op jit(solution)/shard_map/turn/pallas_call | solution.py:517
  292.9 1.6 collective-permute-start.60
  296.5 3.2 add_convert_fusion.8
  303.0 4.9 out_grads.1
  309.0 1.5 collective-permute-start.58
  313.7 27.0 %attend_back.2 = (bf16[2048,384]{1,0:T(8,128)(2,1)}, bf16[4,256,1024]{2,1,0:T(8,128)(2,1)}, bf16[4,256,1024]{2,1,0:T(8,128)(2,1)}) custom-call(s32[18]{0:T(128)} %pad_add_fusion.2.info, bf16[2048,384]{1,0:T(8,128)(2,1)} %get-tuple-element.382.refs_0_, bf16[1024,512]{1,0:T(8,128)(2,1)} %all-gather.5.cloned.1.call-done.refs_8_.refs_1_, ...), custom_call_target="tpu_custom_call" | custom-call | flops 25999998976 | bytes 1000 | tf_op jit(solution)/shard_map/attend_back/pallas_call | solution.py:277
  341.7 3.6 collective-permute-done.64
  345.3 3.4 fusion.36
  350.2 2.0 collective-permute-start.67
  352.2 27.1 %attend_back.3 = (bf16[2048,384]{1,0:T(8,128)(2,1)}, bf16[4,256,1024]{2,1,0:T(8,128)(2,1)}, bf16[4,256,1024]{2,1,0:T(8,128)(2,1)}) custom-call(s32[18]{0:T(128)} %pad_add_fusion.4.info, bf16[2048,384]{1,0:T(8,128)(2,1)} %get-tuple-element.404.refs_0_, bf16[1024,512]{1,0:T(8,128)(2,1)} %all-gather.5.cloned.1.call-done.refs_8_.refs_1_, ...), custom_call_target="tpu_custom_call" | custom-call | flops 25999998976 | bytes 1000 | tf_op jit(solution)/shard_map/attend_back/pallas_call | solution.py:277
  380.1 3.7 collective-permute-done.68
  383.9 3.4 fusion.40
  387.2 9.4 %qkv_grads.1 = bf16[1024,384]{1,0:T(8,128)(2,1)} custom-call(s32[2]{0:T(128)} %pad_add_fusion.1.info, bf16[2,256,1024]{2,1,0:T(8,128)(2,1)} %copy-done.25, bf16[2,256,1024]{2,1,0:T(8,128)(2,1)} %collective-permute-done.1.refs_1_, bf16[2,256,1024]{2,1,0:T(8,128)(2,1)} %collective-permute-done.2.refs_2_, bf16[2,256,1024]{2,1,0:T(8,128)(2,1)} %collective-permute-done.4.refs_3_, ...), custom_call_target="tpu_custom_call" | custom-call | flops 8999999488 | bytes 1000 | tf_op jit(solution)/shard_map/qkv_grads/pallas_call | solution.py:560
  400.1 1.9 collective-permute-start.72
  405.1 9.9 %collective-permute-done.73 = bf16[256,1024]{1,0:T(8,128)(2,1)S(1)} collective-permute-done((bf16[256,1024]{1,0:T(8,128)(2,1)}, bf16[256,1024]{1,0:T(8,128)(2,1)S(1)}, u32[]{:S(2)}, u32[]{:S(2)}) %collective-permute-start.73) | collective-permute-done | bytes 524320 | tf_op jit(solution)/shard_map/ppermute | solution.py:646
  416.0 9.8 %collective-permute-done.72 = bf16[256,1024]{1,0:T(8,128)(2,1)S(1)} collective-permute-done((bf16[256,1024]{1,0:T(8,128)(2,1)S(1)}, bf16[256,1024]{1,0:T(8,128)(2,1)S(1)}, u32[]{:S(2)}, u32[]{:S(2)}) %collective-permute-start.72) | collective-permute-done | bytes 524320 | tf_op jit(solution)/shard_map/ppermute | solution.py:646
  429.2 1.5 fusion.24
  430.7 51.2 %collective-permute-done.69 = bf16[2,256,1024]{2,1,0:T(8,128)(2,1)S(1)} collective-permute-done((bf16[2,256,1024]{2,1,0:T(8,128)(2,1)S(1)}, bf16[2,256,1024]{2,1,0:T(8,128)(2,1)S(1)}, u32[]{:S(2)}, u32[]{:S(2)}) %collective-permute-start.69) | collective-permute-done | bytes 1048608 | tf_op jit(solution)/shard_map/ppermute | solution.py:646
  488.1 2.0 collective-permute-start.78
  490.1 7.2 %finish.1 = (f32[128,4096]{1,0:T(8,128)}, f32[128,4096]{1,0:T(8,128)}, f32[512,1024]{1,0:T(8,128)}, f32[1,128]{1,0:T(1,128)}) custom-call(s32[2]{0:T(128)} %pad_add_fusion.1.info, bf16[384,1024]{1,0:T(8,128)(2,1)} %pad_maximum_fusion.5.refs_0_, bf16[384,1024]{1,0:T(8,128)(2,1)} %collective-permute-done.80.refs_1_, ...), custom_call_target="tpu_custom_call" | custom-call | flops 7000000000 | bytes 1000 | tf_op jit(solution)/shard_map/finish/pallas_call | solution.py:900
  498.4 3.3 maximum_select_fusion
  501.7 8.6 %collective-permute-done.77.refs_2_ = bf16[128,1792]{1,0:T(8,128)(2,1)S(1)} collective-permute-done((bf16[128,1792]{1,0:T(8,128)(2,1)S(1)}, bf16[128,1792]{1,0:T(8,128)(2,1)S(1)}, u32[]{:S(2)}, u32[]{:S(2)}) %collective-permute-start.77) | collective-permute-done | bytes 458784 | tf_op jit(solution)/shard_map/ppermute | solution.py:646
  511.0 4.2 finish_qkv.1
  (373 shorter events, 80.6 us)
Async XLA Ops:
  7.2 41.0 %all-gather.5.cloned.1.call-start = ((), (), s32[]{:S(2)}) async-start(), calls=%async_computation.3 | async-start | bytes 1310720 | tf_op jit(solution)/shard_map/all_gather | solution.py:761
  17.5 87.1 %all-gather.7.cloned.1.call-start = ((), (), s32[]{:S(2)}) async-start(), calls=%async_computation.4 | async-start | bytes 2359296 | tf_op jit(solution)/shard_map/all_gather | solution.py:780
  18.3 26.4 %collective-permute-start.1 = (bf16[2,256,1024]{2,1,0:T(8,128)(2,1)S(1)}, bf16[2,256,1024]{2,1,0:T(8,128)(2,1)}, u32[]{:S(2)}, u32[]{:S(2)}) collective-permute-start(bf16[2,256,1024]{2,1,0:T(8,128)(2,1)S(1)} %fusion.1.refs_0_), channel_id=1, source_target_pairs={{0,8},{8,0},{16,24},{24,16},{1,9},{9,1},{17,25},{25,17},{2,10},{10... | collective-permute-start | bytes 3145736 | tf_op jit(solution)/shard_map/ppermute | solution.py:646
  21.1 25.0 %collective-permute-start.2 = (bf16[2,256,1024]{2,1,0:T(8,128)(2,1)S(1)}, bf16[2,256,1024]{2,1,0:T(8,128)(2,1)}, u32[]{:S(2)}, u32[]{:S(2)}) collective-permute-start(bf16[2,256,1024]{2,1,0:T(8,128)(2,1)S(1)} %fusion.1.refs_0_), channel_id=1, source_target_pairs={{0,16},{8,24},{16,0},{24,8},{1,17},{9,25},{17,1},{25,9},{2,18},{10... | collective-permute-start | bytes 3145736 | tf_op jit(solution)/shard_map/ppermute | solution.py:646
  24.7 26.9 %collective-permute-start.13 = (bf16[256,1024]{1,0:T(8,128)(2,1)}, bf16[256,1024]{1,0:T(8,128)(2,1)}, u32[]{:S(2)}, u32[]{:S(2)}) collective-permute-start(bf16[256,1024]{1,0:T(8,128)(2,1)} %get-tuple-element.488), channel_id=1, source_target_pairs={{0,1},{1,0},{2,3},{3,2},{4,5},{5,4},{6,7},{7,6},{8,9},{9,8},{10,11... | collective-permute-start | bytes 1572872 | tf_op jit(solution)/shard_map/ppermute | solution.py:650
  28.6 45.9 %collective-permute-start.5 = (bf16[2,256,1024]{2,1,0:T(8,128)(2,1)S(1)}, bf16[2,256,1024]{2,1,0:T(8,128)(2,1)}, u32[]{:S(2)}, u32[]{:S(2)}) collective-permute-start(bf16[2,256,1024]{2,1,0:T(8,128)(2,1)S(1)} %fusion.1.refs_0_), channel_id=1, source_target_pairs={{0,1},{1,0},{2,3},{3,2},{4,5},{5,4},{6,7},{7,6},{8,9},{9,8},{10,11... | collective-permute-start | bytes 3145736 | tf_op jit(solution)/shard_map/ppermute | solution.py:650
  53.0 21.5 %collective-permute-start.6 = (bf16[2,256,1024]{2,1,0:T(8,128)(2,1)}, bf16[2,256,1024]{2,1,0:T(8,128)(2,1)}, u32[]{:S(2)}, u32[]{:S(2)}) collective-permute-start(bf16[2,256,1024]{2,1,0:T(8,128)(2,1)} %collective-permute-done.1.refs_1_), channel_id=1, source_target_pairs={{0,1},{1,0},{2,3},{3,2},{4,5},{5,4},{6,7},{7,6},{8,9},{9,8},{10,11... | collective-permute-start | bytes 3145736 | tf_op jit(solution)/shard_map/ppermute | solution.py:650
  56.1 18.4 %collective-permute-start.7 = (bf16[2,256,1024]{2,1,0:T(8,128)(2,1)}, bf16[2,256,1024]{2,1,0:T(8,128)(2,1)}, u32[]{:S(2)}, u32[]{:S(2)}) collective-permute-start(bf16[2,256,1024]{2,1,0:T(8,128)(2,1)} %collective-permute-done.2.refs_2_), channel_id=1, source_target_pairs={{0,1},{1,0},{2,3},{3,2},{4,5},{5,4},{6,7},{7,6},{8,9},{9,8},{10,11... | collective-permute-start | bytes 3145736 | tf_op jit(solution)/shard_map/ppermute | solution.py:650
  56.7 14.9 %collective-permute-start.4 = (bf16[2,256,1024]{2,1,0:T(8,128)(2,1)S(1)}, bf16[2,256,1024]{2,1,0:T(8,128)(2,1)}, u32[]{:S(2)}, u32[]{:S(2)}) collective-permute-start(bf16[2,256,1024]{2,1,0:T(8,128)(2,1)S(1)} %broadcast_select_fusion.1), channel_id=1, source_target_pairs={{0,8},{1,17},{8,0},{9,25},{16,24},{17,1},{24,16},{25,9},{2,10},{3,... | collective-permute-start | bytes 3145736 | tf_op jit(solution)/shard_map/ppermute | solution.py:668
  57.3 122.0 %all-gather.9.cloned.1.call-start = ((), (), s32[]{:S(2)}) async-start(), calls=%async_computation.8 | async-start | bytes 3932160 | tf_op jit(solution)/shard_map/all_gather | solution.py:786
  74.5 25.6 %collective-permute-start.14 = (bf16[2,256,1024]{2,1,0:T(8,128)(2,1)S(1)}, bf16[2,256,1024]{2,1,0:T(8,128)(2,1)S(1)}, u32[]{:S(2)}, u32[]{:S(2)}) collective-permute-start(bf16[2,256,1024]{2,1,0:T(8,128)(2,1)S(1)} %maximum_select_fusion.2.refs_8_.refs_4_.refs_16_), channel_id=1, source_target_pairs={{0,8},{8,0},{16,24},{24,16},{1,9},{9,1},{17,25},{25,17},{2,10},{10... | collective-permute-start | bytes 3145736 | tf_op jit(solution)/shard_map/ppermute | solution.py:646
  75.5 25.6 %collective-permute-start.15 = (bf16[2,256,1024]{2,1,0:T(8,128)(2,1)S(1)}, bf16[2,256,1024]{2,1,0:T(8,128)(2,1)S(1)}, u32[]{:S(2)}, u32[]{:S(2)}) collective-permute-start(bf16[2,256,1024]{2,1,0:T(8,128)(2,1)S(1)} %maximum_select_fusion.2.refs_8_.refs_4_.refs_16_), channel_id=1, source_target_pairs={{0,16},{8,24},{16,0},{24,8},{1,17},{9,25},{17,1},{25,9},{2,18},{10... | collective-permute-start | bytes 3145736 | tf_op jit(solution)/shard_map/ppermute | solution.py:646
  77.0 74.8 %collective-permute-start.27 = (bf16[2,256,1024]{2,1,0:T(8,128)(2,1)S(1)}, bf16[2,256,1024]{2,1,0:T(8,128)(2,1)}, u32[]{:S(2)}, u32[]{:S(2)}) collective-permute-start(bf16[2,256,1024]{2,1,0:T(8,128)(2,1)S(1)} %maximum_select_fusion.2.refs_8_.refs_4_.refs_16_), channel_id=1, source_target_pairs={{0,1},{1,0},{2,3},{3,2},{4,5},{5,4},{6,7},{7,6},{8,9},{9,8},{10,11... | collective-permute-start | bytes 3145736 | tf_op jit(solution)/shard_map/ppermute | solution.py:650
  101.1 10.2 %collective-permute-start.16 = (bf16[2,256,128]{2,1,0:T(8,128)(2,1)}, bf16[2,256,128]{2,1,0:T(8,128)(2,1)S(1)}, u32[]{:S(2)}, u32[]{:S(2)}) collective-permute-start(bf16[2,256,128]{2,1,0:T(8,128)(2,1)} %get-tuple-element.255.refs_5_), channel_id=1, source_target_pairs={{0,8},{8,0},{16,24},{24,16},{1,9},{9,1},{17,25},{25,17},{2,10},{10... | collective-permute-start | bytes 393224 | tf_op jit(solution)/shard_map/ppermute | solution.py:646
  101.9 9.3 %collective-permute-start.17 = (bf16[2,256,128]{2,1,0:T(8,128)(2,1)}, bf16[2,256,128]{2,1,0:T(8,128)(2,1)S(1)}, u32[]{:S(2)}, u32[]{:S(2)}) collective-permute-start(bf16[2,256,128]{2,1,0:T(8,128)(2,1)} %get-tuple-element.256.refs_6_), channel_id=1, source_target_pairs={{0,16},{8,24},{16,0},{24,8},{1,17},{9,25},{17,1},{25,9},{2,18},{10... | collective-permute-start | bytes 393224 | tf_op jit(solution)/shard_map/ppermute | solution.py:646
  104.6 274.8 %reduce-scatter.4.cloned.1.call-start = ((), (), s32[]{:S(2)}) async-start(), calls=%async_computation.5 | async-start | bytes 3932160 | tf_op jit(solution)/shard_map/reduce_scatter | solution.py:839
  105.9 28.5 %collective-permute-start.20 = (bf16[2,256,1024]{2,1,0:T(8,128)(2,1)}, bf16[2,256,1024]{2,1,0:T(8,128)(2,1)}, u32[]{:S(2)}, u32[]{:S(2)}) collective-permute-start(bf16[2,256,1024]{2,1,0:T(8,128)(2,1)} %broadcast_select_fusion), channel_id=1, source_target_pairs={{0,8},{1,17},{8,0},{9,25},{16,24},{17,1},{24,16},{25,9},{2,10},{3,... | collective-permute-start | bytes 3145736 | tf_op jit(solution)/shard_map/ppermute | solution.py:668
  112.6 21.8 %collective-permute-start.19 = (bf16[4,256,128]{2,1,0:T(8,128)(2,1)S(1)}, bf16[4,256,128]{2,1,0:T(8,128)(2,1)}, u32[]{:S(2)}, u32[]{:S(2)}) collective-permute-start(bf16[4,256,128]{2,1,0:T(8,128)(2,1)S(1)} %pad_maximum_fusion.7), channel_id=1, source_target_pairs={{0,1},{1,0},{2,3},{3,2},{4,5},{5,4},{6,7},{7,6},{8,9},{9,8},{10,11... | collective-permute-start | bytes 786440 | tf_op jit(solution)/shard_map/ppermute | solution.py:650
  136.4 7.9 %collective-permute-start.22 = (bf16[2,256,128]{2,1,0:T(8,128)(2,1)}, bf16[2,256,128]{2,1,0:T(8,128)(2,1)S(1)}, u32[]{:S(2)}, u32[]{:S(2)}) collective-permute-start(bf16[2,256,128]{2,1,0:T(8,128)(2,1)} %get-tuple-element.271.refs_6_), channel_id=1, source_target_pairs={{0,16},{8,24},{16,0},{24,8},{1,17},{9,25},{17,1},{25,9},{2,18},{10... | collective-permute-start | bytes 393224 | tf_op jit(solution)/shard_map/ppermute | solution.py:646
  138.8 27.1 %collective-permute-start.28 = (bf16[2,256,1024]{2,1,0:T(8,128)(2,1)S(1)}, bf16[2,256,1024]{2,1,0:T(8,128)(2,1)}, u32[]{:S(2)}, u32[]{:S(2)}) collective-permute-start(bf16[2,256,1024]{2,1,0:T(8,128)(2,1)S(1)} %collective-permute-done.14.refs_9_.refs_17_), channel_id=1, source_target_pairs={{0,1},{1,0},{2,3},{3,2},{4,5},{5,4},{6,7},{7,6},{8,9},{9,8},{10,11... | collective-permute-start | bytes 3145736 | tf_op jit(solution)/shard_map/ppermute | solution.py:650
  141.9 24.1 %collective-permute-start.29 = (bf16[2,256,1024]{2,1,0:T(8,128)(2,1)S(1)}, bf16[2,256,1024]{2,1,0:T(8,128)(2,1)}, u32[]{:S(2)}, u32[]{:S(2)}) collective-permute-start(bf16[2,256,1024]{2,1,0:T(8,128)(2,1)S(1)} %collective-permute-done.15.refs_10_.refs_18_), channel_id=1, source_target_pairs={{0,1},{1,0},{2,3},{3,2},{4,5},{5,4},{6,7},{7,6},{8,9},{9,8},{10,11... | collective-permute-start | bytes 3145736 | tf_op jit(solution)/shard_map/ppermute | solution.py:650
  144.3 21.7 %collective-permute-start.30 = (bf16[2,256,1024]{2,1,0:T(8,128)(2,1)}, bf16[2,256,1024]{2,1,0:T(8,128)(2,1)}, u32[]{:S(2)}, u32[]{:S(2)}) collective-permute-start(bf16[2,256,1024]{2,1,0:T(8,128)(2,1)} %collective-permute-done.20.refs_11_.refs_19_), channel_id=1, source_target_pairs={{0,1},{1,0},{2,3},{3,2},{4,5},{5,4},{6,7},{7,6},{8,9},{9,8},{10,11... | collective-permute-start | bytes 3145736 | tf_op jit(solution)/shard_map/ppermute | solution.py:650
  151.0 14.6 %collective-permute-start.25 = (bf16[256,1024]{1,0:T(8,128)(2,1)}, bf16[256,1024]{1,0:T(8,128)(2,1)}, u32[]{:S(2)}, u32[]{:S(2)}) collective-permute-start(bf16[256,1024]{1,0:T(8,128)(2,1)} %get-tuple-element.290.refs_0_), channel_id=1, source_target_pairs={{0,8},{8,0},{16,24},{24,16},{1,9},{9,1},{17,25},{25,17},{2,10},{10... | collective-permute-start | bytes 1572872 | tf_op jit(solution)/shard_map/ppermute | solution.py:646
  151.8 14.1 %collective-permute-start.26 = (bf16[256,1024]{1,0:T(8,128)(2,1)}, bf16[256,1024]{1,0:T(8,128)(2,1)S(1)}, u32[]{:S(2)}, u32[]{:S(2)}) collective-permute-start(bf16[256,1024]{1,0:T(8,128)(2,1)} %get-tuple-element.290.refs_0_), channel_id=1, source_target_pairs={{0,16},{8,24},{16,0},{24,8},{1,17},{9,25},{17,1},{25,9},{2,18},{10... | collective-permute-start | bytes 1572872 | tf_op jit(solution)/shard_map/ppermute | solution.py:646
  166.1 9.2 %collective-permute-start.31 = (bf16[256,1024]{1,0:T(8,128)(2,1)S(1)}, bf16[256,1024]{1,0:T(8,128)(2,1)S(1)}, u32[]{:S(2)}, u32[]{:S(2)}) collective-permute-start(bf16[256,1024]{1,0:T(8,128)(2,1)S(1)} %broadcast_select_fusion.3), channel_id=1, source_target_pairs={{0,8},{1,17},{8,0},{9,25},{16,24},{17,1},{24,16},{25,9},{2,10},{3,... | collective-permute-start | bytes 1572872 | tf_op jit(solution)/shard_map/ppermute | solution.py:668
  167.4 7.9 %collective-permute-start.32 = (bf16[256,1024]{1,0:T(8,128)(2,1)}, bf16[256,1024]{1,0:T(8,128)(2,1)S(1)}, u32[]{:S(2)}, u32[]{:S(2)}) collective-permute-start(bf16[256,1024]{1,0:T(8,128)(2,1)} %get-tuple-element.290.refs_0_), channel_id=1, source_target_pairs={{0,1},{1,0},{2,3},{3,2},{4,5},{5,4},{6,7},{7,6},{8,9},{9,8},{10,11... | collective-permute-start | bytes 1572872 | tf_op jit(solution)/shard_map/ppermute | solution.py:650
  177.2 22.2 %collective-permute-start.36 = (bf16[256,1024]{1,0:T(8,128)(2,1)}, bf16[256,1024]{1,0:T(8,128)(2,1)S(1)}, u32[]{:S(2)}, u32[]{:S(2)}) collective-permute-start(bf16[256,1024]{1,0:T(8,128)(2,1)} %get-tuple-element.320.refs_0_.refs_8_), channel_id=1, source_target_pairs={{0,8},{8,0},{16,24},{24,16},{1,9},{9,1},{17,25},{25,17},{2,10},{10... | collective-permute-start | bytes 1572872 | tf_op jit(solution)/shard_map/ppermute | solution.py:646
  178.5 21.0 %collective-permute-start.37 = (bf16[256,1024]{1,0:T(8,128)(2,1)}, bf16[256,1024]{1,0:T(8,128)(2,1)S(1)}, u32[]{:S(2)}, u32[]{:S(2)}) collective-permute-start(bf16[256,1024]{1,0:T(8,128)(2,1)} %get-tuple-element.320.refs_0_.refs_8_), channel_id=1, source_target_pairs={{0,16},{8,24},{16,0},{24,8},{1,17},{9,25},{17,1},{25,9},{2,18},{10... | collective-permute-start | bytes 1572872 | tf_op jit(solution)/shard_map/ppermute | solution.py:646
  199.5 9.4 %collective-permute-start.39 = (bf16[4,256,1024]{2,1,0:T(8,128)(2,1)}, bf16[4,256,1024]{2,1,0:T(8,128)(2,1)S(1)}, u32[]{:S(2)}, u32[]{:S(2)}) collective-permute-start(bf16[4,256,1024]{2,1,0:T(8,128)(2,1)} %get-tuple-element.312), channel_id=1, source_target_pairs={{0,1},{1,0},{2,3},{3,2},{4,5},{5,4},{6,7},{7,6},{8,9},{9,8},{10,11... | collective-permute-start | bytes 6291464 | tf_op jit(solution)/shard_map/ppermute | solution.py:650
  199.6 9.2 %collective-permute-start.40 = (bf16[256,1024]{1,0:T(8,128)(2,1)S(1)}, bf16[256,1024]{1,0:T(8,128)(2,1)S(1)}, u32[]{:S(2)}, u32[]{:S(2)}) collective-permute-start(bf16[256,1024]{1,0:T(8,128)(2,1)S(1)} %broadcast_select_fusion.2), channel_id=1, source_target_pairs={{0,8},{1,17},{8,0},{9,25},{16,24},{17,1},{24,16},{25,9},{2,10},{3,... | collective-permute-start | bytes 1572872 | tf_op jit(solution)/shard_map/ppermute | solution.py:668
  201.3 11.1 %collective-permute-start.41 = (bf16[256,1024]{1,0:T(8,128)(2,1)S(1)}, bf16[256,1024]{1,0:T(8,128)(2,1)S(1)}, u32[]{:S(2)}, u32[]{:S(2)}) collective-permute-start(bf16[256,1024]{1,0:T(8,128)(2,1)S(1)} %copy-done.51), channel_id=1, source_target_pairs={{0,1},{1,0},{2,3},{3,2},{4,5},{5,4},{6,7},{7,6},{8,9},{9,8},{10,11... | collective-permute-start | bytes 1572872 | tf_op jit(solution)/shard_map/ppermute | solution.py:650
  201.3 11.1 %collective-permute-start.42 = (bf16[256,1024]{1,0:T(8,128)(2,1)S(1)}, bf16[256,1024]{1,0:T(8,128)(2,1)S(1)}, u32[]{:S(2)}, u32[]{:S(2)}) collective-permute-start(bf16[256,1024]{1,0:T(8,128)(2,1)S(1)} %collective-permute-done.36.refs_1_.refs_9_), channel_id=1, source_target_pairs={{0,1},{1,0},{2,3},{3,2},{4,5},{5,4},{6,7},{7,6},{8,9},{9,8},{10,11... | collective-permute-start | bytes 1572872 | tf_op jit(solution)/shard_map/ppermute | solution.py:650
  201.8 10.6 %collective-permute-start.43 = (bf16[256,1024]{1,0:T(8,128)(2,1)S(1)}, bf16[256,1024]{1,0:T(8,128)(2,1)S(1)}, u32[]{:S(2)}, u32[]{:S(2)}) collective-permute-start(bf16[256,1024]{1,0:T(8,128)(2,1)S(1)} %collective-permute-done.37.refs_2_.refs_10_), channel_id=1, source_target_pairs={{0,1},{1,0},{2,3},{3,2},{4,5},{5,4},{6,7},{7,6},{8,9},{9,8},{10,11... | collective-permute-start | bytes 1572872 | tf_op jit(solution)/shard_map/ppermute | solution.py:650
  212.5 24.1 %collective-permute-start.45 = (bf16[256,1024]{1,0:T(8,128)(2,1)S(1)}, bf16[256,1024]{1,0:T(8,128)(2,1)S(1)}, u32[]{:S(2)}, u32[]{:S(2)}) collective-permute-start(bf16[256,1024]{1,0:T(8,128)(2,1)S(1)} %get-tuple-element.316), channel_id=1, source_target_pairs={{0,8},{8,0},{16,24},{24,16},{1,9},{9,1},{17,25},{25,17},{2,10},{10... | collective-permute-start | bytes 1572872 | tf_op jit(solution)/shard_map/ppermute | solution.py:646
  214.1 25.1 %collective-permute-start.46 = (bf16[256,1024]{1,0:T(8,128)(2,1)S(1)}, bf16[256,1024]{1,0:T(8,128)(2,1)S(1)}, u32[]{:S(2)}, u32[]{:S(2)}) collective-permute-start(bf16[256,1024]{1,0:T(8,128)(2,1)S(1)} %get-tuple-element.317), channel_id=1, source_target_pairs={{0,16},{8,24},{16,0},{24,8},{1,17},{9,25},{17,1},{25,9},{2,18},{10... | collective-permute-start | bytes 1572872 | tf_op jit(solution)/shard_map/ppermute | solution.py:646
  214.6 24.6 %collective-permute-start.47 = (bf16[256,1024]{1,0:T(8,128)(2,1)S(1)}, bf16[256,1024]{1,0:T(8,128)(2,1)S(1)}, u32[]{:S(2)}, u32[]{:S(2)}) collective-permute-start(bf16[256,1024]{1,0:T(8,128)(2,1)S(1)} %get-tuple-element.318), channel_id=1, source_target_pairs={{0,24},{8,16},{16,8},{24,0},{1,25},{9,17},{17,9},{25,1},{2,26},{10... | collective-permute-start | bytes 1572872 | tf_op jit(solution)/shard_map/ppermute | solution.py:646
  259.2 26.4 %collective-permute-start.56 = (bf16[4,256,1024]{2,1,0:T(8,128)(2,1)}, bf16[4,256,1024]{2,1,0:T(8,128)(2,1)S(1)}, u32[]{:S(2)}, u32[]{:S(2)}) collective-permute-start(bf16[4,256,1024]{2,1,0:T(8,128)(2,1)} %get-tuple-element.351), channel_id=1, source_target_pairs={{0,1},{1,0},{2,3},{3,2},{4,5},{5,4},{6,7},{7,6},{8,9},{9,8},{10,11... | collective-permute-start | bytes 6291464 | tf_op jit(solution)/shard_map/ppermute | solution.py:650
  259.7 25.9 %collective-permute-start.57 = (bf16[4,256,1024]{2,1,0:T(8,128)(2,1)}, bf16[4,256,1024]{2,1,0:T(8,128)(2,1)}, u32[]{:S(2)}, u32[]{:S(2)}) collective-permute-start(bf16[4,256,1024]{2,1,0:T(8,128)(2,1)} %get-tuple-element.352), channel_id=1, source_target_pairs={{0,1},{1,0},{2,3},{3,2},{4,5},{5,4},{6,7},{7,6},{8,9},{9,8},{10,11... | collective-permute-start | bytes 6291464 | tf_op jit(solution)/shard_map/ppermute | solution.py:650
  259.8 23.9 %collective-permute-start.49 = (bf16[256,1024]{1,0:T(8,128)(2,1)}, bf16[256,1024]{1,0:T(8,128)(2,1)}, u32[]{:S(2)}, u32[]{:S(2)}) collective-permute-start(bf16[256,1024]{1,0:T(8,128)(2,1)} %get-tuple-element.344), channel_id=1, source_target_pairs={{0,8},{8,0},{16,24},{24,16},{1,9},{9,1},{17,25},{25,17},{2,10},{10... | collective-permute-start | bytes 1572872 | tf_op jit(solution)/shard_map/ppermute | solution.py:646
  260.3 23.4 %collective-permute-start.50 = (bf16[256,1024]{1,0:T(8,128)(2,1)S(1)}, bf16[256,1024]{1,0:T(8,128)(2,1)}, u32[]{:S(2)}, u32[]{:S(2)}) collective-permute-start(bf16[256,1024]{1,0:T(8,128)(2,1)S(1)} %get-tuple-element.345), channel_id=1, source_target_pairs={{0,16},{8,24},{16,0},{24,8},{1,17},{9,25},{17,1},{25,9},{2,18},{10... | collective-permute-start | bytes 1572872 | tf_op jit(solution)/shard_map/ppermute | solution.py:646
  261.5 24.1 %collective-permute-start.51 = (bf16[256,1024]{1,0:T(8,128)(2,1)S(1)}, bf16[256,1024]{1,0:T(8,128)(2,1)}, u32[]{:S(2)}, u32[]{:S(2)}) collective-permute-start(bf16[256,1024]{1,0:T(8,128)(2,1)S(1)} %get-tuple-element.346), channel_id=1, source_target_pairs={{0,24},{8,16},{16,8},{24,0},{1,25},{9,17},{17,9},{25,1},{2,26},{10... | collective-permute-start | bytes 1572872 | tf_op jit(solution)/shard_map/ppermute | solution.py:646
  292.9 20.0 %collective-permute-start.60 = (bf16[2,256,128]{2,1,0:T(8,128)(2,1)}, bf16[2,256,128]{2,1,0:T(8,128)(2,1)S(1)}, u32[]{:S(2)}, u32[]{:S(2)}) collective-permute-start(bf16[2,256,128]{2,1,0:T(8,128)(2,1)} %get-tuple-element.392), channel_id=1, source_target_pairs={{0,8},{8,0},{16,24},{24,16},{1,9},{9,1},{17,25},{25,17},{2,10},{10... | collective-permute-start | bytes 393224 | tf_op jit(solution)/shard_map/ppermute | solution.py:646
  294.5 17.5 %collective-permute-start.61 = (bf16[2,256,128]{2,1,0:T(8,128)(2,1)}, bf16[2,256,128]{2,1,0:T(8,128)(2,1)}, u32[]{:S(2)}, u32[]{:S(2)}) collective-permute-start(bf16[2,256,128]{2,1,0:T(8,128)(2,1)} %get-tuple-element.393), channel_id=1, source_target_pairs={{0,16},{8,24},{16,0},{24,8},{1,17},{9,25},{17,1},{25,9},{2,18},{10... | collective-permute-start | bytes 393224 | tf_op jit(solution)/shard_map/ppermute | solution.py:646
  295.0 16.1 %collective-permute-start.62 = (bf16[2,256,128]{2,1,0:T(8,128)(2,1)}, bf16[2,256,128]{2,1,0:T(8,128)(2,1)}, u32[]{:S(2)}, u32[]{:S(2)}) collective-permute-start(bf16[2,256,128]{2,1,0:T(8,128)(2,1)} %get-tuple-element.394), channel_id=1, source_target_pairs={{0,24},{8,16},{16,8},{24,0},{1,25},{9,17},{17,9},{25,1},{2,26},{10... | collective-permute-start | bytes 393224 | tf_op jit(solution)/shard_map/ppermute | solution.py:646
  309.0 31.7 %collective-permute-start.58 = (bf16[2,256,1024]{2,1,0:T(8,128)(2,1)}, bf16[2,256,1024]{2,1,0:T(8,128)(2,1)S(1)}, u32[]{:S(2)}, u32[]{:S(2)}) collective-permute-start(bf16[2,256,1024]{2,1,0:T(8,128)(2,1)} %pad_maximum_fusion.1), channel_id=1, source_target_pairs={{0,8},{8,0},{16,24},{24,16},{1,9},{9,1},{17,25},{25,17},{2,10},{10... | collective-permute-start | bytes 3145736 | tf_op jit(solution)/shard_map/ppermute | solution.py:646
  310.6 30.2 %collective-permute-start.59 = (bf16[2,256,1024]{2,1,0:T(8,128)(2,1)}, bf16[2,256,1024]{2,1,0:T(8,128)(2,1)S(1)}, u32[]{:S(2)}, u32[]{:S(2)}) collective-permute-start(bf16[2,256,1024]{2,1,0:T(8,128)(2,1)} %pad_maximum_fusion.2), channel_id=1, source_target_pairs={{0,16},{8,24},{16,0},{24,8},{1,17},{9,25},{17,1},{25,9},{2,18},{10... | collective-permute-start | bytes 3145736 | tf_op jit(solution)/shard_map/ppermute | solution.py:646
  311.1 171.9 %reduce-scatter.6.cloned.1.call-start = ((), (), s32[]{:S(2)}) async-start(), calls=%async_computation.6 | async-start | bytes 983040 | tf_op jit(solution)/shard_map/reduce_scatter | solution.py:868
  313.6 27.1 %collective-permute-start.63 = (bf16[4,256,128]{2,1,0:T(8,128)(2,1)S(1)}, bf16[4,256,128]{2,1,0:T(8,128)(2,1)}, u32[]{:S(2)}, u32[]{:S(2)}) collective-permute-start(bf16[4,256,128]{2,1,0:T(8,128)(2,1)S(1)} %pad_maximum_fusion.10), channel_id=1, source_target_pairs={{0,1},{1,0},{2,3},{3,2},{4,5},{5,4},{6,7},{7,6},{8,9},{9,8},{10,11... | collective-permute-start | bytes 786440 | tf_op jit(solution)/shard_map/ppermute | solution.py:650
  348.7 30.6 %collective-permute-start.65 = (bf16[256,1024]{1,0:T(8,128)(2,1)}, bf16[256,1024]{1,0:T(8,128)(2,1)S(1)}, u32[]{:S(2)}, u32[]{:S(2)}) collective-permute-start(bf16[256,1024]{1,0:T(8,128)(2,1)} %get-tuple-element.400), channel_id=1, source_target_pairs={{0,8},{8,0},{16,24},{24,16},{1,9},{9,1},{17,25},{25,17},{2,10},{10... | collective-permute-start | bytes 1572872 | tf_op jit(solution)/shard_map/ppermute | solution.py:646
  350.1 29.3 %collective-permute-start.66 = (bf16[256,1024]{1,0:T(8,128)(2,1)}, bf16[256,1024]{1,0:T(8,128)(2,1)S(1)}, u32[]{:S(2)}, u32[]{:S(2)}) collective-permute-start(bf16[256,1024]{1,0:T(8,128)(2,1)} %get-tuple-element.401), channel_id=1, source_target_pairs={{0,16},{8,24},{16,0},{24,8},{1,17},{9,25},{17,1},{25,9},{2,18},{10... | collective-permute-start | bytes 1572872 | tf_op jit(solution)/shard_map/ppermute | solution.py:646
  350.2 29.2 %collective-permute-start.67 = (bf16[256,1024]{1,0:T(8,128)(2,1)}, bf16[256,1024]{1,0:T(8,128)(2,1)S(1)}, u32[]{:S(2)}, u32[]{:S(2)}) collective-permute-start(bf16[256,1024]{1,0:T(8,128)(2,1)} %get-tuple-element.402), channel_id=1, source_target_pairs={{0,24},{8,16},{16,8},{24,0},{1,25},{9,17},{17,9},{25,1},{2,26},{10... | collective-permute-start | bytes 1572872 | tf_op jit(solution)/shard_map/ppermute | solution.py:646
  396.6 88.8 %reduce-scatter.8.cloned.1.call-start = ((), (), s32[]{:S(2)}) async-start(), calls=%async_computation.7 | async-start | bytes 2359296 | tf_op jit(solution)/shard_map/reduce_scatter | solution.py:845
  399.1 15.9 %collective-permute-start.73 = (bf16[256,1024]{1,0:T(8,128)(2,1)}, bf16[256,1024]{1,0:T(8,128)(2,1)S(1)}, u32[]{:S(2)}, u32[]{:S(2)}) collective-permute-start(bf16[256,1024]{1,0:T(8,128)(2,1)} %get-tuple-element.427), channel_id=1, source_target_pairs={{0,24},{8,16},{16,8},{24,0},{1,25},{9,17},{17,9},{25,1},{2,26},{10... | collective-permute-start | bytes 1572872 | tf_op jit(solution)/shard_map/ppermute | solution.py:646
  400.1 25.7 %collective-permute-start.72 = (bf16[256,1024]{1,0:T(8,128)(2,1)S(1)}, bf16[256,1024]{1,0:T(8,128)(2,1)S(1)}, u32[]{:S(2)}, u32[]{:S(2)}) collective-permute-start(bf16[256,1024]{1,0:T(8,128)(2,1)S(1)} %copy-done.31), channel_id=1, source_target_pairs={{0,16},{8,24},{16,0},{24,8},{1,17},{9,25},{17,1},{25,9},{2,18},{10... | collective-permute-start | bytes 1572872 | tf_op jit(solution)/shard_map/ppermute | solution.py:646
  402.0 24.8 %collective-permute-start.71 = (bf16[256,1024]{1,0:T(8,128)(2,1)S(1)}, bf16[256,1024]{1,0:T(8,128)(2,1)S(1)}, u32[]{:S(2)}, u32[]{:S(2)}) collective-permute-start(bf16[256,1024]{1,0:T(8,128)(2,1)S(1)} %copy-done.30), channel_id=1, source_target_pairs={{0,8},{8,0},{16,24},{24,16},{1,9},{9,1},{17,25},{25,17},{2,10},{10... | collective-permute-start | bytes 1572872 | tf_op jit(solution)/shard_map/ppermute | solution.py:646
  403.6 82.9 %collective-permute-start.80 = (bf16[384,1024]{1,0:T(8,128)(2,1)}, bf16[384,1024]{1,0:T(8,128)(2,1)}, u32[]{:S(2)}, u32[]{:S(2)}) collective-permute-start(bf16[384,1024]{1,0:T(8,128)(2,1)} %pad_maximum_fusion.5.refs_0_), channel_id=1, source_target_pairs={{0,8},{8,0},{16,24},{24,16},{1,9},{9,1},{17,25},{25,17},{2,10},{10... | collective-permute-start | bytes 2359304 | tf_op jit(solution)/shard_map/ppermute | solution.py:646
  405.0 83.0 %collective-permute-start.81 = (bf16[384,1024]{1,0:T(8,128)(2,1)}, bf16[384,1024]{1,0:T(8,128)(2,1)}, u32[]{:S(2)}, u32[]{:S(2)}) collective-permute-start(bf16[384,1024]{1,0:T(8,128)(2,1)} %pad_maximum_fusion.5.refs_0_), channel_id=1, source_target_pairs={{0,16},{8,24},{16,0},{24,8},{1,17},{9,25},{17,1},{25,9},{2,18},{10... | collective-permute-start | bytes 2359304 | tf_op jit(solution)/shard_map/ppermute | solution.py:646
  415.0 73.0 %collective-permute-start.82 = (bf16[384,1024]{1,0:T(8,128)(2,1)}, bf16[384,1024]{1,0:T(8,128)(2,1)}, u32[]{:S(2)}, u32[]{:S(2)}) collective-permute-start(bf16[384,1024]{1,0:T(8,128)(2,1)} %pad_maximum_fusion.5.refs_0_), channel_id=1, source_target_pairs={{0,24},{8,16},{16,8},{24,0},{1,25},{9,17},{17,9},{25,1},{2,26},{10... | collective-permute-start | bytes 2359304 | tf_op jit(solution)/shard_map/ppermute | solution.py:646
  425.7 56.2 %collective-permute-start.69 = (bf16[2,256,1024]{2,1,0:T(8,128)(2,1)S(1)}, bf16[2,256,1024]{2,1,0:T(8,128)(2,1)S(1)}, u32[]{:S(2)}, u32[]{:S(2)}) collective-permute-start(bf16[2,256,1024]{2,1,0:T(8,128)(2,1)S(1)} %copy-done.29), channel_id=1, source_target_pairs={{0,24},{8,16},{16,8},{24,0},{1,25},{9,17},{17,9},{25,1},{2,26},{10... | collective-permute-start | bytes 3145736 | tf_op jit(solution)/shard_map/ppermute | solution.py:646
  430.7 67.7 %collective-permute-start.74 = (f32[256,1024]{1,0:T(8,128)}, f32[256,1024]{1,0:T(8,128)}, u32[]{:S(2)}, u32[]{:S(2)}) collective-permute-start(f32[256,1024]{1,0:T(8,128)} %get-tuple-element.482), channel_id=1, source_target_pairs={{0,1},{1,0},{2,3},{3,2},{4,5},{5,4},{6,7},{7,6},{8,9},{9,8},{10,11... | collective-permute-start | bytes 3145736 | tf_op jit(solution)/shard_map/ppermute | solution.py:650
  485.3 11.9 %collective-permute-start.70 = (bf16[256,1024]{1,0:T(8,128)(2,1)}, bf16[256,1024]{1,0:T(8,128)(2,1)S(1)}, u32[]{:S(2)}, u32[]{:S(2)}) collective-permute-start(bf16[256,1024]{1,0:T(8,128)(2,1)} %get-tuple-element.486), channel_id=1, source_target_pairs={{0,1},{1,0},{2,3},{3,2},{4,5},{5,4},{6,7},{7,6},{8,9},{9,8},{10,11... | collective-permute-start | bytes 1572872 | tf_op jit(solution)/shard_map/ppermute | solution.py:650
  486.5 15.2 %collective-permute-start.76 = (bf16[128,1792]{1,0:T(8,128)(2,1)S(1)}, bf16[128,1792]{1,0:T(8,128)(2,1)S(1)}, u32[]{:S(2)}, u32[]{:S(2)}) collective-permute-start(bf16[128,1792]{1,0:T(8,128)(2,1)S(1)} %pad_maximum_fusion.6.refs_0_), channel_id=1, source_target_pairs={{0,8},{8,0},{16,24},{24,16},{1,9},{9,1},{17,25},{25,17},{2,10},{10... | collective-permute-start | bytes 1376264 | tf_op jit(solution)/shard_map/ppermute | solution.py:646
  487.9 22.3 %collective-permute-start.77 = (bf16[128,1792]{1,0:T(8,128)(2,1)S(1)}, bf16[128,1792]{1,0:T(8,128)(2,1)S(1)}, u32[]{:S(2)}, u32[]{:S(2)}) collective-permute-start(bf16[128,1792]{1,0:T(8,128)(2,1)S(1)} %pad_maximum_fusion.6.refs_0_), channel_id=1, source_target_pairs={{0,16},{8,24},{16,0},{24,8},{1,17},{9,25},{17,1},{25,9},{2,18},{10... | collective-permute-start | bytes 1376264 | tf_op jit(solution)/shard_map/ppermute | solution.py:646
  488.1 22.2 %collective-permute-start.78 = (bf16[128,1792]{1,0:T(8,128)(2,1)S(1)}, bf16[128,1792]{1,0:T(8,128)(2,1)}, u32[]{:S(2)}, u32[]{:S(2)}) collective-permute-start(bf16[128,1792]{1,0:T(8,128)(2,1)S(1)} %pad_maximum_fusion.6.refs_0_), channel_id=1, source_target_pairs={{0,24},{8,16},{16,8},{24,0},{1,25},{9,17},{17,9},{25,1},{2,26},{10... | collective-permute-start | bytes 1376264 | tf_op jit(solution)/shard_map/ppermute | solution.py:646
  (99 other events, 867.9 us)
Sparse Core Ops, SparseCore 0:
  17.6 30.5 all-gather.4
  57.4 28.5 all-gather.6
  104.7 62.3 all-gather.8
  311.2 58.8 reduce-scatter.3
  396.8 21.4 reduce-scatter.5
  421.0 35.0 reduce-scatter.7

commit v3 on v2

--- a/solution.py
+++ b/solution.py
@@ -309,15 +309,18 @@
     return pl.ds(pl.multiple_of((j ^ (info[0] * 2 + info[1])) * width, width), width)
 
 
+def chip_rows(info, r, width):
+    return pl.ds(pl.multiple_of((r ^ info[0]) * 2 * width, 2 * width), 2 * width)
+
+
 def mix_kernel(n, width, info, *refs):
     parts, (others, x, w), (att, hidden, norm) = refs[:n], refs[n : n + 3], refs[n + 3 :]
     total = x[0].astype(F32)
     for r in range(n):
-        for q in range(2):
-            j = r * 2 + q
-            part = others[r] if q else parts[r][0]
-            att[:, j * width : (j + 1) * width] = part
-            total += mm(part, w[head_rows(info, j, width), :])
+        mine, other = parts[r][0], others[r]
+        pair = jnp.concatenate([jnp.where(info[1] == 0, mine, other), jnp.where(info[1] == 0, other, mine)], axis=1)
+        att[:, 2 * r * width : 2 * (r + 1) * width] = pair
+        total += mm(pair, w[chip_rows(info, r, width), :])
     hidden[...] = total
     norm[...] = normed(total)[0].astype(BF16)
 
@@ -508,8 +511,9 @@
     e_rows = total.astype(BF16)
     e_out[...] = e_rows
     for r in range(n):
-        for q in range(2):
-            outs[r][q] = mm_nt(e_rows, w[head_rows(info, r * 2 + q, width), :]).astype(BF16)
+        pair = mm_nt(e_rows, w[chip_rows(info, r, width), :]).astype(BF16)
+        outs[r][info[1]] = pair[:, :width]
+        outs[r][1 - info[1]] = pair[:, width:]
 
 
 def turn(info, parts, cot, which, hidden, w_out, width, n):
@@ -526,10 +530,10 @@
 
 
 def out_grads_kernel(n, width, info, att0, att1, e0, e1, out):
-    for j in range(2 * n):
-        cols = slice(j * width, (j + 1) * width)
+    for r in range(n):
+        cols = slice(2 * r * width, 2 * (r + 1) * width)
         total = mm_tn(att0[:, cols], e0[...]) + mm_tn(att1[:, cols], e1[...])
-        out[head_rows(info, j, width), :] = total.astype(BF16)
+        out[chip_rows(info, r, width), :] = total.astype(BF16)
 
 
 def out_grads(info, atts, es, width, n):
@@ -563,7 +567,7 @@
         shape_of(dim, width3),
         [whole_spec((2, half, dim))] * (2 * n) + [whole_spec((rows, width3))] * 2,
         whole_spec((dim, width3)),
-        estimate=cost(9),
+        estimate=cost(0.2),
     )(info, *blocks, *d_qkvs)
 
 
@@ -659,11 +663,15 @@
     return [send(own, r) for r in range(1, 3 if n == 4 else n)]
 
 
+def onward_of(near):
+    return jnp.where(lax.axis_index("core") == 0, near[1], near[0])
+
+
 def gather_far(near):
     n = lax.axis_size("ctx")
     if n != 4:
         return near
-    onward = jnp.where(lax.axis_index("core") == 0, near[1], near[0])
+    onward = onward_of(near)
     pairs = [(c * 2 + p, (c ^ (1 + p)) * 2 + p) for c in range(n) for p in range(2)]
     return near + [lax.ppermute(onward, ("ctx", "core"), pairs)]
 
@@ -678,8 +686,25 @@
 
 
 def plane_join(mine, other):
-    got = swap(other)
+    return sum_cores(mine, swap(other))
+
+
+def sum_cores(mine, got):
     return [(mine[r].astype(F32) + got[r].astype(F32)).astype(BF16) for r in range(mine.shape[0])]
+
+
+def sum_far(joined):
+    n = lax.axis_size("ctx")
+    pairs = [(c * 2 + p, (c ^ (1 + p)) * 2 + p) for c in range(n) for p in range(2)]
+    return lax.ppermute(joined[3], ("ctx", "core"), pairs)
+
+
+def sum_onward(joined, far):
+    core = lax.axis_index("core")
+    by1, by2 = (
+        (joined[r].astype(F32) + jnp.where(core == 2 - r, far.astype(F32), 0.0)).astype(BF16) for r in (1, 2)
+    )
+    return [by1, by2]
 
 
 def plane_send(joined):
@@ -736,6 +761,7 @@
     n_one, inv1 = normed(x_rows.astype(F32))
     one_own = n_one.astype(BF16)
     one_near = gather_near(one_own)
+    first = after(me, one_own)
 
     def head_cols(which):
         at = (chip * 2 + which) * width
@@ -756,16 +782,20 @@
     def scaled(w, gain):
         return (w.astype(F32) * gain.astype(F32)[:, None]).astype(BF16)
 
+    def core_rows(mine, theirs):
+        return ordered(mine, swap(theirs), core).reshape(2 * shard, -1)
+
     def over_z(mine, theirs):
-        both = ordered(mine, swap(theirs), core).reshape(2 * shard, -1)
-        return lax.all_gather(both, "z", axis=0, tiled=True)
+        return lax.all_gather(core_rows(mine, theirs), "z", axis=0, tiled=True)
 
     g1, g2 = gain_attn.astype(F32)[:, None], gain_ffn.astype(F32)[:, None]
     if cut % 128 == 0:
         packed = after(me, one_own)
-        w_qkv = over_z(
+        w_qkv = core_rows(
             *pack(functools.partial(pack_qkv_kernel, width), "pack_qkv", packed, g1, (w_query, w_key, w_value), 4 * width)
         )
+        packed = after(packed, w_qkv)
+        w_qkv = lax.all_gather(w_qkv, "z", axis=0, tiled=True)
         hidden_pair = pack(
             functools.partial(pack_hidden_kernel, n_z, cut, down_rows),
             "pack_hidden",
@@ -787,14 +817,21 @@
     else:
         w_ffs = [over_z(*hidden_pair), lax.all_gather(down_cut, "z", axis=0, tiled=True)]
 
-    one_near, w_qkv, code = together(one_near, w_qkv, doc_ids[0] * DOC + block_ids[0])
-    one = gather_cores(one_own, gather_far(one_near))
+    code = doc_ids[0] * DOC + block_ids[0]
+    code, cot_rows = after((code, cotangent[0]), hidden_pair)
     codes = jnp.stack([code] + [send(code, r) for r in range(1, n)])
     codes = ordered(codes, swap(codes), core)
     ids = [mask_info(codes[s], half, chip, core) for s in range(2)]
     infos, code_rows = [i[0] for i in ids], [i[1] for i in ids]
-    cot_rows = both_rows(after(cotangent[0], one_own))
-    one, infos, cot_own = together(one, infos, cot_rows)
+    cot_rows = both_rows(cot_rows)
+    one_near, infos, cot_rows = together(one_near, infos, cot_rows)
+    one = gather_cores(one_own, gather_far(one_near))
+    one, cot_own = together(one, cot_rows)
+
+    def to_owner(part):
+        mine = lax.dynamic_slice_in_dim(part, core * shard, shard, axis=0)
+        theirs = lax.dynamic_slice_in_dim(part, (1 - core) * shard, shard, axis=0)
+        return mine, swap(theirs)
 
     cot_near = gather_near(cot_own)
     qkv0, *mixed0, lse0 = attend(one, 0, w_qkv, (infos[0], code_rows[0]), n)
@@ -802,71 +839,101 @@
     got0 = send_heads(mixed0)
     cot_all = gather_far(cot_near)
     qkv1, *mixed1, lse1 = attend(one, 1, w_qkv, (info1, code_rows[1]), n)
+    mixed1, got0, cot_all, go = together(mixed1, got0, cot_all, me)
+    got1 = send_heads(mixed1)
     other0 = other_heads(got0)
-    mixed1, got0, other0, cot_all, go = together(mixed1, got0, other0, cot_all, me)
-    got1 = send_heads(mixed1)
     cots = gather_cores(cot_own, cot_all)
     att0, hidden0, norm0 = mix(go, got0, other0, x_rows, 0, w_out_full, n)
+    norm0, got1, go = together(norm0, got1, me)
+    near0 = gather_near(norm0)
     other1 = other_heads(got1)
-    norm0, got1, other1, go = together(norm0, got1, other1, me)
-    near0 = gather_near(norm0)
     att1, hidden1, norm1 = mix(go, got1, other1, x_rows, 1, w_out_full, n)
     near0, norm1, cots = together(near0, norm1, cots)
-    two0 = gather_cores(norm0, gather_far(near0))
+    far0 = gather_far(near0)
+    two0 = gather_cores(norm0, far0)
     two0, norm1, go = together(two0, norm1, me)
 
-    near1 = gather_near(norm1)
+    two_got = [send(norm1, r) for r in range(1, n)]
     inner0, d_gu0, d_mine0, d_other0, o_mine0, o_other0 = feed(two0, cots, 0, w_ffs, cols, go, n)
-    near1, d_mine0, d_other0 = together(near1, d_mine0, d_other0)
-    far1 = gather_far(near1)
+    two_got, d_mine0, d_other0, o_other0 = together(two_got, d_mine0, d_other0, o_other0)
+    two1 = gather_cores(norm1, two_got)
     joined0 = plane_join(d_mine0, d_other0)
-    two1 = gather_cores(norm1, far1)
+    o_got0 = swap(o_other0)
     joined0, two1, go = together(joined0, two1, me)
     parts0 = plane_send(joined0)
     inner1, d_gu1, d_mine1, d_other1, o_mine1, o_other1 = feed(two1, cots, 1, w_ffs, cols, go, n)
-    parts0, d_mine1, d_other1, go = together(parts0, d_mine1, d_other1, me)
-    joined1 = plane_join(d_mine1, d_other1)
+    parts0, d_mine1, d_other1, o_got0, go = together(parts0, d_mine1, d_other1, o_got0, me)
+    d_got, o_got1 = swap(d_other1), swap(o_other1)
     d_hidden0, e0, *d_mix0 = turn(go, parts0, cot_rows, 0, hidden0, w_out_full, width, n)
-    joined1, d_mix0, o_other0, o_other1, go = together(joined1, d_mix0, o_other0, o_other1, me)
+    d_got, d_mix0, d_mine1, o_mine0, o_mine1, o_got1 = together(d_got, d_mix0, d_mine1, o_mine0, o_mine1, o_got1)
+    joined1 = sum_cores(d_mine1, d_got)
+
+    def out_sum(r, *more):
+        pairs = ((o_mine0, o_got0), (o_mine1, o_got1))
+        sums = [mine[r].astype(F32) + got[r].astype(F32) for mine, got in pairs]
+        for far in more:
+            sums = [a + b for a, b in zip(sums, far)]
+        return jnp.stack([a.astype(BF16) for a in sums])
+
+    out_far = out_sum(n - 1)
+    joined1, d_mix0, out_far, go = together(joined1, d_mix0, out_far, me)
+    d_got0 = send_heads(d_mix0)
+    if n == 4:
+        pairs = [(c * 2 + p, (c ^ (1 + p)) * 2 + p) for c in range(n) for p in range(2)]
+        out_far = lax.ppermute(out_far, ("ctx", "core"), pairs)
     parts1 = plane_send(joined1)
-    d_got0 = send_heads(d_mix0)
-    out_others = [swap(o_other0), swap(o_other1)]
-    grads_ff = feed_grads((two0, two1), cots, (inner0, inner1), (d_gu0, d_gu1), go, n, n_z)
+    raw_ff = feed_grads((two0, two1), cots, (inner0, inner1), (d_gu0, d_gu1), go, n, n_z)
+    grads_ff = [lax.psum_scatter(g, "z", scatter_dimension=0, tiled=True) for g in raw_ff]
+    parts1, d_got0, raw_ff, out_far = together(parts1, d_got0, raw_ff, out_far)
     d_other_heads0 = other_heads(d_got0)
-    parts1, d_got0, d_other_heads0, out_others, raw_ff, go = together(
-        parts1, d_got0, d_other_heads0, out_others, grads_ff, me
-    )
-    grads_ff = [lax.psum_scatter(g, "z", scatter_dimension=0, tiled=True) for g in raw_ff]
-    d_hidden1, e1, *d_mix1 = turn(go, parts1, cot_rows, 1, hidden1, w_out_full, width, n)
-    d_mix1, o_mine0, o_mine1, go = together(d_mix1, o_mine0, o_mine1, me)
-    d_got1 = send_heads(d_mix1)
-    d_other_heads1 = other_heads(d_got1)
-    grads_wo = out_grads(go, (att0, att1), (e0, e1), width, n)
-    wo_shard = lax.psum_scatter(grads_wo, ("z", "core"), scatter_dimension=0, tiled=True)
-    outs = [
-        jnp.stack([(m[r].astype(F32) + t[r].astype(F32)).astype(BF16) for m, t in zip((o_mine0, o_mine1), out_others)])
-        for r in range(n)
-    ]
-    outs, grads_wo, info0 = together(outs, grads_wo, infos[0])
-
-    out_near = [send(outs[r], r) for r in range(1, 3)]
+    if n == 4:
+        outs = [out_sum(0)]
+        for r in range(1, 3):
+            far = jnp.where(core == 2 - r, out_far.astype(F32), 0.0)
+            outs.append(out_sum(r, [far[0], far[1]]))
+    else:
+        outs = [out_sum(r) for r in range(n - 1)] + [out_far]
+    outs, d_other_heads0, info0 = together(outs, d_other_heads0, infos[0])
+
+    out_parts = plane_send(outs)
     d_qkv0, a_mine0, a_other0 = attend_back(
         qkv0, w_qkv, lse0, mixed0, d_got0, d_other_heads0, (info0, code_rows[0]), n
     )
-    out_near, a_mine0, a_other0, d_got1, d_other_heads1 = together(out_near, a_mine0, a_other0, d_got1, d_other_heads1)
-    joined0 = plane_join(a_mine0, a_other0)
-    joined0, info1 = together(joined0, infos[1])
+    out_parts, a_mine0, a_other0, go = together(out_parts, a_mine0, a_other0, me)
+    a_got0 = swap(a_other0)
+    d_hidden1, e1, *d_mix1 = turn(go, parts1, cot_rows, 1, hidden1, w_out_full, width, n)
+    d_mix1, a_mine0, a_got0 = together(d_mix1, a_mine0, a_got0)
+    d_got1 = send_heads(d_mix1)
+    joined0 = sum_cores(a_mine0, a_got0)
+    joined0, go = together(joined0, after(me, d_mix1))
     parts0 = plane_send(joined0)
+    grads_wo = out_grads(go, (att0, att1), (e0, e1), width, n)
+    grads_wo, d_got1 = together(grads_wo, d_got1)
+    wo_shard = lax.psum_scatter(grads_wo, ("z", "core"), scatter_dimension=0, tiled=True)
+    d_other_heads1 = other_heads(d_got1)
+    info1, grads_ff, d_other_heads1 = together(infos[1], grads_ff, d_other_heads1)
+    lanes = cut % 128 == 0
+    if lanes:
+        gu_part, dn_part = grads_ff[0][0, : 2 * shard], grads_ff[0][0, 2 * shard :]
+        ff_own = jnp.concatenate([*to_owner(gu_part), dn_part], axis=0)
+        ff_own, info1 = together(ff_own, info1)
+        ff_packs = gather_near(ff_own)
+    else:
+        ff_own, ff_packs = None, []
     d_qkv1, a_mine1, a_other1 = attend_back(
         qkv1, w_qkv, lse1, mixed1, d_got1, d_other_heads1, (info1, code_rows[1]), n
     )
-    parts0, a_mine1, a_other1, grads_ff = together(parts0, a_mine1, a_other1, grads_ff)
-    joined1 = plane_join(a_mine1, a_other1)
-    joined1, go, outs_far = together(joined1, me, outs[3:])
+    raw_qkv = qkv_grads(me, one, (d_qkv0, d_qkv1), n)
+    parts0, a_mine1, a_other1, ff_packs, wo_shard, _ = together(
+        parts0, a_mine1, a_other1, ff_packs, wo_shard, raw_qkv
+    )
+    grad_qkv = lax.psum_scatter(raw_qkv, "z", scatter_dimension=0, tiled=True)
+    a_got1 = swap(a_other1)
+    if lanes:
+        ff_packs = [ff_own] + gather_far(ff_packs)
+        a_mine1, a_got1, ff_packs = together(a_mine1, a_got1, ff_packs)
+    joined1 = sum_cores(a_mine1, a_got1)
     parts1 = plane_send(joined1)
-    grad_qkv = qkv_grads(go, one, (d_qkv0, d_qkv1), n)
-    grad_qkv = lax.psum_scatter(grad_qkv, "z", scatter_dimension=0, tiled=True)
-    out_parts = [outs[0]] + out_near + [send(o, r) for r, o in enumerate(outs_far, 3)]
     out_rows = jnp.stack([hidden0, hidden1])
     for part in out_parts:
         out_rows = out_rows + part.astype(F32)
@@ -884,28 +951,17 @@
     block_out = own_rows(out_rows)
     input_grad = own_rows(jnp.stack(in_rows))
 
-    def to_owner(part):
-        mine = lax.dynamic_slice_in_dim(part, core * shard, shard, axis=0)
-        theirs = lax.dynamic_slice_in_dim(part, (1 - core) * shard, shard, axis=0)
-        return mine, swap(theirs)
-
-    if len(grads_ff) == 1:
-        gu_part, dn_part = grads_ff[0][0, : 2 * shard], grads_ff[0][0, 2 * shard :]
-    else:
-        gu_part, dn_part = grads_ff
-    if cut % 128 == 0:
-        sent = jnp.concatenate([*to_owner(gu_part), dn_part], axis=0)
-        packs = [sent] + [send(sent, r) for r in range(1, n)]
+    if lanes:
         ff = w_gate.shape[1]
         raw = call(
             functools.partial(finish_kernel, n, shard, cut, down_rows),
             "finish",
             [shape_of(shard, ff, dtype=F32)] * 2
             + [shape_of(down_rows, dim, dtype=F32), shape_of(1, shard, dtype=F32)],
-            [whole_spec(sent.shape)] * n + [whole_spec((shard, 1)), whole_spec((shard, ff)), whole_spec((shard, ff))],
+            [whole_spec(ff_own.shape)] * n + [whole_spec((shard, 1)), whole_spec((shard, ff)), whole_spec((shard, ff))],
             [whole_spec((shard, ff))] * 2 + [whole_spec((down_rows, dim)), whole_spec((1, shard))],
             estimate=cost(7),
-        )(me, *packs, g2, w_gate, w_up)
+        )(me, *ff_packs, g2, w_gate, w_up)
         grad_gate, grad_up, grad_down, grad_gain_ffn = raw
         both = jnp.concatenate([*to_owner(grad_qkv), wo_shard], axis=1)
         boths = [both] + [send(both, r) for r in range(1, n)]
@@ -916,7 +972,7 @@
             [whole_spec(both.shape)] * n + [whole_spec((shard, 1))] + [whole_spec((shard, dim))] * 3,
             [whole_spec((shard, dim))] * 4 + [whole_spec((1, shard))],
             estimate=cost(4),
-        )(me, *boths, g1, w_query, w_key, w_value)
+        )(after(me, grad_gain_ffn, input_grad, block_out), *boths, g1, w_query, w_key, w_value)
         grad_q, grad_k, grad_v, grad_wo, grad_gain_attn = raw
         grad_gain_attn, grad_gain_ffn = grad_gain_attn.reshape(shard), grad_gain_ffn.reshape(shard)
     else:
@@ -927,6 +983,7 @@
 
         qkv_shard = over_ctx(grad_qkv).reshape(shard, 2 * n, 3, width).astype(F32)
         raw_q, raw_k, raw_v = (qkv_shard[:, :, i].reshape(shard, dim) for i in range(3))
+        gu_part, dn_part = grads_ff
         gu_shard = over_ctx(gu_part).reshape(shard, n, 2, 2, n_z, cut).astype(F32)
         raw_g, raw_u = (
             gu_shard[:, :, :, i].transpose(0, 3, 2, 1, 4).reshape(shard, -1) for i in range(2)

time: 530 us -> 492 us (0.928)
  waiting for transfers between devices: 166 us -> 118 us
  other arithmetic: 43.8 us -> 55 us
    ppermute x44 -> x43, waiting for transfers between devices: 124 us -> 65.6 us  [send(): return lax.ppermute(value, 'ctx', [(i, i ^ step) for i in range(count)])]
    ppermute x0 -> x1, waiting for transfers between devices: none -> 10.2 us  [body(): out_far = lax.ppermute(out_far, ('ctx', 'core'), pairs)]
    unnamed x151 -> x125, local copies, waits for them, and re-layouts: 10.9 us -> 6.42 us
    convert_element_type x6 -> x7, other arithmetic: 18 us -> 20.5 us  [the longest x4 14.5 us: sum_cores(): (mine[r].astype(F32) + got[r].astype(F32)).astype(BF16)]
    ppermute x44 -> x43, starting transfers between devices: 51.4 us -> 53.2 us  [send(): return lax.ppermute(value, 'ctx', [(i, i ^ step) for i in range(count)])]
  transfers between devices with their start and end apart: 89 -> 89, of which waited for: 30 -> 27; matrix products, arithmetic and copies ran while one was open for 9% -> 12% of each run, Pallas kernels for 36% -> 41%
where the time goes in v3:
time: 492 us; the launch traced here: 483 us
  Pallas kernels  208 us (42%)
  waiting for transfers between devices  118 us (24%)
  starting transfers between devices  65.6 us (13%)
  other arithmetic  55 us (11%)
  local copies, waits for them, and re-layouts  20.6 us (4%)
  between operations  15.7 us (3%)
    ppermute x43, waiting for transfers between devices, send(): return lax.ppermute(value, 'ctx', [(i, i ^ step) for i in range(count)])  65.6 us
    ppermute x43, starting transfers between devices, send(): return lax.ppermute(value, 'ctx', [(i, i ^ step) for i in range(count)])  53.2 us
    pallas_call x2, Pallas kernels, attend_back(): call(functools.partial(attend_back_kernel, n, heads, half), 'attend_back'...  53.1 us
    pallas_call x2, Pallas kernels, attend(): call(functools.partial(attend_kernel, n, heads, half), 'attend', [shape_o...  42.3 us
    pallas_call x2, Pallas kernels, feed(): call(functools.partial(feed_kernel, n, half, cols, which), 'feed', [shape...  40.3 us
    ppermute x4, waiting for transfers between devices, gather_far(): return near + [lax.ppermute(onward, ('ctx', 'core'), pairs)]  30.3 us
    pallas_call x1, Pallas kernels, feed_grads(): call(functools.partial(feed_grads_kernel, n, n_z, half), 'feed_grads', [s...  20.3 us
    convert_element_type x4, other arithmetic, sum_cores(): (mine[r].astype(F32) + got[r].astype(F32)).astype(BF16)  14.5 us
  transfers between devices with their start and end apart: 89, of which 27 were waited for; matrix products, arithmetic and copies ran while one was open for 12% of the time, Pallas kernels for 41%

profile of v3, /device:TPU:0, one launch (start us, length us, event | category | flops | bytes accessed | tf_op | source)
XLA Modules:
  0.0 483.0 jit_solution(13513875608591518392)
XLA Ops:
  12.0 2.7 pack_qkv.1
  16.3 1.7 maximum_select_fusion.5
  18.0 3.3 pack_hidden.1
  21.3 3.6 collective-permute-start.6
  25.4 2.0 collective-permute-start.1
  27.4 1.5 collective-permute-start.2
  29.1 2.2 dynamic-slice_bitcast_fusion.1
  34.5 2.8 maximum_select_fusion.2.refs_8_.refs_4_.refs_16_
  37.3 13.1 %collective-permute-done.1.refs_1_ = bf16[2,256,1024]{2,1,0:T(8,128)(2,1)S(1)} collective-permute-done((bf16[2,256,1024]{2,1,0:T(8,128)(2,1)S(1)}, bf16[2,256,1024]{2,1,0:T(8,128)(2,1)S(1)}, u32[]{:S(2)}, u32[]{:S(2)}) %collective-permute-start.1) | collective-permute-done | bytes 1048608 | tf_op jit(solution)/shard_map/ppermute | solution.py:650
  51.8 2.3 broadcast_select_fusion.1
  54.7 1.7 all-gather.5.cloned.1.call-done.refs_8_.refs_1_
  57.1 12.1 %collective-permute-done.9.refs_3_ = bf16[2,256,1024]{2,1,0:T(8,128)(2,1)} collective-permute-done((bf16[2,256,1024]{2,1,0:T(8,128)(2,1)}, bf16[2,256,1024]{2,1,0:T(8,128)(2,1)}, u32[]{:S(2)}, u32[]{:S(2)}) %collective-permute-start.9) | collective-permute-done | bytes 1048608 | tf_op jit(solution)/shard_map/ppermute | solution.py:676
  71.0 1.7 collective-permute-done.39
  76.9 21.8 %attend.2 = (bf16[2048,384]{1,0:T(8,128)(2,1)}, bf16[2,256,128]{2,1,0:T(8,128)(2,1)}, bf16[2,256,128]{2,1,0:T(8,128)(2,1)}, bf16[2,256,128]{2,1,0:T(8,128)(2,1)}...) custom-call(s32[18]{0:T(128)} %pad_add_fusion.2.info, bf16[2,256,1024]{2,1,0:T(8,128)(2,1)} %copy-done.4, ...), custom_call_target="tpu_custom_call" | custom-call | flops 20999999488 | bytes 1000 | tf_op jit(solution)/shard_map/attend/pallas_call | solution.py:175
  98.7 1.6 collective-permute-done.14.refs_9_.refs_17_
  107.2 20.5 %attend.3 = (bf16[2048,384]{1,0:T(8,128)(2,1)}, bf16[2,256,128]{2,1,0:T(8,128)(2,1)}, bf16[2,256,128]{2,1,0:T(8,128)(2,1)}, bf16[2,256,128]{2,1,0:T(8,128)(2,1)}...) custom-call(s32[18]{0:T(128)} %pad_add_fusion.4.info, bf16[2,256,1024]{2,1,0:T(8,128)(2,1)} %copy-done.4, ...), custom_call_target="tpu_custom_call" | custom-call | flops 20999999488 | bytes 1000 | tf_op jit(solution)/shard_map/attend/pallas_call | solution.py:175
  132.8 3.1 collective-permute-done.21.refs_1_
  138.6 4.6 mix.2
  145.6 2.4 collective-permute-start.25
  147.9 1.5 collective-permute-start.26
  149.5 4.6 mix.3
  154.1 6.2 %collective-permute-done.25.refs_1_ = bf16[256,1024]{1,0:T(8,128)(2,1)S(1)} collective-permute-done((bf16[256,1024]{1,0:T(8,128)(2,1)}, bf16[256,1024]{1,0:T(8,128)(2,1)S(1)}, u32[]{:S(2)}, u32[]{:S(2)}) %collective-permute-start.25) | collective-permute-done | bytes 524320 | tf_op jit(solution)/shard_map/ppermute | solution.py:650
  161.9 1.8 collective-permute-start.31
  164.2 6.9 %collective-permute-done.31.refs_3_ = bf16[256,1024]{1,0:T(8,128)(2,1)S(1)} collective-permute-done((bf16[256,1024]{1,0:T(8,128)(2,1)S(1)}, bf16[256,1024]{1,0:T(8,128)(2,1)S(1)}, u32[]{:S(2)}, u32[]{:S(2)}) %collective-permute-start.31) | collective-permute-done | bytes 524320 | tf_op jit(solution)/shard_map/ppermute | solution.py:676
  171.2 1.9 collective-permute-done.35.refs_7_
  173.8 1.7 collective-permute-start.36
  175.5 1.5 collective-permute-start.37
  177.3 20.1 %feed.2 = (bf16[2048,512]{1,0:T(8,128)(2,1)}, bf16[2048,1024]{1,0:T(8,128)(2,1)}, bf16[4,256,1024]{2,1,0:T(8,128)(2,1)}, bf16[4,256,1024]{2,1,0:T(8,128)(2,1)}, ...) custom-call(s32[2]{0:T(128)} %pad_add_fusion.1.info, bf16[256,1024]{1,0:T(8,128)(2,1)} %get-tuple-element.307.refs_0_, ...), custom_call_target="tpu_custom_call" | custom-call | flops 20000000000 | bytes 1000 | tf_op jit(solution)/shard_map/feed/pallas_call | solution.py:403
  197.4 3.3 collective-permute-done.37.refs_2_.refs_10_
  201.8 3.3 collective-permute-done.40
  205.3 3.5 fusion.33
  212.5 20.3 %feed.3 = (bf16[2048,512]{1,0:T(8,128)(2,1)}, bf16[2048,1024]{1,0:T(8,128)(2,1)}, bf16[4,256,1024]{2,1,0:T(8,128)(2,1)}, bf16[4,256,1024]{2,1,0:T(8,128)(2,1)}, ...) custom-call(s32[2]{0:T(128)} %pad_add_fusion.1.info, bf16[256,1024]{1,0:T(8,128)(2,1)} %get-tuple-element.337.refs_0_.refs_8_, ...), custom_call_target="tpu_custom_call" | custom-call | flops 20000000000 | bytes 1000 | tf_op jit(solution)/shard_map/feed/pallas_call | solution.py:403
  232.9 2.7 collective-permute-done.47.refs_3_
  235.6 5.7 %turn.2 = (f32[256,1024]{1,0:T(8,128)}, bf16[256,1024]{1,0:T(8,128)(2,1)}, bf16[2,256,128]{2,1,0:T(8,128)(2,1)}, bf16[2,256,128]{2,1,0:T(8,128)(2,1)}, bf16[2,25...) custom-call(s32[2]{0:T(128)} %pad_add_fusion.1.info, bf16[256,1024]{1,0:T(8,128)(2,1)} %get-tuple-element.350.refs_0_, ...), custom_call_target="tpu_custom_call" | custom-call | flops 6000000000 | bytes 1000 | tf_op jit(solution)/shard_map/turn/pallas_call | solution.py:521
  241.3 3.5 fusion.37
  249.4 1.5 collective-permute-start.55
  252.8 1.5 collective-permute-start.53
  255.1 1.6 collective-permute-start.56
  257.1 20.3 %feed_grads.1 = bf16[4,384,1024]{2,1,0:T(8,128)(2,1)} custom-call(s32[2]{0:T(128)} %pad_add_fusion.1.info, bf16[256,1024]{1,0:T(8,128)(2,1)} %get-tuple-element.307.refs_0_, bf16[256,1024]{1,0:T(8,128)(2,1)} %copy-done.21, bf16[256,1024]{1,0:T(8,128)(2,1)} %copy-done.22, bf16[256,1024]{1,0:T(8,128)(2,1)} %copy-done.41, bf16[256,1024]{1,0:T(8,128)(2,1)} %copy-done.42, ...), custom_call_target="tpu_custom_call" | custom-call | flops 20000000000 | bytes 1000 | tf_op jit(solution)/shard_map/feed_grads/pallas_call | solution.py:479
  277.6 2.6 collective-permute-done.56.refs_11_
  281.1 10.2 %collective-permute-done.57 = bf16[2,256,1024]{2,1,0:T(8,128)(2,1)S(1)} collective-permute-done((bf16[2,256,1024]{2,1,0:T(8,128)(2,1)}, bf16[2,256,1024]{2,1,0:T(8,128)(2,1)S(1)}, u32[]{:S(2)}, u32[]{:S(2)}) %collective-permute-start.57) | collective-permute-done | bytes 1048608 | tf_op jit(solution)/shard_map/ppermute | solution.py:883
  294.5 3.2 fusion.24
  298.6 1.5 collective-permute-start.60
  300.2 27.4 %attend_back.2 = (bf16[2048,384]{1,0:T(8,128)(2,1)}, bf16[4,256,1024]{2,1,0:T(8,128)(2,1)}, bf16[4,256,1024]{2,1,0:T(8,128)(2,1)}) custom-call(s32[18]{0:T(128)} %pad_add_fusion.2.info, bf16[2048,384]{1,0:T(8,128)(2,1)} %get-tuple-element.395.refs_0_, bf16[1024,512]{1,0:T(8,128)(2,1)} %all-gather.5.cloned.1.call-done.refs_8_.refs_1_, ...), custom_call_target="tpu_custom_call" | custom-call | flops 25999998976 | bytes 1000 | tf_op jit(solution)/shard_map/attend_back/pallas_call | solution.py:277
  327.6 5.5 %turn.3 = (f32[256,1024]{1,0:T(8,128)}, bf16[256,1024]{1,0:T(8,128)(2,1)}, bf16[2,256,128]{2,1,0:T(8,128)(2,1)}, bf16[2,256,128]{2,1,0:T(8,128)(2,1)}, bf16[2,25...) custom-call(s32[2]{0:T(128)} %pad_add_fusion.1.info, bf16[256,1024]{1,0:T(8,128)(2,1)} %get-tuple-element.405.refs_0_, ...), custom_call_target="tpu_custom_call" | custom-call | flops 6000000000 | bytes 1000 | tf_op jit(solution)/shard_map/turn/pallas_call | solution.py:521
  336.7 4.1 fusion.41
  340.8 4.8 out_grads.1
  346.7 1.5 collective-permute-done.69.refs_12_
  357.1 25.7 %attend_back.3 = (bf16[2048,384]{1,0:T(8,128)(2,1)}, bf16[4,256,1024]{2,1,0:T(8,128)(2,1)}, bf16[4,256,1024]{2,1,0:T(8,128)(2,1)}) custom-call(s32[18]{0:T(128)} %pad_add_fusion.4.info, bf16[2048,384]{1,0:T(8,128)(2,1)} %get-tuple-element.438.refs_0_, bf16[1024,512]{1,0:T(8,128)(2,1)} %all-gather.5.cloned.1.call-done.refs_8_.refs_1_, ...), custom_call_target="tpu_custom_call" | custom-call | flops 25999998976 | bytes 1000 | tf_op jit(solution)/shard_map/attend_back/pallas_call | solution.py:277
  382.8 9.5 %qkv_grads.1 = bf16[1024,384]{1,0:T(8,128)(2,1)} custom-call(s32[2]{0:T(128)} %pad_add_fusion.1.info, bf16[2,256,1024]{2,1,0:T(8,128)(2,1)} %copy-done.4, bf16[2,256,1024]{2,1,0:T(8,128)(2,1)} %copy-done.5, bf16[2,256,1024]{2,1,0:T(8,128)(2,1)} %collective-permute-done.2.refs_2_, bf16[2,256,1024]{2,1,0:T(8,128)(2,1)} %collective-permute-done.9.refs_3_, ...), custom_call_target="tpu_custom_call" | custom-call | flops 200000000 | bytes 1000 | tf_op jit(solution)/shard_map/qkv_grads/pallas_call | solution.py:564
  393.3 2.1 broadcast_select_fusion.2
  396.4 11.3 %collective-permute-done.74.refs_3_ = bf16[384,1024]{1,0:T(8,128)(2,1)} collective-permute-done((bf16[384,1024]{1,0:T(8,128)(2,1)}, bf16[384,1024]{1,0:T(8,128)(2,1)}, u32[]{:S(2)}, u32[]{:S(2)}) %collective-permute-start.74) | collective-permute-done | bytes 786464 | tf_op jit(solution)/shard_map/ppermute | solution.py:676
  407.7 3.4 fusion.43
  414.6 3.3 fusion.4
  418.0 2.4 constant_dynamic-slice_fusion.2
  420.4 6.8 %collective-permute-done.77 = bf16[256,1024]{1,0:T(8,128)(2,1)} collective-permute-done((bf16[256,1024]{1,0:T(8,128)(2,1)}, bf16[256,1024]{1,0:T(8,128)(2,1)}, u32[]{:S(2)}, u32[]{:S(2)}) %collective-permute-start.77) | collective-permute-done | bytes 524320 | tf_op jit(solution)/shard_map/ppermute | solution.py:650
  427.2 9.8 %collective-permute-done.76 = bf16[256,1024]{1,0:T(8,128)(2,1)} collective-permute-done((bf16[256,1024]{1,0:T(8,128)(2,1)}, bf16[256,1024]{1,0:T(8,128)(2,1)}, u32[]{:S(2)}, u32[]{:S(2)}) %collective-permute-start.76) | collective-permute-done | bytes 524320 | tf_op jit(solution)/shard_map/ppermute | solution.py:650
  437.1 2.9 fusion.9
  440.0 2.9 fusion.13
  445.0 2.3 maximum_select_fusion.3
  451.0 7.2 %finish.1 = (f32[128,4096]{1,0:T(8,128)}, f32[128,4096]{1,0:T(8,128)}, f32[512,1024]{1,0:T(8,128)}, f32[1,128]{1,0:T(1,128)}) custom-call(s32[2]{0:T(128)} %pad_add_fusion.1.info, bf16[384,1024]{1,0:T(8,128)(2,1)} %pad_maximum_fusion.5.refs_0_, bf16[384,1024]{1,0:T(8,128)(2,1)} %collective-permute-done.71.refs_1_, ...), custom_call_target="tpu_custom_call" | custom-call | flops 7000000000 | bytes 1000 | tf_op jit(solution)/shard_map/finish/pallas_call | solution.py:956
  458.1 3.3 maximum_select_fusion
  461.5 9.3 %collective-permute-done.81.refs_2_ = bf16[128,1792]{1,0:T(8,128)(2,1)S(1)} collective-permute-done((bf16[128,1792]{1,0:T(8,128)(2,1)S(1)}, bf16[128,1792]{1,0:T(8,128)(2,1)S(1)}, u32[]{:S(2)}, u32[]{:S(2)}) %collective-permute-start.81) | collective-permute-done | bytes 458784 | tf_op jit(solution)/shard_map/ppermute | solution.py:650
  471.6 4.2 finish_qkv.1
  (348 shorter events, 81.8 us)
Async XLA Ops:
  7.2 49.2 %all-gather.5.cloned.1.call-start = ((), (), s32[]{:S(2)}) async-start(), calls=%async_computation.3 | async-start | bytes 1310720 | tf_op jit(solution)/shard_map/all_gather | solution.py:798
  21.3 7.7 %collective-permute-start.6 = (s32[512]{0:T(512)S(1)}, s32[512]{0:T(512)S(1)}, u32[]{:S(2)}, u32[]{:S(2)}) collective-permute-start(s32[512]{0:T(512)S(1)} %bitcast.134), channel_id=1, source_target_pairs={{0,24},{8,16},{16,8},{24,0},{1,25},{9,17},{17,9},{25,1},{2,26},{10... | collective-permute-start | bytes 6152 | tf_op jit(solution)/shard_map/ppermute | solution.py:650
  25.4 24.9 %collective-permute-start.1 = (bf16[2,256,1024]{2,1,0:T(8,128)(2,1)S(1)}, bf16[2,256,1024]{2,1,0:T(8,128)(2,1)S(1)}, u32[]{:S(2)}, u32[]{:S(2)}) collective-permute-start(bf16[2,256,1024]{2,1,0:T(8,128)(2,1)S(1)} %fusion.1.refs_0_), channel_id=1, source_target_pairs={{0,8},{8,0},{16,24},{24,16},{1,9},{9,1},{17,25},{25,17},{2,10},{10... | collective-permute-start | bytes 3145736 | tf_op jit(solution)/shard_map/ppermute | solution.py:650
  27.4 24.4 %collective-permute-start.2 = (bf16[2,256,1024]{2,1,0:T(8,128)(2,1)S(1)}, bf16[2,256,1024]{2,1,0:T(8,128)(2,1)}, u32[]{:S(2)}, u32[]{:S(2)}) collective-permute-start(bf16[2,256,1024]{2,1,0:T(8,128)(2,1)S(1)} %fusion.1.refs_0_), channel_id=1, source_target_pairs={{0,16},{8,24},{16,0},{24,8},{1,17},{9,25},{17,1},{25,9},{2,18},{10... | collective-permute-start | bytes 3145736 | tf_op jit(solution)/shard_map/ppermute | solution.py:650
  29.0 77.6 %all-gather.7.cloned.1.call-start = ((), (), s32[]{:S(2)}) async-start(), calls=%async_computation.4 | async-start | bytes 2359296 | tf_op jit(solution)/shard_map/all_gather | solution.py:810
  54.1 15.1 %collective-permute-start.9 = (bf16[2,256,1024]{2,1,0:T(8,128)(2,1)}, bf16[2,256,1024]{2,1,0:T(8,128)(2,1)}, u32[]{:S(2)}, u32[]{:S(2)}) collective-permute-start(bf16[2,256,1024]{2,1,0:T(8,128)(2,1)} %broadcast_select_fusion.1), channel_id=1, source_target_pairs={{0,8},{1,17},{8,0},{9,25},{16,24},{17,1},{24,16},{25,9},{2,10},{3,... | collective-permute-start | bytes 3145736 | tf_op jit(solution)/shard_map/ppermute | solution.py:676
  56.4 120.9 %all-gather.9.cloned.1.call-start = ((), (), s32[]{:S(2)}) async-start(), calls=%async_computation.8 | async-start | bytes 3932160 | tf_op jit(solution)/shard_map/all_gather | solution.py:816
  56.5 18.3 %collective-permute-start.10 = (bf16[2,256,1024]{2,1,0:T(8,128)(2,1)S(1)}, bf16[2,256,1024]{2,1,0:T(8,128)(2,1)}, u32[]{:S(2)}, u32[]{:S(2)}) collective-permute-start(bf16[2,256,1024]{2,1,0:T(8,128)(2,1)S(1)} %fusion.1.refs_0_), channel_id=1, source_target_pairs={{0,1},{1,0},{2,3},{3,2},{4,5},{5,4},{6,7},{7,6},{8,9},{9,8},{10,11... | collective-permute-start | bytes 3145736 | tf_op jit(solution)/shard_map/ppermute | solution.py:654
  56.6 18.2 %collective-permute-start.11 = (bf16[2,256,1024]{2,1,0:T(8,128)(2,1)S(1)}, bf16[2,256,1024]{2,1,0:T(8,128)(2,1)}, u32[]{:S(2)}, u32[]{:S(2)}) collective-permute-start(bf16[2,256,1024]{2,1,0:T(8,128)(2,1)S(1)} %collective-permute-done.1.refs_1_), channel_id=1, source_target_pairs={{0,1},{1,0},{2,3},{3,2},{4,5},{5,4},{6,7},{7,6},{8,9},{9,8},{10,11... | collective-permute-start | bytes 3145736 | tf_op jit(solution)/shard_map/ppermute | solution.py:654
  57.1 17.7 %collective-permute-start.12 = (bf16[2,256,1024]{2,1,0:T(8,128)(2,1)}, bf16[2,256,1024]{2,1,0:T(8,128)(2,1)}, u32[]{:S(2)}, u32[]{:S(2)}) collective-permute-start(bf16[2,256,1024]{2,1,0:T(8,128)(2,1)} %collective-permute-done.2.refs_2_), channel_id=1, source_target_pairs={{0,1},{1,0},{2,3},{3,2},{4,5},{5,4},{6,7},{7,6},{8,9},{9,8},{10,11... | collective-permute-start | bytes 3145736 | tf_op jit(solution)/shard_map/ppermute | solution.py:654
  74.8 25.5 %collective-permute-start.14 = (bf16[2,256,1024]{2,1,0:T(8,128)(2,1)}, bf16[2,256,1024]{2,1,0:T(8,128)(2,1)S(1)}, u32[]{:S(2)}, u32[]{:S(2)}) collective-permute-start(bf16[2,256,1024]{2,1,0:T(8,128)(2,1)} %maximum_select_fusion.2.refs_8_.refs_4_.refs_16_), channel_id=1, source_target_pairs={{0,8},{8,0},{16,24},{24,16},{1,9},{9,1},{17,25},{25,17},{2,10},{10... | collective-permute-start | bytes 3145736 | tf_op jit(solution)/shard_map/ppermute | solution.py:650
  75.4 25.1 %collective-permute-start.15 = (bf16[2,256,1024]{2,1,0:T(8,128)(2,1)}, bf16[2,256,1024]{2,1,0:T(8,128)(2,1)S(1)}, u32[]{:S(2)}, u32[]{:S(2)}) collective-permute-start(bf16[2,256,1024]{2,1,0:T(8,128)(2,1)} %maximum_select_fusion.2.refs_8_.refs_4_.refs_16_), channel_id=1, source_target_pairs={{0,16},{8,24},{16,0},{24,8},{1,17},{9,25},{17,1},{25,9},{2,18},{10... | collective-permute-start | bytes 3145736 | tf_op jit(solution)/shard_map/ppermute | solution.py:650
  100.5 27.1 %collective-permute-start.16 = (bf16[2,256,128]{2,1,0:T(8,128)(2,1)}, bf16[2,256,128]{2,1,0:T(8,128)(2,1)S(1)}, u32[]{:S(2)}, u32[]{:S(2)}) collective-permute-start(bf16[2,256,128]{2,1,0:T(8,128)(2,1)} %get-tuple-element.274.refs_5_), channel_id=1, source_target_pairs={{0,8},{8,0},{16,24},{24,16},{1,9},{9,1},{17,25},{25,17},{2,10},{10... | collective-permute-start | bytes 393224 | tf_op jit(solution)/shard_map/ppermute | solution.py:650
  102.0 25.6 %collective-permute-start.17 = (bf16[2,256,128]{2,1,0:T(8,128)(2,1)}, bf16[2,256,128]{2,1,0:T(8,128)(2,1)S(1)}, u32[]{:S(2)}, u32[]{:S(2)}) collective-permute-start(bf16[2,256,128]{2,1,0:T(8,128)(2,1)} %get-tuple-element.275.refs_6_), channel_id=1, source_target_pairs={{0,16},{8,24},{16,0},{24,8},{1,17},{9,25},{17,1},{25,9},{2,18},{10... | collective-permute-start | bytes 393224 | tf_op jit(solution)/shard_map/ppermute | solution.py:650
  103.5 24.1 %collective-permute-start.18 = (bf16[2,256,128]{2,1,0:T(8,128)(2,1)}, bf16[2,256,128]{2,1,0:T(8,128)(2,1)}, u32[]{:S(2)}, u32[]{:S(2)}) collective-permute-start(bf16[2,256,128]{2,1,0:T(8,128)(2,1)} %get-tuple-element.276.refs_7_), channel_id=1, source_target_pairs={{0,24},{8,16},{16,8},{24,0},{1,25},{9,17},{17,9},{25,1},{2,26},{10... | collective-permute-start | bytes 393224 | tf_op jit(solution)/shard_map/ppermute | solution.py:650
  105.1 22.6 %collective-permute-start.19 = (bf16[2,256,1024]{2,1,0:T(8,128)(2,1)}, bf16[2,256,1024]{2,1,0:T(8,128)(2,1)}, u32[]{:S(2)}, u32[]{:S(2)}) collective-permute-start(bf16[2,256,1024]{2,1,0:T(8,128)(2,1)} %broadcast_select_fusion), channel_id=1, source_target_pairs={{0,8},{1,17},{8,0},{9,25},{16,24},{17,1},{24,16},{25,9},{2,10},{3,... | collective-permute-start | bytes 3145736 | tf_op jit(solution)/shard_map/ppermute | solution.py:676
  106.6 241.6 %reduce-scatter.4.cloned.1.call-start = ((), (), s32[]{:S(2)}) async-start(), calls=%async_computation.5 | async-start | bytes 3932160 | tf_op jit(solution)/shard_map/reduce_scatter | solution.py:886
  128.7 8.5 %collective-permute-start.20 = (bf16[4,256,128]{2,1,0:T(8,128)(2,1)S(1)}, bf16[4,256,128]{2,1,0:T(8,128)(2,1)S(1)}, u32[]{:S(2)}, u32[]{:S(2)}) collective-permute-start(bf16[4,256,128]{2,1,0:T(8,128)(2,1)S(1)} %pad_maximum_fusion.7), channel_id=1, source_target_pairs={{0,1},{1,0},{2,3},{3,2},{4,5},{5,4},{6,7},{7,6},{8,9},{9,8},{10,11... | collective-permute-start | bytes 786440 | tf_op jit(solution)/shard_map/ppermute | solution.py:654
  128.8 16.7 %collective-permute-start.27 = (bf16[2,256,1024]{2,1,0:T(8,128)(2,1)S(1)}, bf16[2,256,1024]{2,1,0:T(8,128)(2,1)}, u32[]{:S(2)}, u32[]{:S(2)}) collective-permute-start(bf16[2,256,1024]{2,1,0:T(8,128)(2,1)S(1)} %copy-done.16), channel_id=1, source_target_pairs={{0,1},{1,0},{2,3},{3,2},{4,5},{5,4},{6,7},{7,6},{8,9},{9,8},{10,11... | collective-permute-start | bytes 3145736 | tf_op jit(solution)/shard_map/ppermute | solution.py:654
  131.3 11.9 %collective-permute-start.23 = (bf16[2,256,128]{2,1,0:T(8,128)(2,1)}, bf16[2,256,128]{2,1,0:T(8,128)(2,1)}, u32[]{:S(2)}, u32[]{:S(2)}) collective-permute-start(bf16[2,256,128]{2,1,0:T(8,128)(2,1)} %get-tuple-element.290.refs_7_), channel_id=1, source_target_pairs={{0,24},{8,16},{16,8},{24,0},{1,25},{9,17},{17,9},{25,1},{2,26},{10... | collective-permute-start | bytes 393224 | tf_op jit(solution)/shard_map/ppermute | solution.py:650
  135.9 25.9 %collective-permute-start.28 = (bf16[2,256,1024]{2,1,0:T(8,128)(2,1)S(1)}, bf16[2,256,1024]{2,1,0:T(8,128)(2,1)}, u32[]{:S(2)}, u32[]{:S(2)}) collective-permute-start(bf16[2,256,1024]{2,1,0:T(8,128)(2,1)S(1)} %collective-permute-done.14.refs_9_.refs_17_), channel_id=1, source_target_pairs={{0,1},{1,0},{2,3},{3,2},{4,5},{5,4},{6,7},{7,6},{8,9},{9,8},{10,11... | collective-permute-start | bytes 3145736 | tf_op jit(solution)/shard_map/ppermute | solution.py:654
  137.2 24.5 %collective-permute-start.29 = (bf16[2,256,1024]{2,1,0:T(8,128)(2,1)S(1)}, bf16[2,256,1024]{2,1,0:T(8,128)(2,1)}, u32[]{:S(2)}, u32[]{:S(2)}) collective-permute-start(bf16[2,256,1024]{2,1,0:T(8,128)(2,1)S(1)} %collective-permute-done.15.refs_10_.refs_18_), channel_id=1, source_target_pairs={{0,1},{1,0},{2,3},{3,2},{4,5},{5,4},{6,7},{7,6},{8,9},{9,8},{10,11... | collective-permute-start | bytes 3145736 | tf_op jit(solution)/shard_map/ppermute | solution.py:654
  138.6 23.2 %collective-permute-start.30 = (bf16[2,256,1024]{2,1,0:T(8,128)(2,1)}, bf16[2,256,1024]{2,1,0:T(8,128)(2,1)}, u32[]{:S(2)}, u32[]{:S(2)}) collective-permute-start(bf16[2,256,1024]{2,1,0:T(8,128)(2,1)} %collective-permute-done.19.refs_11_.refs_19_), channel_id=1, source_target_pairs={{0,1},{1,0},{2,3},{3,2},{4,5},{5,4},{6,7},{7,6},{8,9},{9,8},{10,11... | collective-permute-start | bytes 3145736 | tf_op jit(solution)/shard_map/ppermute | solution.py:654
  145.6 14.7 %collective-permute-start.25 = (bf16[256,1024]{1,0:T(8,128)(2,1)}, bf16[256,1024]{1,0:T(8,128)(2,1)S(1)}, u32[]{:S(2)}, u32[]{:S(2)}) collective-permute-start(bf16[256,1024]{1,0:T(8,128)(2,1)} %get-tuple-element.307.refs_0_), channel_id=1, source_target_pairs={{0,8},{8,0},{16,24},{24,16},{1,9},{9,1},{17,25},{25,17},{2,10},{10... | collective-permute-start | bytes 1572872 | tf_op jit(solution)/shard_map/ppermute | solution.py:650
  147.9 13.8 %collective-permute-start.26 = (bf16[256,1024]{1,0:T(8,128)(2,1)}, bf16[256,1024]{1,0:T(8,128)(2,1)S(1)}, u32[]{:S(2)}, u32[]{:S(2)}) collective-permute-start(bf16[256,1024]{1,0:T(8,128)(2,1)} %get-tuple-element.307.refs_0_), channel_id=1, source_target_pairs={{0,16},{8,24},{16,0},{24,8},{1,17},{9,25},{17,1},{25,9},{2,18},{10... | collective-permute-start | bytes 1572872 | tf_op jit(solution)/shard_map/ppermute | solution.py:650
  161.9 9.2 %collective-permute-start.31 = (bf16[256,1024]{1,0:T(8,128)(2,1)S(1)}, bf16[256,1024]{1,0:T(8,128)(2,1)S(1)}, u32[]{:S(2)}, u32[]{:S(2)}) collective-permute-start(bf16[256,1024]{1,0:T(8,128)(2,1)S(1)} %broadcast_select_fusion.3), channel_id=1, source_target_pairs={{0,8},{1,17},{8,0},{9,25},{16,24},{17,1},{24,16},{25,9},{2,10},{3,... | collective-permute-start | bytes 1572872 | tf_op jit(solution)/shard_map/ppermute | solution.py:676
  173.8 23.6 %collective-permute-start.36 = (bf16[256,1024]{1,0:T(8,128)(2,1)}, bf16[256,1024]{1,0:T(8,128)(2,1)}, u32[]{:S(2)}, u32[]{:S(2)}) collective-permute-start(bf16[256,1024]{1,0:T(8,128)(2,1)} %get-tuple-element.337.refs_0_.refs_8_), channel_id=1, source_target_pairs={{0,8},{8,0},{16,24},{24,16},{1,9},{9,1},{17,25},{25,17},{2,10},{10... | collective-permute-start | bytes 1572872 | tf_op jit(solution)/shard_map/ppermute | solution.py:650
  175.5 25.2 %collective-permute-start.37 = (bf16[256,1024]{1,0:T(8,128)(2,1)}, bf16[256,1024]{1,0:T(8,128)(2,1)}, u32[]{:S(2)}, u32[]{:S(2)}) collective-permute-start(bf16[256,1024]{1,0:T(8,128)(2,1)} %get-tuple-element.337.refs_0_.refs_8_), channel_id=1, source_target_pairs={{0,16},{8,24},{16,0},{24,8},{1,17},{9,25},{17,1},{25,9},{2,18},{10... | collective-permute-start | bytes 1572872 | tf_op jit(solution)/shard_map/ppermute | solution.py:650
  177.1 23.7 %collective-permute-start.38 = (bf16[256,1024]{1,0:T(8,128)(2,1)}, bf16[256,1024]{1,0:T(8,128)(2,1)}, u32[]{:S(2)}, u32[]{:S(2)}) collective-permute-start(bf16[256,1024]{1,0:T(8,128)(2,1)} %get-tuple-element.337.refs_0_.refs_8_), channel_id=1, source_target_pairs={{0,24},{8,16},{16,8},{24,0},{1,25},{9,17},{17,9},{25,1},{2,26},{10... | collective-permute-start | bytes 1572872 | tf_op jit(solution)/shard_map/ppermute | solution.py:650
  200.8 8.0 %collective-permute-start.41 = (bf16[256,1024]{1,0:T(8,128)(2,1)}, bf16[256,1024]{1,0:T(8,128)(2,1)S(1)}, u32[]{:S(2)}, u32[]{:S(2)}) collective-permute-start(bf16[256,1024]{1,0:T(8,128)(2,1)} %get-tuple-element.337.refs_0_.refs_8_), channel_id=1, source_target_pairs={{0,1},{1,0},{2,3},{3,2},{4,5},{5,4},{6,7},{7,6},{8,9},{9,8},{10,11... | collective-permute-start | bytes 1572872 | tf_op jit(solution)/shard_map/ppermute | solution.py:654
  201.3 7.5 %collective-permute-start.42 = (bf16[256,1024]{1,0:T(8,128)(2,1)}, bf16[256,1024]{1,0:T(8,128)(2,1)S(1)}, u32[]{:S(2)}, u32[]{:S(2)}) collective-permute-start(bf16[256,1024]{1,0:T(8,128)(2,1)} %collective-permute-done.36.refs_1_.refs_9_), channel_id=1, source_target_pairs={{0,1},{1,0},{2,3},{3,2},{4,5},{5,4},{6,7},{7,6},{8,9},{9,8},{10,11... | collective-permute-start | bytes 1572872 | tf_op jit(solution)/shard_map/ppermute | solution.py:654
  201.3 7.5 %collective-permute-start.43 = (bf16[256,1024]{1,0:T(8,128)(2,1)}, bf16[256,1024]{1,0:T(8,128)(2,1)S(1)}, u32[]{:S(2)}, u32[]{:S(2)}) collective-permute-start(bf16[256,1024]{1,0:T(8,128)(2,1)} %collective-permute-done.37.refs_2_.refs_10_), channel_id=1, source_target_pairs={{0,1},{1,0},{2,3},{3,2},{4,5},{5,4},{6,7},{7,6},{8,9},{9,8},{10,11... | collective-permute-start | bytes 1572872 | tf_op jit(solution)/shard_map/ppermute | solution.py:654
  205.2 27.7 %collective-permute-start.48 = (bf16[4,256,1024]{2,1,0:T(8,128)(2,1)}, bf16[4,256,1024]{2,1,0:T(8,128)(2,1)S(1)}, u32[]{:S(2)}, u32[]{:S(2)}) collective-permute-start(bf16[4,256,1024]{2,1,0:T(8,128)(2,1)} %get-tuple-element.347), channel_id=1, source_target_pairs={{0,1},{1,0},{2,3},{3,2},{4,5},{5,4},{6,7},{7,6},{8,9},{9,8},{10,11... | collective-permute-start | bytes 6291464 | tf_op jit(solution)/shard_map/ppermute | solution.py:654
  208.8 24.0 %collective-permute-start.45 = (bf16[256,1024]{1,0:T(8,128)(2,1)}, bf16[256,1024]{1,0:T(8,128)(2,1)}, u32[]{:S(2)}, u32[]{:S(2)}) collective-permute-start(bf16[256,1024]{1,0:T(8,128)(2,1)} %get-tuple-element.333), channel_id=1, source_target_pairs={{0,8},{8,0},{16,24},{24,16},{1,9},{9,1},{17,25},{25,17},{2,10},{10... | collective-permute-start | bytes 1572872 | tf_op jit(solution)/shard_map/ppermute | solution.py:650
  210.1 22.7 %collective-permute-start.46 = (bf16[256,1024]{1,0:T(8,128)(2,1)S(1)}, bf16[256,1024]{1,0:T(8,128)(2,1)}, u32[]{:S(2)}, u32[]{:S(2)}) collective-permute-start(bf16[256,1024]{1,0:T(8,128)(2,1)S(1)} %get-tuple-element.334), channel_id=1, source_target_pairs={{0,16},{8,24},{16,0},{24,8},{1,17},{9,25},{17,1},{25,9},{2,18},{10... | collective-permute-start | bytes 1572872 | tf_op jit(solution)/shard_map/ppermute | solution.py:650
  211.0 24.6 %collective-permute-start.47 = (bf16[256,1024]{1,0:T(8,128)(2,1)S(1)}, bf16[256,1024]{1,0:T(8,128)(2,1)}, u32[]{:S(2)}, u32[]{:S(2)}) collective-permute-start(bf16[256,1024]{1,0:T(8,128)(2,1)S(1)} %get-tuple-element.335), channel_id=1, source_target_pairs={{0,24},{8,16},{16,8},{24,0},{1,25},{9,17},{17,9},{25,1},{2,26},{10... | collective-permute-start | bytes 1572872 | tf_op jit(solution)/shard_map/ppermute | solution.py:650
  232.7 8.6 %collective-permute-start.50 = (bf16[4,256,1024]{2,1,0:T(8,128)(2,1)}, bf16[4,256,1024]{2,1,0:T(8,128)(2,1)}, u32[]{:S(2)}, u32[]{:S(2)}) collective-permute-start(bf16[4,256,1024]{2,1,0:T(8,128)(2,1)} %get-tuple-element.361), channel_id=1, source_target_pairs={{0,1},{1,0},{2,3},{3,2},{4,5},{5,4},{6,7},{7,6},{8,9},{9,8},{10,11... | collective-permute-start | bytes 6291464 | tf_op jit(solution)/shard_map/ppermute | solution.py:654
  250.9 29.3 %collective-permute-start.51 = (bf16[256,1024]{1,0:T(8,128)(2,1)}, bf16[256,1024]{1,0:T(8,128)(2,1)}, u32[]{:S(2)}, u32[]{:S(2)}) collective-permute-start(bf16[256,1024]{1,0:T(8,128)(2,1)} %get-tuple-element.373), channel_id=1, source_target_pairs={{0,8},{8,0},{16,24},{24,16},{1,9},{9,1},{17,25},{25,17},{2,10},{10... | collective-permute-start | bytes 1572872 | tf_op jit(solution)/shard_map/ppermute | solution.py:650
  251.4 29.7 %collective-permute-start.52 = (bf16[256,1024]{1,0:T(8,128)(2,1)}, bf16[256,1024]{1,0:T(8,128)(2,1)}, u32[]{:S(2)}, u32[]{:S(2)}) collective-permute-start(bf16[256,1024]{1,0:T(8,128)(2,1)} %get-tuple-element.374), channel_id=1, source_target_pairs={{0,16},{8,24},{16,0},{24,8},{1,17},{9,25},{17,1},{25,9},{2,18},{10... | collective-permute-start | bytes 1572872 | tf_op jit(solution)/shard_map/ppermute | solution.py:650
  252.8 28.2 %collective-permute-start.53 = (bf16[256,1024]{1,0:T(8,128)(2,1)}, bf16[256,1024]{1,0:T(8,128)(2,1)}, u32[]{:S(2)}, u32[]{:S(2)}) collective-permute-start(bf16[256,1024]{1,0:T(8,128)(2,1)} %get-tuple-element.375), channel_id=1, source_target_pairs={{0,24},{8,16},{16,8},{24,0},{1,25},{9,17},{17,9},{25,1},{2,26},{10... | collective-permute-start | bytes 1572872 | tf_op jit(solution)/shard_map/ppermute | solution.py:650
  255.1 25.1 %collective-permute-start.56 = (bf16[2,256,128]{2,1,0:T(8,128)(2,1)}, bf16[2,256,128]{2,1,0:T(8,128)(2,1)}, u32[]{:S(2)}, u32[]{:S(2)}) collective-permute-start(bf16[2,256,128]{2,1,0:T(8,128)(2,1)} %get-tuple-element.379), channel_id=1, source_target_pairs={{0,24},{8,16},{16,8},{24,0},{1,25},{9,17},{17,9},{25,1},{2,26},{10... | collective-permute-start | bytes 393224 | tf_op jit(solution)/shard_map/ppermute | solution.py:650
  256.6 34.6 %collective-permute-start.57 = (bf16[2,256,1024]{2,1,0:T(8,128)(2,1)}, bf16[2,256,1024]{2,1,0:T(8,128)(2,1)S(1)}, u32[]{:S(2)}, u32[]{:S(2)}) collective-permute-start(bf16[2,256,1024]{2,1,0:T(8,128)(2,1)} %pad_maximum_fusion.1), channel_id=1, source_target_pairs={{0,8},{1,17},{8,0},{9,25},{16,24},{17,1},{24,16},{25,9},{2,10},{3,... | collective-permute-start | bytes 3145736 | tf_op jit(solution)/shard_map/ppermute | solution.py:883
  277.5 115.7 %reduce-scatter.6.cloned.1.call-start = ((), (), s32[]{:S(2)}) async-start(), calls=%async_computation.6 | async-start | bytes 2359296 | tf_op jit(solution)/shard_map/reduce_scatter | solution.py:912
  298.0 29.5 %collective-permute-start.59 = (bf16[2,256,1024]{2,1,0:T(8,128)(2,1)S(1)}, bf16[2,256,1024]{2,1,0:T(8,128)(2,1)}, u32[]{:S(2)}, u32[]{:S(2)}) collective-permute-start(bf16[2,256,1024]{2,1,0:T(8,128)(2,1)S(1)} %pad_maximum_fusion.2), channel_id=1, source_target_pairs={{0,8},{8,0},{16,24},{24,16},{1,9},{9,1},{17,25},{25,17},{2,10},{10... | collective-permute-start | bytes 3145736 | tf_op jit(solution)/shard_map/ppermute | solution.py:650
  298.6 28.9 %collective-permute-start.60 = (bf16[2,256,1024]{2,1,0:T(8,128)(2,1)S(1)}, bf16[2,256,1024]{2,1,0:T(8,128)(2,1)}, u32[]{:S(2)}, u32[]{:S(2)}) collective-permute-start(bf16[2,256,1024]{2,1,0:T(8,128)(2,1)S(1)} %pad_maximum_fusion.3), channel_id=1, source_target_pairs={{0,16},{8,24},{16,0},{24,8},{1,17},{9,25},{17,1},{25,9},{2,18},{10... | collective-permute-start | bytes 3145736 | tf_op jit(solution)/shard_map/ppermute | solution.py:650
  333.2 12.4 %collective-permute-start.66 = (bf16[2,256,128]{2,1,0:T(8,128)(2,1)}, bf16[2,256,128]{2,1,0:T(8,128)(2,1)S(1)}, u32[]{:S(2)}, u32[]{:S(2)}) collective-permute-start(bf16[2,256,128]{2,1,0:T(8,128)(2,1)} %get-tuple-element.418), channel_id=1, source_target_pairs={{0,8},{8,0},{16,24},{24,16},{1,9},{9,1},{17,25},{25,17},{2,10},{10... | collective-permute-start | bytes 393224 | tf_op jit(solution)/shard_map/ppermute | solution.py:650
  334.5 11.1 %collective-permute-start.67 = (bf16[2,256,128]{2,1,0:T(8,128)(2,1)}, bf16[2,256,128]{2,1,0:T(8,128)(2,1)S(1)}, u32[]{:S(2)}, u32[]{:S(2)}) collective-permute-start(bf16[2,256,128]{2,1,0:T(8,128)(2,1)} %get-tuple-element.419), channel_id=1, source_target_pairs={{0,16},{8,24},{16,0},{24,8},{1,17},{9,25},{17,1},{25,9},{2,18},{10... | collective-permute-start | bytes 393224 | tf_op jit(solution)/shard_map/ppermute | solution.py:650
  335.2 10.4 %collective-permute-start.68 = (bf16[2,256,128]{2,1,0:T(8,128)(2,1)}, bf16[2,256,128]{2,1,0:T(8,128)(2,1)S(1)}, u32[]{:S(2)}, u32[]{:S(2)}) collective-permute-start(bf16[2,256,128]{2,1,0:T(8,128)(2,1)} %get-tuple-element.420), channel_id=1, source_target_pairs={{0,24},{8,16},{16,8},{24,0},{1,25},{9,17},{17,9},{25,1},{2,26},{10... | collective-permute-start | bytes 393224 | tf_op jit(solution)/shard_map/ppermute | solution.py:650
  345.6 97.9 %reduce-scatter.8.cloned.1.call-start = ((), (), s32[]{:S(2)}) async-start(), calls=%async_computation.7 | async-start | bytes 983040 | tf_op jit(solution)/shard_map/reduce_scatter | solution.py:930
  349.7 42.7 %collective-permute-start.63 = (bf16[256,1024]{1,0:T(8,128)(2,1)}, bf16[256,1024]{1,0:T(8,128)(2,1)S(1)}, u32[]{:S(2)}, u32[]{:S(2)}) collective-permute-start(bf16[256,1024]{1,0:T(8,128)(2,1)} %get-tuple-element.423), channel_id=1, source_target_pairs={{0,8},{8,0},{16,24},{24,16},{1,9},{9,1},{17,25},{25,17},{2,10},{10... | collective-permute-start | bytes 1572872 | tf_op jit(solution)/shard_map/ppermute | solution.py:650
  351.0 41.4 %collective-permute-start.64 = (bf16[256,1024]{1,0:T(8,128)(2,1)}, bf16[256,1024]{1,0:T(8,128)(2,1)}, u32[]{:S(2)}, u32[]{:S(2)}) collective-permute-start(bf16[256,1024]{1,0:T(8,128)(2,1)} %get-tuple-element.424), channel_id=1, source_target_pairs={{0,16},{8,24},{16,0},{24,8},{1,17},{9,25},{17,1},{25,9},{2,18},{10... | collective-permute-start | bytes 1572872 | tf_op jit(solution)/shard_map/ppermute | solution.py:650
  351.7 40.7 %collective-permute-start.65 = (bf16[256,1024]{1,0:T(8,128)(2,1)}, bf16[256,1024]{1,0:T(8,128)(2,1)}, u32[]{:S(2)}, u32[]{:S(2)}) collective-permute-start(bf16[256,1024]{1,0:T(8,128)(2,1)} %get-tuple-element.425), channel_id=1, source_target_pairs={{0,24},{8,16},{16,8},{24,0},{1,25},{9,17},{17,9},{25,1},{2,26},{10... | collective-permute-start | bytes 1572872 | tf_op jit(solution)/shard_map/ppermute | solution.py:650
  355.1 37.3 %collective-permute-start.71 = (bf16[384,1024]{1,0:T(8,128)(2,1)}, bf16[384,1024]{1,0:T(8,128)(2,1)}, u32[]{:S(2)}, u32[]{:S(2)}) collective-permute-start(bf16[384,1024]{1,0:T(8,128)(2,1)} %pad_maximum_fusion.5.refs_0_), channel_id=1, source_target_pairs={{0,8},{8,0},{16,24},{24,16},{1,9},{9,1},{17,25},{25,17},{2,10},{10... | collective-permute-start | bytes 2359304 | tf_op jit(solution)/shard_map/ppermute | solution.py:650
  356.4 36.9 %collective-permute-start.72 = (bf16[384,1024]{1,0:T(8,128)(2,1)}, bf16[384,1024]{1,0:T(8,128)(2,1)}, u32[]{:S(2)}, u32[]{:S(2)}) collective-permute-start(bf16[384,1024]{1,0:T(8,128)(2,1)} %pad_maximum_fusion.5.refs_0_), channel_id=1, source_target_pairs={{0,16},{8,24},{16,0},{24,8},{1,17},{9,25},{17,1},{25,9},{2,18},{10... | collective-permute-start | bytes 2359304 | tf_op jit(solution)/shard_map/ppermute | solution.py:650
  393.3 14.4 %collective-permute-start.73 = (bf16[4,256,1024]{2,1,0:T(8,128)(2,1)}, bf16[4,256,1024]{2,1,0:T(8,128)(2,1)}, u32[]{:S(2)}, u32[]{:S(2)}) collective-permute-start(bf16[4,256,1024]{2,1,0:T(8,128)(2,1)} %get-tuple-element.453), channel_id=1, source_target_pairs={{0,1},{1,0},{2,3},{3,2},{4,5},{5,4},{6,7},{7,6},{8,9},{9,8},{10,11... | collective-permute-start | bytes 6291464 | tf_op jit(solution)/shard_map/ppermute | solution.py:654
  395.4 12.3 %collective-permute-start.74 = (bf16[384,1024]{1,0:T(8,128)(2,1)}, bf16[384,1024]{1,0:T(8,128)(2,1)}, u32[]{:S(2)}, u32[]{:S(2)}) collective-permute-start(bf16[384,1024]{1,0:T(8,128)(2,1)} %broadcast_select_fusion.2), channel_id=1, source_target_pairs={{0,8},{1,17},{8,0},{9,25},{16,24},{17,1},{24,16},{25,9},{2,10},{3,... | collective-permute-start | bytes 2359304 | tf_op jit(solution)/shard_map/ppermute | solution.py:676
  411.1 16.1 %collective-permute-start.77 = (bf16[256,1024]{1,0:T(8,128)(2,1)}, bf16[256,1024]{1,0:T(8,128)(2,1)}, u32[]{:S(2)}, u32[]{:S(2)}) collective-permute-start(bf16[256,1024]{1,0:T(8,128)(2,1)} %get-tuple-element.490), channel_id=1, source_target_pairs={{0,24},{8,16},{16,8},{24,0},{1,25},{9,17},{17,9},{25,1},{2,26},{10... | collective-permute-start | bytes 1572872 | tf_op jit(solution)/shard_map/ppermute | solution.py:650
  412.5 24.5 %collective-permute-start.76 = (bf16[256,1024]{1,0:T(8,128)(2,1)}, bf16[256,1024]{1,0:T(8,128)(2,1)}, u32[]{:S(2)}, u32[]{:S(2)}) collective-permute-start(bf16[256,1024]{1,0:T(8,128)(2,1)} %get-tuple-element.491), channel_id=1, source_target_pairs={{0,16},{8,24},{16,0},{24,8},{1,17},{9,25},{17,1},{25,9},{2,18},{10... | collective-permute-start | bytes 1572872 | tf_op jit(solution)/shard_map/ppermute | solution.py:650
  413.3 23.7 %collective-permute-start.75 = (bf16[256,1024]{1,0:T(8,128)(2,1)}, bf16[256,1024]{1,0:T(8,128)(2,1)}, u32[]{:S(2)}, u32[]{:S(2)}) collective-permute-start(bf16[256,1024]{1,0:T(8,128)(2,1)} %get-tuple-element.489), channel_id=1, source_target_pairs={{0,8},{8,0},{16,24},{24,16},{1,9},{9,1},{17,25},{25,17},{2,10},{10... | collective-permute-start | bytes 1572872 | tf_op jit(solution)/shard_map/ppermute | solution.py:650
  420.4 24.6 %collective-permute-start.61 = (bf16[256,1024]{1,0:T(8,128)(2,1)}, bf16[256,1024]{1,0:T(8,128)(2,1)}, u32[]{:S(2)}, u32[]{:S(2)}) collective-permute-start(bf16[256,1024]{1,0:T(8,128)(2,1)} %get-tuple-element.518), channel_id=1, source_target_pairs={{0,1},{1,0},{2,3},{3,2},{4,5},{5,4},{6,7},{7,6},{8,9},{9,8},{10,11... | collective-permute-start | bytes 1572872 | tf_op jit(solution)/shard_map/ppermute | solution.py:654
  443.4 14.8 %collective-permute-start.78 = (f32[256,1024]{1,0:T(8,128)S(1)}, f32[256,1024]{1,0:T(8,128)}, u32[]{:S(2)}, u32[]{:S(2)}) collective-permute-start(f32[256,1024]{1,0:T(8,128)S(1)} %get-tuple-element.514), channel_id=1, source_target_pairs={{0,1},{1,0},{2,3},{3,2},{4,5},{5,4},{6,7},{7,6},{8,9},{9,8},{10,11... | collective-permute-start | bytes 3145736 | tf_op jit(solution)/shard_map/ppermute | solution.py:654
  447.4 14.1 %collective-permute-start.80 = (bf16[128,1792]{1,0:T(8,128)(2,1)S(1)}, bf16[128,1792]{1,0:T(8,128)(2,1)S(1)}, u32[]{:S(2)}, u32[]{:S(2)}) collective-permute-start(bf16[128,1792]{1,0:T(8,128)(2,1)S(1)} %pad_maximum_fusion.6.refs_0_), channel_id=1, source_target_pairs={{0,8},{8,0},{16,24},{24,16},{1,9},{9,1},{17,25},{25,17},{2,10},{10... | collective-permute-start | bytes 1376264 | tf_op jit(solution)/shard_map/ppermute | solution.py:650
  448.3 22.5 %collective-permute-start.81 = (bf16[128,1792]{1,0:T(8,128)(2,1)S(1)}, bf16[128,1792]{1,0:T(8,128)(2,1)S(1)}, u32[]{:S(2)}, u32[]{:S(2)}) collective-permute-start(bf16[128,1792]{1,0:T(8,128)(2,1)S(1)} %pad_maximum_fusion.6.refs_0_), channel_id=1, source_target_pairs={{0,16},{8,24},{16,0},{24,8},{1,17},{9,25},{17,1},{25,9},{2,18},{10... | collective-permute-start | bytes 1376264 | tf_op jit(solution)/shard_map/ppermute | solution.py:650
  449.8 21.0 %collective-permute-start.82 = (bf16[128,1792]{1,0:T(8,128)(2,1)S(1)}, bf16[128,1792]{1,0:T(8,128)(2,1)}, u32[]{:S(2)}, u32[]{:S(2)}) collective-permute-start(bf16[128,1792]{1,0:T(8,128)(2,1)S(1)} %pad_maximum_fusion.6.refs_0_), channel_id=1, source_target_pairs={{0,24},{8,16},{16,8},{24,0},{1,25},{9,17},{17,9},{25,1},{2,26},{10... | collective-permute-start | bytes 1376264 | tf_op jit(solution)/shard_map/ppermute | solution.py:650
  (85 other events, 761.1 us)
Sparse Core Ops, SparseCore 0:
  29.1 27.2 all-gather.4
  58.0 28.6 all-gather.6
  106.7 63.8 all-gather.8
  277.6 61.9 reduce-scatter.3
  345.8 36.3 reduce-scatter.5
  418.1 25.1 reduce-scatter.7

commit v4 on v3

--- a/solution.py
+++ b/solution.py
@@ -931,13 +931,18 @@
     a_got1 = swap(a_other1)
     if lanes:
         ff_packs = [ff_own] + gather_far(ff_packs)
-        a_mine1, a_got1, ff_packs = together(a_mine1, a_got1, ff_packs)
     joined1 = sum_cores(a_mine1, a_got1)
+    if lanes:
+        joined1, ff_packs = together(joined1, ff_packs)
     parts1 = plane_send(joined1)
     out_rows = jnp.stack([hidden0, hidden1])
     for part in out_parts:
         out_rows = out_rows + part.astype(F32)
     out_rows = out_rows.astype(BF16)
+    if lanes:
+        both = jnp.concatenate([*to_owner(grad_qkv), wo_shard], axis=1)
+        parts1 = after(parts1, both)
+        boths = [both] + [send(both, r) for r in range(1, n)]
     in_rows = [
         d_hidden + back_normed(x_rows[s].astype(F32), sum(p.astype(F32) for p in parts))
         for s, (d_hidden, parts) in enumerate(((d_hidden0, parts0), (d_hidden1, parts1)))
@@ -963,8 +968,6 @@
             estimate=cost(7),
         )(me, *ff_packs, g2, w_gate, w_up)
         grad_gate, grad_up, grad_down, grad_gain_ffn = raw
-        both = jnp.concatenate([*to_owner(grad_qkv), wo_shard], axis=1)
-        boths = [both] + [send(both, r) for r in range(1, n)]
         raw = call(
             functools.partial(finish_qkv_kernel, n, width),
             "finish_qkv",

time: 492 us -> 484 us (0.984)
    ppermute x4, waiting for transfers between devices: 30.3 us -> 25.1 us  [gather_far(): return near + [lax.ppermute(onward, ('ctx', 'core'), pairs)]]
  transfers between devices with their start and end apart: 89 -> 89, of which waited for: 27 -> 30; matrix products, arithmetic and copies ran while one was open for 12% -> 12% of each run, Pallas kernels for 41% -> 42%
where the time goes in v4:
time: 484 us; the launch traced here: 478 us
  Pallas kernels  210 us (43%)
  waiting for transfers between devices  114 us (24%)
  starting transfers between devices  66.3 us (14%)
  other arithmetic  53.4 us (11%)
  local copies, waits for them, and re-layouts  18.7 us (4%)
  between operations  15.7 us (3%)
    ppermute x43, waiting for transfers between devices, send(): return lax.ppermute(value, 'ctx', [(i, i ^ step) for i in range(count)])  66.4 us
    pallas_call x2, Pallas kernels, attend_back(): call(functools.partial(attend_back_kernel, n, heads, half), 'attend_back'...  53.9 us
    ppermute x43, starting transfers between devices, send(): return lax.ppermute(value, 'ctx', [(i, i ^ step) for i in range(count)])  52.9 us
    pallas_call x2, Pallas kernels, attend(): call(functools.partial(attend_kernel, n, heads, half), 'attend', [shape_o...  42.9 us
    pallas_call x2, Pallas kernels, feed(): call(functools.partial(feed_kernel, n, half, cols, which), 'feed', [shape...  40.3 us
    ppermute x4, waiting for transfers between devices, gather_far(): return near + [lax.ppermute(onward, ('ctx', 'core'), pairs)]  25.1 us
    pallas_call x1, Pallas kernels, feed_grads(): call(functools.partial(feed_grads_kernel, n, n_z, half), 'feed_grads', [s...  20.3 us
    convert_element_type x4, other arithmetic, sum_cores(): (mine[r].astype(F32) + got[r].astype(F32)).astype(BF16)  15.3 us
  transfers between devices with their start and end apart: 89, of which 30 were waited for; matrix products, arithmetic and copies ran while one was open for 12% of the time, Pallas kernels for 42%

profile of v4, /device:TPU:0, one launch (start us, length us, event | category | flops | bytes accessed | tf_op | source)
XLA Modules:
  0.0 477.7 jit_solution(7031000856739297409)
XLA Ops:
  12.0 2.7 pack_qkv.1
  16.3 1.7 maximum_select_fusion.5
  18.0 3.3 pack_hidden.1
  21.2 3.6 collective-permute-start.6
  25.4 2.0 collective-permute-start.1
  29.1 2.2 dynamic-slice_bitcast_fusion.1
  34.5 2.8 maximum_select_fusion.2.refs_8_.refs_4_.refs_16_
  37.2 13.0 %collective-permute-done.1.refs_1_ = bf16[2,256,1024]{2,1,0:T(8,128)(2,1)S(1)} collective-permute-done((bf16[2,256,1024]{2,1,0:T(8,128)(2,1)S(1)}, bf16[2,256,1024]{2,1,0:T(8,128)(2,1)S(1)}, u32[]{:S(2)}, u32[]{:S(2)}) %collective-permute-start.1) | collective-permute-done | bytes 1048608 | tf_op jit(solution)/shard_map/ppermute | solution.py:650
  51.8 2.3 broadcast_select_fusion.1
  54.6 1.7 all-gather.5.cloned.1.call-done.refs_8_.refs_1_
  57.1 12.1 %collective-permute-done.9.refs_3_ = bf16[2,256,1024]{2,1,0:T(8,128)(2,1)} collective-permute-done((bf16[2,256,1024]{2,1,0:T(8,128)(2,1)}, bf16[2,256,1024]{2,1,0:T(8,128)(2,1)}, u32[]{:S(2)}, u32[]{:S(2)}) %collective-permute-start.9) | collective-permute-done | bytes 1048608 | tf_op jit(solution)/shard_map/ppermute | solution.py:676
  70.9 1.7 collective-permute-done.39
  76.9 20.4 %attend.2 = (bf16[2048,384]{1,0:T(8,128)(2,1)}, bf16[2,256,128]{2,1,0:T(8,128)(2,1)}, bf16[2,256,128]{2,1,0:T(8,128)(2,1)}, bf16[2,256,128]{2,1,0:T(8,128)(2,1)}...) custom-call(s32[18]{0:T(128)} %pad_add_fusion.2.info, bf16[2,256,1024]{2,1,0:T(8,128)(2,1)} %copy-done.4, ...), custom_call_target="tpu_custom_call" | custom-call | flops 20999999488 | bytes 1000 | tf_op jit(solution)/shard_map/attend/pallas_call | solution.py:175
  97.3 3.0 collective-permute-done.14.refs_9_.refs_17_
  107.1 22.5 %attend.3 = (bf16[2048,384]{1,0:T(8,128)(2,1)}, bf16[2,256,128]{2,1,0:T(8,128)(2,1)}, bf16[2,256,128]{2,1,0:T(8,128)(2,1)}, bf16[2,256,128]{2,1,0:T(8,128)(2,1)}...) custom-call(s32[18]{0:T(128)} %pad_add_fusion.4.info, bf16[2,256,1024]{2,1,0:T(8,128)(2,1)} %copy-done.4, ...), custom_call_target="tpu_custom_call" | custom-call | flops 20999999488 | bytes 1000 | tf_op jit(solution)/shard_map/attend/pallas_call | solution.py:175
  134.8 3.1 collective-permute-done.21.refs_1_
  140.6 4.6 mix.2
  147.6 2.3 collective-permute-start.25
  149.9 1.5 collective-permute-start.26
  151.4 4.6 mix.3
  156.0 6.2 %collective-permute-done.25.refs_1_ = bf16[256,1024]{1,0:T(8,128)(2,1)S(1)} collective-permute-done((bf16[256,1024]{1,0:T(8,128)(2,1)}, bf16[256,1024]{1,0:T(8,128)(2,1)S(1)}, u32[]{:S(2)}, u32[]{:S(2)}) %collective-permute-start.25) | collective-permute-done | bytes 524320 | tf_op jit(solution)/shard_map/ppermute | solution.py:650
  163.8 1.8 collective-permute-start.31
  166.1 6.9 %collective-permute-done.31.refs_3_ = bf16[256,1024]{1,0:T(8,128)(2,1)S(1)} collective-permute-done((bf16[256,1024]{1,0:T(8,128)(2,1)S(1)}, bf16[256,1024]{1,0:T(8,128)(2,1)S(1)}, u32[]{:S(2)}, u32[]{:S(2)}) %collective-permute-start.31) | collective-permute-done | bytes 524320 | tf_op jit(solution)/shard_map/ppermute | solution.py:676
  173.2 1.9 collective-permute-done.35.refs_7_
  175.8 1.7 collective-permute-start.36
  177.5 1.5 collective-permute-start.37
  179.3 20.1 %feed.2 = (bf16[2048,512]{1,0:T(8,128)(2,1)}, bf16[2048,1024]{1,0:T(8,128)(2,1)}, bf16[4,256,1024]{2,1,0:T(8,128)(2,1)}, bf16[4,256,1024]{2,1,0:T(8,128)(2,1)}, ...) custom-call(s32[2]{0:T(128)} %pad_add_fusion.1.info, bf16[256,1024]{1,0:T(8,128)(2,1)} %get-tuple-element.313.refs_0_, ...), custom_call_target="tpu_custom_call" | custom-call | flops 20000000000 | bytes 1000 | tf_op jit(solution)/shard_map/feed/pallas_call | solution.py:403
  199.4 3.3 collective-permute-done.37.refs_2_.refs_10_
  203.8 3.3 collective-permute-done.40
  207.3 3.5 fusion.31
  214.5 20.3 %feed.3 = (bf16[2048,512]{1,0:T(8,128)(2,1)}, bf16[2048,1024]{1,0:T(8,128)(2,1)}, bf16[4,256,1024]{2,1,0:T(8,128)(2,1)}, bf16[4,256,1024]{2,1,0:T(8,128)(2,1)}, ...) custom-call(s32[2]{0:T(128)} %pad_add_fusion.1.info, bf16[256,1024]{1,0:T(8,128)(2,1)} %get-tuple-element.343.refs_0_.refs_8_, ...), custom_call_target="tpu_custom_call" | custom-call | flops 20000000000 | bytes 1000 | tf_op jit(solution)/shard_map/feed/pallas_call | solution.py:403
  234.9 2.7 collective-permute-done.47.refs_3_
  237.6 5.7 %turn.2 = (f32[256,1024]{1,0:T(8,128)}, bf16[256,1024]{1,0:T(8,128)(2,1)}, bf16[2,256,128]{2,1,0:T(8,128)(2,1)}, bf16[2,256,128]{2,1,0:T(8,128)(2,1)}, bf16[2,25...) custom-call(s32[2]{0:T(128)} %pad_add_fusion.1.info, bf16[256,1024]{1,0:T(8,128)(2,1)} %get-tuple-element.356.refs_0_, ...), custom_call_target="tpu_custom_call" | custom-call | flops 6000000000 | bytes 1000 | tf_op jit(solution)/shard_map/turn/pallas_call | solution.py:521
  243.3 3.5 fusion.35
  251.3 1.5 collective-permute-start.55
  254.8 1.6 collective-permute-start.53
  257.0 1.6 collective-permute-start.56
  259.1 20.3 %feed_grads.1 = bf16[4,384,1024]{2,1,0:T(8,128)(2,1)} custom-call(s32[2]{0:T(128)} %pad_add_fusion.1.info, bf16[256,1024]{1,0:T(8,128)(2,1)} %get-tuple-element.313.refs_0_, bf16[256,1024]{1,0:T(8,128)(2,1)} %copy-done.21, bf16[256,1024]{1,0:T(8,128)(2,1)} %copy-done.22, bf16[256,1024]{1,0:T(8,128)(2,1)} %copy-done.39, bf16[256,1024]{1,0:T(8,128)(2,1)} %copy-done.40, ...), custom_call_target="tpu_custom_call" | custom-call | flops 20000000000 | bytes 1000 | tf_op jit(solution)/shard_map/feed_grads/pallas_call | solution.py:479
  279.6 2.6 collective-permute-done.56.refs_11_
  283.1 10.2 %collective-permute-done.57 = bf16[2,256,1024]{2,1,0:T(8,128)(2,1)S(1)} collective-permute-done((bf16[2,256,1024]{2,1,0:T(8,128)(2,1)}, bf16[2,256,1024]{2,1,0:T(8,128)(2,1)S(1)}, u32[]{:S(2)}, u32[]{:S(2)}) %collective-permute-start.57) | collective-permute-done | bytes 1048608 | tf_op jit(solution)/shard_map/ppermute | solution.py:883
  296.4 3.2 fusion.24
  300.6 1.5 collective-permute-start.60
  302.2 25.6 %attend_back.2 = (bf16[2048,384]{1,0:T(8,128)(2,1)}, bf16[4,256,1024]{2,1,0:T(8,128)(2,1)}, bf16[4,256,1024]{2,1,0:T(8,128)(2,1)}) custom-call(s32[18]{0:T(128)} %pad_add_fusion.2.info, bf16[2048,384]{1,0:T(8,128)(2,1)} %get-tuple-element.401.refs_0_, bf16[1024,512]{1,0:T(8,128)(2,1)} %all-gather.5.cloned.1.call-done.refs_8_.refs_1_, ...), custom_call_target="tpu_custom_call" | custom-call | flops 25999998976 | bytes 1000 | tf_op jit(solution)/shard_map/attend_back/pallas_call | solution.py:277
  327.9 5.6 %turn.3 = (f32[256,1024]{1,0:T(8,128)}, bf16[256,1024]{1,0:T(8,128)(2,1)}, bf16[2,256,128]{2,1,0:T(8,128)(2,1)}, bf16[2,256,128]{2,1,0:T(8,128)(2,1)}, bf16[2,25...) custom-call(s32[2]{0:T(128)} %pad_add_fusion.1.info, bf16[256,1024]{1,0:T(8,128)(2,1)} %get-tuple-element.411.refs_0_, ...), custom_call_target="tpu_custom_call" | custom-call | flops 6000000000 | bytes 1000 | tf_op jit(solution)/shard_map/turn/pallas_call | solution.py:521
  335.4 1.6 collective-permute-start.68
  337.0 4.1 fusion.39
  341.1 4.8 %out_grads.1 = bf16[1024,1024]{1,0:T(8,128)(2,1)} custom-call(s32[2]{0:T(128)} %pad_add_fusion.1.info, bf16[256,1024]{1,0:T(8,128)(2,1)} %get-tuple-element.433.att0, bf16[256,1024]{1,0:T(8,128)(2,1)} %get-tuple-element.434.att1, bf16[256,1024]{1,0:T(8,128)(2,1)} %get-tuple-element.435.e0, bf16[256,1024]{1,0:T(8,128)(2,1)} %get-tuple-element.436.e1), custom_call_target="tpu_custom_call" | custom-call | flops 5000000000 | bytes 1000 | tf_op jit(solution)/shard_map/out_grads/pallas_call | solution.py:541
  347.1 1.5 collective-permute-done.69.refs_12_
  351.9 1.6 collective-permute-start.65
  357.3 28.2 %attend_back.3 = (bf16[2048,384]{1,0:T(8,128)(2,1)}, bf16[4,256,1024]{2,1,0:T(8,128)(2,1)}, bf16[4,256,1024]{2,1,0:T(8,128)(2,1)}) custom-call(s32[18]{0:T(128)} %pad_add_fusion.4.info, bf16[2048,384]{1,0:T(8,128)(2,1)} %get-tuple-element.444.refs_0_, bf16[1024,512]{1,0:T(8,128)(2,1)} %all-gather.5.cloned.1.call-done.refs_8_.refs_1_, ...), custom_call_target="tpu_custom_call" | custom-call | flops 25999998976 | bytes 1000 | tf_op jit(solution)/shard_map/attend_back/pallas_call | solution.py:277
  385.6 9.5 %qkv_grads.1 = bf16[1024,384]{1,0:T(8,128)(2,1)} custom-call(s32[2]{0:T(128)} %pad_add_fusion.1.info, bf16[2,256,1024]{2,1,0:T(8,128)(2,1)} %copy-done.4, bf16[2,256,1024]{2,1,0:T(8,128)(2,1)} %copy-done.5, bf16[2,256,1024]{2,1,0:T(8,128)(2,1)} %collective-permute-done.2.refs_2_, bf16[2,256,1024]{2,1,0:T(8,128)(2,1)} %collective-permute-done.9.refs_3_, ...), custom_call_target="tpu_custom_call" | custom-call | flops 200000000 | bytes 1000 | tf_op jit(solution)/shard_map/qkv_grads/pallas_call | solution.py:564
  395.3 2.4 broadcast_select_fusion.2
  399.7 4.2 fusion.43
  403.9 6.1 %collective-permute-done.74.refs_3_ = bf16[384,1024]{1,0:T(8,128)(2,1)} collective-permute-done((bf16[384,1024]{1,0:T(8,128)(2,1)}, bf16[384,1024]{1,0:T(8,128)(2,1)}, u32[]{:S(2)}, u32[]{:S(2)}) %collective-permute-start.74) | collective-permute-done | bytes 786464 | tf_op jit(solution)/shard_map/ppermute | solution.py:676
  413.5 3.3 fusion.4
  420.8 4.4 collective-permute-done.75
  425.2 10.8 %collective-permute-done.76 = bf16[256,1024]{1,0:T(8,128)(2,1)} collective-permute-done((bf16[256,1024]{1,0:T(8,128)(2,1)}, bf16[256,1024]{1,0:T(8,128)(2,1)}, u32[]{:S(2)}, u32[]{:S(2)}) %collective-permute-start.76) | collective-permute-done | bytes 524320 | tf_op jit(solution)/shard_map/ppermute | solution.py:650
  435.9 2.7 fusion.9
  438.6 2.6 fusion.13
  443.5 1.5 collective-permute-start.81
  446.5 7.2 %finish.1 = (f32[128,4096]{1,0:T(8,128)}, f32[128,4096]{1,0:T(8,128)}, f32[512,1024]{1,0:T(8,128)}, f32[1,128]{1,0:T(1,128)}) custom-call(s32[2]{0:T(128)} %pad_add_fusion.1.info, bf16[384,1024]{1,0:T(8,128)(2,1)} %pad_maximum_fusion.5.refs_0_, bf16[384,1024]{1,0:T(8,128)(2,1)} %collective-permute-done.71.refs_1_, ...), custom_call_target="tpu_custom_call" | custom-call | flops 7000000000 | bytes 1000 | tf_op jit(solution)/shard_map/finish/pallas_call | solution.py:961
  453.7 1.5 maximum_select_fusion
  456.6 8.8 %collective-permute-done.81.refs_2_ = bf16[128,1792]{1,0:T(8,128)(2,1)} collective-permute-done((bf16[128,1792]{1,0:T(8,128)(2,1)}, bf16[128,1792]{1,0:T(8,128)(2,1)}, u32[]{:S(2)}, u32[]{:S(2)}) %collective-permute-start.81) | collective-permute-done | bytes 458784 | tf_op jit(solution)/shard_map/ppermute | solution.py:650
  466.3 4.2 finish_qkv.1
  (340 shorter events, 83.5 us)
Async XLA Ops:
  7.2 49.2 %all-gather.5.cloned.1.call-start = ((), (), s32[]{:S(2)}) async-start(), calls=%async_computation.3 | async-start | bytes 1310720 | tf_op jit(solution)/shard_map/all_gather | solution.py:798
  21.2 7.7 %collective-permute-start.6 = (s32[512]{0:T(512)S(1)}, s32[512]{0:T(512)S(1)}, u32[]{:S(2)}, u32[]{:S(2)}) collective-permute-start(s32[512]{0:T(512)S(1)} %bitcast.129), channel_id=1, source_target_pairs={{0,24},{8,16},{16,8},{24,0},{1,25},{9,17},{17,9},{25,1},{2,26},{10... | collective-permute-start | bytes 6152 | tf_op jit(solution)/shard_map/ppermute | solution.py:650
  25.4 24.9 %collective-permute-start.1 = (bf16[2,256,1024]{2,1,0:T(8,128)(2,1)S(1)}, bf16[2,256,1024]{2,1,0:T(8,128)(2,1)S(1)}, u32[]{:S(2)}, u32[]{:S(2)}) collective-permute-start(bf16[2,256,1024]{2,1,0:T(8,128)(2,1)S(1)} %fusion.1.refs_0_), channel_id=1, source_target_pairs={{0,8},{8,0},{16,24},{24,16},{1,9},{9,1},{17,25},{25,17},{2,10},{10... | collective-permute-start | bytes 3145736 | tf_op jit(solution)/shard_map/ppermute | solution.py:650
  27.4 24.4 %collective-permute-start.2 = (bf16[2,256,1024]{2,1,0:T(8,128)(2,1)S(1)}, bf16[2,256,1024]{2,1,0:T(8,128)(2,1)}, u32[]{:S(2)}, u32[]{:S(2)}) collective-permute-start(bf16[2,256,1024]{2,1,0:T(8,128)(2,1)S(1)} %fusion.1.refs_0_), channel_id=1, source_target_pairs={{0,16},{8,24},{16,0},{24,8},{1,17},{9,25},{17,1},{25,9},{2,18},{10... | collective-permute-start | bytes 3145736 | tf_op jit(solution)/shard_map/ppermute | solution.py:650
  28.9 77.6 %all-gather.7.cloned.1.call-start = ((), (), s32[]{:S(2)}) async-start(), calls=%async_computation.4 | async-start | bytes 2359296 | tf_op jit(solution)/shard_map/all_gather | solution.py:810
  54.1 15.1 %collective-permute-start.9 = (bf16[2,256,1024]{2,1,0:T(8,128)(2,1)}, bf16[2,256,1024]{2,1,0:T(8,128)(2,1)}, u32[]{:S(2)}, u32[]{:S(2)}) collective-permute-start(bf16[2,256,1024]{2,1,0:T(8,128)(2,1)} %broadcast_select_fusion.1), channel_id=1, source_target_pairs={{0,8},{1,17},{8,0},{9,25},{16,24},{17,1},{24,16},{25,9},{2,10},{3,... | collective-permute-start | bytes 3145736 | tf_op jit(solution)/shard_map/ppermute | solution.py:676
  56.4 122.9 %all-gather.9.cloned.1.call-start = ((), (), s32[]{:S(2)}) async-start(), calls=%async_computation.8 | async-start | bytes 3932160 | tf_op jit(solution)/shard_map/all_gather | solution.py:816
  56.5 18.3 %collective-permute-start.10 = (bf16[2,256,1024]{2,1,0:T(8,128)(2,1)S(1)}, bf16[2,256,1024]{2,1,0:T(8,128)(2,1)}, u32[]{:S(2)}, u32[]{:S(2)}) collective-permute-start(bf16[2,256,1024]{2,1,0:T(8,128)(2,1)S(1)} %fusion.1.refs_0_), channel_id=1, source_target_pairs={{0,1},{1,0},{2,3},{3,2},{4,5},{5,4},{6,7},{7,6},{8,9},{9,8},{10,11... | collective-permute-start | bytes 3145736 | tf_op jit(solution)/shard_map/ppermute | solution.py:654
  56.5 18.2 %collective-permute-start.11 = (bf16[2,256,1024]{2,1,0:T(8,128)(2,1)S(1)}, bf16[2,256,1024]{2,1,0:T(8,128)(2,1)}, u32[]{:S(2)}, u32[]{:S(2)}) collective-permute-start(bf16[2,256,1024]{2,1,0:T(8,128)(2,1)S(1)} %collective-permute-done.1.refs_1_), channel_id=1, source_target_pairs={{0,1},{1,0},{2,3},{3,2},{4,5},{5,4},{6,7},{7,6},{8,9},{9,8},{10,11... | collective-permute-start | bytes 3145736 | tf_op jit(solution)/shard_map/ppermute | solution.py:654
  57.0 17.7 %collective-permute-start.12 = (bf16[2,256,1024]{2,1,0:T(8,128)(2,1)}, bf16[2,256,1024]{2,1,0:T(8,128)(2,1)}, u32[]{:S(2)}, u32[]{:S(2)}) collective-permute-start(bf16[2,256,1024]{2,1,0:T(8,128)(2,1)} %collective-permute-done.2.refs_2_), channel_id=1, source_target_pairs={{0,1},{1,0},{2,3},{3,2},{4,5},{5,4},{6,7},{7,6},{8,9},{9,8},{10,11... | collective-permute-start | bytes 3145736 | tf_op jit(solution)/shard_map/ppermute | solution.py:654
  74.7 25.5 %collective-permute-start.14 = (bf16[2,256,1024]{2,1,0:T(8,128)(2,1)}, bf16[2,256,1024]{2,1,0:T(8,128)(2,1)S(1)}, u32[]{:S(2)}, u32[]{:S(2)}) collective-permute-start(bf16[2,256,1024]{2,1,0:T(8,128)(2,1)} %maximum_select_fusion.2.refs_8_.refs_4_.refs_16_), channel_id=1, source_target_pairs={{0,8},{8,0},{16,24},{24,16},{1,9},{9,1},{17,25},{25,17},{2,10},{10... | collective-permute-start | bytes 3145736 | tf_op jit(solution)/shard_map/ppermute | solution.py:650
  75.4 25.1 %collective-permute-start.15 = (bf16[2,256,1024]{2,1,0:T(8,128)(2,1)}, bf16[2,256,1024]{2,1,0:T(8,128)(2,1)S(1)}, u32[]{:S(2)}, u32[]{:S(2)}) collective-permute-start(bf16[2,256,1024]{2,1,0:T(8,128)(2,1)} %maximum_select_fusion.2.refs_8_.refs_4_.refs_16_), channel_id=1, source_target_pairs={{0,16},{8,24},{16,0},{24,8},{1,17},{9,25},{17,1},{25,9},{2,18},{10... | collective-permute-start | bytes 3145736 | tf_op jit(solution)/shard_map/ppermute | solution.py:650
  100.5 29.2 %collective-permute-start.16 = (bf16[2,256,128]{2,1,0:T(8,128)(2,1)}, bf16[2,256,128]{2,1,0:T(8,128)(2,1)S(1)}, u32[]{:S(2)}, u32[]{:S(2)}) collective-permute-start(bf16[2,256,128]{2,1,0:T(8,128)(2,1)} %get-tuple-element.280.refs_5_), channel_id=1, source_target_pairs={{0,8},{8,0},{16,24},{24,16},{1,9},{9,1},{17,25},{25,17},{2,10},{10... | collective-permute-start | bytes 393224 | tf_op jit(solution)/shard_map/ppermute | solution.py:650
  102.0 27.7 %collective-permute-start.17 = (bf16[2,256,128]{2,1,0:T(8,128)(2,1)}, bf16[2,256,128]{2,1,0:T(8,128)(2,1)S(1)}, u32[]{:S(2)}, u32[]{:S(2)}) collective-permute-start(bf16[2,256,128]{2,1,0:T(8,128)(2,1)} %get-tuple-element.281.refs_6_), channel_id=1, source_target_pairs={{0,16},{8,24},{16,0},{24,8},{1,17},{9,25},{17,1},{25,9},{2,18},{10... | collective-permute-start | bytes 393224 | tf_op jit(solution)/shard_map/ppermute | solution.py:650
  103.5 26.2 %collective-permute-start.18 = (bf16[2,256,128]{2,1,0:T(8,128)(2,1)}, bf16[2,256,128]{2,1,0:T(8,128)(2,1)}, u32[]{:S(2)}, u32[]{:S(2)}) collective-permute-start(bf16[2,256,128]{2,1,0:T(8,128)(2,1)} %get-tuple-element.282.refs_7_), channel_id=1, source_target_pairs={{0,24},{8,16},{16,8},{24,0},{1,25},{9,17},{17,9},{25,1},{2,26},{10... | collective-permute-start | bytes 393224 | tf_op jit(solution)/shard_map/ppermute | solution.py:650
  105.1 24.6 %collective-permute-start.19 = (bf16[2,256,1024]{2,1,0:T(8,128)(2,1)}, bf16[2,256,1024]{2,1,0:T(8,128)(2,1)}, u32[]{:S(2)}, u32[]{:S(2)}) collective-permute-start(bf16[2,256,1024]{2,1,0:T(8,128)(2,1)} %broadcast_select_fusion), channel_id=1, source_target_pairs={{0,8},{1,17},{8,0},{9,25},{16,24},{17,1},{24,16},{25,9},{2,10},{3,... | collective-permute-start | bytes 3145736 | tf_op jit(solution)/shard_map/ppermute | solution.py:676
  106.6 242.0 %reduce-scatter.4.cloned.1.call-start = ((), (), s32[]{:S(2)}) async-start(), calls=%async_computation.5 | async-start | bytes 3932160 | tf_op jit(solution)/shard_map/reduce_scatter | solution.py:886
  130.7 8.5 %collective-permute-start.20 = (bf16[4,256,128]{2,1,0:T(8,128)(2,1)S(1)}, bf16[4,256,128]{2,1,0:T(8,128)(2,1)S(1)}, u32[]{:S(2)}, u32[]{:S(2)}) collective-permute-start(bf16[4,256,128]{2,1,0:T(8,128)(2,1)S(1)} %pad_maximum_fusion.7), channel_id=1, source_target_pairs={{0,1},{1,0},{2,3},{3,2},{4,5},{5,4},{6,7},{7,6},{8,9},{9,8},{10,11... | collective-permute-start | bytes 786440 | tf_op jit(solution)/shard_map/ppermute | solution.py:654
  130.8 16.8 %collective-permute-start.27 = (bf16[2,256,1024]{2,1,0:T(8,128)(2,1)S(1)}, bf16[2,256,1024]{2,1,0:T(8,128)(2,1)}, u32[]{:S(2)}, u32[]{:S(2)}) collective-permute-start(bf16[2,256,1024]{2,1,0:T(8,128)(2,1)S(1)} %copy-done.16), channel_id=1, source_target_pairs={{0,1},{1,0},{2,3},{3,2},{4,5},{5,4},{6,7},{7,6},{8,9},{9,8},{10,11... | collective-permute-start | bytes 3145736 | tf_op jit(solution)/shard_map/ppermute | solution.py:654
  133.4 11.9 %collective-permute-start.23 = (bf16[2,256,128]{2,1,0:T(8,128)(2,1)}, bf16[2,256,128]{2,1,0:T(8,128)(2,1)}, u32[]{:S(2)}, u32[]{:S(2)}) collective-permute-start(bf16[2,256,128]{2,1,0:T(8,128)(2,1)} %get-tuple-element.296.refs_7_), channel_id=1, source_target_pairs={{0,24},{8,16},{16,8},{24,0},{1,25},{9,17},{17,9},{25,1},{2,26},{10... | collective-permute-start | bytes 393224 | tf_op jit(solution)/shard_map/ppermute | solution.py:650
  137.9 25.9 %collective-permute-start.28 = (bf16[2,256,1024]{2,1,0:T(8,128)(2,1)S(1)}, bf16[2,256,1024]{2,1,0:T(8,128)(2,1)}, u32[]{:S(2)}, u32[]{:S(2)}) collective-permute-start(bf16[2,256,1024]{2,1,0:T(8,128)(2,1)S(1)} %collective-permute-done.14.refs_9_.refs_17_), channel_id=1, source_target_pairs={{0,1},{1,0},{2,3},{3,2},{4,5},{5,4},{6,7},{7,6},{8,9},{9,8},{10,11... | collective-permute-start | bytes 3145736 | tf_op jit(solution)/shard_map/ppermute | solution.py:654
  139.3 24.5 %collective-permute-start.29 = (bf16[2,256,1024]{2,1,0:T(8,128)(2,1)S(1)}, bf16[2,256,1024]{2,1,0:T(8,128)(2,1)}, u32[]{:S(2)}, u32[]{:S(2)}) collective-permute-start(bf16[2,256,1024]{2,1,0:T(8,128)(2,1)S(1)} %collective-permute-done.15.refs_10_.refs_18_), channel_id=1, source_target_pairs={{0,1},{1,0},{2,3},{3,2},{4,5},{5,4},{6,7},{7,6},{8,9},{9,8},{10,11... | collective-permute-start | bytes 3145736 | tf_op jit(solution)/shard_map/ppermute | solution.py:654
  140.6 23.2 %collective-permute-start.30 = (bf16[2,256,1024]{2,1,0:T(8,128)(2,1)}, bf16[2,256,1024]{2,1,0:T(8,128)(2,1)}, u32[]{:S(2)}, u32[]{:S(2)}) collective-permute-start(bf16[2,256,1024]{2,1,0:T(8,128)(2,1)} %collective-permute-done.19.refs_11_.refs_19_), channel_id=1, source_target_pairs={{0,1},{1,0},{2,3},{3,2},{4,5},{5,4},{6,7},{7,6},{8,9},{9,8},{10,11... | collective-permute-start | bytes 3145736 | tf_op jit(solution)/shard_map/ppermute | solution.py:654
  147.6 14.7 %collective-permute-start.25 = (bf16[256,1024]{1,0:T(8,128)(2,1)}, bf16[256,1024]{1,0:T(8,128)(2,1)S(1)}, u32[]{:S(2)}, u32[]{:S(2)}) collective-permute-start(bf16[256,1024]{1,0:T(8,128)(2,1)} %get-tuple-element.313.refs_0_), channel_id=1, source_target_pairs={{0,8},{8,0},{16,24},{24,16},{1,9},{9,1},{17,25},{25,17},{2,10},{10... | collective-permute-start | bytes 1572872 | tf_op jit(solution)/shard_map/ppermute | solution.py:650
  149.9 13.9 %collective-permute-start.26 = (bf16[256,1024]{1,0:T(8,128)(2,1)}, bf16[256,1024]{1,0:T(8,128)(2,1)S(1)}, u32[]{:S(2)}, u32[]{:S(2)}) collective-permute-start(bf16[256,1024]{1,0:T(8,128)(2,1)} %get-tuple-element.313.refs_0_), channel_id=1, source_target_pairs={{0,16},{8,24},{16,0},{24,8},{1,17},{9,25},{17,1},{25,9},{2,18},{10... | collective-permute-start | bytes 1572872 | tf_op jit(solution)/shard_map/ppermute | solution.py:650
  163.8 9.2 %collective-permute-start.31 = (bf16[256,1024]{1,0:T(8,128)(2,1)S(1)}, bf16[256,1024]{1,0:T(8,128)(2,1)S(1)}, u32[]{:S(2)}, u32[]{:S(2)}) collective-permute-start(bf16[256,1024]{1,0:T(8,128)(2,1)S(1)} %broadcast_select_fusion.3), channel_id=1, source_target_pairs={{0,8},{1,17},{8,0},{9,25},{16,24},{17,1},{24,16},{25,9},{2,10},{3,... | collective-permute-start | bytes 1572872 | tf_op jit(solution)/shard_map/ppermute | solution.py:676
  165.6 7.5 %collective-permute-start.33 = (bf16[256,1024]{1,0:T(8,128)(2,1)S(1)}, bf16[256,1024]{1,0:T(8,128)(2,1)S(1)}, u32[]{:S(2)}, u32[]{:S(2)}) collective-permute-start(bf16[256,1024]{1,0:T(8,128)(2,1)S(1)} %collective-permute-done.25.refs_1_), channel_id=1, source_target_pairs={{0,1},{1,0},{2,3},{3,2},{4,5},{5,4},{6,7},{7,6},{8,9},{9,8},{10,11... | collective-permute-start | bytes 1572872 | tf_op jit(solution)/shard_map/ppermute | solution.py:654
  175.8 23.6 %collective-permute-start.36 = (bf16[256,1024]{1,0:T(8,128)(2,1)}, bf16[256,1024]{1,0:T(8,128)(2,1)}, u32[]{:S(2)}, u32[]{:S(2)}) collective-permute-start(bf16[256,1024]{1,0:T(8,128)(2,1)} %get-tuple-element.343.refs_0_.refs_8_), channel_id=1, source_target_pairs={{0,8},{8,0},{16,24},{24,16},{1,9},{9,1},{17,25},{25,17},{2,10},{10... | collective-permute-start | bytes 1572872 | tf_op jit(solution)/shard_map/ppermute | solution.py:650
  177.5 25.2 %collective-permute-start.37 = (bf16[256,1024]{1,0:T(8,128)(2,1)}, bf16[256,1024]{1,0:T(8,128)(2,1)}, u32[]{:S(2)}, u32[]{:S(2)}) collective-permute-start(bf16[256,1024]{1,0:T(8,128)(2,1)} %get-tuple-element.343.refs_0_.refs_8_), channel_id=1, source_target_pairs={{0,16},{8,24},{16,0},{24,8},{1,17},{9,25},{17,1},{25,9},{2,18},{10... | collective-permute-start | bytes 1572872 | tf_op jit(solution)/shard_map/ppermute | solution.py:650
  179.1 23.7 %collective-permute-start.38 = (bf16[256,1024]{1,0:T(8,128)(2,1)}, bf16[256,1024]{1,0:T(8,128)(2,1)}, u32[]{:S(2)}, u32[]{:S(2)}) collective-permute-start(bf16[256,1024]{1,0:T(8,128)(2,1)} %get-tuple-element.343.refs_0_.refs_8_), channel_id=1, source_target_pairs={{0,24},{8,16},{16,8},{24,0},{1,25},{9,17},{17,9},{25,1},{2,26},{10... | collective-permute-start | bytes 1572872 | tf_op jit(solution)/shard_map/ppermute | solution.py:650
  202.8 8.0 %collective-permute-start.41 = (bf16[256,1024]{1,0:T(8,128)(2,1)}, bf16[256,1024]{1,0:T(8,128)(2,1)S(1)}, u32[]{:S(2)}, u32[]{:S(2)}) collective-permute-start(bf16[256,1024]{1,0:T(8,128)(2,1)} %get-tuple-element.343.refs_0_.refs_8_), channel_id=1, source_target_pairs={{0,1},{1,0},{2,3},{3,2},{4,5},{5,4},{6,7},{7,6},{8,9},{9,8},{10,11... | collective-permute-start | bytes 1572872 | tf_op jit(solution)/shard_map/ppermute | solution.py:654
  203.3 7.5 %collective-permute-start.42 = (bf16[256,1024]{1,0:T(8,128)(2,1)}, bf16[256,1024]{1,0:T(8,128)(2,1)S(1)}, u32[]{:S(2)}, u32[]{:S(2)}) collective-permute-start(bf16[256,1024]{1,0:T(8,128)(2,1)} %collective-permute-done.36.refs_1_.refs_9_), channel_id=1, source_target_pairs={{0,1},{1,0},{2,3},{3,2},{4,5},{5,4},{6,7},{7,6},{8,9},{9,8},{10,11... | collective-permute-start | bytes 1572872 | tf_op jit(solution)/shard_map/ppermute | solution.py:654
  203.3 7.5 %collective-permute-start.43 = (bf16[256,1024]{1,0:T(8,128)(2,1)}, bf16[256,1024]{1,0:T(8,128)(2,1)S(1)}, u32[]{:S(2)}, u32[]{:S(2)}) collective-permute-start(bf16[256,1024]{1,0:T(8,128)(2,1)} %collective-permute-done.37.refs_2_.refs_10_), channel_id=1, source_target_pairs={{0,1},{1,0},{2,3},{3,2},{4,5},{5,4},{6,7},{7,6},{8,9},{9,8},{10,11... | collective-permute-start | bytes 1572872 | tf_op jit(solution)/shard_map/ppermute | solution.py:654
  207.1 27.7 %collective-permute-start.48 = (bf16[4,256,1024]{2,1,0:T(8,128)(2,1)}, bf16[4,256,1024]{2,1,0:T(8,128)(2,1)S(1)}, u32[]{:S(2)}, u32[]{:S(2)}) collective-permute-start(bf16[4,256,1024]{2,1,0:T(8,128)(2,1)} %get-tuple-element.353), channel_id=1, source_target_pairs={{0,1},{1,0},{2,3},{3,2},{4,5},{5,4},{6,7},{7,6},{8,9},{9,8},{10,11... | collective-permute-start | bytes 6291464 | tf_op jit(solution)/shard_map/ppermute | solution.py:654
  210.8 24.0 %collective-permute-start.45 = (bf16[256,1024]{1,0:T(8,128)(2,1)}, bf16[256,1024]{1,0:T(8,128)(2,1)}, u32[]{:S(2)}, u32[]{:S(2)}) collective-permute-start(bf16[256,1024]{1,0:T(8,128)(2,1)} %get-tuple-element.339), channel_id=1, source_target_pairs={{0,8},{8,0},{16,24},{24,16},{1,9},{9,1},{17,25},{25,17},{2,10},{10... | collective-permute-start | bytes 1572872 | tf_op jit(solution)/shard_map/ppermute | solution.py:650
  212.1 22.7 %collective-permute-start.46 = (bf16[256,1024]{1,0:T(8,128)(2,1)S(1)}, bf16[256,1024]{1,0:T(8,128)(2,1)}, u32[]{:S(2)}, u32[]{:S(2)}) collective-permute-start(bf16[256,1024]{1,0:T(8,128)(2,1)S(1)} %get-tuple-element.340), channel_id=1, source_target_pairs={{0,16},{8,24},{16,0},{24,8},{1,17},{9,25},{17,1},{25,9},{2,18},{10... | collective-permute-start | bytes 1572872 | tf_op jit(solution)/shard_map/ppermute | solution.py:650
  213.0 24.6 %collective-permute-start.47 = (bf16[256,1024]{1,0:T(8,128)(2,1)S(1)}, bf16[256,1024]{1,0:T(8,128)(2,1)}, u32[]{:S(2)}, u32[]{:S(2)}) collective-permute-start(bf16[256,1024]{1,0:T(8,128)(2,1)S(1)} %get-tuple-element.341), channel_id=1, source_target_pairs={{0,24},{8,16},{16,8},{24,0},{1,25},{9,17},{17,9},{25,1},{2,26},{10... | collective-permute-start | bytes 1572872 | tf_op jit(solution)/shard_map/ppermute | solution.py:650
  234.7 8.6 %collective-permute-start.50 = (bf16[4,256,1024]{2,1,0:T(8,128)(2,1)}, bf16[4,256,1024]{2,1,0:T(8,128)(2,1)}, u32[]{:S(2)}, u32[]{:S(2)}) collective-permute-start(bf16[4,256,1024]{2,1,0:T(8,128)(2,1)} %get-tuple-element.367), channel_id=1, source_target_pairs={{0,1},{1,0},{2,3},{3,2},{4,5},{5,4},{6,7},{7,6},{8,9},{9,8},{10,11... | collective-permute-start | bytes 6291464 | tf_op jit(solution)/shard_map/ppermute | solution.py:654
  252.9 29.3 %collective-permute-start.51 = (bf16[256,1024]{1,0:T(8,128)(2,1)}, bf16[256,1024]{1,0:T(8,128)(2,1)}, u32[]{:S(2)}, u32[]{:S(2)}) collective-permute-start(bf16[256,1024]{1,0:T(8,128)(2,1)} %get-tuple-element.379), channel_id=1, source_target_pairs={{0,8},{8,0},{16,24},{24,16},{1,9},{9,1},{17,25},{25,17},{2,10},{10... | collective-permute-start | bytes 1572872 | tf_op jit(solution)/shard_map/ppermute | solution.py:650
  253.4 29.7 %collective-permute-start.52 = (bf16[256,1024]{1,0:T(8,128)(2,1)}, bf16[256,1024]{1,0:T(8,128)(2,1)}, u32[]{:S(2)}, u32[]{:S(2)}) collective-permute-start(bf16[256,1024]{1,0:T(8,128)(2,1)} %get-tuple-element.380), channel_id=1, source_target_pairs={{0,16},{8,24},{16,0},{24,8},{1,17},{9,25},{17,1},{25,9},{2,18},{10... | collective-permute-start | bytes 1572872 | tf_op jit(solution)/shard_map/ppermute | solution.py:650
  254.8 28.2 %collective-permute-start.53 = (bf16[256,1024]{1,0:T(8,128)(2,1)}, bf16[256,1024]{1,0:T(8,128)(2,1)}, u32[]{:S(2)}, u32[]{:S(2)}) collective-permute-start(bf16[256,1024]{1,0:T(8,128)(2,1)} %get-tuple-element.381), channel_id=1, source_target_pairs={{0,24},{8,16},{16,8},{24,0},{1,25},{9,17},{17,9},{25,1},{2,26},{10... | collective-permute-start | bytes 1572872 | tf_op jit(solution)/shard_map/ppermute | solution.py:650
  257.0 25.1 %collective-permute-start.56 = (bf16[2,256,128]{2,1,0:T(8,128)(2,1)}, bf16[2,256,128]{2,1,0:T(8,128)(2,1)}, u32[]{:S(2)}, u32[]{:S(2)}) collective-permute-start(bf16[2,256,128]{2,1,0:T(8,128)(2,1)} %get-tuple-element.385), channel_id=1, source_target_pairs={{0,24},{8,16},{16,8},{24,0},{1,25},{9,17},{17,9},{25,1},{2,26},{10... | collective-permute-start | bytes 393224 | tf_op jit(solution)/shard_map/ppermute | solution.py:650
  258.6 34.6 %collective-permute-start.57 = (bf16[2,256,1024]{2,1,0:T(8,128)(2,1)}, bf16[2,256,1024]{2,1,0:T(8,128)(2,1)S(1)}, u32[]{:S(2)}, u32[]{:S(2)}) collective-permute-start(bf16[2,256,1024]{2,1,0:T(8,128)(2,1)} %pad_maximum_fusion.1), channel_id=1, source_target_pairs={{0,8},{1,17},{8,0},{9,25},{16,24},{17,1},{24,16},{25,9},{2,10},{3,... | collective-permute-start | bytes 3145736 | tf_op jit(solution)/shard_map/ppermute | solution.py:883
  279.5 115.7 %reduce-scatter.6.cloned.1.call-start = ((), (), s32[]{:S(2)}) async-start(), calls=%async_computation.6 | async-start | bytes 2359296 | tf_op jit(solution)/shard_map/reduce_scatter | solution.py:912
  300.0 27.8 %collective-permute-start.59 = (bf16[2,256,1024]{2,1,0:T(8,128)(2,1)S(1)}, bf16[2,256,1024]{2,1,0:T(8,128)(2,1)}, u32[]{:S(2)}, u32[]{:S(2)}) collective-permute-start(bf16[2,256,1024]{2,1,0:T(8,128)(2,1)S(1)} %pad_maximum_fusion.2), channel_id=1, source_target_pairs={{0,8},{8,0},{16,24},{24,16},{1,9},{9,1},{17,25},{25,17},{2,10},{10... | collective-permute-start | bytes 3145736 | tf_op jit(solution)/shard_map/ppermute | solution.py:650
  300.6 27.2 %collective-permute-start.60 = (bf16[2,256,1024]{2,1,0:T(8,128)(2,1)S(1)}, bf16[2,256,1024]{2,1,0:T(8,128)(2,1)}, u32[]{:S(2)}, u32[]{:S(2)}) collective-permute-start(bf16[2,256,1024]{2,1,0:T(8,128)(2,1)S(1)} %pad_maximum_fusion.3), channel_id=1, source_target_pairs={{0,16},{8,24},{16,0},{24,8},{1,17},{9,25},{17,1},{25,9},{2,18},{10... | collective-permute-start | bytes 3145736 | tf_op jit(solution)/shard_map/ppermute | solution.py:650
  333.5 12.5 %collective-permute-start.66 = (bf16[2,256,128]{2,1,0:T(8,128)(2,1)}, bf16[2,256,128]{2,1,0:T(8,128)(2,1)S(1)}, u32[]{:S(2)}, u32[]{:S(2)}) collective-permute-start(bf16[2,256,128]{2,1,0:T(8,128)(2,1)} %get-tuple-element.424), channel_id=1, source_target_pairs={{0,8},{8,0},{16,24},{24,16},{1,9},{9,1},{17,25},{25,17},{2,10},{10... | collective-permute-start | bytes 393224 | tf_op jit(solution)/shard_map/ppermute | solution.py:650
  334.9 11.0 %collective-permute-start.67 = (bf16[2,256,128]{2,1,0:T(8,128)(2,1)}, bf16[2,256,128]{2,1,0:T(8,128)(2,1)S(1)}, u32[]{:S(2)}, u32[]{:S(2)}) collective-permute-start(bf16[2,256,128]{2,1,0:T(8,128)(2,1)} %get-tuple-element.425), channel_id=1, source_target_pairs={{0,16},{8,24},{16,0},{24,8},{1,17},{9,25},{17,1},{25,9},{2,18},{10... | collective-permute-start | bytes 393224 | tf_op jit(solution)/shard_map/ppermute | solution.py:650
  335.4 10.5 %collective-permute-start.68 = (bf16[2,256,128]{2,1,0:T(8,128)(2,1)}, bf16[2,256,128]{2,1,0:T(8,128)(2,1)}, u32[]{:S(2)}, u32[]{:S(2)}) collective-permute-start(bf16[2,256,128]{2,1,0:T(8,128)(2,1)} %get-tuple-element.426), channel_id=1, source_target_pairs={{0,24},{8,16},{16,8},{24,0},{1,25},{9,17},{17,9},{25,1},{2,26},{10... | collective-permute-start | bytes 393224 | tf_op jit(solution)/shard_map/ppermute | solution.py:650
  346.0 71.1 %reduce-scatter.8.cloned.1.call-start = ((), (), s32[]{:S(2)}) async-start(), calls=%async_computation.7 | async-start | bytes 983040 | tf_op jit(solution)/shard_map/reduce_scatter | solution.py:930
  350.1 45.0 %collective-permute-start.63 = (bf16[256,1024]{1,0:T(8,128)(2,1)}, bf16[256,1024]{1,0:T(8,128)(2,1)S(1)}, u32[]{:S(2)}, u32[]{:S(2)}) collective-permute-start(bf16[256,1024]{1,0:T(8,128)(2,1)} %get-tuple-element.429), channel_id=1, source_target_pairs={{0,8},{8,0},{16,24},{24,16},{1,9},{9,1},{17,25},{25,17},{2,10},{10... | collective-permute-start | bytes 1572872 | tf_op jit(solution)/shard_map/ppermute | solution.py:650
  351.4 43.7 %collective-permute-start.64 = (bf16[256,1024]{1,0:T(8,128)(2,1)}, bf16[256,1024]{1,0:T(8,128)(2,1)}, u32[]{:S(2)}, u32[]{:S(2)}) collective-permute-start(bf16[256,1024]{1,0:T(8,128)(2,1)} %get-tuple-element.430), channel_id=1, source_target_pairs={{0,16},{8,24},{16,0},{24,8},{1,17},{9,25},{17,1},{25,9},{2,18},{10... | collective-permute-start | bytes 1572872 | tf_op jit(solution)/shard_map/ppermute | solution.py:650
  351.9 43.2 %collective-permute-start.65 = (bf16[256,1024]{1,0:T(8,128)(2,1)}, bf16[256,1024]{1,0:T(8,128)(2,1)}, u32[]{:S(2)}, u32[]{:S(2)}) collective-permute-start(bf16[256,1024]{1,0:T(8,128)(2,1)} %get-tuple-element.431), channel_id=1, source_target_pairs={{0,24},{8,16},{16,8},{24,0},{1,25},{9,17},{17,9},{25,1},{2,26},{10... | collective-permute-start | bytes 1572872 | tf_op jit(solution)/shard_map/ppermute | solution.py:650
  355.5 39.6 %collective-permute-start.71 = (bf16[384,1024]{1,0:T(8,128)(2,1)}, bf16[384,1024]{1,0:T(8,128)(2,1)}, u32[]{:S(2)}, u32[]{:S(2)}) collective-permute-start(bf16[384,1024]{1,0:T(8,128)(2,1)} %pad_maximum_fusion.5.refs_0_), channel_id=1, source_target_pairs={{0,8},{8,0},{16,24},{24,16},{1,9},{9,1},{17,25},{25,17},{2,10},{10... | collective-permute-start | bytes 2359304 | tf_op jit(solution)/shard_map/ppermute | solution.py:650
  356.9 38.3 %collective-permute-start.72 = (bf16[384,1024]{1,0:T(8,128)(2,1)}, bf16[384,1024]{1,0:T(8,128)(2,1)}, u32[]{:S(2)}, u32[]{:S(2)}) collective-permute-start(bf16[384,1024]{1,0:T(8,128)(2,1)} %pad_maximum_fusion.5.refs_0_), channel_id=1, source_target_pairs={{0,16},{8,24},{16,0},{24,8},{1,17},{9,25},{17,1},{25,9},{2,18},{10... | collective-permute-start | bytes 2359304 | tf_op jit(solution)/shard_map/ppermute | solution.py:650
  397.7 12.3 %collective-permute-start.74 = (bf16[384,1024]{1,0:T(8,128)(2,1)}, bf16[384,1024]{1,0:T(8,128)(2,1)}, u32[]{:S(2)}, u32[]{:S(2)}) collective-permute-start(bf16[384,1024]{1,0:T(8,128)(2,1)} %broadcast_select_fusion.2), channel_id=1, source_target_pairs={{0,8},{1,17},{8,0},{9,25},{16,24},{17,1},{24,16},{25,9},{2,10},{3,... | collective-permute-start | bytes 2359304 | tf_op jit(solution)/shard_map/ppermute | solution.py:676
  410.0 15.2 %collective-permute-start.75 = (bf16[256,1024]{1,0:T(8,128)(2,1)}, bf16[256,1024]{1,0:T(8,128)(2,1)}, u32[]{:S(2)}, u32[]{:S(2)}) collective-permute-start(bf16[256,1024]{1,0:T(8,128)(2,1)} %get-tuple-element.463), channel_id=1, source_target_pairs={{0,8},{8,0},{16,24},{24,16},{1,9},{9,1},{17,25},{25,17},{2,10},{10... | collective-permute-start | bytes 1572872 | tf_op jit(solution)/shard_map/ppermute | solution.py:650
  411.5 24.4 %collective-permute-start.76 = (bf16[256,1024]{1,0:T(8,128)(2,1)}, bf16[256,1024]{1,0:T(8,128)(2,1)}, u32[]{:S(2)}, u32[]{:S(2)}) collective-permute-start(bf16[256,1024]{1,0:T(8,128)(2,1)} %get-tuple-element.464), channel_id=1, source_target_pairs={{0,16},{8,24},{16,0},{24,8},{1,17},{9,25},{17,1},{25,9},{2,18},{10... | collective-permute-start | bytes 1572872 | tf_op jit(solution)/shard_map/ppermute | solution.py:650
  412.2 23.7 %collective-permute-start.77 = (bf16[256,1024]{1,0:T(8,128)(2,1)}, bf16[256,1024]{1,0:T(8,128)(2,1)}, u32[]{:S(2)}, u32[]{:S(2)}) collective-permute-start(bf16[256,1024]{1,0:T(8,128)(2,1)} %get-tuple-element.465), channel_id=1, source_target_pairs={{0,24},{8,16},{16,8},{24,0},{1,25},{9,17},{17,9},{25,1},{2,26},{10... | collective-permute-start | bytes 1572872 | tf_op jit(solution)/shard_map/ppermute | solution.py:650
  419.4 22.5 %collective-permute-start.61 = (bf16[256,1024]{1,0:T(8,128)(2,1)S(1)}, bf16[256,1024]{1,0:T(8,128)(2,1)S(1)}, u32[]{:S(2)}, u32[]{:S(2)}) collective-permute-start(bf16[256,1024]{1,0:T(8,128)(2,1)S(1)} %get-tuple-element.531), channel_id=1, source_target_pairs={{0,1},{1,0},{2,3},{3,2},{4,5},{5,4},{6,7},{7,6},{8,9},{9,8},{10,11... | collective-permute-start | bytes 1572872 | tf_op jit(solution)/shard_map/ppermute | solution.py:654
  441.8 11.9 %collective-permute-start.79 = (f32[256,1024]{1,0:T(8,128)S(1)}, f32[256,1024]{1,0:T(8,128)S(1)}, u32[]{:S(2)}, u32[]{:S(2)}) collective-permute-start(f32[256,1024]{1,0:T(8,128)S(1)} %get-tuple-element.527), channel_id=1, source_target_pairs={{0,1},{1,0},{2,3},{3,2},{4,5},{5,4},{6,7},{7,6},{8,9},{9,8},{10,11... | collective-permute-start | bytes 3145736 | tf_op jit(solution)/shard_map/ppermute | solution.py:654
  443.0 13.6 %collective-permute-start.80 = (bf16[128,1792]{1,0:T(8,128)(2,1)}, bf16[128,1792]{1,0:T(8,128)(2,1)}, u32[]{:S(2)}, u32[]{:S(2)}) collective-permute-start(bf16[128,1792]{1,0:T(8,128)(2,1)} %pad_maximum_fusion.6.refs_0_), channel_id=1, source_target_pairs={{0,8},{8,0},{16,24},{24,16},{1,9},{9,1},{17,25},{25,17},{2,10},{10... | collective-permute-start | bytes 1376264 | tf_op jit(solution)/shard_map/ppermute | solution.py:650
  443.5 21.9 %collective-permute-start.81 = (bf16[128,1792]{1,0:T(8,128)(2,1)}, bf16[128,1792]{1,0:T(8,128)(2,1)}, u32[]{:S(2)}, u32[]{:S(2)}) collective-permute-start(bf16[128,1792]{1,0:T(8,128)(2,1)} %pad_maximum_fusion.6.refs_0_), channel_id=1, source_target_pairs={{0,16},{8,24},{16,0},{24,8},{1,17},{9,25},{17,1},{25,9},{2,18},{10... | collective-permute-start | bytes 1376264 | tf_op jit(solution)/shard_map/ppermute | solution.py:650
  445.0 21.2 %collective-permute-start.82 = (bf16[128,1792]{1,0:T(8,128)(2,1)}, bf16[128,1792]{1,0:T(8,128)(2,1)}, u32[]{:S(2)}, u32[]{:S(2)}) collective-permute-start(bf16[128,1792]{1,0:T(8,128)(2,1)} %pad_maximum_fusion.6.refs_0_), channel_id=1, source_target_pairs={{0,24},{8,16},{16,8},{24,0},{1,25},{9,17},{17,9},{25,1},{2,26},{10... | collective-permute-start | bytes 1376264 | tf_op jit(solution)/shard_map/ppermute | solution.py:650
  (81 other events, 730.2 us)
Sparse Core Ops, SparseCore 0:
  29.0 27.2 all-gather.4
  58.0 28.6 all-gather.6
  106.7 63.8 all-gather.8
  279.6 58.6 reduce-scatter.3
  346.1 35.3 reduce-scatter.5
  395.4 21.6 reduce-scatter.7

commit v5 on v4

--- a/solution.py
+++ b/solution.py
@@ -813,7 +813,7 @@
     if 2 * cols == dim:
         gu_cut = ordered(hidden_pair[0], swap(hidden_pair[1]), core).reshape(2 * shard, dim)
         w_ff = jnp.concatenate([gu_cut, down_cut], axis=0)
-        w_ffs = [lax.all_gather(after(w_ff, w_out_full), "z", axis=0)]
+        w_ffs = [lax.all_gather(w_ff, "z", axis=0)]
     else:
         w_ffs = [over_z(*hidden_pair), lax.all_gather(down_cut, "z", axis=0, tiled=True)]
 
@@ -835,23 +835,22 @@
 
     cot_near = gather_near(cot_own)
     qkv0, *mixed0, lse0 = attend(one, 0, w_qkv, (infos[0], code_rows[0]), n)
-    mixed0, cot_near, info1 = together(mixed0, cot_near, infos[1])
+    mixed0, cot_near, go = together(mixed0, cot_near, me)
     got0 = send_heads(mixed0)
+    other0 = other_heads(got0)
+    att0, hidden0, norm0 = mix(go, got0, other0, x_rows, 0, w_out_full, n)
+    norm0, cot_near, info1 = together(norm0, cot_near, infos[1])
+    near0 = gather_near(norm0)
     cot_all = gather_far(cot_near)
     qkv1, *mixed1, lse1 = attend(one, 1, w_qkv, (info1, code_rows[1]), n)
-    mixed1, got0, cot_all, go = together(mixed1, got0, cot_all, me)
+    mixed1, near0, cot_all, go = together(mixed1, near0, cot_all, me)
+    far0 = gather_far(near0)
     got1 = send_heads(mixed1)
-    other0 = other_heads(got0)
     cots = gather_cores(cot_own, cot_all)
-    att0, hidden0, norm0 = mix(go, got0, other0, x_rows, 0, w_out_full, n)
-    norm0, got1, go = together(norm0, got1, me)
-    near0 = gather_near(norm0)
     other1 = other_heads(got1)
+    two0 = gather_cores(norm0, far0)
     att1, hidden1, norm1 = mix(go, got1, other1, x_rows, 1, w_out_full, n)
-    near0, norm1, cots = together(near0, norm1, cots)
-    far0 = gather_far(near0)
-    two0 = gather_cores(norm0, far0)
-    two0, norm1, go = together(two0, norm1, me)
+    two0, norm1, cots, go = together(two0, norm1, cots, me)
 
     two_got = [send(norm1, r) for r in range(1, n)]
     inner0, d_gu0, d_mine0, d_other0, o_mine0, o_other0 = feed(two0, cots, 0, w_ffs, cols, go, n)
@@ -881,10 +880,10 @@
     if n == 4:
         pairs = [(c * 2 + p, (c ^ (1 + p)) * 2 + p) for c in range(n) for p in range(2)]
         out_far = lax.ppermute(out_far, ("ctx", "core"), pairs)
-    parts1 = plane_send(joined1)
+    parts1, d_last = plane_send(joined1[: n - 1]), joined1[n - 1]
     raw_ff = feed_grads((two0, two1), cots, (inner0, inner1), (d_gu0, d_gu1), go, n, n_z)
     grads_ff = [lax.psum_scatter(g, "z", scatter_dimension=0, tiled=True) for g in raw_ff]
-    parts1, d_got0, raw_ff, out_far = together(parts1, d_got0, raw_ff, out_far)
+    parts1, d_got0, raw_ff, out_far, d_last = together(parts1, d_got0, raw_ff, out_far, d_last)
     d_other_heads0 = other_heads(d_got0)
     if n == 4:
         outs = [out_sum(0)]
@@ -893,13 +892,14 @@
             outs.append(out_sum(r, [far[0], far[1]]))
     else:
         outs = [out_sum(r) for r in range(n - 1)] + [out_far]
-    outs, d_other_heads0, info0 = together(outs, d_other_heads0, infos[0])
-
+    outs, d_other_heads0, info0, d_last = together(outs, d_other_heads0, infos[0], d_last)
+
+    parts1 = parts1 + [send(d_last, n - 1)]
     out_parts = plane_send(outs)
     d_qkv0, a_mine0, a_other0 = attend_back(
         qkv0, w_qkv, lse0, mixed0, d_got0, d_other_heads0, (info0, code_rows[0]), n
     )
-    out_parts, a_mine0, a_other0, go = together(out_parts, a_mine0, a_other0, me)
+    out_parts, parts1, a_mine0, a_other0, go = together(out_parts, parts1, a_mine0, a_other0, me)
     a_got0 = swap(a_other0)
     d_hidden1, e1, *d_mix1 = turn(go, parts1, cot_rows, 1, hidden1, w_out_full, width, n)
     d_mix1, a_mine0, a_got0 = together(d_mix1, a_mine0, a_got0)

time: 484 us -> 475 us (0.981)
  waiting for transfers between devices: 114 us -> 106 us
    ppermute x1, waiting for transfers between devices: 10.2 us -> 3.68 us  [body(): out_far = lax.ppermute(out_far, ('ctx', 'core'), pairs)]
  transfers between devices with their start and end apart: 89 -> 89, of which waited for: 30 -> 29; matrix products, arithmetic and copies ran while one was open for 12% -> 12% of each run, Pallas kernels for 42% -> 43%
where the time goes in v5:
time: 475 us; the launch traced here: 468 us
  Pallas kernels  211 us (44%)
  waiting for transfers between devices  106 us (22%)
  starting transfers between devices  65.2 us (14%)
  other arithmetic  55 us (12%)
  between operations  15.7 us (3%)
  local copies, waits for them, and re-layouts  15 us (3%)
    ppermute x43, waiting for transfers between devices, send(): return lax.ppermute(value, 'ctx', [(i, i ^ step) for i in range(count)])  64 us
    pallas_call x2, Pallas kernels, attend_back(): call(functools.partial(attend_back_kernel, n, heads, half), 'attend_back'...  54.7 us
    ppermute x43, starting transfers between devices, send(): return lax.ppermute(value, 'ctx', [(i, i ^ step) for i in range(count)])  50.4 us
    pallas_call x2, Pallas kernels, attend(): call(functools.partial(attend_kernel, n, heads, half), 'attend', [shape_o...  43.5 us
    pallas_call x2, Pallas kernels, feed(): call(functools.partial(feed_kernel, n, half, cols, which), 'feed', [shape...  40.4 us
    ppermute x4, waiting for transfers between devices, gather_far(): return near + [lax.ppermute(onward, ('ctx', 'core'), pairs)]  25.5 us
    pallas_call x1, Pallas kernels, feed_grads(): call(functools.partial(feed_grads_kernel, n, n_z, half), 'feed_grads', [s...  20.3 us
    convert_element_type x4, other arithmetic, sum_cores(): (mine[r].astype(F32) + got[r].astype(F32)).astype(BF16)  15.4 us
  transfers between devices with their start and end apart: 89, of which 29 were waited for; matrix products, arithmetic and copies ran while one was open for 12% of the time, Pallas kernels for 43%

profile of v5, /device:TPU:0, one launch (start us, length us, event | category | flops | bytes accessed | tf_op | source)
XLA Modules:
  0.0 468.3 jit_solution(17564834815405020848)
XLA Ops:
  12.0 2.7 pack_qkv.1
  14.8 1.5 collective-permute-done.3
  16.3 1.7 maximum_select_fusion.5
  18.0 3.3 pack_hidden.1
  21.3 3.6 collective-permute-start.6
  25.5 2.0 collective-permute-start.1
  27.4 1.5 collective-permute-start.2
  29.2 2.2 dynamic-slice_bitcast_fusion.1
  34.4 2.8 maximum_select_fusion.2.refs_8_.refs_4_.refs_16_
  37.2 13.2 %collective-permute-done.1.refs_1_ = bf16[2,256,1024]{2,1,0:T(8,128)(2,1)S(1)} collective-permute-done((bf16[2,256,1024]{2,1,0:T(8,128)(2,1)S(1)}, bf16[2,256,1024]{2,1,0:T(8,128)(2,1)S(1)}, u32[]{:S(2)}, u32[]{:S(2)}) %collective-permute-start.1) | collective-permute-done | bytes 1048608 | tf_op jit(solution)/shard_map/ppermute | solution.py:650
  50.3 1.5 collective-permute-done.2.refs_2_
  51.8 2.3 broadcast_select_fusion.1
  54.7 1.7 all-gather.5.cloned.1.call-done.refs_8_.refs_1_
  57.2 12.1 %collective-permute-done.9.refs_3_ = bf16[2,256,1024]{2,1,0:T(8,128)(2,1)} collective-permute-done((bf16[2,256,1024]{2,1,0:T(8,128)(2,1)}, bf16[2,256,1024]{2,1,0:T(8,128)(2,1)}, u32[]{:S(2)}, u32[]{:S(2)}) %collective-permute-start.9) | collective-permute-done | bytes 1048608 | tf_op jit(solution)/shard_map/ppermute | solution.py:676
  70.4 2.3 collective-permute-done.39
  74.7 1.5 collective-permute-start.15
  76.2 21.1 %attend.2 = (bf16[2048,384]{1,0:T(8,128)(2,1)}, bf16[2,256,128]{2,1,0:T(8,128)(2,1)}, bf16[2,256,128]{2,1,0:T(8,128)(2,1)}, bf16[2,256,128]{2,1,0:T(8,128)(2,1)}...) custom-call(s32[18]{0:T(128)} %pad_add_fusion.2.info, bf16[2,256,1024]{2,1,0:T(8,128)(2,1)} %copy-done.4, ...), custom_call_target="tpu_custom_call" | custom-call | flops 20999999488 | bytes 1000 | tf_op jit(solution)/shard_map/attend/pallas_call | solution.py:175
  97.3 2.3 collective-permute-done.14.refs_9_.refs_17_
  101.5 1.5 collective-permute-start.17
  105.0 4.1 collective-permute-done.18.refs_3_
  111.7 4.9 %mix.2 = (bf16[256,1024]{1,0:T(8,128)(2,1)}, f32[256,1024]{1,0:T(8,128)}, bf16[256,1024]{1,0:T(8,128)(2,1)}) custom-call(s32[2]{0:T(128)} %pad_add_fusion.1.info, bf16[2,256,128]{2,1,0:T(8,128)(2,1)} %get-tuple-element.271.refs_0_.refs_4_, bf16[2,256,128]{2,1,0:T(8,128)(2,1)} %copy-done.31, bf16[2,256,128]{2,1,0:T(8,128)(2,1)} %copy-done.32, ...), custom_call_target="tpu_custom_call" | custom-call | flops 5000000000 | bytes 1000 | tf_op jit(solution)/shard_map/mix/pallas_call | solution.py:331
  119.2 1.9 collective-permute-start.22
  121.1 22.4 %attend.3 = (bf16[2048,384]{1,0:T(8,128)(2,1)}, bf16[2,256,128]{2,1,0:T(8,128)(2,1)}, bf16[2,256,128]{2,1,0:T(8,128)(2,1)}, bf16[2,256,128]{2,1,0:T(8,128)(2,1)}...) custom-call(s32[18]{0:T(128)} %pad_add_fusion.4.info, bf16[2,256,1024]{2,1,0:T(8,128)(2,1)} %copy-done.4, ...), custom_call_target="tpu_custom_call" | custom-call | flops 20999999488 | bytes 1000 | tf_op jit(solution)/shard_map/attend/pallas_call | solution.py:175
  145.3 1.8 collective-permute-start.23
  147.9 3.1 collective-permute-done.25.refs_3_
  155.0 7.6 %collective-permute-done.27.refs_3_ = bf16[256,1024]{1,0:T(8,128)(2,1)} collective-permute-done((bf16[256,1024]{1,0:T(8,128)(2,1)S(1)}, bf16[256,1024]{1,0:T(8,128)(2,1)}, u32[]{:S(2)}, u32[]{:S(2)}) %collective-permute-start.27) | collective-permute-done | bytes 524320 | tf_op jit(solution)/shard_map/ppermute | solution.py:676
  163.1 4.6 mix.3
  171.3 20.1 %feed.2 = (bf16[2048,512]{1,0:T(8,128)(2,1)}, bf16[2048,1024]{1,0:T(8,128)(2,1)}, bf16[4,256,1024]{2,1,0:T(8,128)(2,1)}, bf16[4,256,1024]{2,1,0:T(8,128)(2,1)}, ...) custom-call(s32[2]{0:T(128)} %pad_add_fusion.1.info, bf16[256,1024]{1,0:T(8,128)(2,1)} %get-tuple-element.303.refs_0_, ...), custom_call_target="tpu_custom_call" | custom-call | flops 20000000000 | bytes 1000 | tf_op jit(solution)/shard_map/feed/pallas_call | solution.py:403
  191.4 2.5 collective-permute-done.37.refs_2_.refs_10_
  195.0 3.3 collective-permute-done.40
  198.4 3.5 fusion.31
  204.1 1.5 collective-permute-start.47
  205.7 20.3 %feed.3 = (bf16[2048,512]{1,0:T(8,128)(2,1)}, bf16[2048,1024]{1,0:T(8,128)(2,1)}, bf16[4,256,1024]{2,1,0:T(8,128)(2,1)}, bf16[4,256,1024]{2,1,0:T(8,128)(2,1)}, ...) custom-call(s32[2]{0:T(128)} %pad_add_fusion.1.info, bf16[256,1024]{1,0:T(8,128)(2,1)} %get-tuple-element.332.refs_0_.refs_8_, ...), custom_call_target="tpu_custom_call" | custom-call | flops 20000000000 | bytes 1000 | tf_op jit(solution)/shard_map/feed/pallas_call | solution.py:403
  226.1 2.5 collective-permute-done.47.refs_3_
  228.6 5.7 %turn.2 = (f32[256,1024]{1,0:T(8,128)}, bf16[256,1024]{1,0:T(8,128)(2,1)}, bf16[2,256,128]{2,1,0:T(8,128)(2,1)}, bf16[2,256,128]{2,1,0:T(8,128)(2,1)}, bf16[2,25...) custom-call(s32[2]{0:T(128)} %pad_add_fusion.1.info, bf16[256,1024]{1,0:T(8,128)(2,1)} %get-tuple-element.345.refs_0_, ...), custom_call_target="tpu_custom_call" | custom-call | flops 6000000000 | bytes 1000 | tf_op jit(solution)/shard_map/turn/pallas_call | solution.py:521
  234.3 3.5 fusion.35
  245.8 1.5 collective-permute-start.55
  248.8 20.3 %feed_grads.1 = bf16[4,384,1024]{2,1,0:T(8,128)(2,1)} custom-call(s32[2]{0:T(128)} %pad_add_fusion.1.info, bf16[256,1024]{1,0:T(8,128)(2,1)} %get-tuple-element.303.refs_0_, bf16[256,1024]{1,0:T(8,128)(2,1)} %collective-permute-done.20.refs_1_, bf16[256,1024]{1,0:T(8,128)(2,1)} %collective-permute-done.21.refs_2_, ...), custom_call_target="tpu_custom_call" | custom-call | flops 20000000000 | bytes 1000 | tf_op jit(solution)/shard_map/feed_grads/pallas_call | solution.py:479
  269.3 3.7 collective-permute-done.56
  273.9 1.5 collective-permute-start.57
  276.7 3.2 fusion.24
  282.2 1.5 collective-permute-start.60
  283.8 26.5 %attend_back.2 = (bf16[2048,384]{1,0:T(8,128)(2,1)}, bf16[4,256,1024]{2,1,0:T(8,128)(2,1)}, bf16[4,256,1024]{2,1,0:T(8,128)(2,1)}) custom-call(s32[18]{0:T(128)} %pad_add_fusion.2.info, bf16[2048,384]{1,0:T(8,128)(2,1)} %get-tuple-element.395.refs_0_, bf16[1024,512]{1,0:T(8,128)(2,1)} %all-gather.5.cloned.1.call-done.refs_8_.refs_1_, ...), custom_call_target="tpu_custom_call" | custom-call | flops 25999998976 | bytes 1000 | tf_op jit(solution)/shard_map/attend_back/pallas_call | solution.py:277
  310.3 6.8 %collective-permute-done.60.refs_3_ = bf16[256,1024]{1,0:T(8,128)(2,1)} collective-permute-done((bf16[256,1024]{1,0:T(8,128)(2,1)}, bf16[256,1024]{1,0:T(8,128)(2,1)}, u32[]{:S(2)}, u32[]{:S(2)}) %collective-permute-start.60) | collective-permute-done | bytes 524320 | tf_op jit(solution)/shard_map/ppermute | solution.py:650
  318.3 5.5 %turn.3 = (f32[256,1024]{1,0:T(8,128)}, bf16[256,1024]{1,0:T(8,128)(2,1)}, bf16[2,256,128]{2,1,0:T(8,128)(2,1)}, bf16[2,256,128]{2,1,0:T(8,128)(2,1)}, bf16[2,25...) custom-call(s32[2]{0:T(128)} %pad_add_fusion.1.info, bf16[256,1024]{1,0:T(8,128)(2,1)} %get-tuple-element.405.refs_0_, ...), custom_call_target="tpu_custom_call" | custom-call | flops 6000000000 | bytes 1000 | tf_op jit(solution)/shard_map/turn/pallas_call | solution.py:521
  323.9 1.5 collective-permute-start.66
  327.4 4.1 fusion.39
  331.5 4.8 %out_grads.1 = bf16[1024,1024]{1,0:T(8,128)(2,1)} custom-call(s32[2]{0:T(128)} %pad_add_fusion.1.info, bf16[256,1024]{1,0:T(8,128)(2,1)} %get-tuple-element.427.att0, bf16[256,1024]{1,0:T(8,128)(2,1)} %get-tuple-element.428.att1, bf16[256,1024]{1,0:T(8,128)(2,1)} %get-tuple-element.429.e0, bf16[256,1024]{1,0:T(8,128)(2,1)} %get-tuple-element.430.e1), custom_call_target="tpu_custom_call" | custom-call | flops 5000000000 | bytes 1000 | tf_op jit(solution)/shard_map/out_grads/pallas_call | solution.py:541
  337.4 1.5 collective-permute-done.69.refs_12_
  347.8 28.3 %attend_back.3 = (bf16[2048,384]{1,0:T(8,128)(2,1)}, bf16[4,256,1024]{2,1,0:T(8,128)(2,1)}, bf16[4,256,1024]{2,1,0:T(8,128)(2,1)}) custom-call(s32[18]{0:T(128)} %pad_add_fusion.4.info, bf16[2048,384]{1,0:T(8,128)(2,1)} %get-tuple-element.438.refs_0_, bf16[1024,512]{1,0:T(8,128)(2,1)} %all-gather.5.cloned.1.call-done.refs_8_.refs_1_, ...), custom_call_target="tpu_custom_call" | custom-call | flops 25999998976 | bytes 1000 | tf_op jit(solution)/shard_map/attend_back/pallas_call | solution.py:277
  376.1 9.5 %qkv_grads.1 = bf16[1024,384]{1,0:T(8,128)(2,1)} custom-call(s32[2]{0:T(128)} %pad_add_fusion.1.info, bf16[2,256,1024]{2,1,0:T(8,128)(2,1)} %copy-done.4, bf16[2,256,1024]{2,1,0:T(8,128)(2,1)} %copy-done.5, bf16[2,256,1024]{2,1,0:T(8,128)(2,1)} %collective-permute-done.2.refs_2_, bf16[2,256,1024]{2,1,0:T(8,128)(2,1)} %collective-permute-done.9.refs_3_, ...), custom_call_target="tpu_custom_call" | custom-call | flops 200000000 | bytes 1000 | tf_op jit(solution)/shard_map/qkv_grads/pallas_call | solution.py:564
  385.8 2.4 broadcast_select_fusion.2
  390.3 4.3 fusion.43
  394.6 5.9 %collective-permute-done.74.refs_3_ = bf16[384,1024]{1,0:T(8,128)(2,1)} collective-permute-done((bf16[384,1024]{1,0:T(8,128)(2,1)}, bf16[384,1024]{1,0:T(8,128)(2,1)}, u32[]{:S(2)}, u32[]{:S(2)}) %collective-permute-start.74) | collective-permute-done | bytes 786464 | tf_op jit(solution)/shard_map/ppermute | solution.py:676
  404.0 3.3 fusion.4
  407.4 1.5 reduce-scatter.8.cloned.1.call-done
  412.5 3.2 collective-permute-done.75
  415.7 10.7 %collective-permute-done.76 = bf16[256,1024]{1,0:T(8,128)(2,1)} collective-permute-done((bf16[256,1024]{1,0:T(8,128)(2,1)}, bf16[256,1024]{1,0:T(8,128)(2,1)}, u32[]{:S(2)}, u32[]{:S(2)}) %collective-permute-start.76) | collective-permute-done | bytes 524320 | tf_op jit(solution)/shard_map/ppermute | solution.py:650
  426.4 2.7 fusion.9
  429.1 2.6 fusion.13
  436.9 7.2 %finish.1 = (f32[128,4096]{1,0:T(8,128)}, f32[128,4096]{1,0:T(8,128)}, f32[512,1024]{1,0:T(8,128)}, f32[1,128]{1,0:T(1,128)}) custom-call(s32[2]{0:T(128)} %pad_add_fusion.1.info, bf16[384,1024]{1,0:T(8,128)(2,1)} %pad_maximum_fusion.5.refs_0_, bf16[384,1024]{1,0:T(8,128)(2,1)} %collective-permute-done.71.refs_1_, ...), custom_call_target="tpu_custom_call" | custom-call | flops 7000000000 | bytes 1000 | tf_op jit(solution)/shard_map/finish/pallas_call | solution.py:961
  444.1 1.5 maximum_select_fusion
  447.1 9.8 %collective-permute-done.81.refs_2_ = bf16[128,1792]{1,0:T(8,128)(2,1)} collective-permute-done((bf16[128,1792]{1,0:T(8,128)(2,1)}, bf16[128,1792]{1,0:T(8,128)(2,1)}, u32[]{:S(2)}, u32[]{:S(2)}) %collective-permute-start.81) | collective-permute-done | bytes 458784 | tf_op jit(solution)/shard_map/ppermute | solution.py:650
  456.9 4.2 finish_qkv.1
  (328 shorter events, 78.9 us)
Async XLA Ops:
  7.2 49.2 %all-gather.5.cloned.1.call-start = ((), (), s32[]{:S(2)}) async-start(), calls=%async_computation.3 | async-start | bytes 1310720 | tf_op jit(solution)/shard_map/all_gather | solution.py:798
  21.3 7.7 %collective-permute-start.6 = (s32[512]{0:T(512)S(1)}, s32[512]{0:T(512)S(1)}, u32[]{:S(2)}, u32[]{:S(2)}) collective-permute-start(s32[512]{0:T(512)S(1)} %bitcast.129), channel_id=1, source_target_pairs={{0,24},{8,16},{16,8},{24,0},{1,25},{9,17},{17,9},{25,1},{2,26},{10... | collective-permute-start | bytes 6152 | tf_op jit(solution)/shard_map/ppermute | solution.py:650
  25.5 24.9 %collective-permute-start.1 = (bf16[2,256,1024]{2,1,0:T(8,128)(2,1)S(1)}, bf16[2,256,1024]{2,1,0:T(8,128)(2,1)S(1)}, u32[]{:S(2)}, u32[]{:S(2)}) collective-permute-start(bf16[2,256,1024]{2,1,0:T(8,128)(2,1)S(1)} %fusion.1.refs_0_), channel_id=1, source_target_pairs={{0,8},{8,0},{16,24},{24,16},{1,9},{9,1},{17,25},{25,17},{2,10},{10... | collective-permute-start | bytes 3145736 | tf_op jit(solution)/shard_map/ppermute | solution.py:650
  27.4 24.4 %collective-permute-start.2 = (bf16[2,256,1024]{2,1,0:T(8,128)(2,1)S(1)}, bf16[2,256,1024]{2,1,0:T(8,128)(2,1)}, u32[]{:S(2)}, u32[]{:S(2)}) collective-permute-start(bf16[2,256,1024]{2,1,0:T(8,128)(2,1)S(1)} %fusion.1.refs_0_), channel_id=1, source_target_pairs={{0,16},{8,24},{16,0},{24,8},{1,17},{9,25},{17,1},{25,9},{2,18},{10... | collective-permute-start | bytes 3145736 | tf_op jit(solution)/shard_map/ppermute | solution.py:650
  29.0 82.0 %all-gather.7.cloned.1.call-start = ((), (), s32[]{:S(2)}) async-start(), calls=%async_computation.4 | async-start | bytes 2359296 | tf_op jit(solution)/shard_map/all_gather | solution.py:810
  54.1 15.1 %collective-permute-start.9 = (bf16[2,256,1024]{2,1,0:T(8,128)(2,1)}, bf16[2,256,1024]{2,1,0:T(8,128)(2,1)}, u32[]{:S(2)}, u32[]{:S(2)}) collective-permute-start(bf16[2,256,1024]{2,1,0:T(8,128)(2,1)} %broadcast_select_fusion.1), channel_id=1, source_target_pairs={{0,8},{1,17},{8,0},{9,25},{16,24},{17,1},{24,16},{25,9},{2,10},{3,... | collective-permute-start | bytes 3145736 | tf_op jit(solution)/shard_map/ppermute | solution.py:676
  56.5 114.8 %all-gather.9.cloned.1.call-start = ((), (), s32[]{:S(2)}) async-start(), calls=%async_computation.8 | async-start | bytes 3932160 | tf_op jit(solution)/shard_map/all_gather | solution.py:816
  56.5 17.6 %collective-permute-start.10 = (bf16[2,256,1024]{2,1,0:T(8,128)(2,1)S(1)}, bf16[2,256,1024]{2,1,0:T(8,128)(2,1)}, u32[]{:S(2)}, u32[]{:S(2)}) collective-permute-start(bf16[2,256,1024]{2,1,0:T(8,128)(2,1)S(1)} %fusion.1.refs_0_), channel_id=1, source_target_pairs={{0,1},{1,0},{2,3},{3,2},{4,5},{5,4},{6,7},{7,6},{8,9},{9,8},{10,11... | collective-permute-start | bytes 3145736 | tf_op jit(solution)/shard_map/ppermute | solution.py:654
  56.6 17.5 %collective-permute-start.11 = (bf16[2,256,1024]{2,1,0:T(8,128)(2,1)S(1)}, bf16[2,256,1024]{2,1,0:T(8,128)(2,1)}, u32[]{:S(2)}, u32[]{:S(2)}) collective-permute-start(bf16[2,256,1024]{2,1,0:T(8,128)(2,1)S(1)} %collective-permute-done.1.refs_1_), channel_id=1, source_target_pairs={{0,1},{1,0},{2,3},{3,2},{4,5},{5,4},{6,7},{7,6},{8,9},{9,8},{10,11... | collective-permute-start | bytes 3145736 | tf_op jit(solution)/shard_map/ppermute | solution.py:654
  57.1 17.0 %collective-permute-start.12 = (bf16[2,256,1024]{2,1,0:T(8,128)(2,1)}, bf16[2,256,1024]{2,1,0:T(8,128)(2,1)}, u32[]{:S(2)}, u32[]{:S(2)}) collective-permute-start(bf16[2,256,1024]{2,1,0:T(8,128)(2,1)} %collective-permute-done.2.refs_2_), channel_id=1, source_target_pairs={{0,1},{1,0},{2,3},{3,2},{4,5},{5,4},{6,7},{7,6},{8,9},{9,8},{10,11... | collective-permute-start | bytes 3145736 | tf_op jit(solution)/shard_map/ppermute | solution.py:654
  74.1 25.5 %collective-permute-start.14 = (bf16[2,256,1024]{2,1,0:T(8,128)(2,1)}, bf16[2,256,1024]{2,1,0:T(8,128)(2,1)S(1)}, u32[]{:S(2)}, u32[]{:S(2)}) collective-permute-start(bf16[2,256,1024]{2,1,0:T(8,128)(2,1)} %maximum_select_fusion.2.refs_8_.refs_4_.refs_16_), channel_id=1, source_target_pairs={{0,8},{8,0},{16,24},{24,16},{1,9},{9,1},{17,25},{25,17},{2,10},{10... | collective-permute-start | bytes 3145736 | tf_op jit(solution)/shard_map/ppermute | solution.py:650
  74.7 25.2 %collective-permute-start.15 = (bf16[2,256,1024]{2,1,0:T(8,128)(2,1)}, bf16[2,256,1024]{2,1,0:T(8,128)(2,1)}, u32[]{:S(2)}, u32[]{:S(2)}) collective-permute-start(bf16[2,256,1024]{2,1,0:T(8,128)(2,1)} %maximum_select_fusion.2.refs_8_.refs_4_.refs_16_), channel_id=1, source_target_pairs={{0,16},{8,24},{16,0},{24,8},{1,17},{9,25},{17,1},{25,9},{2,18},{10... | collective-permute-start | bytes 3145736 | tf_op jit(solution)/shard_map/ppermute | solution.py:650
  100.0 9.4 %collective-permute-start.16 = (bf16[2,256,128]{2,1,0:T(8,128)(2,1)}, bf16[2,256,128]{2,1,0:T(8,128)(2,1)S(1)}, u32[]{:S(2)}, u32[]{:S(2)}) collective-permute-start(bf16[2,256,128]{2,1,0:T(8,128)(2,1)} %get-tuple-element.272.refs_5_), channel_id=1, source_target_pairs={{0,8},{8,0},{16,24},{24,16},{1,9},{9,1},{17,25},{25,17},{2,10},{10... | collective-permute-start | bytes 393224 | tf_op jit(solution)/shard_map/ppermute | solution.py:650
  101.5 7.9 %collective-permute-start.17 = (bf16[2,256,128]{2,1,0:T(8,128)(2,1)}, bf16[2,256,128]{2,1,0:T(8,128)(2,1)S(1)}, u32[]{:S(2)}, u32[]{:S(2)}) collective-permute-start(bf16[2,256,128]{2,1,0:T(8,128)(2,1)} %get-tuple-element.273.refs_6_), channel_id=1, source_target_pairs={{0,16},{8,24},{16,0},{24,8},{1,17},{9,25},{17,1},{25,9},{2,18},{10... | collective-permute-start | bytes 393224 | tf_op jit(solution)/shard_map/ppermute | solution.py:650
  104.4 234.5 %reduce-scatter.4.cloned.1.call-start = ((), (), s32[]{:S(2)}) async-start(), calls=%async_computation.5 | async-start | bytes 3932160 | tf_op jit(solution)/shard_map/reduce_scatter | solution.py:885
  110.1 44.1 %collective-permute-start.32 = (bf16[2,256,1024]{2,1,0:T(8,128)(2,1)S(1)}, bf16[2,256,1024]{2,1,0:T(8,128)(2,1)}, u32[]{:S(2)}, u32[]{:S(2)}) collective-permute-start(bf16[2,256,1024]{2,1,0:T(8,128)(2,1)S(1)} %copy-done.16), channel_id=1, source_target_pairs={{0,1},{1,0},{2,3},{3,2},{4,5},{5,4},{6,7},{7,6},{8,9},{9,8},{10,11... | collective-permute-start | bytes 3145736 | tf_op jit(solution)/shard_map/ppermute | solution.py:654
  116.6 26.9 %collective-permute-start.20 = (bf16[256,1024]{1,0:T(8,128)(2,1)}, bf16[256,1024]{1,0:T(8,128)(2,1)}, u32[]{:S(2)}, u32[]{:S(2)}) collective-permute-start(bf16[256,1024]{1,0:T(8,128)(2,1)} %get-tuple-element.303.refs_0_), channel_id=1, source_target_pairs={{0,8},{8,0},{16,24},{24,16},{1,9},{9,1},{17,25},{25,17},{2,10},{10... | collective-permute-start | bytes 1572872 | tf_op jit(solution)/shard_map/ppermute | solution.py:650
  117.2 26.3 %collective-permute-start.21 = (bf16[256,1024]{1,0:T(8,128)(2,1)}, bf16[256,1024]{1,0:T(8,128)(2,1)}, u32[]{:S(2)}, u32[]{:S(2)}) collective-permute-start(bf16[256,1024]{1,0:T(8,128)(2,1)} %get-tuple-element.303.refs_0_), channel_id=1, source_target_pairs={{0,16},{8,24},{16,0},{24,8},{1,17},{9,25},{17,1},{25,9},{2,18},{10... | collective-permute-start | bytes 1572872 | tf_op jit(solution)/shard_map/ppermute | solution.py:650
  117.9 36.6 %collective-permute-start.28 = (bf16[256,1024]{1,0:T(8,128)(2,1)}, bf16[256,1024]{1,0:T(8,128)(2,1)}, u32[]{:S(2)}, u32[]{:S(2)}) collective-permute-start(bf16[256,1024]{1,0:T(8,128)(2,1)} %get-tuple-element.303.refs_0_), channel_id=1, source_target_pairs={{0,1},{1,0},{2,3},{3,2},{4,5},{5,4},{6,7},{7,6},{8,9},{9,8},{10,11... | collective-permute-start | bytes 1572872 | tf_op jit(solution)/shard_map/ppermute | solution.py:654
  119.2 24.3 %collective-permute-start.22 = (bf16[2,256,1024]{2,1,0:T(8,128)(2,1)S(1)}, bf16[2,256,1024]{2,1,0:T(8,128)(2,1)}, u32[]{:S(2)}, u32[]{:S(2)}) collective-permute-start(bf16[2,256,1024]{2,1,0:T(8,128)(2,1)S(1)} %broadcast_select_fusion), channel_id=1, source_target_pairs={{0,8},{1,17},{8,0},{9,25},{16,24},{17,1},{24,16},{25,9},{2,10},{3,... | collective-permute-start | bytes 3145736 | tf_op jit(solution)/shard_map/ppermute | solution.py:676
  143.5 7.5 %collective-permute-start.25 = (bf16[2,256,128]{2,1,0:T(8,128)(2,1)}, bf16[2,256,128]{2,1,0:T(8,128)(2,1)S(1)}, u32[]{:S(2)}, u32[]{:S(2)}) collective-permute-start(bf16[2,256,128]{2,1,0:T(8,128)(2,1)} %get-tuple-element.293.refs_7_), channel_id=1, source_target_pairs={{0,24},{8,16},{16,8},{24,0},{1,25},{9,17},{17,9},{25,1},{2,26},{10... | collective-permute-start | bytes 393224 | tf_op jit(solution)/shard_map/ppermute | solution.py:650
  151.1 11.5 %collective-permute-start.29 = (bf16[256,1024]{1,0:T(8,128)(2,1)}, bf16[256,1024]{1,0:T(8,128)(2,1)}, u32[]{:S(2)}, u32[]{:S(2)}) collective-permute-start(bf16[256,1024]{1,0:T(8,128)(2,1)} %collective-permute-done.20.refs_1_), channel_id=1, source_target_pairs={{0,1},{1,0},{2,3},{3,2},{4,5},{5,4},{6,7},{7,6},{8,9},{9,8},{10,11... | collective-permute-start | bytes 1572872 | tf_op jit(solution)/shard_map/ppermute | solution.py:654
  153.2 9.4 %collective-permute-start.27 = (bf16[256,1024]{1,0:T(8,128)(2,1)S(1)}, bf16[256,1024]{1,0:T(8,128)(2,1)}, u32[]{:S(2)}, u32[]{:S(2)}) collective-permute-start(bf16[256,1024]{1,0:T(8,128)(2,1)S(1)} %broadcast_select_fusion.3), channel_id=1, source_target_pairs={{0,8},{1,17},{8,0},{9,25},{16,24},{17,1},{24,16},{25,9},{2,10},{3,... | collective-permute-start | bytes 1572872 | tf_op jit(solution)/shard_map/ppermute | solution.py:676
  154.2 13.5 %collective-permute-start.33 = (bf16[2,256,1024]{2,1,0:T(8,128)(2,1)S(1)}, bf16[2,256,1024]{2,1,0:T(8,128)(2,1)S(1)}, u32[]{:S(2)}, u32[]{:S(2)}) collective-permute-start(bf16[2,256,1024]{2,1,0:T(8,128)(2,1)S(1)} %collective-permute-done.14.refs_9_.refs_17_), channel_id=1, source_target_pairs={{0,1},{1,0},{2,3},{3,2},{4,5},{5,4},{6,7},{7,6},{8,9},{9,8},{10,11... | collective-permute-start | bytes 3145736 | tf_op jit(solution)/shard_map/ppermute | solution.py:654
  154.4 13.2 %collective-permute-start.34 = (bf16[2,256,1024]{2,1,0:T(8,128)(2,1)}, bf16[2,256,1024]{2,1,0:T(8,128)(2,1)}, u32[]{:S(2)}, u32[]{:S(2)}) collective-permute-start(bf16[2,256,1024]{2,1,0:T(8,128)(2,1)} %collective-permute-done.15.refs_10_.refs_18_), channel_id=1, source_target_pairs={{0,1},{1,0},{2,3},{3,2},{4,5},{5,4},{6,7},{7,6},{8,9},{9,8},{10,11... | collective-permute-start | bytes 3145736 | tf_op jit(solution)/shard_map/ppermute | solution.py:654
  154.7 13.0 %collective-permute-start.35 = (bf16[2,256,1024]{2,1,0:T(8,128)(2,1)}, bf16[2,256,1024]{2,1,0:T(8,128)(2,1)}, u32[]{:S(2)}, u32[]{:S(2)}) collective-permute-start(bf16[2,256,1024]{2,1,0:T(8,128)(2,1)} %collective-permute-done.22.refs_11_.refs_19_), channel_id=1, source_target_pairs={{0,1},{1,0},{2,3},{3,2},{4,5},{5,4},{6,7},{7,6},{8,9},{9,8},{10,11... | collective-permute-start | bytes 3145736 | tf_op jit(solution)/shard_map/ppermute | solution.py:654
  167.7 23.6 %collective-permute-start.36 = (bf16[256,1024]{1,0:T(8,128)(2,1)}, bf16[256,1024]{1,0:T(8,128)(2,1)}, u32[]{:S(2)}, u32[]{:S(2)}) collective-permute-start(bf16[256,1024]{1,0:T(8,128)(2,1)} %get-tuple-element.332.refs_0_.refs_8_), channel_id=1, source_target_pairs={{0,8},{8,0},{16,24},{24,16},{1,9},{9,1},{17,25},{25,17},{2,10},{10... | collective-permute-start | bytes 1572872 | tf_op jit(solution)/shard_map/ppermute | solution.py:650
  168.8 25.2 %collective-permute-start.37 = (bf16[256,1024]{1,0:T(8,128)(2,1)}, bf16[256,1024]{1,0:T(8,128)(2,1)}, u32[]{:S(2)}, u32[]{:S(2)}) collective-permute-start(bf16[256,1024]{1,0:T(8,128)(2,1)} %get-tuple-element.332.refs_0_.refs_8_), channel_id=1, source_target_pairs={{0,16},{8,24},{16,0},{24,8},{1,17},{9,25},{17,1},{25,9},{2,18},{10... | collective-permute-start | bytes 1572872 | tf_op jit(solution)/shard_map/ppermute | solution.py:650
  170.1 23.8 %collective-permute-start.38 = (bf16[256,1024]{1,0:T(8,128)(2,1)}, bf16[256,1024]{1,0:T(8,128)(2,1)}, u32[]{:S(2)}, u32[]{:S(2)}) collective-permute-start(bf16[256,1024]{1,0:T(8,128)(2,1)} %get-tuple-element.332.refs_0_.refs_8_), channel_id=1, source_target_pairs={{0,24},{8,16},{16,8},{24,0},{1,25},{9,17},{17,9},{25,1},{2,26},{10... | collective-permute-start | bytes 1572872 | tf_op jit(solution)/shard_map/ppermute | solution.py:650
  193.9 8.0 %collective-permute-start.41 = (bf16[256,1024]{1,0:T(8,128)(2,1)}, bf16[256,1024]{1,0:T(8,128)(2,1)S(1)}, u32[]{:S(2)}, u32[]{:S(2)}) collective-permute-start(bf16[256,1024]{1,0:T(8,128)(2,1)} %get-tuple-element.332.refs_0_.refs_8_), channel_id=1, source_target_pairs={{0,1},{1,0},{2,3},{3,2},{4,5},{5,4},{6,7},{7,6},{8,9},{9,8},{10,11... | collective-permute-start | bytes 1572872 | tf_op jit(solution)/shard_map/ppermute | solution.py:654
  194.5 7.5 %collective-permute-start.42 = (bf16[256,1024]{1,0:T(8,128)(2,1)}, bf16[256,1024]{1,0:T(8,128)(2,1)S(1)}, u32[]{:S(2)}, u32[]{:S(2)}) collective-permute-start(bf16[256,1024]{1,0:T(8,128)(2,1)} %collective-permute-done.36.refs_1_.refs_9_), channel_id=1, source_target_pairs={{0,1},{1,0},{2,3},{3,2},{4,5},{5,4},{6,7},{7,6},{8,9},{9,8},{10,11... | collective-permute-start | bytes 1572872 | tf_op jit(solution)/shard_map/ppermute | solution.py:654
  194.5 7.5 %collective-permute-start.43 = (bf16[256,1024]{1,0:T(8,128)(2,1)}, bf16[256,1024]{1,0:T(8,128)(2,1)S(1)}, u32[]{:S(2)}, u32[]{:S(2)}) collective-permute-start(bf16[256,1024]{1,0:T(8,128)(2,1)} %collective-permute-done.37.refs_2_.refs_10_), channel_id=1, source_target_pairs={{0,1},{1,0},{2,3},{3,2},{4,5},{5,4},{6,7},{7,6},{8,9},{9,8},{10,11... | collective-permute-start | bytes 1572872 | tf_op jit(solution)/shard_map/ppermute | solution.py:654
  198.3 27.7 %collective-permute-start.48 = (bf16[4,256,1024]{2,1,0:T(8,128)(2,1)}, bf16[4,256,1024]{2,1,0:T(8,128)(2,1)S(1)}, u32[]{:S(2)}, u32[]{:S(2)}) collective-permute-start(bf16[4,256,1024]{2,1,0:T(8,128)(2,1)} %get-tuple-element.342), channel_id=1, source_target_pairs={{0,1},{1,0},{2,3},{3,2},{4,5},{5,4},{6,7},{7,6},{8,9},{9,8},{10,11... | collective-permute-start | bytes 6291464 | tf_op jit(solution)/shard_map/ppermute | solution.py:654
  202.0 24.0 %collective-permute-start.45 = (bf16[256,1024]{1,0:T(8,128)(2,1)}, bf16[256,1024]{1,0:T(8,128)(2,1)}, u32[]{:S(2)}, u32[]{:S(2)}) collective-permute-start(bf16[256,1024]{1,0:T(8,128)(2,1)} %get-tuple-element.328), channel_id=1, source_target_pairs={{0,8},{8,0},{16,24},{24,16},{1,9},{9,1},{17,25},{25,17},{2,10},{10... | collective-permute-start | bytes 1572872 | tf_op jit(solution)/shard_map/ppermute | solution.py:650
  203.1 22.9 %collective-permute-start.46 = (bf16[256,1024]{1,0:T(8,128)(2,1)S(1)}, bf16[256,1024]{1,0:T(8,128)(2,1)}, u32[]{:S(2)}, u32[]{:S(2)}) collective-permute-start(bf16[256,1024]{1,0:T(8,128)(2,1)S(1)} %get-tuple-element.329), channel_id=1, source_target_pairs={{0,16},{8,24},{16,0},{24,8},{1,17},{9,25},{17,1},{25,9},{2,18},{10... | collective-permute-start | bytes 1572872 | tf_op jit(solution)/shard_map/ppermute | solution.py:650
  204.1 24.4 %collective-permute-start.47 = (bf16[256,1024]{1,0:T(8,128)(2,1)S(1)}, bf16[256,1024]{1,0:T(8,128)(2,1)}, u32[]{:S(2)}, u32[]{:S(2)}) collective-permute-start(bf16[256,1024]{1,0:T(8,128)(2,1)S(1)} %get-tuple-element.330), channel_id=1, source_target_pairs={{0,24},{8,16},{16,8},{24,0},{1,25},{9,17},{17,9},{25,1},{2,26},{10... | collective-permute-start | bytes 1572872 | tf_op jit(solution)/shard_map/ppermute | solution.py:650
  225.9 8.3 %collective-permute-start.50 = (bf16[4,256,1024]{2,1,0:T(8,128)(2,1)}, bf16[4,256,1024]{2,1,0:T(8,128)(2,1)}, u32[]{:S(2)}, u32[]{:S(2)}) collective-permute-start(bf16[4,256,1024]{2,1,0:T(8,128)(2,1)} %get-tuple-element.356), channel_id=1, source_target_pairs={{0,1},{1,0},{2,3},{3,2},{4,5},{5,4},{6,7},{7,6},{8,9},{9,8},{10,11... | collective-permute-start | bytes 6291464 | tf_op jit(solution)/shard_map/ppermute | solution.py:654
  242.5 26.8 %collective-permute-start.51 = (bf16[256,1024]{1,0:T(8,128)(2,1)}, bf16[256,1024]{1,0:T(8,128)(2,1)}, u32[]{:S(2)}, u32[]{:S(2)}) collective-permute-start(bf16[256,1024]{1,0:T(8,128)(2,1)} %get-tuple-element.368), channel_id=1, source_target_pairs={{0,8},{8,0},{16,24},{24,16},{1,9},{9,1},{17,25},{25,17},{2,10},{10... | collective-permute-start | bytes 1572872 | tf_op jit(solution)/shard_map/ppermute | solution.py:650
  243.7 25.5 %collective-permute-start.52 = (bf16[256,1024]{1,0:T(8,128)(2,1)}, bf16[256,1024]{1,0:T(8,128)(2,1)}, u32[]{:S(2)}, u32[]{:S(2)}) collective-permute-start(bf16[256,1024]{1,0:T(8,128)(2,1)} %get-tuple-element.369), channel_id=1, source_target_pairs={{0,16},{8,24},{16,0},{24,8},{1,17},{9,25},{17,1},{25,9},{2,18},{10... | collective-permute-start | bytes 1572872 | tf_op jit(solution)/shard_map/ppermute | solution.py:650
  244.5 24.7 %collective-permute-start.54 = (bf16[2,256,128]{2,1,0:T(8,128)(2,1)}, bf16[2,256,128]{2,1,0:T(8,128)(2,1)S(1)}, u32[]{:S(2)}, u32[]{:S(2)}) collective-permute-start(bf16[2,256,128]{2,1,0:T(8,128)(2,1)} %get-tuple-element.372), channel_id=1, source_target_pairs={{0,16},{8,24},{16,0},{24,8},{1,17},{9,25},{17,1},{25,9},{2,18},{10... | collective-permute-start | bytes 393224 | tf_op jit(solution)/shard_map/ppermute | solution.py:650
  245.8 23.5 %collective-permute-start.55 = (bf16[2,256,128]{2,1,0:T(8,128)(2,1)}, bf16[2,256,128]{2,1,0:T(8,128)(2,1)}, u32[]{:S(2)}, u32[]{:S(2)}) collective-permute-start(bf16[2,256,128]{2,1,0:T(8,128)(2,1)} %get-tuple-element.373), channel_id=1, source_target_pairs={{0,24},{8,16},{16,8},{24,0},{1,25},{9,17},{17,9},{25,1},{2,26},{10... | collective-permute-start | bytes 393224 | tf_op jit(solution)/shard_map/ppermute | solution.py:650
  248.0 24.9 %collective-permute-start.56 = (bf16[2,256,1024]{2,1,0:T(8,128)(2,1)}, bf16[2,256,1024]{2,1,0:T(8,128)(2,1)S(1)}, u32[]{:S(2)}, u32[]{:S(2)}) collective-permute-start(bf16[2,256,1024]{2,1,0:T(8,128)(2,1)} %pad_maximum_fusion.1), channel_id=1, source_target_pairs={{0,8},{1,17},{8,0},{9,25},{16,24},{17,1},{24,16},{25,9},{2,10},{3,... | collective-permute-start | bytes 3145736 | tf_op jit(solution)/shard_map/ppermute | solution.py:882
  269.2 116.6 %reduce-scatter.6.cloned.1.call-start = ((), (), s32[]{:S(2)}) async-start(), calls=%async_computation.6 | async-start | bytes 2359296 | tf_op jit(solution)/shard_map/reduce_scatter | solution.py:912
  280.2 36.8 %collective-permute-start.58 = (bf16[2,256,1024]{2,1,0:T(8,128)(2,1)S(1)}, bf16[2,256,1024]{2,1,0:T(8,128)(2,1)}, u32[]{:S(2)}, u32[]{:S(2)}) collective-permute-start(bf16[2,256,1024]{2,1,0:T(8,128)(2,1)S(1)} %pad_maximum_fusion.2), channel_id=1, source_target_pairs={{0,8},{8,0},{16,24},{24,16},{1,9},{9,1},{17,25},{25,17},{2,10},{10... | collective-permute-start | bytes 3145736 | tf_op jit(solution)/shard_map/ppermute | solution.py:650
  280.8 37.0 %collective-permute-start.59 = (bf16[2,256,1024]{2,1,0:T(8,128)(2,1)S(1)}, bf16[2,256,1024]{2,1,0:T(8,128)(2,1)}, u32[]{:S(2)}, u32[]{:S(2)}) collective-permute-start(bf16[2,256,1024]{2,1,0:T(8,128)(2,1)S(1)} %pad_maximum_fusion.3), channel_id=1, source_target_pairs={{0,16},{8,24},{16,0},{24,8},{1,17},{9,25},{17,1},{25,9},{2,18},{10... | collective-permute-start | bytes 3145736 | tf_op jit(solution)/shard_map/ppermute | solution.py:650
  282.2 34.8 %collective-permute-start.60 = (bf16[256,1024]{1,0:T(8,128)(2,1)}, bf16[256,1024]{1,0:T(8,128)(2,1)}, u32[]{:S(2)}, u32[]{:S(2)}) collective-permute-start(bf16[256,1024]{1,0:T(8,128)(2,1)} %get-tuple-element.393), channel_id=1, source_target_pairs={{0,24},{8,16},{16,8},{24,0},{1,25},{9,17},{17,9},{25,1},{2,26},{10... | collective-permute-start | bytes 1572872 | tf_op jit(solution)/shard_map/ppermute | solution.py:650
  323.9 12.4 %collective-permute-start.66 = (bf16[2,256,128]{2,1,0:T(8,128)(2,1)}, bf16[2,256,128]{2,1,0:T(8,128)(2,1)S(1)}, u32[]{:S(2)}, u32[]{:S(2)}) collective-permute-start(bf16[2,256,128]{2,1,0:T(8,128)(2,1)} %get-tuple-element.418), channel_id=1, source_target_pairs={{0,8},{8,0},{16,24},{24,16},{1,9},{9,1},{17,25},{25,17},{2,10},{10... | collective-permute-start | bytes 393224 | tf_op jit(solution)/shard_map/ppermute | solution.py:650
  325.4 10.9 %collective-permute-start.67 = (bf16[2,256,128]{2,1,0:T(8,128)(2,1)}, bf16[2,256,128]{2,1,0:T(8,128)(2,1)S(1)}, u32[]{:S(2)}, u32[]{:S(2)}) collective-permute-start(bf16[2,256,128]{2,1,0:T(8,128)(2,1)} %get-tuple-element.419), channel_id=1, source_target_pairs={{0,16},{8,24},{16,0},{24,8},{1,17},{9,25},{17,1},{25,9},{2,18},{10... | collective-permute-start | bytes 393224 | tf_op jit(solution)/shard_map/ppermute | solution.py:650
  325.9 10.4 %collective-permute-start.68 = (bf16[2,256,128]{2,1,0:T(8,128)(2,1)}, bf16[2,256,128]{2,1,0:T(8,128)(2,1)}, u32[]{:S(2)}, u32[]{:S(2)}) collective-permute-start(bf16[2,256,128]{2,1,0:T(8,128)(2,1)} %get-tuple-element.420), channel_id=1, source_target_pairs={{0,24},{8,16},{16,8},{24,0},{1,25},{9,17},{17,9},{25,1},{2,26},{10... | collective-permute-start | bytes 393224 | tf_op jit(solution)/shard_map/ppermute | solution.py:650
  336.3 72.5 %reduce-scatter.8.cloned.1.call-start = ((), (), s32[]{:S(2)}) async-start(), calls=%async_computation.7 | async-start | bytes 983040 | tf_op jit(solution)/shard_map/reduce_scatter | solution.py:930
  340.4 45.2 %collective-permute-start.63 = (bf16[256,1024]{1,0:T(8,128)(2,1)}, bf16[256,1024]{1,0:T(8,128)(2,1)S(1)}, u32[]{:S(2)}, u32[]{:S(2)}) collective-permute-start(bf16[256,1024]{1,0:T(8,128)(2,1)} %get-tuple-element.423), channel_id=1, source_target_pairs={{0,8},{8,0},{16,24},{24,16},{1,9},{9,1},{17,25},{25,17},{2,10},{10... | collective-permute-start | bytes 1572872 | tf_op jit(solution)/shard_map/ppermute | solution.py:650
  341.9 43.8 %collective-permute-start.64 = (bf16[256,1024]{1,0:T(8,128)(2,1)}, bf16[256,1024]{1,0:T(8,128)(2,1)}, u32[]{:S(2)}, u32[]{:S(2)}) collective-permute-start(bf16[256,1024]{1,0:T(8,128)(2,1)} %get-tuple-element.424), channel_id=1, source_target_pairs={{0,16},{8,24},{16,0},{24,8},{1,17},{9,25},{17,1},{25,9},{2,18},{10... | collective-permute-start | bytes 1572872 | tf_op jit(solution)/shard_map/ppermute | solution.py:650
  342.4 43.2 %collective-permute-start.65 = (bf16[256,1024]{1,0:T(8,128)(2,1)}, bf16[256,1024]{1,0:T(8,128)(2,1)}, u32[]{:S(2)}, u32[]{:S(2)}) collective-permute-start(bf16[256,1024]{1,0:T(8,128)(2,1)} %get-tuple-element.425), channel_id=1, source_target_pairs={{0,24},{8,16},{16,8},{24,0},{1,25},{9,17},{17,9},{25,1},{2,26},{10... | collective-permute-start | bytes 1572872 | tf_op jit(solution)/shard_map/ppermute | solution.py:650
  345.8 39.9 %collective-permute-start.71 = (bf16[384,1024]{1,0:T(8,128)(2,1)}, bf16[384,1024]{1,0:T(8,128)(2,1)}, u32[]{:S(2)}, u32[]{:S(2)}) collective-permute-start(bf16[384,1024]{1,0:T(8,128)(2,1)} %pad_maximum_fusion.5.refs_0_), channel_id=1, source_target_pairs={{0,8},{8,0},{16,24},{24,16},{1,9},{9,1},{17,25},{25,17},{2,10},{10... | collective-permute-start | bytes 2359304 | tf_op jit(solution)/shard_map/ppermute | solution.py:650
  347.3 38.4 %collective-permute-start.72 = (bf16[384,1024]{1,0:T(8,128)(2,1)}, bf16[384,1024]{1,0:T(8,128)(2,1)}, u32[]{:S(2)}, u32[]{:S(2)}) collective-permute-start(bf16[384,1024]{1,0:T(8,128)(2,1)} %pad_maximum_fusion.5.refs_0_), channel_id=1, source_target_pairs={{0,16},{8,24},{16,0},{24,8},{1,17},{9,25},{17,1},{25,9},{2,18},{10... | collective-permute-start | bytes 2359304 | tf_op jit(solution)/shard_map/ppermute | solution.py:650
  388.2 12.3 %collective-permute-start.74 = (bf16[384,1024]{1,0:T(8,128)(2,1)}, bf16[384,1024]{1,0:T(8,128)(2,1)}, u32[]{:S(2)}, u32[]{:S(2)}) collective-permute-start(bf16[384,1024]{1,0:T(8,128)(2,1)} %broadcast_select_fusion.2), channel_id=1, source_target_pairs={{0,8},{1,17},{8,0},{9,25},{16,24},{17,1},{24,16},{25,9},{2,10},{3,... | collective-permute-start | bytes 2359304 | tf_op jit(solution)/shard_map/ppermute | solution.py:676
  400.5 15.2 %collective-permute-start.75 = (bf16[256,1024]{1,0:T(8,128)(2,1)}, bf16[256,1024]{1,0:T(8,128)(2,1)}, u32[]{:S(2)}, u32[]{:S(2)}) collective-permute-start(bf16[256,1024]{1,0:T(8,128)(2,1)} %get-tuple-element.457), channel_id=1, source_target_pairs={{0,8},{8,0},{16,24},{24,16},{1,9},{9,1},{17,25},{25,17},{2,10},{10... | collective-permute-start | bytes 1572872 | tf_op jit(solution)/shard_map/ppermute | solution.py:650
  401.9 24.4 %collective-permute-start.76 = (bf16[256,1024]{1,0:T(8,128)(2,1)}, bf16[256,1024]{1,0:T(8,128)(2,1)}, u32[]{:S(2)}, u32[]{:S(2)}) collective-permute-start(bf16[256,1024]{1,0:T(8,128)(2,1)} %get-tuple-element.458), channel_id=1, source_target_pairs={{0,16},{8,24},{16,0},{24,8},{1,17},{9,25},{17,1},{25,9},{2,18},{10... | collective-permute-start | bytes 1572872 | tf_op jit(solution)/shard_map/ppermute | solution.py:650
  402.6 23.8 %collective-permute-start.77 = (bf16[256,1024]{1,0:T(8,128)(2,1)}, bf16[256,1024]{1,0:T(8,128)(2,1)}, u32[]{:S(2)}, u32[]{:S(2)}) collective-permute-start(bf16[256,1024]{1,0:T(8,128)(2,1)} %get-tuple-element.459), channel_id=1, source_target_pairs={{0,24},{8,16},{16,8},{24,0},{1,25},{9,17},{17,9},{25,1},{2,26},{10... | collective-permute-start | bytes 1572872 | tf_op jit(solution)/shard_map/ppermute | solution.py:650
  411.2 21.1 %collective-permute-start.61 = (bf16[256,1024]{1,0:T(8,128)(2,1)S(1)}, bf16[256,1024]{1,0:T(8,128)(2,1)S(1)}, u32[]{:S(2)}, u32[]{:S(2)}) collective-permute-start(bf16[256,1024]{1,0:T(8,128)(2,1)S(1)} %get-tuple-element.525), channel_id=1, source_target_pairs={{0,1},{1,0},{2,3},{3,2},{4,5},{5,4},{6,7},{7,6},{8,9},{9,8},{10,11... | collective-permute-start | bytes 1572872 | tf_op jit(solution)/shard_map/ppermute | solution.py:654
  432.2 11.9 %collective-permute-start.79 = (f32[256,1024]{1,0:T(8,128)S(1)}, f32[256,1024]{1,0:T(8,128)S(1)}, u32[]{:S(2)}, u32[]{:S(2)}) collective-permute-start(f32[256,1024]{1,0:T(8,128)S(1)} %get-tuple-element.521), channel_id=1, source_target_pairs={{0,1},{1,0},{2,3},{3,2},{4,5},{5,4},{6,7},{7,6},{8,9},{9,8},{10,11... | collective-permute-start | bytes 3145736 | tf_op jit(solution)/shard_map/ppermute | solution.py:654
  433.4 13.6 %collective-permute-start.80 = (bf16[128,1792]{1,0:T(8,128)(2,1)}, bf16[128,1792]{1,0:T(8,128)(2,1)}, u32[]{:S(2)}, u32[]{:S(2)}) collective-permute-start(bf16[128,1792]{1,0:T(8,128)(2,1)} %pad_maximum_fusion.6.refs_0_), channel_id=1, source_target_pairs={{0,8},{8,0},{16,24},{24,16},{1,9},{9,1},{17,25},{25,17},{2,10},{10... | collective-permute-start | bytes 1376264 | tf_op jit(solution)/shard_map/ppermute | solution.py:650
  434.1 22.8 %collective-permute-start.81 = (bf16[128,1792]{1,0:T(8,128)(2,1)}, bf16[128,1792]{1,0:T(8,128)(2,1)}, u32[]{:S(2)}, u32[]{:S(2)}) collective-permute-start(bf16[128,1792]{1,0:T(8,128)(2,1)} %pad_maximum_fusion.6.refs_0_), channel_id=1, source_target_pairs={{0,16},{8,24},{16,0},{24,8},{1,17},{9,25},{17,1},{25,9},{2,18},{10... | collective-permute-start | bytes 1376264 | tf_op jit(solution)/shard_map/ppermute | solution.py:650
  435.5 21.3 %collective-permute-start.82 = (bf16[128,1792]{1,0:T(8,128)(2,1)}, bf16[128,1792]{1,0:T(8,128)(2,1)}, u32[]{:S(2)}, u32[]{:S(2)}) collective-permute-start(bf16[128,1792]{1,0:T(8,128)(2,1)} %pad_maximum_fusion.6.refs_0_), channel_id=1, source_target_pairs={{0,24},{8,16},{16,8},{24,0},{1,25},{9,17},{17,9},{25,1},{2,26},{10... | collective-permute-start | bytes 1376264 | tf_op jit(solution)/shard_map/ppermute | solution.py:650
  (75 other events, 543.0 us)
Sparse Core Ops, SparseCore 0:
  29.1 27.2 all-gather.4
  58.0 28.5 all-gather.6
  104.5 64.7 all-gather.8
  269.3 60.4 reduce-scatter.3
  336.4 35.9 reduce-scatter.5
  386.0 22.8 reduce-scatter.7
